TPU v7x, 32 devices: a whole 2x2x4 slice. The times are simulated.
32 devices in a mesh: coil: 4 (over z), slab: 8 (over y, x, core).
Axes of the slice: x: 2, y: 2, z: 4, core: 2. Of those that a mesh axis runs over, the one named last changes fastest.
Arguments:
- image: float32 [2, 256, 256, 128], P(None, 'slab'), may hold values from -6 to 6
- sensitivity: bfloat16 [16, 2, 256, 256, 128], P('coil', None, 'slab'), may hold values from -5 to 5
- blocks: bfloat16 [8, 24, 128, 2048], P('slab'), may hold values from -0.125 to 0.125
- samples: bfloat16 [8, 24, 128, 16, 2, 128], P('slab', None, None, 'coil'), may hold values from -6 to 6
- offsets: int32 [8, 24], P('slab'), may hold values from 0 to 192
- counts: int32 [8], P('slab'), may hold values from 1 to 24, as said below
- auxiliary: float32 [2, 256, 256, 128], P(None, 'slab', 'coil'), may hold values from -4 to 4
- scaled_dual: float32 [2, 256, 256, 128], P(None, 'slab', 'coil'), may hold values from -3 to 3
Outputs:
- image_next: float32 [2, 256, 256, 128], P(None, 'slab', 'coil')
- auxiliary_next: float32 [2, 256, 256, 128], P(None, 'slab', 'coil')
- dual_next: float32 [2, 256, 256, 128], P(None, 'slab', 'coil')
Inputs may be any that keep to these rules, and one draw needn't show every extreme that they name: Each tile's live groups are its first counts slots; some tile holds 24 live groups.
All inputs are finite; a program needn't handle non-finite values.
Results may differ from a plain program's by a relative error of at most 0.014.
Values may be sent and summed in bfloat16 or wider, within the bound.
A program may use at most 192 MiB of HBM per device.

v0:
```python
import functools
import math

import jax
import jax.numpy as jnp
import numpy as np
from jax import lax
from jax.experimental import pallas as pl
from jax.experimental.pallas import tpu as pltpu
from jax.sharding import PartitionSpec as P

step_size = 0.5
penalty = 1.0
threshold = 0.3
VMEM_LIMIT = 62 * 1024 * 1024
F32 = jnp.float32
BF16 = jnp.bfloat16


def complex_table(length, inverse):
    index = np.arange(length, dtype=np.int64)
    angle = (index[:, None] * index[None, :] % length).astype(np.float64) * (2.0 * math.pi / length)
    factor = 1.0 / math.sqrt(length)
    re = np.cos(angle) * factor
    im = -np.sin(angle) * factor
    if inverse:
        whole = np.block([[re, im], [-im, re]])
    else:
        whole = np.block([[re, -im], [im, re]])
    return jnp.asarray(whole.astype(np.float32)).astype(BF16)


def params(**extra):
    return pltpu.CompilerParams(vmem_limit_bytes=VMEM_LIMIT, **extra)


def once(shape):
    return pl.BlockSpec(shape, lambda *i: (0,) * len(shape), pipeline_mode=pl.Buffered(1))


def cost(flops, nbytes):
    return pl.CostEstimate(flops=int(flops), bytes_accessed=int(nbytes), transcendentals=0)


def pitch(rows):
    tiles = -(-rows // 8)
    return 8 * (tiles + 1 - tiles % 2)


def gather_rows(ref, row, size, parts_n):
    pieces = []
    for p in range(2):
        for s in range(parts_n):
            pieces.append(ref[s, 0, p, pl.ds(row, size), :])
    return jnp.concatenate(pieces, axis=0)


def forward_kernel(n, kl, xl, table, image, sens, out, flat):
    length = image.shape[2]

    def pair(i, carry):
        columns = []
        for h in range(2):
            x = 2 * i + h
            sr = sens[0, 0, x].astype(F32)
            si = sens[0, 1, x].astype(F32)
            ir = image[0, x]
            ii = image[1, x]
            columns.append(
                jnp.concatenate(
                    [(sr * ir - si * ii).astype(BF16), (sr * ii + si * ir).astype(BF16)], axis=0
                )
            )
        both = jnp.concatenate(columns, axis=1)
        half = jnp.dot(table[...], both, preferred_element_type=F32)
        depth = half.shape[1] // 2
        for h in range(2):
            flat[pl.ds(2 * i + h, 2 * length, stride=pitch(xl)), :] = half[:, h * depth : (h + 1) * depth]
        return carry

    lax.fori_loop(0, xl // 2, pair, 0)
    for p in range(2):
        for d in range(n):

            def settle(k, carry):
                base = pl.multiple_of(((p * n + d) * kl + 2 * k) * pitch(xl), 8)
                rows = [flat[pl.ds(base + h * pitch(xl), xl), :] for h in range(2)]
                target = pl.ds(pl.multiple_of(2 * k * xl, 2 * xl), 2 * xl)
                out[d, 0, p, target, :] = jnp.concatenate(rows, axis=0).astype(BF16)
                return carry

            lax.fori_loop(0, kl // 2, settle, 0, unroll=4)


def forward_call(table, image, sensitivity, first, n, kl):
    _, _, xl, length, depth = sensitivity.shape
    return pl.pallas_call(
        functools.partial(forward_kernel, n, kl, xl),
        grid=(1,),
        in_specs=[
            once(table.shape),
            once(image.shape),
            pl.BlockSpec((1, 2, xl, length, depth), lambda i: (first, 0, 0, 0, 0)),
        ],
        out_specs=pl.BlockSpec((n, 1, 2, kl * xl, depth), lambda i: (0, 0, 0, 0, 0)),
        out_shape=jax.ShapeDtypeStruct((n, 1, 2, kl * xl, depth), BF16),
        scratch_shapes=[pltpu.VMEM(((2 * length + 1) * pitch(xl), depth), F32)],
        compiler_params=params(),
        cost_estimate=cost(8 * length * length * xl * depth, 12 * xl * length * depth),
        name="forward",
    )(table, image, sensitivity)


def tile_kernel(n, kl, xl, win, offsets, counts, fwd, inv, piece, blocks, samples, out, total, kspace, weights, sem, *wide):
    fetch = pltpu.make_async_copy(blocks.at[0], weights, sem)
    fetch.start()
    length = n * xl
    depth = piece.shape[-1]
    if wide:
        source = wide[0]
        for p in range(2):
            for s in range(n):
                source[s, 0, p] = piece[s, 0, p].astype(F32)
    else:
        source = piece

    def to_kspace(i, carry):
        columns = []
        for h in range(2):
            row = pl.multiple_of((2 * i + h) * xl, xl)
            columns.append(gather_rows(source, row, xl, n).astype(BF16))
        spec = jnp.dot(fwd[...], jnp.concatenate(columns, axis=1), preferred_element_type=F32)
        for h in range(2):
            for p in range(2):
                total[p, pl.ds(2 * i + h, length, stride=pitch(kl)), :] = spec[
                    p * length : (p + 1) * length, h * depth : (h + 1) * depth
                ]
        return carry

    lax.fori_loop(0, kl // 2, to_kspace, 0)

    def settle(i, carry):
        rows = pl.ds(pl.multiple_of(i * pitch(kl), 8), kl)
        target = pl.ds(pl.multiple_of(i * kl, kl), kl)
        for p in range(2):
            kspace[target, p * depth : (p + 1) * depth] = total[p, rows, :].astype(kspace.dtype)
            total[p, rows, :] = jnp.zeros((kl, depth), F32)
        return carry

    lax.fori_loop(0, length, settle, 0, unroll=8)
    fetch.wait()
    cells = win * kl
    chunk = min(cells, 512)

    def group(slot, carry):
        first = offsets[0, slot]
        start = pl.multiple_of(first * kl, kl)
        window = kspace[pl.ds(start, cells), :].astype(BF16)
        predicted = jnp.dot(weights[slot], window, preferred_element_type=F32)
        misfit = (predicted - samples[slot].astype(F32)).astype(BF16)
        for c in range(0, cells, chunk):
            update = lax.dot_general(
                weights[slot, :, c : c + chunk],
                misfit,
                (((0,), (0,)), ((), ())),
                preferred_element_type=F32,
            )
            for k in range(chunk // kl):
                rows = pl.ds(pl.multiple_of((first + c // kl + k) * pitch(kl), 8), kl)
                for p in range(2):
                    total[p, rows, :] += update[k * kl : (k + 1) * kl, p * depth : (p + 1) * depth]
        return carry

    lax.fori_loop(0, counts[0], group, 0)

    def to_rows(i, carry):
        columns = []
        for h in range(2):
            columns.append(
                jnp.concatenate(
                    [total[p, pl.ds(2 * i + h, length, stride=pitch(kl)), :].astype(BF16) for p in range(2)], axis=0
                )
            )
        back = jnp.dot(inv[...], jnp.concatenate(columns, axis=1), preferred_element_type=F32)
        for h in range(2):
            for p in range(2):
                total[p, pl.ds(2 * i + h, length, stride=pitch(kl)), :] = back[
                    p * length : (p + 1) * length, h * depth : (h + 1) * depth
                ]
        return carry

    lax.fori_loop(0, kl // 2, to_rows, 0)
    for p in range(2):
        for d in range(n):

            def leave(k, carry):
                base = pl.multiple_of((d * xl + 2 * k) * pitch(kl), 8)
                rows = [total[p, pl.ds(base + h * pitch(kl), kl), :] for h in range(2)]
                target = pl.ds(pl.multiple_of(2 * k * kl, 2 * kl), 2 * kl)
                out[d, 0, p, target, :] = jnp.concatenate(rows, axis=0).astype(BF16)
                return carry

            lax.fori_loop(0, xl // 2, leave, 0, unroll=4)


def tile_call(fwd, inv, piece, blocks, samples, offsets, counts, coil, n, kl, xl):
    depth = piece.shape[-1]
    _, slots, psize, cells = blocks.shape
    length = n * xl
    narrow = kl % 16 == 0 and xl % 16 == 0
    scratch = [
        pltpu.VMEM((2, (length + 1) * pitch(kl), depth), F32),
        pltpu.VMEM((length * kl, 2 * depth), BF16 if narrow else F32),
        pltpu.VMEM(blocks.shape[1:], BF16),
        pltpu.SemaphoreType.DMA,
    ]
    if not narrow:
        scratch.append(pltpu.VMEM(piece.shape, F32))
    smem = pl.BlockSpec(memory_space=pltpu.SMEM)
    return pl.pallas_call(
        functools.partial(tile_kernel, n, kl, xl, cells // kl),
        grid=(1,),
        in_specs=[
            smem,
            smem,
            once(fwd.shape),
            once(inv.shape),
            once(piece.shape),
            pl.BlockSpec(memory_space=pl.ANY),
            pl.BlockSpec((slots, psize, 2 * depth), lambda i: (0, 0, coil), pipeline_mode=pl.Buffered(1)),
        ],
        out_specs=pl.BlockSpec(piece.shape, lambda i: (0, 0, 0, 0, 0)),
        out_shape=jax.ShapeDtypeStruct(piece.shape, BF16),
        scratch_shapes=scratch,
        compiler_params=params(),
        cost_estimate=cost(
            16 * length * length * kl * depth + 8 * slots * psize * cells * depth,
            8 * length * kl * depth + 2 * blocks.size,
        ),
        name="tile",
    )(offsets, counts, fwd, inv, piece, blocks, samples)


def finish_kernel(n, shares, kl, xl, chunks, sent, table, sens, *refs):
    coils = sens.shape[0]
    backs, refs = refs[:coils], refs[coils:]
    out, landing, sens_v, grad, got, recv, send, local, grad_recv, grad_send, *wide = refs
    ready = coils - sent
    length = n * kl
    depth = landing.shape[-1]
    share = length // shares
    rows = xl // chunks
    band = rows * kl
    me = lax.axis_index("slab")
    mine = lax.axis_index("coil")

    barrier = pltpu.get_barrier_semaphore()

    def greet(off, carry):
        pl.semaphore_signal(
            barrier, inc=1, device_id={"slab": lax.rem(me + off, n)}, device_id_type=pl.DeviceIdType.MESH
        )
        return carry

    lax.fori_loop(1, n, greet, 0)
    for off in range(1, shares):
        pl.semaphore_signal(
            barrier, inc=1, device_id={"coil": lax.rem(mine + off, shares)}, device_id_type=pl.DeviceIdType.MESH
        )
    pl.semaphore_wait(barrier, n - 1 + shares - 1)

    def send_band(j, carry):
        where = pl.ds(pl.multiple_of(j * band, band), band)
        for k in range(ready, coils):

            def one(off, carry):
                target = lax.rem(me + off, n)
                pltpu.make_async_remote_copy(
                    src_ref=backs[k].at[target, 0, :, where, :],
                    dst_ref=landing.at[k, me, :, where, :],
                    send_sem=send,
                    recv_sem=recv.at[j],
                    device_id={"slab": target},
                    device_id_type=pl.DeviceIdType.MESH,
                ).start()
                return carry

            lax.fori_loop(1, n, one, 0)
        return carry

    lax.fori_loop(0, chunks, send_band, 0)
    copies = []
    for k in range(coils):
        if k < ready:
            copies.append(pltpu.make_async_copy(backs[k].at[:, 0], landing.at[k], local.at[2 * k]))
        else:
            copies.append(pltpu.make_async_copy(backs[k].at[me, 0], landing.at[k, me], local.at[2 * k]))
        copies.append(pltpu.make_async_copy(sens.at[k], sens_v.at[k], local.at[2 * k + 1]))
    for copy in copies:
        copy.start()
    for copy in copies:
        copy.wait()

    def do_band(j, carry):
        where = pl.ds(pl.multiple_of(j * band, band), band)
        arrived = landing.at[ready:coils, 0 : n - 1, :, where, :]
        pltpu.make_async_copy(arrived, arrived, recv.at[j]).wait()
        if wide:
            for k in range(coils):
                for s in range(n):
                    for p in range(2):
                        wide[0][k, s, p] = landing[k, s, p, where, :].astype(F32)

        def columns_of(k, i):
            pieces = []
            for p in range(2):
                for s in range(n):
                    if wide:
                        pieces.append(wide[0][k, s, p, pl.ds(pl.multiple_of(i * kl, kl), kl), :])
                    else:
                        row = pl.multiple_of((j * rows + i) * kl, kl)
                        pieces.append(landing[k, s, p, pl.ds(row, kl), :])
            return jnp.concatenate(pieces, axis=0).astype(BF16)

        def pair(i, carry):
            total = [[None, None], [None, None]]
            for k in range(coils):
                both = jnp.concatenate([columns_of(k, 2 * i), columns_of(k, 2 * i + 1)], axis=1)
                adj = jnp.dot(table[...], both, preferred_element_type=F32)
                adj = adj.astype(BF16).astype(F32)
                for h in range(2):
                    x = j * rows + 2 * i + h
                    ar = adj[:length, h * depth : (h + 1) * depth]
                    ai = adj[length:, h * depth : (h + 1) * depth]
                    sr = sens_v[k, 0, x].astype(F32)
                    si = sens_v[k, 1, x].astype(F32)
                    re = sr * ar + si * ai
                    im = sr * ai - si * ar
                    total[h] = [re, im] if k == 0 else [total[h][0] + re, total[h][1] + im]
            for h in range(2):
                x = j * rows + 2 * i + h
                for p in range(2):
                    for q in range(shares):
                        grad[q, p, x] = total[h][p][q * share : (q + 1) * share].astype(BF16)
            return carry

        lax.fori_loop(0, rows // 2, pair, 0)
        lines = pl.ds(j * rows, rows)
        for off in range(1, shares):
            target = lax.rem(mine + off, shares)
            pltpu.make_async_remote_copy(
                src_ref=grad.at[target, :, lines],
                dst_ref=got.at[mine, :, lines],
                send_sem=grad_send,
                recv_sem=grad_recv.at[j],
                device_id={"coil": target},
                device_id_type=pl.DeviceIdType.MESH,
            ).start()
        return carry

    lax.fori_loop(0, chunks, do_band, 0)

    def add_band(j, carry):
        arrived = got.at[0 : shares - 1, :, pl.ds(j * rows, rows)]
        pltpu.make_async_copy(arrived, arrived, grad_recv.at[j]).wait()

        def line(i, carry):
            x = j * rows + i
            for p in range(2):
                value = grad[mine, p, x].astype(F32)
                for off in range(1, shares):
                    value += got[lax.rem(mine + off, shares), p, x].astype(F32)
                out[p, x] = value
            return carry

        lax.fori_loop(0, rows, line, 0)
        return carry

    lax.fori_loop(0, chunks, add_band, 0)
    gone = landing.at[ready:coils, 0 : n - 1]
    pltpu.make_async_copy(gone, gone, send).wait()
    gone = got.at[0 : shares - 1]
    pltpu.make_async_copy(gone, gone, grad_send).wait()


def finish_call(table, backs, sent, sensitivity, shares, n, kl):
    coils, _, xl, length, depth = sensitivity.shape
    chunks = xl // 4 if xl % 4 == 0 else 1
    rows = xl // chunks
    share = length // shares
    anywhere = pl.BlockSpec(memory_space=pl.ANY)
    vmem = pl.BlockSpec(memory_space=pltpu.VMEM)
    scratch = [
        pltpu.VMEM((coils, n, 2, xl * kl, depth), BF16),
        pltpu.VMEM(sensitivity.shape, BF16),
        pltpu.VMEM((shares, 2, xl, share, depth), BF16),
        pltpu.VMEM((shares, 2, xl, share, depth), BF16),
        pltpu.SemaphoreType.DMA((chunks,)),
        pltpu.SemaphoreType.DMA,
        pltpu.SemaphoreType.DMA((2 * coils,)),
        pltpu.SemaphoreType.DMA((chunks,)),
        pltpu.SemaphoreType.DMA,
    ]
    if kl % 16:
        scratch.append(pltpu.VMEM((coils, n, 2, rows * kl, depth), F32))
    return pl.pallas_call(
        functools.partial(finish_kernel, n, shares, kl, xl, chunks, sent),
        in_specs=[vmem, anywhere] + [anywhere] * coils,
        out_specs=vmem,
        out_shape=jax.ShapeDtypeStruct((2, xl, share, depth), F32),
        scratch_shapes=scratch,
        compiler_params=params(collective_id=0, has_side_effects=True),
        name="finish",
    )(table, sensitivity, *backs)


def haar_rows(first, second):
    even = lax.broadcasted_iota(jnp.int32, first.shape, 0) % 2 == 0
    rows = first.shape[0]

    def along(v):
        after = pltpu.roll(v, rows - 1, 0)
        ahead = pltpu.roll(v, 1, 0)
        return jnp.where(even, v + after, ahead - v) * 0.5

    return along(first + second), along(first - second)


def update_kernel(where, image, gradient, auxiliary, dual, image_out, aux_out, dual_out):
    del where
    rows = image.shape[1]
    for m in range(0, rows, 2):
        coeffs = []
        for p in range(2):
            target = haar_rows(
                auxiliary[p, m] - dual[p, m], auxiliary[p, m + 1] - dual[p, m + 1]
            )
            following = []
            for h in range(2):
                current = image[p, m + h]
                value = current - step_size * (
                    gradient[p, m + h].astype(F32) + penalty * (current - target[h])
                )
                image_out[p, m + h] = value
                following.append(value)
            spread = haar_rows(*following)
            coeffs.append([spread[h] + dual[p, m + h] for h in range(2)])
        for h in range(2):
            re, im = coeffs[0][h], coeffs[1][h]
            magnitude = jnp.sqrt(re * re + im * im)
            factor = jnp.maximum(1.0 - threshold / jnp.maximum(magnitude, threshold), 0.0)
            for p, value in enumerate((re, im)):
                kept = value * factor
                aux_out[p, m + h] = kept
                dual_out[p, m + h] = value - kept


def update_call(image, gradient, auxiliary, dual, position):
    _, xl, share, depth = auxiliary.shape
    rows = 8 if xl % 8 == 0 else 2
    block = (2, rows, share, depth)
    plain = pl.BlockSpec(block, lambda i, w: (0, i, 0, 0))
    shape = jax.ShapeDtypeStruct(auxiliary.shape, F32)
    return pl.pallas_call(
        update_kernel,
        grid_spec=pltpu.PrefetchScalarGridSpec(
            num_scalar_prefetch=1,
            grid=(xl // rows,),
            in_specs=[pl.BlockSpec(block, lambda i, w: (0, i, w[0], 0)), plain, plain, plain],
            out_specs=[plain, plain, plain],
        ),
        out_shape=[shape, shape, shape],
        compiler_params=params(),
        name="update",
    )(position, image, gradient, auxiliary, dual)


def body(image, sensitivity, blocks, samples, offsets, counts, auxiliary, scaled_dual):
    coils, _, xl, length_y, depth = sensitivity.shape
    n = lax.axis_size("slab")
    shares = lax.axis_size("coil")
    kl = length_y // n
    y_fwd = complex_table(length_y, False)
    y_inv = complex_table(length_y, True)
    x_fwd = complex_table(n * xl, False)
    x_inv = complex_table(n * xl, True)
    flat_samples = samples.reshape(samples.shape[1], samples.shape[2], -1)

    def swap(values):
        return lax.all_to_all(values, "slab", split_axis=0, concat_axis=0, tiled=True)

    def tile_of(piece, c):
        return tile_call(x_fwd, x_inv, piece, blocks, flat_samples, offsets, counts, c, n, kl, xl)

    halves = [forward_call(y_fwd, image, sensitivity, c, n, kl) for c in range(coils)]
    tied = lax.optimization_barrier((*halves[1:], flat_samples))
    halves, flat_samples = halves[:1] + list(tied[:-1]), tied[-1]
    pieces, tiles = [], []
    for c in range(coils):
        half = halves[c]
        if c >= 2:
            half, tiles[c - 2] = lax.optimization_barrier((half, tiles[c - 2]))
        pieces.append(swap(half))
        if c >= 1:
            tiles.append(tile_of(pieces[c - 1], c - 1))
    early = 1 if coils >= 3 else 0
    backs = []
    if early:
        held, tiles[-1] = lax.optimization_barrier((tiles[0], tiles[-1]))
        backs.append(swap(held))
    tiles.append(tile_of(pieces[-1], coils - 1))
    backs += tiles[early:]
    gradient = finish_call(y_inv, backs, coils - early, sensitivity, shares, n, kl)
    position = lax.axis_index("coil").astype(jnp.int32).reshape(1)
    return tuple(update_call(image, gradient, auxiliary, scaled_dual, position))


def solution(mesh):
    return jax.shard_map(
        body,
        mesh=mesh,
        in_specs=(
            P(None, "slab", None, None),
            P("coil", None, "slab", None, None),
            P("slab", None, None, None),
            P("slab", None, None, "coil", None, None),
            P("slab", None),
            P("slab"),
            P(None, "slab", "coil", None),
            P(None, "slab", "coil", None),
        ),
        out_specs=(
            P(None, "slab", "coil", None),
            P(None, "slab", "coil", None),
            P(None, "slab", "coil", None),
        ),
        check_vma=False,
    )
```

profile of v0, /device:TPU:9, one launch (start us, length us, event | category | flops | bytes accessed | tf_op | source)
XLA Modules:
  0.0 447.1 jit_solution(4540020138567831050)
XLA Ops:
  0.6 12.9 %forward.7 = bf16[8,1,2,1024,128]{4,3,2,1,0:T(8,128)(2,1)} custom-call(bf16[512,512]{1,0:T(8,128)(2,1)} %constant.16.table.fwd, f32[2,32,256,128]{3,2,1,0:T(8,128)} %image.9, bf16[4,2,32,256,128]{4,3,2,1,0:T(8,128)(2,1)} %sens.9), custom_call_target="tpu_custom_call" | custom-call | flops 2147483648 | bytes 12582912 | tf_op jit(solution)/shard_map/forward/pallas_call | solution.py:97
  13.6 5.1 %all-to-all-start = ((bf16[8,1,2,1024,128]{4,3,2,1,0:T(8,128)(2,1)}), bf16[8,1,2,1024,128]{4,3,2,1,0:T(8,128)(2,1)}, u32[]{:S(2)}, u32[]{:S(2)}) async-start(bf16[8,1,2,1024,128]{4,3,2,1,0:T(8,128)(2,1)} %forward.7), calls=%async_computation | async-start | bytes 8388608 | tf_op jit(solution)/shard_map/all_to_all | solution.py:490
  18.7 11.0 %reshape.13.samples = bf16[24,128,1024]{2,1,0:T(8,128)(2,1)} reshape(bf16[1,24,128,4,2,128]{5,4,3,2,1,0:T(2,128)(2,1)} %param.15) | data formatting | bytes 12582912 | tf_op jit(solution)/shard_map/reshape | solution.py:487
  29.7 12.9 %forward.4 = bf16[8,1,2,1024,128]{4,3,2,1,0:T(8,128)(2,1)} custom-call(bf16[512,512]{1,0:T(8,128)(2,1)} %constant.16.table.fwd, f32[2,32,256,128]{3,2,1,0:T(8,128)} %image.9, bf16[4,2,32,256,128]{4,3,2,1,0:T(8,128)(2,1)} %sens.9), custom_call_target="tpu_custom_call" | custom-call | flops 2147483648 | bytes 12582912 | tf_op jit(solution)/shard_map/forward/pallas_call | solution.py:97
  42.6 13.0 %forward.5 = bf16[8,1,2,1024,128]{4,3,2,1,0:T(8,128)(2,1)} custom-call(bf16[512,512]{1,0:T(8,128)(2,1)} %constant.16.table.fwd, f32[2,32,256,128]{3,2,1,0:T(8,128)} %image.9, bf16[4,2,32,256,128]{4,3,2,1,0:T(8,128)(2,1)} %sens.9), custom_call_target="tpu_custom_call" | custom-call | flops 2147483648 | bytes 12582912 | tf_op jit(solution)/shard_map/forward/pallas_call | solution.py:97
  55.6 12.9 %forward.6 = bf16[8,1,2,1024,128]{4,3,2,1,0:T(8,128)(2,1)} custom-call(bf16[512,512]{1,0:T(8,128)(2,1)} %constant.16.table.fwd, f32[2,32,256,128]{3,2,1,0:T(8,128)} %image.9, bf16[4,2,32,256,128]{4,3,2,1,0:T(8,128)(2,1)} %sens.9), custom_call_target="tpu_custom_call" | custom-call | flops 2147483648 | bytes 12582912 | tf_op jit(solution)/shard_map/forward/pallas_call | solution.py:97
  68.5 0.0 all-to-all-done.piece
  68.5 4.6 %all-to-all-start.3 = ((bf16[8,1,2,1024,128]{4,3,2,1,0:T(8,128)(2,1)}), bf16[8,1,2,1024,128]{4,3,2,1,0:T(8,128)(2,1)}, u32[]{:S(2)}, u32[]{:S(2)}) async-start(bf16[8,1,2,1024,128]{4,3,2,1,0:T(8,128)(2,1)} %forward.4), calls=%async_computation.3 | async-start | bytes 8388608 | tf_op jit(solution)/shard_map/all_to_all | solution.py:490
  73.7 20.9 %tile.4 = bf16[8,1,2,1024,128]{4,3,2,1,0:T(8,128)(2,1)} custom-call(s32[1,24]{1,0:T(1,128)} %offsets.7, s32[1]{0:T(128)S(6)} %copy.15.counts, bf16[512,512]{1,0:T(8,128)(2,1)} %constant.16.table.fwd, bf16[512,512]{1,0:T(8,128)(2,1)} %constant.15.inv.table, bf16[8,1,2,1024,128]{4,3,2,1,0:T(8,128)(2,1)} %all-to-all-done.piece, ...), custom_call_target="tpu_custom_call" | custom-call | flops 10737418240 | bytes 20971520 | tf_op jit(solution)/shard_map/tile/pallas_call | solution.py:220
  94.6 24.0 %all-to-all-done.3.piece = bf16[8,1,2,1024,128]{4,3,2,1,0:T(8,128)(2,1)} async-done(((bf16[8,1,2,1024,128]{4,3,2,1,0:T(8,128)(2,1)}), bf16[8,1,2,1024,128]{4,3,2,1,0:T(8,128)(2,1)}, u32[]{:S(2)}, u32[]{:S(2)}) %all-to-all-start.3) | async-done | bytes 4194336 | tf_op jit(solution)/shard_map/all_to_all | solution.py:490
  118.6 8.1 %all-to-all-start.1 = ((bf16[8,1,2,1024,128]{4,3,2,1,0:T(8,128)(2,1)}), bf16[8,1,2,1024,128]{4,3,2,1,0:T(8,128)(2,1)}, u32[]{:S(2)}, u32[]{:S(2)}) async-start(bf16[8,1,2,1024,128]{4,3,2,1,0:T(8,128)(2,1)} %forward.5), calls=%async_computation.1 | async-start | bytes 8388608 | tf_op jit(solution)/shard_map/all_to_all | solution.py:490
  126.7 20.9 %tile.6.refs_1_ = bf16[8,1,2,1024,128]{4,3,2,1,0:T(8,128)(2,1)} custom-call(s32[1,24]{1,0:T(1,128)} %offsets.7, s32[1]{0:T(128)S(6)} %copy.15.counts, bf16[512,512]{1,0:T(8,128)(2,1)} %constant.16.table.fwd, bf16[512,512]{1,0:T(8,128)(2,1)} %constant.15.inv.table, bf16[8,1,2,1024,128]{4,3,2,1,0:T(8,128)(2,1)} %all-to-all-done.3.piece, ...), custom_call_target="tpu_custom_call" | custom-call | flops 10737418240 | bytes 20971520 | tf_op jit(solution)/shard_map/tile/pallas_call | solution.py:220
  147.6 24.7 %all-to-all-done.1.piece = bf16[8,1,2,1024,128]{4,3,2,1,0:T(8,128)(2,1)} async-done(((bf16[8,1,2,1024,128]{4,3,2,1,0:T(8,128)(2,1)}), bf16[8,1,2,1024,128]{4,3,2,1,0:T(8,128)(2,1)}, u32[]{:S(2)}, u32[]{:S(2)}) %all-to-all-start.1) | async-done | bytes 4194336 | tf_op jit(solution)/shard_map/all_to_all | solution.py:490
  172.3 8.1 %all-to-all-start.4 = ((bf16[8,1,2,1024,128]{4,3,2,1,0:T(8,128)(2,1)}), bf16[8,1,2,1024,128]{4,3,2,1,0:T(8,128)(2,1)}, u32[]{:S(2)}, u32[]{:S(2)}) async-start(bf16[8,1,2,1024,128]{4,3,2,1,0:T(8,128)(2,1)} %forward.6), calls=%async_computation.4 | async-start | bytes 8388608 | tf_op jit(solution)/shard_map/all_to_all | solution.py:490
  180.4 20.9 %tile.5.refs_2_ = bf16[8,1,2,1024,128]{4,3,2,1,0:T(8,128)(2,1)} custom-call(s32[1,24]{1,0:T(1,128)} %offsets.7, s32[1]{0:T(128)S(6)} %copy.15.counts, bf16[512,512]{1,0:T(8,128)(2,1)} %constant.16.table.fwd, bf16[512,512]{1,0:T(8,128)(2,1)} %constant.15.inv.table, bf16[8,1,2,1024,128]{4,3,2,1,0:T(8,128)(2,1)} %all-to-all-done.1.piece, ...), custom_call_target="tpu_custom_call" | custom-call | flops 10737418240 | bytes 20971520 | tf_op jit(solution)/shard_map/tile/pallas_call | solution.py:220
  201.3 24.7 %all-to-all-done.4.piece = bf16[8,1,2,1024,128]{4,3,2,1,0:T(8,128)(2,1)} async-done(((bf16[8,1,2,1024,128]{4,3,2,1,0:T(8,128)(2,1)}), bf16[8,1,2,1024,128]{4,3,2,1,0:T(8,128)(2,1)}, u32[]{:S(2)}, u32[]{:S(2)}) %all-to-all-start.4) | async-done | bytes 4194336 | tf_op jit(solution)/shard_map/all_to_all | solution.py:490
  226.0 8.0 %all-to-all-start.2 = ((bf16[8,1,2,1024,128]{4,3,2,1,0:T(8,128)(2,1)}), bf16[8,1,2,1024,128]{4,3,2,1,0:T(8,128)(2,1)}, u32[]{:S(2)}, u32[]{:S(2)}) async-start(bf16[8,1,2,1024,128]{4,3,2,1,0:T(8,128)(2,1)} %tile.4), calls=%async_computation.2 | async-start | bytes 8388608 | tf_op jit(solution)/shard_map/all_to_all | solution.py:490
  234.0 21.0 %tile.7.refs_3_ = bf16[8,1,2,1024,128]{4,3,2,1,0:T(8,128)(2,1)} custom-call(s32[1,24]{1,0:T(1,128)} %offsets.7, s32[1]{0:T(128)S(6)} %copy.15.counts, bf16[512,512]{1,0:T(8,128)(2,1)} %constant.16.table.fwd, bf16[512,512]{1,0:T(8,128)(2,1)} %constant.15.inv.table, bf16[8,1,2,1024,128]{4,3,2,1,0:T(8,128)(2,1)} %all-to-all-done.4.piece, ...), custom_call_target="tpu_custom_call" | custom-call | flops 10737418240 | bytes 20971520 | tf_op jit(solution)/shard_map/tile/pallas_call | solution.py:220
  255.0 24.6 %all-to-all-done.2.refs_0_ = bf16[8,1,2,1024,128]{4,3,2,1,0:T(8,128)(2,1)} async-done(((bf16[8,1,2,1024,128]{4,3,2,1,0:T(8,128)(2,1)}), bf16[8,1,2,1024,128]{4,3,2,1,0:T(8,128)(2,1)}, u32[]{:S(2)}, u32[]{:S(2)}) %all-to-all-start.2) | async-done | bytes 4194336 | tf_op jit(solution)/shard_map/all_to_all | solution.py:490
  279.6 160.2 %finish.1.gradient = f32[2,32,64,128]{3,2,1,0:T(8,128)} custom-call(bf16[512,512]{1,0:T(8,128)(2,1)} %constant.15.inv.table, bf16[4,2,32,256,128]{4,3,2,1,0:T(8,128)(2,1)} %sens.9, bf16[8,1,2,1024,128]{4,3,2,1,0:T(8,128)(2,1)} %all-to-all-done.2.refs_0_, bf16[8,1,2,1024,128]{4,3,2,1,0:T(8,128)(2,1)} %tile.6.refs_1_, ...), custom_call_target="tpu_custom_call" | custom-call | tf_op jit(solution)/shard_map/finish/pallas_call | solution.py:406
  439.8 7.3 %update.1 = (f32[2,32,64,128]{3,2,1,0:T(8,128)}, f32[2,32,64,128]{3,2,1,0:T(8,128)}, f32[2,32,64,128]{3,2,1,0:T(8,128)}) custom-call(s32[1]{0:T(128)} %bitcast.where, f32[2,32,256,128]{3,2,1,0:T(8,128)} %image.9, f32[2,32,64,128]{3,2,1,0:T(8,128)} %finish.1.gradient, f32[2,32,64,128]{3,2,1,0:T(8,128)} %auxiliary.1, f32[2,32,64,128]{3,2,1,0:T(8,128)} %dual.1), custom_call_target="tpu_custom_call" | custom-call | tf_op jit(solution)/shard_map/update/pallas_call | solution.py:464
Async XLA Ops:
  13.6 54.9 %all-to-all-start = ((bf16[8,1,2,1024,128]{4,3,2,1,0:T(8,128)(2,1)}), bf16[8,1,2,1024,128]{4,3,2,1,0:T(8,128)(2,1)}, u32[]{:S(2)}, u32[]{:S(2)}) async-start(bf16[8,1,2,1024,128]{4,3,2,1,0:T(8,128)(2,1)} %forward.7), calls=%async_computation | async-start | bytes 8388608 | tf_op jit(solution)/shard_map/all_to_all | solution.py:490
  68.5 50.2 %all-to-all-start.3 = ((bf16[8,1,2,1024,128]{4,3,2,1,0:T(8,128)(2,1)}), bf16[8,1,2,1024,128]{4,3,2,1,0:T(8,128)(2,1)}, u32[]{:S(2)}, u32[]{:S(2)}) async-start(bf16[8,1,2,1024,128]{4,3,2,1,0:T(8,128)(2,1)} %forward.4), calls=%async_computation.3 | async-start | bytes 8388608 | tf_op jit(solution)/shard_map/all_to_all | solution.py:490
  118.6 53.7 %all-to-all-start.1 = ((bf16[8,1,2,1024,128]{4,3,2,1,0:T(8,128)(2,1)}), bf16[8,1,2,1024,128]{4,3,2,1,0:T(8,128)(2,1)}, u32[]{:S(2)}, u32[]{:S(2)}) async-start(bf16[8,1,2,1024,128]{4,3,2,1,0:T(8,128)(2,1)} %forward.5), calls=%async_computation.1 | async-start | bytes 8388608 | tf_op jit(solution)/shard_map/all_to_all | solution.py:490
  172.3 53.7 %all-to-all-start.4 = ((bf16[8,1,2,1024,128]{4,3,2,1,0:T(8,128)(2,1)}), bf16[8,1,2,1024,128]{4,3,2,1,0:T(8,128)(2,1)}, u32[]{:S(2)}, u32[]{:S(2)}) async-start(bf16[8,1,2,1024,128]{4,3,2,1,0:T(8,128)(2,1)} %forward.6), calls=%async_computation.4 | async-start | bytes 8388608 | tf_op jit(solution)/shard_map/all_to_all | solution.py:490
  226.0 53.7 %all-to-all-start.2 = ((bf16[8,1,2,1024,128]{4,3,2,1,0:T(8,128)(2,1)}), bf16[8,1,2,1024,128]{4,3,2,1,0:T(8,128)(2,1)}, u32[]{:S(2)}, u32[]{:S(2)}) async-start(bf16[8,1,2,1024,128]{4,3,2,1,0:T(8,128)(2,1)} %tile.4), calls=%async_computation.2 | async-start | bytes 8388608 | tf_op jit(solution)/shard_map/all_to_all | solution.py:490
where the time goes:
time: 448 us; the launch traced here: 447 us
  Pallas kernels  303 us (68%)
  waiting for transfers between devices  98 us (22%)
  starting transfers between devices  33.8 us (8%)
  local copies, waits for them, and re-layouts  11 us (2%)
    pallas_call x1, Pallas kernels, finish_call(): pl.pallas_call(functools.partial(finish_kernel, n, shares, kl, xl, chunks...  160 us
    all_to_all x5, waiting for transfers between devices, swap(): lax.all_to_all(values, 'slab', split_axis=0, concat_axis=0, tiled=True)  98 us
    pallas_call x4, Pallas kernels, tile_call(): pl.pallas_call(functools.partial(tile_kernel, n, kl, xl, cells // kl), gr...  83.8 us
    pallas_call x4, Pallas kernels, forward_call(): pl.pallas_call(functools.partial(forward_kernel, n, kl, xl), grid=(1,), i...  51.7 us
    all_to_all x5, starting transfers between devices, swap(): lax.all_to_all(values, 'slab', split_axis=0, concat_axis=0, tiled=True)  33.8 us
    reshape x1, local copies, waits for them, and re-layouts, body(): flat_samples = samples.reshape(samples.shape[1], samples.shape[2], -1)  11 us
  transfers between devices with their start and end apart: 5, of which 4 were waited for; matrix products, arithmetic and copies ran while one was open for 2% of the time, Pallas kernels for 27%

commit v1 on v0

--- a/solution.py
+++ b/solution.py
@@ -51,12 +51,14 @@
     pieces = []
     for p in range(2):
         for s in range(parts_n):
-            pieces.append(ref[s, 0, p, pl.ds(row, size), :])
+            pieces.append(ref[s, p, pl.ds(row, size), :])
     return jnp.concatenate(pieces, axis=0)
 
 
-def forward_kernel(n, kl, xl, table, image, sens, out, flat):
+def forward_kernel(n, kl, xl, table, image, sens, *refs):
+    outs, flat = refs[:n], refs[n]
     length = image.shape[2]
+    me = lax.axis_index("slab")
 
     def pair(i, carry):
         columns = []
@@ -79,14 +81,15 @@
         return carry
 
     lax.fori_loop(0, xl // 2, pair, 0)
-    for p in range(2):
-        for d in range(n):
+    for off in range(n):
+        d = lax.rem(me + off, n)
+        for p in range(2):
 
             def settle(k, carry):
                 base = pl.multiple_of(((p * n + d) * kl + 2 * k) * pitch(xl), 8)
                 rows = [flat[pl.ds(base + h * pitch(xl), xl), :] for h in range(2)]
                 target = pl.ds(pl.multiple_of(2 * k * xl, 2 * xl), 2 * xl)
-                out[d, 0, p, target, :] = jnp.concatenate(rows, axis=0).astype(BF16)
+                outs[off][p, target, :] = jnp.concatenate(rows, axis=0).astype(BF16)
                 return carry
 
             lax.fori_loop(0, kl // 2, settle, 0, unroll=4)
@@ -102,8 +105,8 @@
             once(image.shape),
             pl.BlockSpec((1, 2, xl, length, depth), lambda i: (first, 0, 0, 0, 0)),
         ],
-        out_specs=pl.BlockSpec((n, 1, 2, kl * xl, depth), lambda i: (0, 0, 0, 0, 0)),
-        out_shape=jax.ShapeDtypeStruct((n, 1, 2, kl * xl, depth), BF16),
+        out_specs=[pl.BlockSpec((2, kl * xl, depth), lambda i: (0, 0, 0))] * n,
+        out_shape=[jax.ShapeDtypeStruct((2, kl * xl, depth), BF16)] * n,
         scratch_shapes=[pltpu.VMEM(((2 * length + 1) * pitch(xl), depth), F32)],
         compiler_params=params(),
         cost_estimate=cost(8 * length * length * xl * depth, 12 * xl * length * depth),
@@ -111,16 +114,27 @@
     )(table, image, sensitivity)
 
 
-def tile_kernel(n, kl, xl, win, offsets, counts, fwd, inv, piece, blocks, samples, out, total, kspace, weights, sem, *wide):
+def tile_kernel(n, kl, xl, win, offsets, counts, fwd, inv, blocks, samples, *refs):
+    pieces, outs, refs = refs[:n], refs[n : 2 * n], refs[2 * n :]
+    total, kspace, weights, piece, sem, piece_sem, *wide = refs
+    me = lax.axis_index("slab")
+    copies = []
+    for off in range(n):
+        origin = lax.rem(me + n - off, n)
+        copies.append(pltpu.make_async_copy(pieces[off], piece.at[origin], piece_sem.at[off]))
+    for copy in copies:
+        copy.start()
     fetch = pltpu.make_async_copy(blocks.at[0], weights, sem)
     fetch.start()
+    for copy in copies:
+        copy.wait()
     length = n * xl
     depth = piece.shape[-1]
     if wide:
         source = wide[0]
         for p in range(2):
             for s in range(n):
-                source[s, 0, p] = piece[s, 0, p].astype(F32)
+                source[s, p] = piece[s, p].astype(F32)
     else:
         source = piece
 
@@ -190,21 +204,23 @@
         return carry
 
     lax.fori_loop(0, kl // 2, to_rows, 0)
-    for p in range(2):
-        for d in range(n):
+    for off in range(n):
+        d = lax.rem(me + off, n)
+        for p in range(2):
 
             def leave(k, carry):
                 base = pl.multiple_of((d * xl + 2 * k) * pitch(kl), 8)
                 rows = [total[p, pl.ds(base + h * pitch(kl), kl), :] for h in range(2)]
                 target = pl.ds(pl.multiple_of(2 * k * kl, 2 * kl), 2 * kl)
-                out[d, 0, p, target, :] = jnp.concatenate(rows, axis=0).astype(BF16)
+                outs[off][p, target, :] = jnp.concatenate(rows, axis=0).astype(BF16)
                 return carry
 
             lax.fori_loop(0, xl // 2, leave, 0, unroll=4)
 
 
-def tile_call(fwd, inv, piece, blocks, samples, offsets, counts, coil, n, kl, xl):
-    depth = piece.shape[-1]
+def tile_call(fwd, inv, pieces, blocks, samples, offsets, counts, coil, n, kl, xl):
+    shape = pieces[0].shape
+    depth = shape[-1]
     _, slots, psize, cells = blocks.shape
     length = n * xl
     narrow = kl % 16 == 0 and xl % 16 == 0
@@ -212,10 +228,13 @@
         pltpu.VMEM((2, (length + 1) * pitch(kl), depth), F32),
         pltpu.VMEM((length * kl, 2 * depth), BF16 if narrow else F32),
         pltpu.VMEM(blocks.shape[1:], BF16),
+        pltpu.VMEM((n, *shape), BF16),
         pltpu.SemaphoreType.DMA,
+        pltpu.SemaphoreType.DMA((n,)),
     ]
     if not narrow:
-        scratch.append(pltpu.VMEM(piece.shape, F32))
+        scratch.append(pltpu.VMEM((n, *shape), F32))
+    anywhere = pl.BlockSpec(memory_space=pl.ANY)
     smem = pl.BlockSpec(memory_space=pltpu.SMEM)
     return pl.pallas_call(
         functools.partial(tile_kernel, n, kl, xl, cells // kl),
@@ -225,12 +244,12 @@
             smem,
             once(fwd.shape),
             once(inv.shape),
-            once(piece.shape),
-            pl.BlockSpec(memory_space=pl.ANY),
+            anywhere,
             pl.BlockSpec((slots, psize, 2 * depth), lambda i: (0, 0, coil), pipeline_mode=pl.Buffered(1)),
-        ],
-        out_specs=pl.BlockSpec(piece.shape, lambda i: (0, 0, 0, 0, 0)),
-        out_shape=jax.ShapeDtypeStruct(piece.shape, BF16),
+        ]
+        + [anywhere] * n,
+        out_specs=[pl.BlockSpec(shape, lambda i: (0, 0, 0))] * n,
+        out_shape=[jax.ShapeDtypeStruct(shape, BF16)] * n,
         scratch_shapes=scratch,
         compiler_params=params(),
         cost_estimate=cost(
@@ -238,12 +257,12 @@
             8 * length * kl * depth + 2 * blocks.size,
         ),
         name="tile",
-    )(offsets, counts, fwd, inv, piece, blocks, samples)
+    )(offsets, counts, fwd, inv, blocks, samples, *pieces)
 
 
 def finish_kernel(n, shares, kl, xl, chunks, sent, table, sens, *refs):
     coils = sens.shape[0]
-    backs, refs = refs[:coils], refs[coils:]
+    backs, refs = [refs[k * n : (k + 1) * n] for k in range(coils)], refs[coils * n :]
     out, landing, sens_v, grad, got, recv, send, local, grad_recv, grad_send, *wide = refs
     ready = coils - sent
     length = n * kl
@@ -272,30 +291,24 @@
     def send_band(j, carry):
         where = pl.ds(pl.multiple_of(j * band, band), band)
         for k in range(ready, coils):
-
-            def one(off, carry):
-                target = lax.rem(me + off, n)
+            for off in range(1, n):
                 pltpu.make_async_remote_copy(
-                    src_ref=backs[k].at[target, 0, :, where, :],
+                    src_ref=backs[k][off].at[:, where, :],
                     dst_ref=landing.at[k, me, :, where, :],
                     send_sem=send,
                     recv_sem=recv.at[j],
-                    device_id={"slab": target},
+                    device_id={"slab": lax.rem(me + off, n)},
                     device_id_type=pl.DeviceIdType.MESH,
                 ).start()
-                return carry
-
-            lax.fori_loop(1, n, one, 0)
         return carry
 
     lax.fori_loop(0, chunks, send_band, 0)
     copies = []
     for k in range(coils):
-        if k < ready:
-            copies.append(pltpu.make_async_copy(backs[k].at[:, 0], landing.at[k], local.at[2 * k]))
-        else:
-            copies.append(pltpu.make_async_copy(backs[k].at[me, 0], landing.at[k, me], local.at[2 * k]))
-        copies.append(pltpu.make_async_copy(sens.at[k], sens_v.at[k], local.at[2 * k + 1]))
+        for off in range(n if k < ready else 1):
+            origin = lax.rem(me + n - off, n)
+            copies.append(pltpu.make_async_copy(backs[k][off], landing.at[k, origin], local.at[k * n + off]))
+        copies.append(pltpu.make_async_copy(sens.at[k], sens_v.at[k], local.at[coils * n + k]))
     for copy in copies:
         copy.start()
     for copy in copies:
@@ -397,7 +410,7 @@
         pltpu.VMEM((shares, 2, xl, share, depth), BF16),
         pltpu.SemaphoreType.DMA((chunks,)),
         pltpu.SemaphoreType.DMA,
-        pltpu.SemaphoreType.DMA((2 * coils,)),
+        pltpu.SemaphoreType.DMA((coils * n + coils,)),
         pltpu.SemaphoreType.DMA((chunks,)),
         pltpu.SemaphoreType.DMA,
     ]
@@ -405,13 +418,13 @@
         scratch.append(pltpu.VMEM((coils, n, 2, rows * kl, depth), F32))
     return pl.pallas_call(
         functools.partial(finish_kernel, n, shares, kl, xl, chunks, sent),
-        in_specs=[vmem, anywhere] + [anywhere] * coils,
+        in_specs=[vmem, anywhere] + [anywhere] * (coils * n),
         out_specs=vmem,
         out_shape=jax.ShapeDtypeStruct((2, xl, share, depth), F32),
         scratch_shapes=scratch,
         compiler_params=params(collective_id=0, has_side_effects=True),
         name="finish",
-    )(table, sensitivity, *backs)
+    )(table, sensitivity, *[piece for back in backs for piece in back])
 
 
 def haar_rows(first, second):
@@ -476,7 +489,7 @@
 
 
 def body(image, sensitivity, blocks, samples, offsets, counts, auxiliary, scaled_dual):
-    coils, _, xl, length_y, depth = sensitivity.shape
+    coils, _, xl, length_y, _ = sensitivity.shape
     n = lax.axis_size("slab")
     shares = lax.axis_size("coil")
     kl = length_y // n
@@ -486,30 +499,29 @@
     x_inv = complex_table(n * xl, True)
     flat_samples = samples.reshape(samples.shape[1], samples.shape[2], -1)
 
-    def swap(values):
-        return lax.all_to_all(values, "slab", split_axis=0, concat_axis=0, tiled=True)
-
-    def tile_of(piece, c):
-        return tile_call(x_fwd, x_inv, piece, blocks, flat_samples, offsets, counts, c, n, kl, xl)
-
-    halves = [forward_call(y_fwd, image, sensitivity, c, n, kl) for c in range(coils)]
-    tied = lax.optimization_barrier((*halves[1:], flat_samples))
-    halves, flat_samples = halves[:1] + list(tied[:-1]), tied[-1]
-    pieces, tiles = [], []
+    def swap(parts):
+        moved = [parts[0]]
+        for off in range(1, n):
+            ring = [(i, (i + off) % n) for i in range(n)]
+            moved.append(lax.ppermute(parts[off], "slab", ring))
+        return moved
+
+    def tile_of(pieces, c):
+        return tile_call(x_fwd, x_inv, pieces, blocks, flat_samples, offsets, counts, c, n, kl, xl)
+
+    pieces, tiles, table = [], [], y_fwd
     for c in range(coils):
-        half = halves[c]
-        if c >= 2:
-            half, tiles[c - 2] = lax.optimization_barrier((half, tiles[c - 2]))
+        half = list(forward_call(table, image, sensitivity, c, n, kl))
+        table, half[0] = lax.optimization_barrier((table, half[0]))
         pieces.append(swap(half))
-        if c >= 1:
-            tiles.append(tile_of(pieces[c - 1], c - 1))
-    early = 1 if coils >= 3 else 0
-    backs = []
-    if early:
-        held, tiles[-1] = lax.optimization_barrier((tiles[0], tiles[-1]))
-        backs.append(swap(held))
-    tiles.append(tile_of(pieces[-1], coils - 1))
-    backs += tiles[early:]
+    for c in range(coils):
+        if c:
+            pieces[c][0], tiles[-1][0] = lax.optimization_barrier((pieces[c][0], tiles[-1][0]))
+        tiles.append(list(tile_of(pieces[c], c)))
+    early = max(coils - 2, 0)
+    backs = list(tiles)
+    for c in range(early):
+        backs[c] = swap(tiles[c])
     gradient = finish_call(y_inv, backs, coils - early, sensitivity, shares, n, kl)
     position = lax.axis_index("coil").astype(jnp.int32).reshape(1)
     return tuple(update_call(image, gradient, auxiliary, scaled_dual, position))

time: 448 us -> 504 us (1.12)
  starting transfers between devices: 33.8 us -> 96.7 us
  waiting for transfers between devices: 98 us -> 83.5 us
    all_to_all x5 -> x0, waiting for transfers between devices: 98 us -> none  [swap(): lax.all_to_all(values, 'slab', split_axis=0, concat_axis=0, tiled=True)]
    ppermute x0 -> x42, starting transfers between devices: none -> 96.7 us  [swap(): moved.append(lax.ppermute(parts[off], 'slab', ring))]
    ppermute x0 -> x42, waiting for transfers between devices: none -> 83.5 us  [swap(): moved.append(lax.ppermute(parts[off], 'slab', ring))]
    pallas_call x4, Pallas kernels: 83.8 us -> 121 us  [tile_call(): pl.pallas_call(functools.partial(tile_kernel, n, kl, xl, cells // kl), gr...]
    pallas_call x1, Pallas kernels: 160 us -> 126 us  [finish_call(): pl.pallas_call(functools.partial(finish_kernel, n, shares, kl, xl, chunks...]
    all_to_all x5 -> x0, starting transfers between devices: 33.8 us -> none  [swap(): lax.all_to_all(values, 'slab', split_axis=0, concat_axis=0, tiled=True)]
  transfers between devices with their start and end apart: 5 -> 42, of which waited for: 4 -> 9; matrix products, arithmetic and copies ran while one was open for 2% -> 2% of each run, Pallas kernels for 27% -> 32%
where the time goes in v1:
time: 504 us
  Pallas kernels  306 us (61%)
  starting transfers between devices  96.7 us (19%)
  waiting for transfers between devices  83.5 us (17%)
  local copies, waits for them, and re-layouts  15.7 us (3%)
    pallas_call x1, Pallas kernels, finish_call(): pl.pallas_call(functools.partial(finish_kernel, n, shares, kl, xl, chunks...  126 us
    pallas_call x4, Pallas kernels, tile_call(): pl.pallas_call(functools.partial(tile_kernel, n, kl, xl, cells // kl), gr...  121 us
    ppermute x42, starting transfers between devices, swap(): moved.append(lax.ppermute(parts[off], 'slab', ring))  96.7 us
    ppermute x42, waiting for transfers between devices, swap(): moved.append(lax.ppermute(parts[off], 'slab', ring))  83.5 us
    pallas_call x4, Pallas kernels, forward_call(): pl.pallas_call(functools.partial(forward_kernel, n, kl, xl), grid=(1,), i...  51.8 us
    reshape x1, local copies, waits for them, and re-layouts, body(): flat_samples = samples.reshape(samples.shape[1], samples.shape[2], -1)  11 us
  transfers between devices with their start and end apart: 42, of which 9 were waited for; matrix products, arithmetic and copies ran while one was open for 2% of the time, Pallas kernels for 32%

profile of v1, /device:TPU:9, one launch (start us, length us, event | category | flops | bytes accessed | tf_op | source)
XLA Modules:
  0.0 503.6 jit_solution(10130463088203245527)
XLA Ops:
  0.6 12.9 %forward.4 = (bf16[2,1024,128]{2,1,0:T(8,128)(2,1)}, bf16[2,1024,128]{2,1,0:T(8,128)(2,1)}, bf16[2,1024,128]{2,1,0:T(8,128)(2,1)}, bf16[2,1024,128]{2,1,0:T(8,12...) custom-call(bf16[512,512]{1,0:T(8,128)(2,1)} %constant.16.table.fwd,, ...), custom_call_target="tpu_custom_call" | custom-call | flops 2147483648 | bytes 12582912 | tf_op jit(solution)/shard_map/forward/pallas_call | solution.py:100
  13.6 1.8 collective-permute-start
  15.3 1.2 collective-permute-start.1
  16.6 0.3 collective-permute-start.2
  16.9 0.2 collective-permute-start.3
  17.1 2.6 collective-permute-start.4
  19.7 7.1 %collective-permute-done.refs_1_ = bf16[2,1024,128]{2,1,0:T(8,128)(2,1)} collective-permute-done((bf16[2,1024,128]{2,1,0:T(8,128)(2,1)}, bf16[2,1024,128]{2,1,0:T(8,128)(2,1)}, u32[]{:S(2)}, u32[]{:S(2)}) %collective-permute-start) | collective-permute-done | bytes 524320 | tf_op jit(solution)/shard_map/ppermute | solution.py:506
  26.8 1.2 collective-permute-start.5
  28.0 11.7 %collective-permute-done.1.refs_2_ = bf16[2,1024,128]{2,1,0:T(8,128)(2,1)} collective-permute-done((bf16[2,1024,128]{2,1,0:T(8,128)(2,1)}, bf16[2,1024,128]{2,1,0:T(8,128)(2,1)}, u32[]{:S(2)}, u32[]{:S(2)}) %collective-permute-start.1) | collective-permute-done | bytes 524320 | tf_op jit(solution)/shard_map/ppermute | solution.py:506
  39.8 13.0 %forward.5 = (bf16[2,1024,128]{2,1,0:T(8,128)(2,1)}, bf16[2,1024,128]{2,1,0:T(8,128)(2,1)}, bf16[2,1024,128]{2,1,0:T(8,128)(2,1)}, bf16[2,1024,128]{2,1,0:T(8,12...) custom-call(bf16[512,512]{1,0:T(8,128)(2,1)} %constant.16.table.fwd,, ...), custom_call_target="tpu_custom_call" | custom-call | flops 2147483648 | bytes 12582912 | tf_op jit(solution)/shard_map/forward/pallas_call | solution.py:100
  52.8 0.8 copy-done.14
  53.6 1.7 collective-permute-start.14
  55.3 7.9 %collective-permute-done.3.refs_4_ = bf16[2,1024,128]{2,1,0:T(8,128)(2,1)S(1)} collective-permute-done((bf16[2,1024,128]{2,1,0:T(8,128)(2,1)}, bf16[2,1024,128]{2,1,0:T(8,128)(2,1)S(1)}, u32[]{:S(2)}, u32[]{:S(2)}) %collective-permute-start.3) | collective-permute-done | bytes 524320 | tf_op jit(solution)/shard_map/ppermute | solution.py:506
  63.2 0.8 copy-done.16
  64.0 0.0 collective-permute-start.15
  64.0 0.0 collective-permute-done.4.refs_5_
  64.0 0.8 copy-done.17
  64.9 0.0 collective-permute-done.5.refs_6_
  64.9 1.2 collective-permute-start.17
  66.1 2.9 collective-permute-start.18
  69.0 12.9 %forward.6 = (bf16[2,1024,128]{2,1,0:T(8,128)(2,1)}, bf16[2,1024,128]{2,1,0:T(8,128)(2,1)}, bf16[2,1024,128]{2,1,0:T(8,128)(2,1)}, bf16[2,1024,128]{2,1,0:T(8,12...) custom-call(bf16[512,512]{1,0:T(8,128)(2,1)} %constant.16.table.fwd,, ...), custom_call_target="tpu_custom_call" | custom-call | flops 2147483648 | bytes 12582912 | tf_op jit(solution)/shard_map/forward/pallas_call | solution.py:100
  82.0 1.5 collective-permute-start.19
  83.5 1.2 collective-permute-done.15.refs_2_
  84.6 11.1 %collective-permute-done.16.refs_3_ = bf16[2,1024,128]{2,1,0:T(8,128)(2,1)S(1)} collective-permute-done((bf16[2,1024,128]{2,1,0:T(8,128)(2,1)}, bf16[2,1024,128]{2,1,0:T(8,128)(2,1)S(1)}, u32[]{:S(2)}, u32[]{:S(2)}) %collective-permute-start.16) | collective-permute-done | bytes 524320 | tf_op jit(solution)/shard_map/ppermute | solution.py:506
  95.7 12.5 %collective-permute-done.17.refs_4_ = bf16[2,1024,128]{2,1,0:T(8,128)(2,1)} collective-permute-done((bf16[2,1024,128]{2,1,0:T(8,128)(2,1)}, bf16[2,1024,128]{2,1,0:T(8,128)(2,1)}, u32[]{:S(2)}, u32[]{:S(2)}) %collective-permute-start.17) | collective-permute-done | bytes 524320 | tf_op jit(solution)/shard_map/ppermute | solution.py:506
  108.2 3.8 collective-permute-start.29
  112.0 11.0 %reshape.13.samples = bf16[24,128,1024]{2,1,0:T(8,128)(2,1)} reshape(bf16[1,24,128,4,2,128]{5,4,3,2,1,0:T(2,128)(2,1)} %param.15) | data formatting | bytes 12582912 | tf_op jit(solution)/shard_map/reshape | solution.py:500
  123.6 12.9 %forward.7 = (bf16[2,1024,128]{2,1,0:T(8,128)(2,1)}, bf16[2,1024,128]{2,1,0:T(8,128)(2,1)}, bf16[2,1024,128]{2,1,0:T(8,128)(2,1)}, bf16[2,1024,128]{2,1,0:T(8,12...) custom-call(bf16[512,512]{1,0:T(8,128)(2,1)} %constant.16.table.fwd,, ...), custom_call_target="tpu_custom_call" | custom-call | flops 2147483648 | bytes 12582912 | tf_op jit(solution)/shard_map/forward/pallas_call | solution.py:100
  136.6 2.1 collective-permute-start.31
  138.7 2.9 collective-permute-start.32
  141.6 0.1 collective-permute-start.33
  141.7 0.4 collective-permute-start.34
  142.1 0.8 copy-done.9
  142.9 1.4 collective-permute-start.35
  144.3 30.2 %tile.4 = (bf16[2,1024,128]{2,1,0:T(8,128)(2,1)}, bf16[2,1024,128]{2,1,0:T(8,128)(2,1)}, bf16[2,1024,128]{2,1,0:T(8,128)(2,1)}, bf16[2,1024,128]{2,1,0:T(8,128)(...) custom-call(s32[1,24]{1,0:T(1,128)} %offsets.7, ...), custom_call_target="tpu_custom_call" | custom-call | flops 10737418240 | bytes 20971520 | tf_op jit(solution)/shard_map/tile/pallas_call | solution.py:239
  174.6 8.1 %collective-permute-start.36 = (bf16[2,1024,128]{2,1,0:T(8,128)(2,1)}, bf16[2,1024,128]{2,1,0:T(8,128)(2,1)S(1)}, u32[]{:S(2)}, u32[]{:S(2)}) collective-permute-start(bf16[2,1024,128]{2,1,0:T(8,128)(2,1)} %get-tuple-element.143), channel_id=1, source_target_pairs={{0,2},{1,3},{2,4},{3,5},{4,6},{5,7},{6,0},{7,1},{8,10},{9,11},{10,... | collective-permute-start | bytes 1572872 | tf_op jit(solution)/shard_map/ppermute | solution.py:506
  182.7 7.5 %collective-permute-start.37 = (bf16[2,1024,128]{2,1,0:T(8,128)(2,1)}, bf16[2,1024,128]{2,1,0:T(8,128)(2,1)S(1)}, u32[]{:S(2)}, u32[]{:S(2)}) collective-permute-start(bf16[2,1024,128]{2,1,0:T(8,128)(2,1)} %get-tuple-element.144), channel_id=1, source_target_pairs={{0,3},{1,4},{2,5},{3,6},{4,7},{5,0},{6,1},{7,2},{8,11},{9,12},{10,... | collective-permute-start | bytes 1572872 | tf_op jit(solution)/shard_map/ppermute | solution.py:506
  190.3 2.9 collective-permute-start.39
  193.2 30.4 %tile.5 = (bf16[2,1024,128]{2,1,0:T(8,128)(2,1)}, bf16[2,1024,128]{2,1,0:T(8,128)(2,1)}, bf16[2,1024,128]{2,1,0:T(8,128)(2,1)}, bf16[2,1024,128]{2,1,0:T(8,128)(...) custom-call(s32[1,24]{1,0:T(1,128)} %offsets.7, ...), custom_call_target="tpu_custom_call" | custom-call | flops 10737418240 | bytes 20971520 | tf_op jit(solution)/shard_map/tile/pallas_call | solution.py:239
  223.6 0.1 collective-permute-start.41
  223.7 0.7 copy-done.10
  224.4 1.1 collective-permute-start.21
  225.5 16.0 %collective-permute-start.22 = (bf16[2,1024,128]{2,1,0:T(8,128)(2,1)}, bf16[2,1024,128]{2,1,0:T(8,128)(2,1)S(1)}, u32[]{:S(2)}, u32[]{:S(2)}) collective-permute-start(bf16[2,1024,128]{2,1,0:T(8,128)(2,1)} %get-tuple-element.115), channel_id=1, source_target_pairs={{0,2},{1,3},{2,4},{3,5},{4,6},{5,7},{6,0},{7,1},{8,10},{9,11},{10,... | collective-permute-start | bytes 1572872 | tf_op jit(solution)/shard_map/ppermute | solution.py:506
  241.5 0.1 collective-permute-start.24
  241.6 2.6 collective-permute-start.25
  244.2 9.2 %collective-permute-start.26 = (bf16[2,1024,128]{2,1,0:T(8,128)(2,1)}, bf16[2,1024,128]{2,1,0:T(8,128)(2,1)}, u32[]{:S(2)}, u32[]{:S(2)}) collective-permute-start(bf16[2,1024,128]{2,1,0:T(8,128)(2,1)} %get-tuple-element.119), channel_id=1, source_target_pairs={{0,6},{1,7},{2,0},{3,1},{4,2},{5,3},{6,4},{7,5},{8,14},{9,15},{10,... | collective-permute-start | bytes 1572872 | tf_op jit(solution)/shard_map/ppermute | solution.py:506
  253.4 1.9 collective-permute-start.27
  255.3 20.4 %collective-permute-done.23.refs_11_ = bf16[2,1024,128]{2,1,0:T(8,128)(2,1)S(1)} collective-permute-done((bf16[2,1024,128]{2,1,0:T(8,128)(2,1)}, bf16[2,1024,128]{2,1,0:T(8,128)(2,1)S(1)}, u32[]{:S(2)}, u32[]{:S(2)}) %collective-permute-start.23) | collective-permute-done | bytes 524320 | tf_op jit(solution)/shard_map/ppermute | solution.py:506
  275.7 11.2 %collective-permute-done.24.refs_12_ = bf16[2,1024,128]{2,1,0:T(8,128)(2,1)} collective-permute-done((bf16[2,1024,128]{2,1,0:T(8,128)(2,1)}, bf16[2,1024,128]{2,1,0:T(8,128)(2,1)}, u32[]{:S(2)}, u32[]{:S(2)}) %collective-permute-start.24) | collective-permute-done | bytes 524320 | tf_op jit(solution)/shard_map/ppermute | solution.py:506
  286.9 30.3 %tile.6 = (bf16[2,1024,128]{2,1,0:T(8,128)(2,1)}, bf16[2,1024,128]{2,1,0:T(8,128)(2,1)}, bf16[2,1024,128]{2,1,0:T(8,128)(2,1)}, bf16[2,1024,128]{2,1,0:T(8,128)(...) custom-call(s32[1,24]{1,0:T(1,128)} %offsets.7, ...), custom_call_target="tpu_custom_call" | custom-call | flops 10737418240 | bytes 20971520 | tf_op jit(solution)/shard_map/tile/pallas_call | solution.py:239
  317.3 6.2 %collective-permute-start.12 = (bf16[2,1024,128]{2,1,0:T(8,128)(2,1)}, bf16[2,1024,128]{2,1,0:T(8,128)(2,1)S(1)}, u32[]{:S(2)}, u32[]{:S(2)}) collective-permute-start(bf16[2,1024,128]{2,1,0:T(8,128)(2,1)} %get-tuple-element.99), channel_id=1, source_target_pairs={{0,6},{1,7},{2,0},{3,1},{4,2},{5,3},{6,4},{7,5},{8,14},{9,15},{10,... | collective-permute-start | bytes 1572872 | tf_op jit(solution)/shard_map/ppermute | solution.py:506
  323.5 8.4 %collective-permute-start.13 = (bf16[2,1024,128]{2,1,0:T(8,128)(2,1)}, bf16[2,1024,128]{2,1,0:T(8,128)(2,1)S(1)}, u32[]{:S(2)}, u32[]{:S(2)}) collective-permute-start(bf16[2,1024,128]{2,1,0:T(8,128)(2,1)} %get-tuple-element.100), channel_id=1, source_target_pairs={{0,7},{1,0},{2,1},{3,2},{4,3},{5,4},{6,5},{7,6},{8,15},{9,8},{10,9... | collective-permute-start | bytes 1572872 | tf_op jit(solution)/shard_map/ppermute | solution.py:506
  331.8 6.7 %collective-permute-start.8 = (bf16[2,1024,128]{2,1,0:T(8,128)(2,1)}, bf16[2,1024,128]{2,1,0:T(8,128)(2,1)}, u32[]{:S(2)}, u32[]{:S(2)}) collective-permute-start(bf16[2,1024,128]{2,1,0:T(8,128)(2,1)} %get-tuple-element.95), channel_id=1, source_target_pairs={{0,2},{1,3},{2,4},{3,5},{4,6},{5,7},{6,0},{7,1},{8,10},{9,11},{10,... | collective-permute-start | bytes 1572872 | tf_op jit(solution)/shard_map/ppermute | solution.py:506
  338.5 0.5 collective-permute-start.9
  339.1 30.4 %tile.7 = (bf16[2,1024,128]{2,1,0:T(8,128)(2,1)}, bf16[2,1024,128]{2,1,0:T(8,128)(2,1)}, bf16[2,1024,128]{2,1,0:T(8,128)(2,1)}, bf16[2,1024,128]{2,1,0:T(8,128)(...) custom-call(s32[1,24]{1,0:T(1,128)} %offsets.7, ...), custom_call_target="tpu_custom_call" | custom-call | flops 10737418240 | bytes 20971520 | tf_op jit(solution)/shard_map/tile/pallas_call | solution.py:239
  369.5 0.0 copy-start.3
  369.6 0.0 copy-start.4
  369.6 0.0 copy-start.5
  369.6 0.4 collective-permute-done.9.refs_3_
  370.0 0.4 copy-done.3
  370.3 0.2 copy-done.4
  370.5 0.2 copy-done.5
  370.7 125.6 %finish.1.gradient = f32[2,32,64,128]{3,2,1,0:T(8,128)} custom-call(bf16[512,512]{1,0:T(8,128)(2,1)} %constant.15.inv.table, bf16[4,2,32,256,128]{4,3,2,1,0:T(8,128)(2,1)} %sens.9, bf16[2,1024,128]{2,1,0:T(8,128)(2,1)} %get-tuple-element.93.refs_0_, bf16[2,1024,128]{2,1,0:T(8,128)(2,1)} %copy-done.5, bf16[2,1024,128]{2,1,0:T(8,128)(2,1)} %collective-permute-done.8.refs_2_, ...), custom_call_target="tpu_custom_call" | custom-call | tf_op jit(solution)/shard_map/finish/pallas_call | solution.py:419
  496.3 7.3 %update.1 = (f32[2,32,64,128]{3,2,1,0:T(8,128)}, f32[2,32,64,128]{3,2,1,0:T(8,128)}, f32[2,32,64,128]{3,2,1,0:T(8,128)}) custom-call(s32[1]{0:T(128)} %bitcast.where, f32[2,32,256,128]{3,2,1,0:T(8,128)} %image.9, f32[2,32,64,128]{3,2,1,0:T(8,128)} %finish.1.gradient, f32[2,32,64,128]{3,2,1,0:T(8,128)} %auxiliary.1, f32[2,32,64,128]{3,2,1,0:T(8,128)} %dual.1), custom_call_target="tpu_custom_call" | custom-call | tf_op jit(solution)/shard_map/update/pallas_call | solution.py:477
  (69 shorter events, 0.2 us)
Async XLA Ops:
  13.6 13.3 %collective-permute-start = (bf16[2,1024,128]{2,1,0:T(8,128)(2,1)}, bf16[2,1024,128]{2,1,0:T(8,128)(2,1)}, u32[]{:S(2)}, u32[]{:S(2)}) collective-permute-start(bf16[2,1024,128]{2,1,0:T(8,128)(2,1)} %get-tuple-element.85), channel_id=1, source_target_pairs={{0,1},{1,2},{2,3},{3,4},{4,5},{5,6},{6,7},{7,0},{8,9},{9,10},{10,1... | collective-permute-start | bytes 1572872 | tf_op jit(solution)/shard_map/ppermute | solution.py:506
  15.3 24.4 %collective-permute-start.1 = (bf16[2,1024,128]{2,1,0:T(8,128)(2,1)}, bf16[2,1024,128]{2,1,0:T(8,128)(2,1)}, u32[]{:S(2)}, u32[]{:S(2)}) collective-permute-start(bf16[2,1024,128]{2,1,0:T(8,128)(2,1)} %get-tuple-element.86), channel_id=1, source_target_pairs={{0,2},{1,3},{2,4},{3,5},{4,6},{5,7},{6,0},{7,1},{8,10},{9,11},{10,... | collective-permute-start | bytes 1572872 | tf_op jit(solution)/shard_map/ppermute | solution.py:506
  16.6 36.2 %collective-permute-start.2 = (bf16[2,1024,128]{2,1,0:T(8,128)(2,1)}, bf16[2,1024,128]{2,1,0:T(8,128)(2,1)S(1)}, u32[]{:S(2)}, u32[]{:S(2)}) collective-permute-start(bf16[2,1024,128]{2,1,0:T(8,128)(2,1)} %get-tuple-element.87), channel_id=1, source_target_pairs={{0,3},{1,4},{2,5},{3,6},{4,7},{5,0},{6,1},{7,2},{8,11},{9,12},{10,... | collective-permute-start | bytes 1572872 | tf_op jit(solution)/shard_map/ppermute | solution.py:506
  16.9 46.4 %collective-permute-start.3 = (bf16[2,1024,128]{2,1,0:T(8,128)(2,1)}, bf16[2,1024,128]{2,1,0:T(8,128)(2,1)S(1)}, u32[]{:S(2)}, u32[]{:S(2)}) collective-permute-start(bf16[2,1024,128]{2,1,0:T(8,128)(2,1)} %get-tuple-element.88), channel_id=1, source_target_pairs={{0,4},{1,5},{2,6},{3,7},{4,0},{5,1},{6,2},{7,3},{8,12},{9,13},{10,... | collective-permute-start | bytes 1572872 | tf_op jit(solution)/shard_map/ppermute | solution.py:506
  17.1 46.9 %collective-permute-start.4 = (bf16[2,1024,128]{2,1,0:T(8,128)(2,1)}, bf16[2,1024,128]{2,1,0:T(8,128)(2,1)S(1)}, u32[]{:S(2)}, u32[]{:S(2)}) collective-permute-start(bf16[2,1024,128]{2,1,0:T(8,128)(2,1)} %get-tuple-element.89), channel_id=1, source_target_pairs={{0,5},{1,6},{2,7},{3,0},{4,1},{5,2},{6,3},{7,4},{8,13},{9,14},{10,... | collective-permute-start | bytes 1572872 | tf_op jit(solution)/shard_map/ppermute | solution.py:506
  26.8 38.0 %collective-permute-start.5 = (bf16[2,1024,128]{2,1,0:T(8,128)(2,1)}, bf16[2,1024,128]{2,1,0:T(8,128)(2,1)}, u32[]{:S(2)}, u32[]{:S(2)}) collective-permute-start(bf16[2,1024,128]{2,1,0:T(8,128)(2,1)} %get-tuple-element.90), channel_id=1, source_target_pairs={{0,6},{1,7},{2,0},{3,1},{4,2},{5,3},{6,4},{7,5},{8,14},{9,15},{10,... | collective-permute-start | bytes 1572872 | tf_op jit(solution)/shard_map/ppermute | solution.py:506
  39.7 26.4 %collective-permute-start.6 = (bf16[2,1024,128]{2,1,0:T(8,128)(2,1)}, bf16[2,1024,128]{2,1,0:T(8,128)(2,1)}, u32[]{:S(2)}, u32[]{:S(2)}) collective-permute-start(bf16[2,1024,128]{2,1,0:T(8,128)(2,1)} %get-tuple-element.91), channel_id=1, source_target_pairs={{0,7},{1,0},{2,1},{3,2},{4,3},{5,4},{6,5},{7,6},{8,15},{9,8},{10,9... | collective-permute-start | bytes 1572872 | tf_op jit(solution)/shard_map/ppermute | solution.py:506
  52.8 0.8 copy-start.14
  53.6 28.4 %collective-permute-start.14 = (bf16[2,1024,128]{2,1,0:T(8,128)(2,1)}, bf16[2,1024,128]{2,1,0:T(8,128)(2,1)S(1)}, u32[]{:S(2)}, u32[]{:S(2)}) collective-permute-start(bf16[2,1024,128]{2,1,0:T(8,128)(2,1)} %get-tuple-element.105), channel_id=1, source_target_pairs={{0,1},{1,2},{2,3},{3,4},{4,5},{5,6},{6,7},{7,0},{8,9},{9,10},{10,1... | collective-permute-start | bytes 1572872 | tf_op jit(solution)/shard_map/ppermute | solution.py:506
  63.2 0.8 copy-start.16
  64.0 20.6 %collective-permute-start.15 = (bf16[2,1024,128]{2,1,0:T(8,128)(2,1)}, bf16[2,1024,128]{2,1,0:T(8,128)(2,1)S(1)}, u32[]{:S(2)}, u32[]{:S(2)}) collective-permute-start(bf16[2,1024,128]{2,1,0:T(8,128)(2,1)} %get-tuple-element.106), channel_id=1, source_target_pairs={{0,2},{1,3},{2,4},{3,5},{4,6},{5,7},{6,0},{7,1},{8,10},{9,11},{10,... | collective-permute-start | bytes 1572872 | tf_op jit(solution)/shard_map/ppermute | solution.py:506
  64.0 0.8 copy-start.17
  64.8 30.8 %collective-permute-start.16 = (bf16[2,1024,128]{2,1,0:T(8,128)(2,1)}, bf16[2,1024,128]{2,1,0:T(8,128)(2,1)S(1)}, u32[]{:S(2)}, u32[]{:S(2)}) collective-permute-start(bf16[2,1024,128]{2,1,0:T(8,128)(2,1)} %get-tuple-element.107), channel_id=1, source_target_pairs={{0,3},{1,4},{2,5},{3,6},{4,7},{5,0},{6,1},{7,2},{8,11},{9,12},{10,... | collective-permute-start | bytes 1572872 | tf_op jit(solution)/shard_map/ppermute | solution.py:506
  64.9 43.4 %collective-permute-start.17 = (bf16[2,1024,128]{2,1,0:T(8,128)(2,1)}, bf16[2,1024,128]{2,1,0:T(8,128)(2,1)}, u32[]{:S(2)}, u32[]{:S(2)}) collective-permute-start(bf16[2,1024,128]{2,1,0:T(8,128)(2,1)} %get-tuple-element.108), channel_id=1, source_target_pairs={{0,4},{1,5},{2,6},{3,7},{4,0},{5,1},{6,2},{7,3},{8,12},{9,13},{10,... | collective-permute-start | bytes 1572872 | tf_op jit(solution)/shard_map/ppermute | solution.py:506
  66.1 45.9 %collective-permute-start.18 = (bf16[2,1024,128]{2,1,0:T(8,128)(2,1)}, bf16[2,1024,128]{2,1,0:T(8,128)(2,1)}, u32[]{:S(2)}, u32[]{:S(2)}) collective-permute-start(bf16[2,1024,128]{2,1,0:T(8,128)(2,1)} %get-tuple-element.109), channel_id=1, source_target_pairs={{0,5},{1,6},{2,7},{3,0},{4,1},{5,2},{6,3},{7,4},{8,13},{9,14},{10,... | collective-permute-start | bytes 1572872 | tf_op jit(solution)/shard_map/ppermute | solution.py:506
  82.0 13.7 %copy-start.12 = (bf16[2,1024,128]{2,1,0:T(8,128)(2,1)}, bf16[2,1024,128]{2,1,0:T(8,128)(2,1)S(1)}, u32[]{:S(2)}) copy-start(bf16[2,1024,128]{2,1,0:T(8,128)(2,1)S(1)} %collective-permute-done.14.refs_1_) | copy-start | bytes 1572868
  82.0 54.6 %collective-permute-start.19 = (bf16[2,1024,128]{2,1,0:T(8,128)(2,1)}, bf16[2,1024,128]{2,1,0:T(8,128)(2,1)}, u32[]{:S(2)}, u32[]{:S(2)}) collective-permute-start(bf16[2,1024,128]{2,1,0:T(8,128)(2,1)} %get-tuple-element.110), channel_id=1, source_target_pairs={{0,6},{1,7},{2,0},{3,1},{4,2},{5,3},{6,4},{7,5},{8,14},{9,15},{10,... | collective-permute-start | bytes 1572872 | tf_op jit(solution)/shard_map/ppermute | solution.py:506
  84.6 23.6 %copy-start.13 = (bf16[2,1024,128]{2,1,0:T(8,128)(2,1)}, bf16[2,1024,128]{2,1,0:T(8,128)(2,1)S(1)}, u32[]{:S(2)}) copy-start(bf16[2,1024,128]{2,1,0:T(8,128)(2,1)S(1)} %collective-permute-done.15.refs_2_) | copy-start | bytes 1572868
  84.6 54.1 %collective-permute-start.20 = (bf16[2,1024,128]{2,1,0:T(8,128)(2,1)}, bf16[2,1024,128]{2,1,0:T(8,128)(2,1)}, u32[]{:S(2)}, u32[]{:S(2)}) collective-permute-start(bf16[2,1024,128]{2,1,0:T(8,128)(2,1)} %get-tuple-element.111), channel_id=1, source_target_pairs={{0,7},{1,0},{2,1},{3,2},{4,3},{5,4},{6,5},{7,6},{8,15},{9,8},{10,9... | collective-permute-start | bytes 1572872 | tf_op jit(solution)/shard_map/ppermute | solution.py:506
  95.7 16.3 %copy-start.15 = (bf16[2,1024,128]{2,1,0:T(8,128)(2,1)}, bf16[2,1024,128]{2,1,0:T(8,128)(2,1)S(1)}, u32[]{:S(2)}) copy-start(bf16[2,1024,128]{2,1,0:T(8,128)(2,1)S(1)} %collective-permute-done.16.refs_3_) | copy-start | bytes 1572868
  95.7 45.9 %collective-permute-start.28 = (bf16[2,1024,128]{2,1,0:T(8,128)(2,1)}, bf16[2,1024,128]{2,1,0:T(8,128)(2,1)S(1)}, u32[]{:S(2)}, u32[]{:S(2)}) collective-permute-start(bf16[2,1024,128]{2,1,0:T(8,128)(2,1)} %get-tuple-element.125), channel_id=1, source_target_pairs={{0,1},{1,2},{2,3},{3,4},{4,5},{5,6},{6,7},{7,0},{8,9},{9,10},{10,1... | collective-permute-start | bytes 1572872 | tf_op jit(solution)/shard_map/ppermute | solution.py:506
  108.2 33.5 %collective-permute-start.29 = (bf16[2,1024,128]{2,1,0:T(8,128)(2,1)}, bf16[2,1024,128]{2,1,0:T(8,128)(2,1)S(1)}, u32[]{:S(2)}, u32[]{:S(2)}) collective-permute-start(bf16[2,1024,128]{2,1,0:T(8,128)(2,1)} %get-tuple-element.126), channel_id=1, source_target_pairs={{0,2},{1,3},{2,4},{3,5},{4,6},{5,7},{6,0},{7,1},{8,10},{9,11},{10,... | collective-permute-start | bytes 1572872 | tf_op jit(solution)/shard_map/ppermute | solution.py:506
  112.0 30.1 %collective-permute-start.30 = (bf16[2,1024,128]{2,1,0:T(8,128)(2,1)}, bf16[2,1024,128]{2,1,0:T(8,128)(2,1)S(1)}, u32[]{:S(2)}, u32[]{:S(2)}) collective-permute-start(bf16[2,1024,128]{2,1,0:T(8,128)(2,1)} %get-tuple-element.127), channel_id=1, source_target_pairs={{0,3},{1,4},{2,5},{3,6},{4,7},{5,0},{6,1},{7,2},{8,11},{9,12},{10,... | collective-permute-start | bytes 1572872 | tf_op jit(solution)/shard_map/ppermute | solution.py:506
  136.6 38.0 %collective-permute-start.31 = (bf16[2,1024,128]{2,1,0:T(8,128)(2,1)}, bf16[2,1024,128]{2,1,0:T(8,128)(2,1)}, u32[]{:S(2)}, u32[]{:S(2)}) collective-permute-start(bf16[2,1024,128]{2,1,0:T(8,128)(2,1)} %get-tuple-element.128), channel_id=1, source_target_pairs={{0,4},{1,5},{2,6},{3,7},{4,0},{5,1},{6,2},{7,3},{8,12},{9,13},{10,... | collective-permute-start | bytes 1572872 | tf_op jit(solution)/shard_map/ppermute | solution.py:506
  138.7 44.0 %collective-permute-start.32 = (bf16[2,1024,128]{2,1,0:T(8,128)(2,1)}, bf16[2,1024,128]{2,1,0:T(8,128)(2,1)}, u32[]{:S(2)}, u32[]{:S(2)}) collective-permute-start(bf16[2,1024,128]{2,1,0:T(8,128)(2,1)} %get-tuple-element.129), channel_id=1, source_target_pairs={{0,5},{1,6},{2,7},{3,0},{4,1},{5,2},{6,3},{7,4},{8,13},{9,14},{10,... | collective-permute-start | bytes 1572872 | tf_op jit(solution)/shard_map/ppermute | solution.py:506
  141.6 32.9 %copy-start.6 = (bf16[2,1024,128]{2,1,0:T(8,128)(2,1)}, bf16[2,1024,128]{2,1,0:T(8,128)(2,1)S(1)}, u32[]{:S(2)}) copy-start(bf16[2,1024,128]{2,1,0:T(8,128)(2,1)S(1)} %collective-permute-done.28.refs_1_) | copy-start | bytes 1572868
  141.6 48.6 %collective-permute-start.33 = (bf16[2,1024,128]{2,1,0:T(8,128)(2,1)}, bf16[2,1024,128]{2,1,0:T(8,128)(2,1)}, u32[]{:S(2)}, u32[]{:S(2)}) collective-permute-start(bf16[2,1024,128]{2,1,0:T(8,128)(2,1)} %get-tuple-element.130), channel_id=1, source_target_pairs={{0,6},{1,7},{2,0},{3,1},{4,2},{5,3},{6,4},{7,5},{8,14},{9,15},{10,... | collective-permute-start | bytes 1572872 | tf_op jit(solution)/shard_map/ppermute | solution.py:506
  141.7 32.8 %copy-start.7 = (bf16[2,1024,128]{2,1,0:T(8,128)(2,1)}, bf16[2,1024,128]{2,1,0:T(8,128)(2,1)S(1)}, u32[]{:S(2)}) copy-start(bf16[2,1024,128]{2,1,0:T(8,128)(2,1)S(1)} %collective-permute-done.29.refs_2_) | copy-start | bytes 1572868
  141.7 48.5 %collective-permute-start.34 = (bf16[2,1024,128]{2,1,0:T(8,128)(2,1)}, bf16[2,1024,128]{2,1,0:T(8,128)(2,1)}, u32[]{:S(2)}, u32[]{:S(2)}) collective-permute-start(bf16[2,1024,128]{2,1,0:T(8,128)(2,1)} %get-tuple-element.131), channel_id=1, source_target_pairs={{0,7},{1,0},{2,1},{3,2},{4,3},{5,4},{6,5},{7,6},{8,15},{9,8},{10,9... | collective-permute-start | bytes 1572872 | tf_op jit(solution)/shard_map/ppermute | solution.py:506
  142.1 0.8 copy-start.9
  142.9 50.3 %collective-permute-start.35 = (bf16[2,1024,128]{2,1,0:T(8,128)(2,1)}, bf16[2,1024,128]{2,1,0:T(8,128)(2,1)S(1)}, u32[]{:S(2)}, u32[]{:S(2)}) collective-permute-start(bf16[2,1024,128]{2,1,0:T(8,128)(2,1)} %get-tuple-element.142), channel_id=1, source_target_pairs={{0,1},{1,2},{2,3},{3,4},{4,5},{5,6},{6,7},{7,0},{8,9},{9,10},{10,1... | collective-permute-start | bytes 1572872 | tf_op jit(solution)/shard_map/ppermute | solution.py:506
  174.6 49.1 %collective-permute-start.36 = (bf16[2,1024,128]{2,1,0:T(8,128)(2,1)}, bf16[2,1024,128]{2,1,0:T(8,128)(2,1)S(1)}, u32[]{:S(2)}, u32[]{:S(2)}) collective-permute-start(bf16[2,1024,128]{2,1,0:T(8,128)(2,1)} %get-tuple-element.143), channel_id=1, source_target_pairs={{0,2},{1,3},{2,4},{3,5},{4,6},{5,7},{6,0},{7,1},{8,10},{9,11},{10,... | collective-permute-start | bytes 1572872 | tf_op jit(solution)/shard_map/ppermute | solution.py:506
  182.7 41.0 %collective-permute-start.37 = (bf16[2,1024,128]{2,1,0:T(8,128)(2,1)}, bf16[2,1024,128]{2,1,0:T(8,128)(2,1)S(1)}, u32[]{:S(2)}, u32[]{:S(2)}) collective-permute-start(bf16[2,1024,128]{2,1,0:T(8,128)(2,1)} %get-tuple-element.144), channel_id=1, source_target_pairs={{0,3},{1,4},{2,5},{3,6},{4,7},{5,0},{6,1},{7,2},{8,11},{9,12},{10,... | collective-permute-start | bytes 1572872 | tf_op jit(solution)/shard_map/ppermute | solution.py:506
  190.2 35.3 %collective-permute-start.38 = (bf16[2,1024,128]{2,1,0:T(8,128)(2,1)}, bf16[2,1024,128]{2,1,0:T(8,128)(2,1)}, u32[]{:S(2)}, u32[]{:S(2)}) collective-permute-start(bf16[2,1024,128]{2,1,0:T(8,128)(2,1)} %get-tuple-element.145), channel_id=1, source_target_pairs={{0,4},{1,5},{2,6},{3,7},{4,0},{5,1},{6,2},{7,3},{8,12},{9,13},{10,... | collective-permute-start | bytes 1572872 | tf_op jit(solution)/shard_map/ppermute | solution.py:506
  190.3 51.3 %collective-permute-start.39 = (bf16[2,1024,128]{2,1,0:T(8,128)(2,1)}, bf16[2,1024,128]{2,1,0:T(8,128)(2,1)}, u32[]{:S(2)}, u32[]{:S(2)}) collective-permute-start(bf16[2,1024,128]{2,1,0:T(8,128)(2,1)} %get-tuple-element.146), channel_id=1, source_target_pairs={{0,5},{1,6},{2,7},{3,0},{4,1},{5,2},{6,3},{7,4},{8,13},{9,14},{10,... | collective-permute-start | bytes 1572872 | tf_op jit(solution)/shard_map/ppermute | solution.py:506
  193.2 30.4 %copy-start.8 = (bf16[2,1024,128]{2,1,0:T(8,128)(2,1)}, bf16[2,1024,128]{2,1,0:T(8,128)(2,1)S(1)}, u32[]{:S(2)}) copy-start(bf16[2,1024,128]{2,1,0:T(8,128)(2,1)S(1)} %collective-permute-done.35.refs_1_) | copy-start | bytes 1572868
  193.2 48.4 %collective-permute-start.40 = (bf16[2,1024,128]{2,1,0:T(8,128)(2,1)}, bf16[2,1024,128]{2,1,0:T(8,128)(2,1)}, u32[]{:S(2)}, u32[]{:S(2)}) collective-permute-start(bf16[2,1024,128]{2,1,0:T(8,128)(2,1)} %get-tuple-element.147), channel_id=1, source_target_pairs={{0,6},{1,7},{2,0},{3,1},{4,2},{5,3},{6,4},{7,5},{8,14},{9,15},{10,... | collective-permute-start | bytes 1572872 | tf_op jit(solution)/shard_map/ppermute | solution.py:506
  223.6 0.8 copy-start.10
  223.6 18.0 %collective-permute-start.41 = (bf16[2,1024,128]{2,1,0:T(8,128)(2,1)}, bf16[2,1024,128]{2,1,0:T(8,128)(2,1)S(1)}, u32[]{:S(2)}, u32[]{:S(2)}) collective-permute-start(bf16[2,1024,128]{2,1,0:T(8,128)(2,1)} %get-tuple-element.148), channel_id=1, source_target_pairs={{0,7},{1,0},{2,1},{3,2},{4,3},{5,4},{6,5},{7,6},{8,15},{9,8},{10,9... | collective-permute-start | bytes 1572872 | tf_op jit(solution)/shard_map/ppermute | solution.py:506
  224.4 1.1 copy-start.11
  224.4 19.8 %collective-permute-start.21 = (bf16[2,1024,128]{2,1,0:T(8,128)(2,1)}, bf16[2,1024,128]{2,1,0:T(8,128)(2,1)S(1)}, u32[]{:S(2)}, u32[]{:S(2)}) collective-permute-start(bf16[2,1024,128]{2,1,0:T(8,128)(2,1)} %get-tuple-element.114), channel_id=1, source_target_pairs={{0,1},{1,2},{2,3},{3,4},{4,5},{5,6},{6,7},{7,0},{8,9},{9,10},{10,1... | collective-permute-start | bytes 1572872 | tf_op jit(solution)/shard_map/ppermute | solution.py:506
  225.5 27.9 %collective-permute-start.22 = (bf16[2,1024,128]{2,1,0:T(8,128)(2,1)}, bf16[2,1024,128]{2,1,0:T(8,128)(2,1)S(1)}, u32[]{:S(2)}, u32[]{:S(2)}) collective-permute-start(bf16[2,1024,128]{2,1,0:T(8,128)(2,1)} %get-tuple-element.115), channel_id=1, source_target_pairs={{0,2},{1,3},{2,4},{3,5},{4,6},{5,7},{6,0},{7,1},{8,10},{9,11},{10,... | collective-permute-start | bytes 1572872 | tf_op jit(solution)/shard_map/ppermute | solution.py:506
  241.5 34.2 %collective-permute-start.23 = (bf16[2,1024,128]{2,1,0:T(8,128)(2,1)}, bf16[2,1024,128]{2,1,0:T(8,128)(2,1)S(1)}, u32[]{:S(2)}, u32[]{:S(2)}) collective-permute-start(bf16[2,1024,128]{2,1,0:T(8,128)(2,1)} %get-tuple-element.116), channel_id=1, source_target_pairs={{0,3},{1,4},{2,5},{3,6},{4,7},{5,0},{6,1},{7,2},{8,11},{9,12},{10,... | collective-permute-start | bytes 1572872 | tf_op jit(solution)/shard_map/ppermute | solution.py:506
  241.5 45.4 %collective-permute-start.24 = (bf16[2,1024,128]{2,1,0:T(8,128)(2,1)}, bf16[2,1024,128]{2,1,0:T(8,128)(2,1)}, u32[]{:S(2)}, u32[]{:S(2)}) collective-permute-start(bf16[2,1024,128]{2,1,0:T(8,128)(2,1)} %get-tuple-element.117), channel_id=1, source_target_pairs={{0,4},{1,5},{2,6},{3,7},{4,0},{5,1},{6,2},{7,3},{8,12},{9,13},{10,... | collective-permute-start | bytes 1572872 | tf_op jit(solution)/shard_map/ppermute | solution.py:506
  241.6 34.1 %copy-start.18 = (bf16[2,1024,128]{2,1,0:T(8,128)(2,1)}, bf16[2,1024,128]{2,1,0:T(8,128)(2,1)S(1)}, u32[]{:S(2)}) copy-start(bf16[2,1024,128]{2,1,0:T(8,128)(2,1)S(1)} %collective-permute-done.41.refs_7_) | copy-start | bytes 1572868
  241.6 75.6 %collective-permute-start.25 = (bf16[2,1024,128]{2,1,0:T(8,128)(2,1)}, bf16[2,1024,128]{2,1,0:T(8,128)(2,1)}, u32[]{:S(2)}, u32[]{:S(2)}) collective-permute-start(bf16[2,1024,128]{2,1,0:T(8,128)(2,1)} %get-tuple-element.118), channel_id=1, source_target_pairs={{0,5},{1,6},{2,7},{3,0},{4,1},{5,2},{6,3},{7,4},{8,13},{9,14},{10,... | collective-permute-start | bytes 1572872 | tf_op jit(solution)/shard_map/ppermute | solution.py:506
  244.2 73.0 %copy-start = (bf16[2,1024,128]{2,1,0:T(8,128)(2,1)}, bf16[2,1024,128]{2,1,0:T(8,128)(2,1)S(1)}, u32[]{:S(2)}) copy-start(bf16[2,1024,128]{2,1,0:T(8,128)(2,1)S(1)} %collective-permute-done.21.refs_9_) | copy-start | bytes 1572868
  244.2 79.2 %collective-permute-start.26 = (bf16[2,1024,128]{2,1,0:T(8,128)(2,1)}, bf16[2,1024,128]{2,1,0:T(8,128)(2,1)}, u32[]{:S(2)}, u32[]{:S(2)}) collective-permute-start(bf16[2,1024,128]{2,1,0:T(8,128)(2,1)} %get-tuple-element.119), channel_id=1, source_target_pairs={{0,6},{1,7},{2,0},{3,1},{4,2},{5,3},{6,4},{7,5},{8,14},{9,15},{10,... | collective-permute-start | bytes 1572872 | tf_op jit(solution)/shard_map/ppermute | solution.py:506
  253.4 63.8 %copy-start.1 = (bf16[2,1024,128]{2,1,0:T(8,128)(2,1)}, bf16[2,1024,128]{2,1,0:T(8,128)(2,1)S(1)}, u32[]{:S(2)}) copy-start(bf16[2,1024,128]{2,1,0:T(8,128)(2,1)S(1)} %collective-permute-done.22.refs_10_) | copy-start | bytes 1572868
  253.4 78.4 %collective-permute-start.27 = (bf16[2,1024,128]{2,1,0:T(8,128)(2,1)}, bf16[2,1024,128]{2,1,0:T(8,128)(2,1)}, u32[]{:S(2)}, u32[]{:S(2)}) collective-permute-start(bf16[2,1024,128]{2,1,0:T(8,128)(2,1)} %get-tuple-element.120), channel_id=1, source_target_pairs={{0,7},{1,0},{2,1},{3,2},{4,3},{5,4},{6,5},{7,6},{8,15},{9,8},{10,9... | collective-permute-start | bytes 1572872 | tf_op jit(solution)/shard_map/ppermute | solution.py:506
  275.7 41.5 %copy-start.2 = (bf16[2,1024,128]{2,1,0:T(8,128)(2,1)}, bf16[2,1024,128]{2,1,0:T(8,128)(2,1)S(1)}, u32[]{:S(2)}) copy-start(bf16[2,1024,128]{2,1,0:T(8,128)(2,1)S(1)} %collective-permute-done.23.refs_11_) | copy-start | bytes 1572868
  275.7 56.1 %collective-permute-start.10 = (bf16[2,1024,128]{2,1,0:T(8,128)(2,1)}, bf16[2,1024,128]{2,1,0:T(8,128)(2,1)}, u32[]{:S(2)}, u32[]{:S(2)}) collective-permute-start(bf16[2,1024,128]{2,1,0:T(8,128)(2,1)} %get-tuple-element.97), channel_id=1, source_target_pairs={{0,4},{1,5},{2,6},{3,7},{4,0},{5,1},{6,2},{7,3},{8,12},{9,13},{10,... | collective-permute-start | bytes 1572872 | tf_op jit(solution)/shard_map/ppermute | solution.py:506
  286.9 51.6 %collective-permute-start.11 = (bf16[2,1024,128]{2,1,0:T(8,128)(2,1)}, bf16[2,1024,128]{2,1,0:T(8,128)(2,1)}, u32[]{:S(2)}, u32[]{:S(2)}) collective-permute-start(bf16[2,1024,128]{2,1,0:T(8,128)(2,1)} %get-tuple-element.98), channel_id=1, source_target_pairs={{0,5},{1,6},{2,7},{3,0},{4,1},{5,2},{6,3},{7,4},{8,13},{9,14},{10,... | collective-permute-start | bytes 1572872 | tf_op jit(solution)/shard_map/ppermute | solution.py:506
  317.3 52.3 %collective-permute-start.12 = (bf16[2,1024,128]{2,1,0:T(8,128)(2,1)}, bf16[2,1024,128]{2,1,0:T(8,128)(2,1)S(1)}, u32[]{:S(2)}, u32[]{:S(2)}) collective-permute-start(bf16[2,1024,128]{2,1,0:T(8,128)(2,1)} %get-tuple-element.99), channel_id=1, source_target_pairs={{0,6},{1,7},{2,0},{3,1},{4,2},{5,3},{6,4},{7,5},{8,14},{9,15},{10,... | collective-permute-start | bytes 1572872 | tf_op jit(solution)/shard_map/ppermute | solution.py:506
  323.5 46.1 %collective-permute-start.13 = (bf16[2,1024,128]{2,1,0:T(8,128)(2,1)}, bf16[2,1024,128]{2,1,0:T(8,128)(2,1)S(1)}, u32[]{:S(2)}, u32[]{:S(2)}) collective-permute-start(bf16[2,1024,128]{2,1,0:T(8,128)(2,1)} %get-tuple-element.100), channel_id=1, source_target_pairs={{0,7},{1,0},{2,1},{3,2},{4,3},{5,4},{6,5},{7,6},{8,15},{9,8},{10,9... | collective-permute-start | bytes 1572872 | tf_op jit(solution)/shard_map/ppermute | solution.py:506
  331.8 37.7 %collective-permute-start.7 = (bf16[2,1024,128]{2,1,0:T(8,128)(2,1)}, bf16[2,1024,128]{2,1,0:T(8,128)(2,1)S(1)}, u32[]{:S(2)}, u32[]{:S(2)}) collective-permute-start(bf16[2,1024,128]{2,1,0:T(8,128)(2,1)} %get-tuple-element.94), channel_id=1, source_target_pairs={{0,1},{1,2},{2,3},{3,4},{4,5},{5,6},{6,7},{7,0},{8,9},{9,10},{10,1... | collective-permute-start | bytes 1572872 | tf_op jit(solution)/shard_map/ppermute | solution.py:506
  331.8 37.8 %collective-permute-start.8 = (bf16[2,1024,128]{2,1,0:T(8,128)(2,1)}, bf16[2,1024,128]{2,1,0:T(8,128)(2,1)}, u32[]{:S(2)}, u32[]{:S(2)}) collective-permute-start(bf16[2,1024,128]{2,1,0:T(8,128)(2,1)} %get-tuple-element.95), channel_id=1, source_target_pairs={{0,2},{1,3},{2,4},{3,5},{4,6},{5,7},{6,0},{7,1},{8,10},{9,11},{10,... | collective-permute-start | bytes 1572872 | tf_op jit(solution)/shard_map/ppermute | solution.py:506
  338.5 31.4 %collective-permute-start.9 = (bf16[2,1024,128]{2,1,0:T(8,128)(2,1)}, bf16[2,1024,128]{2,1,0:T(8,128)(2,1)}, u32[]{:S(2)}, u32[]{:S(2)}) collective-permute-start(bf16[2,1024,128]{2,1,0:T(8,128)(2,1)} %get-tuple-element.96), channel_id=1, source_target_pairs={{0,3},{1,4},{2,5},{3,6},{4,7},{5,0},{6,1},{7,2},{8,11},{9,12},{10,... | collective-permute-start | bytes 1572872 | tf_op jit(solution)/shard_map/ppermute | solution.py:506
  369.5 0.8 copy-start.3
  369.6 0.9 copy-start.4
  369.6 1.1 copy-start.5

commit v2 on v1

--- a/solution.py
+++ b/solution.py
@@ -12,7 +12,7 @@
 step_size = 0.5
 penalty = 1.0
 threshold = 0.3
-VMEM_LIMIT = 62 * 1024 * 1024
+VMEM_LIMIT = 67000000
 F32 = jnp.float32
 BF16 = jnp.bfloat16
 
@@ -30,6 +30,9 @@
     return jnp.asarray(whole.astype(np.float32)).astype(BF16)
 
 
+HBM = pl.BlockSpec(memory_space=pltpu.HBM)
+
+
 def params(**extra):
     return pltpu.CompilerParams(vmem_limit_bytes=VMEM_LIMIT, **extra)
 
@@ -47,18 +50,19 @@
     return 8 * (tiles + 1 - tiles % 2)
 
 
-def gather_rows(ref, row, size, parts_n):
+def gather_rows(ref, row, parts_n):
     pieces = []
     for p in range(2):
         for s in range(parts_n):
-            pieces.append(ref[s, p, pl.ds(row, size), :])
+            pieces.append(ref[s, p, row])
     return jnp.concatenate(pieces, axis=0)
 
 
-def forward_kernel(n, kl, xl, table, image, sens, *refs):
+def forward_kernel(n, kl, xp, table, image, sens, *refs):
     outs, flat = refs[:n], refs[n]
-    length = image.shape[2]
+    rows, length = image.shape[1], image.shape[2]
     me = lax.axis_index("slab")
+    step = pl.program_id(0)
 
     def pair(i, carry):
         columns = []
@@ -77,57 +81,99 @@
         half = jnp.dot(table[...], both, preferred_element_type=F32)
         depth = half.shape[1] // 2
         for h in range(2):
-            flat[pl.ds(2 * i + h, 2 * length, stride=pitch(xl)), :] = half[:, h * depth : (h + 1) * depth]
-        return carry
-
-    lax.fori_loop(0, xl // 2, pair, 0)
-    for off in range(n):
-        d = lax.rem(me + off, n)
-        for p in range(2):
-
-            def settle(k, carry):
-                base = pl.multiple_of(((p * n + d) * kl + 2 * k) * pitch(xl), 8)
-                rows = [flat[pl.ds(base + h * pitch(xl), xl), :] for h in range(2)]
-                target = pl.ds(pl.multiple_of(2 * k * xl, 2 * xl), 2 * xl)
-                outs[off][p, target, :] = jnp.concatenate(rows, axis=0).astype(BF16)
-                return carry
-
-            lax.fori_loop(0, kl // 2, settle, 0, unroll=4)
-
-
-def forward_call(table, image, sensitivity, first, n, kl):
+            where = pl.ds(step * rows + 2 * i + h, 2 * length, stride=pitch(xp))
+            flat[where, :] = half[:, h * depth : (h + 1) * depth]
+        return carry
+
+    lax.fori_loop(0, rows // 2, pair, 0)
+
+    @pl.when(step == pl.num_programs(0) - 1)
+    def last():
+        for off in range(n):
+            d = lax.rem(me + off, n)
+            for p in range(2):
+
+                def settle(k, carry):
+                    base = pl.multiple_of(((p * n + d) * kl + 2 * k) * pitch(xp), 8)
+                    for h in range(2):
+                        outs[off][p, 2 * k + h] = flat[pl.ds(base + h * pitch(xp), xp), :].astype(BF16)
+                    return carry
+
+                lax.fori_loop(0, kl // 2, settle, 0, unroll=4)
+
+
+def forward_call(table, image, sensitivity, coil, part, parts, n, kl):
     _, _, xl, length, depth = sensitivity.shape
+    xp = xl // parts
+    rows = 8 if xp % 8 == 0 else xp
+    steps = xp // rows
     return pl.pallas_call(
-        functools.partial(forward_kernel, n, kl, xl),
-        grid=(1,),
+        functools.partial(forward_kernel, n, kl, xp),
+        grid=(steps,),
         in_specs=[
             once(table.shape),
-            once(image.shape),
-            pl.BlockSpec((1, 2, xl, length, depth), lambda i: (first, 0, 0, 0, 0)),
+            pl.BlockSpec((2, rows, length, depth), lambda i: (0, part * steps + i, 0, 0)),
+            pl.BlockSpec((1, 2, rows, length, depth), lambda i: (coil, 0, part * steps + i, 0, 0)),
         ],
-        out_specs=[pl.BlockSpec((2, kl * xl, depth), lambda i: (0, 0, 0))] * n,
-        out_shape=[jax.ShapeDtypeStruct((2, kl * xl, depth), BF16)] * n,
-        scratch_shapes=[pltpu.VMEM(((2 * length + 1) * pitch(xl), depth), F32)],
+        out_specs=[once((2, kl, xp, depth))] * n,
+        out_shape=[jax.ShapeDtypeStruct((2, kl, xp, depth), BF16)] * n,
+        scratch_shapes=[pltpu.VMEM(((2 * length + 1) * pitch(xp), depth), F32)],
         compiler_params=params(),
-        cost_estimate=cost(8 * length * length * xl * depth, 12 * xl * length * depth),
+        cost_estimate=cost(8 * length * length * xp * depth, 12 * xp * length * depth),
         name="forward",
     )(table, image, sensitivity)
 
 
-def tile_kernel(n, kl, xl, win, offsets, counts, fwd, inv, blocks, samples, *refs):
-    pieces, outs, refs = refs[:n], refs[n : 2 * n], refs[2 * n :]
-    total, kspace, weights, piece, sem, piece_sem, *wide = refs
+def sort_kernel(samples, out, flat):
+    parts = out.shape[0]
+    psize = out.shape[2]
+    depth = samples.shape[2]
+    for g in range(samples.shape[0]):
+        flat[...] = samples[g].astype(F32)
+        for c in range(parts):
+            for p in range(2):
+                rows = flat[pl.ds(2 * c + p, psize, stride=2 * parts), :]
+                out[c, g, :, p * depth : (p + 1) * depth] = rows.astype(BF16)
+
+
+def sort_call(samples):
+    _, slots, psize, coils, parts, depth = samples.shape
+    group = 4 if slots % 4 == 0 else 1
+    lines = psize * coils * parts
+    return pl.pallas_call(
+        sort_kernel,
+        grid=(slots // group,),
+        in_specs=[pl.BlockSpec((group, lines, depth), lambda i: (i, 0, 0))],
+        out_specs=pl.BlockSpec((coils, group, psize, parts * depth), lambda i: (0, i, 0, 0)),
+        out_shape=jax.ShapeDtypeStruct((coils, slots, psize, parts * depth), BF16),
+        scratch_shapes=[pltpu.VMEM((lines, depth), F32)],
+        compiler_params=params(),
+        cost_estimate=cost(samples.size, 4 * samples.size),
+        name="sort",
+    )(samples.reshape(slots, lines, depth))
+
+
+def tile_kernel(n, kl, xl, win, parts, coil, offsets, counts, fwd, inv, blocks, sorted_samples, *refs):
+    pieces, outs, refs = refs[: n * parts], refs[n * parts : n * parts + n], refs[n * parts + n :]
+    total, kspace, weights, piece, samples, leaving, sem, piece_sem, *wide = refs
     me = lax.axis_index("slab")
     copies = []
+    xp = xl // parts
     for off in range(n):
         origin = lax.rem(me + n - off, n)
-        copies.append(pltpu.make_async_copy(pieces[off], piece.at[origin], piece_sem.at[off]))
+        for h in range(parts):
+            target = piece.at[origin, :, :, pl.ds(h * xp, xp)]
+            copies.append(pltpu.make_async_copy(pieces[h * n + off], target, piece_sem.at[h * n + off]))
     for copy in copies:
         copy.start()
-    fetch = pltpu.make_async_copy(blocks.at[0], weights, sem)
-    fetch.start()
     for copy in copies:
         copy.wait()
+    fetches = [
+        pltpu.make_async_copy(blocks.at[0], weights, sem.at[0]),
+        pltpu.make_async_copy(sorted_samples.at[coil], samples, sem.at[1]),
+    ]
+    for fetch in fetches:
+        fetch.start()
     length = n * xl
     depth = piece.shape[-1]
     if wide:
@@ -141,8 +187,7 @@
     def to_kspace(i, carry):
         columns = []
         for h in range(2):
-            row = pl.multiple_of((2 * i + h) * xl, xl)
-            columns.append(gather_rows(source, row, xl, n).astype(BF16))
+            columns.append(gather_rows(source, 2 * i + h, n).astype(BF16))
         spec = jnp.dot(fwd[...], jnp.concatenate(columns, axis=1), preferred_element_type=F32)
         for h in range(2):
             for p in range(2):
@@ -162,7 +207,8 @@
         return carry
 
     lax.fori_loop(0, length, settle, 0, unroll=8)
-    fetch.wait()
+    for fetch in fetches:
+        fetch.wait()
     cells = win * kl
     chunk = min(cells, 512)
 
@@ -212,15 +258,18 @@
                 base = pl.multiple_of((d * xl + 2 * k) * pitch(kl), 8)
                 rows = [total[p, pl.ds(base + h * pitch(kl), kl), :] for h in range(2)]
                 target = pl.ds(pl.multiple_of(2 * k * kl, 2 * kl), 2 * kl)
-                outs[off][p, target, :] = jnp.concatenate(rows, axis=0).astype(BF16)
+                leaving[off, p, target, :] = jnp.concatenate(rows, axis=0).astype(BF16)
                 return carry
 
             lax.fori_loop(0, xl // 2, leave, 0, unroll=4)
+        pltpu.make_async_copy(leaving.at[off], outs[off], piece_sem.at[off]).start()
+    for off in range(n):
+        pltpu.make_async_copy(leaving.at[off], outs[off], piece_sem.at[off]).wait()
 
 
 def tile_call(fwd, inv, pieces, blocks, samples, offsets, counts, coil, n, kl, xl):
-    shape = pieces[0].shape
-    depth = shape[-1]
+    depth = pieces[0].shape[-1]
+    parts = len(pieces) // n
     _, slots, psize, cells = blocks.shape
     length = n * xl
     narrow = kl % 16 == 0 and xl % 16 == 0
@@ -228,28 +277,21 @@
         pltpu.VMEM((2, (length + 1) * pitch(kl), depth), F32),
         pltpu.VMEM((length * kl, 2 * depth), BF16 if narrow else F32),
         pltpu.VMEM(blocks.shape[1:], BF16),
-        pltpu.VMEM((n, *shape), BF16),
-        pltpu.SemaphoreType.DMA,
-        pltpu.SemaphoreType.DMA((n,)),
+        pltpu.VMEM((n, 2, kl, xl, depth), BF16),
+        pltpu.VMEM((slots, psize, 2 * depth), BF16),
+        pltpu.VMEM((n, 2, xl * kl, depth), BF16),
+        pltpu.SemaphoreType.DMA((2,)),
+        pltpu.SemaphoreType.DMA((n * parts,)),
     ]
     if not narrow:
-        scratch.append(pltpu.VMEM((n, *shape), F32))
-    anywhere = pl.BlockSpec(memory_space=pl.ANY)
+        scratch.append(pltpu.VMEM((n, 2, kl, xl, depth), F32))
     smem = pl.BlockSpec(memory_space=pltpu.SMEM)
     return pl.pallas_call(
-        functools.partial(tile_kernel, n, kl, xl, cells // kl),
+        functools.partial(tile_kernel, n, kl, xl, cells // kl, parts, coil),
         grid=(1,),
-        in_specs=[
-            smem,
-            smem,
-            once(fwd.shape),
-            once(inv.shape),
-            anywhere,
-            pl.BlockSpec((slots, psize, 2 * depth), lambda i: (0, 0, coil), pipeline_mode=pl.Buffered(1)),
-        ]
-        + [anywhere] * n,
-        out_specs=[pl.BlockSpec(shape, lambda i: (0, 0, 0))] * n,
-        out_shape=[jax.ShapeDtypeStruct(shape, BF16)] * n,
+        in_specs=[smem, smem, once(fwd.shape), once(inv.shape), HBM, HBM] + [HBM] * (n * parts),
+        out_specs=[HBM] * n,
+        out_shape=[jax.ShapeDtypeStruct((2, xl * kl, depth), BF16)] * n,
         scratch_shapes=scratch,
         compiler_params=params(),
         cost_estimate=cost(
@@ -398,10 +440,9 @@
 
 def finish_call(table, backs, sent, sensitivity, shares, n, kl):
     coils, _, xl, length, depth = sensitivity.shape
-    chunks = xl // 4 if xl % 4 == 0 else 1
+    chunks = xl // 2 if xl % 2 == 0 else 1
     rows = xl // chunks
     share = length // shares
-    anywhere = pl.BlockSpec(memory_space=pl.ANY)
     vmem = pl.BlockSpec(memory_space=pltpu.VMEM)
     scratch = [
         pltpu.VMEM((coils, n, 2, xl * kl, depth), BF16),
@@ -418,7 +459,7 @@
         scratch.append(pltpu.VMEM((coils, n, 2, rows * kl, depth), F32))
     return pl.pallas_call(
         functools.partial(finish_kernel, n, shares, kl, xl, chunks, sent),
-        in_specs=[vmem, anywhere] + [anywhere] * (coils * n),
+        in_specs=[vmem, HBM] + [HBM] * (coils * n),
         out_specs=vmem,
         out_shape=jax.ShapeDtypeStruct((2, xl, share, depth), F32),
         scratch_shapes=scratch,
@@ -470,7 +511,7 @@
 
 def update_call(image, gradient, auxiliary, dual, position):
     _, xl, share, depth = auxiliary.shape
-    rows = 8 if xl % 8 == 0 else 2
+    rows = 4 if xl % 4 == 0 else 2
     block = (2, rows, share, depth)
     plain = pl.BlockSpec(block, lambda i, w: (0, i, 0, 0))
     shape = jax.ShapeDtypeStruct(auxiliary.shape, F32)
@@ -497,7 +538,6 @@
     y_inv = complex_table(length_y, True)
     x_fwd = complex_table(n * xl, False)
     x_inv = complex_table(n * xl, True)
-    flat_samples = samples.reshape(samples.shape[1], samples.shape[2], -1)
 
     def swap(parts):
         moved = [parts[0]]
@@ -507,13 +547,19 @@
         return moved
 
     def tile_of(pieces, c):
-        return tile_call(x_fwd, x_inv, pieces, blocks, flat_samples, offsets, counts, c, n, kl, xl)
+        return tile_call(x_fwd, x_inv, pieces, blocks, sorted_samples, offsets, counts, c, n, kl, xl)
 
     pieces, tiles, table = [], [], y_fwd
     for c in range(coils):
-        half = list(forward_call(table, image, sensitivity, c, n, kl))
-        table, half[0] = lax.optimization_barrier((table, half[0]))
-        pieces.append(swap(half))
+        parts = 2 if c == 0 and xl % 32 == 0 else 1
+        moved = []
+        for part in range(parts):
+            half = list(forward_call(table, image, sensitivity, c, part, parts, n, kl))
+            table, half[0] = lax.optimization_barrier((table, half[0]))
+            moved += swap(half)
+        pieces.append(moved)
+    table, samples = lax.optimization_barrier((table, samples))
+    sorted_samples = sort_call(samples)
     for c in range(coils):
         if c:
             pieces[c][0], tiles[-1][0] = lax.optimization_barrier((pieces[c][0], tiles[-1][0]))

time: 504 us -> 472 us (0.937)
  Pallas kernels: 306 us -> 285 us
  local copies, waits for them, and re-layouts: 15.7 us -> 0 us
    pallas_call x8 -> x10, Pallas kernels: 173 us -> 157 us  [the longest x4 103 us: tile_call(): pl.pallas_call(functools.partial(tile_kernel, n, kl, xl, cells // kl, par...]
    reshape x1 -> x0, local copies, waits for them, and re-layouts: 11 us -> none  [body(): flat_samples = samples.reshape(samples.shape[1], samples.shape[2], -1)]
    pallas_call x1, Pallas kernels: 126 us -> 119 us  [finish_call(): pl.pallas_call(functools.partial(finish_kernel, n, shares, kl, xl, chunks...]
    ppermute x42 -> x49, starting transfers between devices: 96.7 us -> 98.4 us  [swap(): moved.append(lax.ppermute(parts[off], 'slab', ring))]
    ppermute x42 -> x49, waiting for transfers between devices: 83.5 us -> 83.6 us  [swap(): moved.append(lax.ppermute(parts[off], 'slab', ring))]
  transfers between devices with their start and end apart: 42 -> 49, of which waited for: 9 -> 12; matrix products, arithmetic and copies ran while one was open for 2% -> 0% of each run, Pallas kernels for 32% -> 31%
where the time goes in v2:
time: 472 us; the launch traced here: 469 us
  Pallas kernels  285 us (60%)
  starting transfers between devices  98.4 us (21%)
  waiting for transfers between devices  83.6 us (18%)
    pallas_call x1, Pallas kernels, finish_call(): pl.pallas_call(functools.partial(finish_kernel, n, shares, kl, xl, chunks...  119 us
    pallas_call x4, Pallas kernels, tile_call(): pl.pallas_call(functools.partial(tile_kernel, n, kl, xl, cells // kl, par...  103 us
    ppermute x49, starting transfers between devices, swap(): moved.append(lax.ppermute(parts[off], 'slab', ring))  98.4 us
    ppermute x49, waiting for transfers between devices, swap(): moved.append(lax.ppermute(parts[off], 'slab', ring))  83.6 us
    pallas_call x5, Pallas kernels, forward_call(): pl.pallas_call(functools.partial(forward_kernel, n, kl, xp), grid=(steps,...  46 us
  transfers between devices with their start and end apart: 49, of which 12 were waited for; matrix products, arithmetic and copies ran while one was open for 0% of the time, Pallas kernels for 31%

profile of v2, /device:TPU:9, one launch (start us, length us, event | category | flops | bytes accessed | tf_op | source)
XLA Modules:
  0.0 469.0 jit_solution(14585574931011002767)
XLA Ops:
  0.6 6.7 %forward.5 = (bf16[2,32,16,128]{3,2,1,0:T(8,128)(2,1)}, bf16[2,32,16,128]{3,2,1,0:T(8,128)(2,1)}, bf16[2,32,16,128]{3,2,1,0:T(8,128)(2,1)}, bf16[2,32,16,128]{3,...) custom-call(bf16[512,512]{1,0:T(8,128)(2,1)} %constant.16.table.fwd,, ...), custom_call_target="tpu_custom_call" | custom-call | flops 1073741824 | bytes 6291456 | tf_op jit(solution)/shard_map/forward/pallas_call | solution.py:110
  7.3 6.6 %forward.6 = (bf16[2,32,16,128]{3,2,1,0:T(8,128)(2,1)}, bf16[2,32,16,128]{3,2,1,0:T(8,128)(2,1)}, bf16[2,32,16,128]{3,2,1,0:T(8,128)(2,1)}, bf16[2,32,16,128]{3,...) custom-call(bf16[512,512]{1,0:T(8,128)(2,1)} %constant.16.table.fwd,, ...), custom_call_target="tpu_custom_call" | custom-call | flops 1073741824 | bytes 6291456 | tf_op jit(solution)/shard_map/forward/pallas_call | solution.py:110
  13.9 1.2 collective-permute-start.10
  15.2 2.0 collective-permute-start.11
  17.2 0.2 collective-permute-start.12
  17.4 0.8 collective-permute-start.13
  18.2 0.9 collective-permute-start.7
  19.1 2.3 collective-permute-done.10.refs_12_
  21.4 12.4 %collective-permute-start.8 = (bf16[2,32,16,128]{3,2,1,0:T(8,128)(2,1)}, bf16[2,32,16,128]{3,2,1,0:T(8,128)(2,1)}, u32[]{:S(2)}, u32[]{:S(2)}) collective-permute-start(bf16[2,32,16,128]{3,2,1,0:T(8,128)(2,1)} %get-tuple-element.106), channel_id=1, source_target_pairs={{0,2},{1,3},{2,4},{3,5},{4,6},{5,7},{6,0},{7,1},{8,10},{9,11},{10,... | collective-permute-start | bytes 786440 | tf_op jit(solution)/shard_map/ppermute | solution.py:546
  33.9 3.0 collective-permute-start.9
  36.8 0.0 collective-permute-done.12.refs_14_
  36.8 0.3 collective-permute-start
  37.1 3.1 collective-permute-start.1
  40.2 0.1 collective-permute-done.8.refs_10_
  40.3 0.2 collective-permute-start.3
  40.5 19.0 %collective-permute-done.9.refs_11_ = bf16[2,32,16,128]{3,2,1,0:T(8,128)(2,1)} collective-permute-done((bf16[2,32,16,128]{3,2,1,0:T(8,128)(2,1)}, bf16[2,32,16,128]{3,2,1,0:T(8,128)(2,1)}, u32[]{:S(2)}, u32[]{:S(2)}) %collective-permute-start.9) | collective-permute-done | bytes 262176 | tf_op jit(solution)/shard_map/ppermute | solution.py:546
  59.6 0.0 collective-permute-start.4
  59.6 0.0 collective-permute-done.refs_1_
  59.6 3.7 collective-permute-start.5
  63.2 0.0 collective-permute-start.6
  63.3 10.9 %forward.7 = (bf16[2,32,32,128]{3,2,1,0:T(8,128)(2,1)}, bf16[2,32,32,128]{3,2,1,0:T(8,128)(2,1)}, bf16[2,32,32,128]{3,2,1,0:T(8,128)(2,1)}, bf16[2,32,32,128]{3,...) custom-call(bf16[512,512]{1,0:T(8,128)(2,1)} %constant.16.table.fwd,, ...), custom_call_target="tpu_custom_call" | custom-call | flops 2147483648 | bytes 12582912 | tf_op jit(solution)/shard_map/forward/pallas_call | solution.py:110
  74.2 0.0 collective-permute-done.2.refs_3_
  74.2 1.8 collective-permute-start.21
  75.9 1.0 collective-permute-start.22
  77.0 0.6 collective-permute-start.23
  77.6 0.2 collective-permute-start.24
  77.8 2.4 collective-permute-start.25
  80.2 10.9 %forward.8 = (bf16[2,32,32,128]{3,2,1,0:T(8,128)(2,1)}, bf16[2,32,32,128]{3,2,1,0:T(8,128)(2,1)}, bf16[2,32,32,128]{3,2,1,0:T(8,128)(2,1)}, bf16[2,32,32,128]{3,...) custom-call(bf16[512,512]{1,0:T(8,128)(2,1)} %constant.16.table.fwd,, ...), custom_call_target="tpu_custom_call" | custom-call | flops 2147483648 | bytes 12582912 | tf_op jit(solution)/shard_map/forward/pallas_call | solution.py:110
  91.1 1.5 collective-permute-start.26
  92.6 7.5 %collective-permute-done.22.refs_2_ = bf16[2,32,32,128]{3,2,1,0:T(8,128)(2,1)} collective-permute-done((bf16[2,32,32,128]{3,2,1,0:T(8,128)(2,1)}, bf16[2,32,32,128]{3,2,1,0:T(8,128)(2,1)}, u32[]{:S(2)}, u32[]{:S(2)}) %collective-permute-start.22) | collective-permute-done | bytes 524320 | tf_op jit(solution)/shard_map/ppermute | solution.py:546
  100.1 11.1 %collective-permute-done.23.refs_3_ = bf16[2,32,32,128]{3,2,1,0:T(8,128)(2,1)} collective-permute-done((bf16[2,32,32,128]{3,2,1,0:T(8,128)(2,1)}, bf16[2,32,32,128]{3,2,1,0:T(8,128)(2,1)}, u32[]{:S(2)}, u32[]{:S(2)}) %collective-permute-start.23) | collective-permute-done | bytes 524320 | tf_op jit(solution)/shard_map/ppermute | solution.py:546
  111.1 12.7 %collective-permute-done.24.refs_4_ = bf16[2,32,32,128]{3,2,1,0:T(8,128)(2,1)} collective-permute-done((bf16[2,32,32,128]{3,2,1,0:T(8,128)(2,1)}, bf16[2,32,32,128]{3,2,1,0:T(8,128)(2,1)}, u32[]{:S(2)}, u32[]{:S(2)}) %collective-permute-start.24) | collective-permute-done | bytes 524320 | tf_op jit(solution)/shard_map/ppermute | solution.py:546
  123.8 0.2 collective-permute-done.25.refs_5_
  124.0 10.9 %forward.9 = (bf16[2,32,32,128]{3,2,1,0:T(8,128)(2,1)}, bf16[2,32,32,128]{3,2,1,0:T(8,128)(2,1)}, bf16[2,32,32,128]{3,2,1,0:T(8,128)(2,1)}, bf16[2,32,32,128]{3,...) custom-call(bf16[512,512]{1,0:T(8,128)(2,1)} %constant.16.table.fwd,, ...), custom_call_target="tpu_custom_call" | custom-call | flops 2147483648 | bytes 12582912 | tf_op jit(solution)/shard_map/forward/pallas_call | solution.py:110
  134.9 1.3 collective-permute-start.38
  136.3 2.9 collective-permute-start.39
  139.2 1.3 collective-permute-start.40
  140.4 4.6 collective-permute-done.36.refs_2_
  145.1 11.1 %collective-permute-done.37.refs_3_ = bf16[2,32,32,128]{3,2,1,0:T(8,128)(2,1)} collective-permute-done((bf16[2,32,32,128]{3,2,1,0:T(8,128)(2,1)}, bf16[2,32,32,128]{3,2,1,0:T(8,128)(2,1)}, u32[]{:S(2)}, u32[]{:S(2)}) %collective-permute-start.37) | collective-permute-done | bytes 524320 | tf_op jit(solution)/shard_map/ppermute | solution.py:546
  156.8 8.3 %sort.1.sorted_samples = bf16[4,24,128,256]{3,2,1,0:T(8,128)(2,1)} custom-call(bf16[24,1024,128]{2,1,0:T(8,128)(2,1)} %bitcast.2), custom_call_target="tpu_custom_call" | custom-call | flops 3145728 | bytes 12582912 | tf_op jit(solution)/shard_map/sort/pallas_call | solution.py:143
  165.1 3.7 collective-permute-done.38.refs_4_
  168.8 4.1 collective-permute-start.43
  172.9 1.8 collective-permute-start.44
  174.8 1.3 collective-permute-start.45
  176.0 3.3 collective-permute-start.46
  179.4 3.5 collective-permute-start.47
  182.8 25.6 %tile.4 = (bf16[2,1024,128]{2,1,0:T(8,128)(2,1)}, bf16[2,1024,128]{2,1,0:T(8,128)(2,1)}, bf16[2,1024,128]{2,1,0:T(8,128)(2,1)}, bf16[2,1024,128]{2,1,0:T(8,128)(...) custom-call(s32[1,24]{1,0:T(1,128)} %offsets.7, ...), custom_call_target="tpu_custom_call" | custom-call | flops 10737418240 | bytes 20971520 | tf_op jit(solution)/shard_map/tile/pallas_call | solution.py:289
  208.5 0.1 collective-permute-start.48
  208.5 1.7 collective-permute-start.14
  210.3 8.7 %collective-permute-done.45.refs_4_ = bf16[2,32,32,128]{3,2,1,0:T(8,128)(2,1)} collective-permute-done((bf16[2,32,32,128]{3,2,1,0:T(8,128)(2,1)}, bf16[2,32,32,128]{3,2,1,0:T(8,128)(2,1)}, u32[]{:S(2)}, u32[]{:S(2)}) %collective-permute-start.45) | collective-permute-done | bytes 524320 | tf_op jit(solution)/shard_map/ppermute | solution.py:546
  219.0 6.3 %collective-permute-start.15 = (bf16[2,1024,128]{2,1,0:T(8,128)(2,1)}, bf16[2,1024,128]{2,1,0:T(8,128)(2,1)}, u32[]{:S(2)}, u32[]{:S(2)}) collective-permute-start(bf16[2,1024,128]{2,1,0:T(8,128)(2,1)} %get-tuple-element.115), channel_id=1, source_target_pairs={{0,2},{1,3},{2,4},{3,5},{4,6},{5,7},{6,0},{7,1},{8,10},{9,11},{10,... | collective-permute-start | bytes 1572872 | tf_op jit(solution)/shard_map/ppermute | solution.py:546
  225.3 2.3 collective-permute-start.17
  227.5 25.6 %tile.5 = (bf16[2,1024,128]{2,1,0:T(8,128)(2,1)}, bf16[2,1024,128]{2,1,0:T(8,128)(2,1)}, bf16[2,1024,128]{2,1,0:T(8,128)(2,1)}, bf16[2,1024,128]{2,1,0:T(8,128)(...) custom-call(s32[1,24]{1,0:T(1,128)} %offsets.7, ...), custom_call_target="tpu_custom_call" | custom-call | flops 10737418240 | bytes 20971520 | tf_op jit(solution)/shard_map/tile/pallas_call | solution.py:289
  253.1 2.9 collective-permute-start.18
  256.0 13.1 %collective-permute-start.19 = (bf16[2,1024,128]{2,1,0:T(8,128)(2,1)}, bf16[2,1024,128]{2,1,0:T(8,128)(2,1)}, u32[]{:S(2)}, u32[]{:S(2)}) collective-permute-start(bf16[2,1024,128]{2,1,0:T(8,128)(2,1)} %get-tuple-element.119), channel_id=1, source_target_pairs={{0,6},{1,7},{2,0},{3,1},{4,2},{5,3},{6,4},{7,5},{8,14},{9,15},{10,... | collective-permute-start | bytes 1572872 | tf_op jit(solution)/shard_map/ppermute | solution.py:546
  269.1 1.7 collective-permute-start.28
  270.9 25.8 %tile.6 = (bf16[2,1024,128]{2,1,0:T(8,128)(2,1)}, bf16[2,1024,128]{2,1,0:T(8,128)(2,1)}, bf16[2,1024,128]{2,1,0:T(8,128)(2,1)}, bf16[2,1024,128]{2,1,0:T(8,128)(...) custom-call(s32[1,24]{1,0:T(1,128)} %offsets.7, ...), custom_call_target="tpu_custom_call" | custom-call | flops 10737418240 | bytes 20971520 | tf_op jit(solution)/shard_map/tile/pallas_call | solution.py:289
  296.7 14.2 %collective-permute-start.30 = (bf16[2,1024,128]{2,1,0:T(8,128)(2,1)}, bf16[2,1024,128]{2,1,0:T(8,128)(2,1)}, u32[]{:S(2)}, u32[]{:S(2)}) collective-permute-start(bf16[2,1024,128]{2,1,0:T(8,128)(2,1)} %get-tuple-element.136), channel_id=1, source_target_pairs={{0,3},{1,4},{2,5},{3,6},{4,7},{5,0},{6,1},{7,2},{8,11},{9,12},{10,... | collective-permute-start | bytes 1572872 | tf_op jit(solution)/shard_map/ppermute | solution.py:546
  310.8 0.1 collective-permute-start.32
  310.9 1.3 collective-permute-start.33
  312.2 2.6 collective-permute-done.29.refs_10_
  314.8 25.6 %tile.7 = (bf16[2,1024,128]{2,1,0:T(8,128)(2,1)}, bf16[2,1024,128]{2,1,0:T(8,128)(2,1)}, bf16[2,1024,128]{2,1,0:T(8,128)(2,1)}, bf16[2,1024,128]{2,1,0:T(8,128)(...) custom-call(s32[1,24]{1,0:T(1,128)} %offsets.7, ...), custom_call_target="tpu_custom_call" | custom-call | flops 10737418240 | bytes 20971520 | tf_op jit(solution)/shard_map/tile/pallas_call | solution.py:289
  340.4 119.5 %finish.1.gradient = f32[2,32,64,128]{3,2,1,0:T(8,128)} custom-call(bf16[512,512]{1,0:T(8,128)(2,1)} %constant.15.inv.table, bf16[4,2,32,256,128]{4,3,2,1,0:T(8,128)(2,1)} %sens.11, bf16[2,1024,128]{2,1,0:T(8,128)(2,1)} %get-tuple-element.113.refs_0_, bf16[2,1024,128]{2,1,0:T(8,128)(2,1)} %collective-permute-done.14.refs_1_, ...), custom_call_target="tpu_custom_call" | custom-call | tf_op jit(solution)/shard_map/finish/pallas_call | solution.py:460
  459.9 9.0 %update.1 = (f32[2,32,64,128]{3,2,1,0:T(8,128)}, f32[2,32,64,128]{3,2,1,0:T(8,128)}, f32[2,32,64,128]{3,2,1,0:T(8,128)}) custom-call(s32[1]{0:T(128)} %bitcast.where, f32[2,32,256,128]{3,2,1,0:T(8,128)} %image.11, f32[2,32,64,128]{3,2,1,0:T(8,128)} %finish.1.gradient, f32[2,32,64,128]{3,2,1,0:T(8,128)} %auxiliary.1, f32[2,32,64,128]{3,2,1,0:T(8,128)} %dual.1), custom_call_target="tpu_custom_call" | custom-call | tf_op jit(solution)/shard_map/update/pallas_call | solution.py:518
  (46 shorter events, 0.1 us)
Async XLA Ops:
  13.9 7.5 %collective-permute-start.10 = (bf16[2,32,16,128]{3,2,1,0:T(8,128)(2,1)}, bf16[2,32,16,128]{3,2,1,0:T(8,128)(2,1)}, u32[]{:S(2)}, u32[]{:S(2)}) collective-permute-start(bf16[2,32,16,128]{3,2,1,0:T(8,128)(2,1)} %get-tuple-element.108), channel_id=1, source_target_pairs={{0,4},{1,5},{2,6},{3,7},{4,0},{5,1},{6,2},{7,3},{8,12},{9,13},{10,... | collective-permute-start | bytes 786440 | tf_op jit(solution)/shard_map/ppermute | solution.py:546
  15.2 18.7 %collective-permute-start.11 = (bf16[2,32,16,128]{3,2,1,0:T(8,128)(2,1)}, bf16[2,32,16,128]{3,2,1,0:T(8,128)(2,1)}, u32[]{:S(2)}, u32[]{:S(2)}) collective-permute-start(bf16[2,32,16,128]{3,2,1,0:T(8,128)(2,1)} %get-tuple-element.109), channel_id=1, source_target_pairs={{0,5},{1,6},{2,7},{3,0},{4,1},{5,2},{6,3},{7,4},{8,13},{9,14},{10,... | collective-permute-start | bytes 786440 | tf_op jit(solution)/shard_map/ppermute | solution.py:546
  17.2 19.7 %collective-permute-start.12 = (bf16[2,32,16,128]{3,2,1,0:T(8,128)(2,1)}, bf16[2,32,16,128]{3,2,1,0:T(8,128)(2,1)}, u32[]{:S(2)}, u32[]{:S(2)}) collective-permute-start(bf16[2,32,16,128]{3,2,1,0:T(8,128)(2,1)} %get-tuple-element.110), channel_id=1, source_target_pairs={{0,6},{1,7},{2,0},{3,1},{4,2},{5,3},{6,4},{7,5},{8,14},{9,15},{10,... | collective-permute-start | bytes 786440 | tf_op jit(solution)/shard_map/ppermute | solution.py:546
  17.4 19.7 %collective-permute-start.13 = (bf16[2,32,16,128]{3,2,1,0:T(8,128)(2,1)}, bf16[2,32,16,128]{3,2,1,0:T(8,128)(2,1)}, u32[]{:S(2)}, u32[]{:S(2)}) collective-permute-start(bf16[2,32,16,128]{3,2,1,0:T(8,128)(2,1)} %get-tuple-element.111), channel_id=1, source_target_pairs={{0,7},{1,0},{2,1},{3,2},{4,3},{5,4},{6,5},{7,6},{8,15},{9,8},{10,9... | collective-permute-start | bytes 786440 | tf_op jit(solution)/shard_map/ppermute | solution.py:546
  18.2 22.0 %collective-permute-start.7 = (bf16[2,32,16,128]{3,2,1,0:T(8,128)(2,1)}, bf16[2,32,16,128]{3,2,1,0:T(8,128)(2,1)}, u32[]{:S(2)}, u32[]{:S(2)}) collective-permute-start(bf16[2,32,16,128]{3,2,1,0:T(8,128)(2,1)} %get-tuple-element.105), channel_id=1, source_target_pairs={{0,1},{1,2},{2,3},{3,4},{4,5},{5,6},{6,7},{7,0},{8,9},{9,10},{10,1... | collective-permute-start | bytes 786440 | tf_op jit(solution)/shard_map/ppermute | solution.py:546
  21.4 18.9 %collective-permute-start.8 = (bf16[2,32,16,128]{3,2,1,0:T(8,128)(2,1)}, bf16[2,32,16,128]{3,2,1,0:T(8,128)(2,1)}, u32[]{:S(2)}, u32[]{:S(2)}) collective-permute-start(bf16[2,32,16,128]{3,2,1,0:T(8,128)(2,1)} %get-tuple-element.106), channel_id=1, source_target_pairs={{0,2},{1,3},{2,4},{3,5},{4,6},{5,7},{6,0},{7,1},{8,10},{9,11},{10,... | collective-permute-start | bytes 786440 | tf_op jit(solution)/shard_map/ppermute | solution.py:546
  33.9 25.7 %collective-permute-start.9 = (bf16[2,32,16,128]{3,2,1,0:T(8,128)(2,1)}, bf16[2,32,16,128]{3,2,1,0:T(8,128)(2,1)}, u32[]{:S(2)}, u32[]{:S(2)}) collective-permute-start(bf16[2,32,16,128]{3,2,1,0:T(8,128)(2,1)} %get-tuple-element.107), channel_id=1, source_target_pairs={{0,3},{1,4},{2,5},{3,6},{4,7},{5,0},{6,1},{7,2},{8,11},{9,12},{10,... | collective-permute-start | bytes 786440 | tf_op jit(solution)/shard_map/ppermute | solution.py:546
  36.8 22.8 %collective-permute-start = (bf16[2,32,16,128]{3,2,1,0:T(8,128)(2,1)}, bf16[2,32,16,128]{3,2,1,0:T(8,128)(2,1)}, u32[]{:S(2)}, u32[]{:S(2)}) collective-permute-start(bf16[2,32,16,128]{3,2,1,0:T(8,128)(2,1)} %get-tuple-element.97), channel_id=1, source_target_pairs={{0,1},{1,2},{2,3},{3,4},{4,5},{5,6},{6,7},{7,0},{8,9},{9,10},{10,1... | collective-permute-start | bytes 786440 | tf_op jit(solution)/shard_map/ppermute | solution.py:546
  37.1 26.1 %collective-permute-start.1 = (bf16[2,32,16,128]{3,2,1,0:T(8,128)(2,1)}, bf16[2,32,16,128]{3,2,1,0:T(8,128)(2,1)}, u32[]{:S(2)}, u32[]{:S(2)}) collective-permute-start(bf16[2,32,16,128]{3,2,1,0:T(8,128)(2,1)} %get-tuple-element.98), channel_id=1, source_target_pairs={{0,2},{1,3},{2,4},{3,5},{4,6},{5,7},{6,0},{7,1},{8,10},{9,11},{10,... | collective-permute-start | bytes 786440 | tf_op jit(solution)/shard_map/ppermute | solution.py:546
  40.2 33.9 %collective-permute-start.2 = (bf16[2,32,16,128]{3,2,1,0:T(8,128)(2,1)}, bf16[2,32,16,128]{3,2,1,0:T(8,128)(2,1)}, u32[]{:S(2)}, u32[]{:S(2)}) collective-permute-start(bf16[2,32,16,128]{3,2,1,0:T(8,128)(2,1)} %get-tuple-element.99), channel_id=1, source_target_pairs={{0,3},{1,4},{2,5},{3,6},{4,7},{5,0},{6,1},{7,2},{8,11},{9,12},{10,... | collective-permute-start | bytes 786440 | tf_op jit(solution)/shard_map/ppermute | solution.py:546
  40.3 35.6 %collective-permute-start.3 = (bf16[2,32,16,128]{3,2,1,0:T(8,128)(2,1)}, bf16[2,32,16,128]{3,2,1,0:T(8,128)(2,1)}, u32[]{:S(2)}, u32[]{:S(2)}) collective-permute-start(bf16[2,32,16,128]{3,2,1,0:T(8,128)(2,1)} %get-tuple-element.100), channel_id=1, source_target_pairs={{0,4},{1,5},{2,6},{3,7},{4,0},{5,1},{6,2},{7,3},{8,12},{9,13},{10,... | collective-permute-start | bytes 786440 | tf_op jit(solution)/shard_map/ppermute | solution.py:546
  59.6 17.4 %collective-permute-start.4 = (bf16[2,32,16,128]{3,2,1,0:T(8,128)(2,1)}, bf16[2,32,16,128]{3,2,1,0:T(8,128)(2,1)}, u32[]{:S(2)}, u32[]{:S(2)}) collective-permute-start(bf16[2,32,16,128]{3,2,1,0:T(8,128)(2,1)} %get-tuple-element.101), channel_id=1, source_target_pairs={{0,5},{1,6},{2,7},{3,0},{4,1},{5,2},{6,3},{7,4},{8,13},{9,14},{10,... | collective-permute-start | bytes 786440 | tf_op jit(solution)/shard_map/ppermute | solution.py:546
  59.6 18.0 %collective-permute-start.5 = (bf16[2,32,16,128]{3,2,1,0:T(8,128)(2,1)}, bf16[2,32,16,128]{3,2,1,0:T(8,128)(2,1)}, u32[]{:S(2)}, u32[]{:S(2)}) collective-permute-start(bf16[2,32,16,128]{3,2,1,0:T(8,128)(2,1)} %get-tuple-element.102), channel_id=1, source_target_pairs={{0,6},{1,7},{2,0},{3,1},{4,2},{5,3},{6,4},{7,5},{8,14},{9,15},{10,... | collective-permute-start | bytes 786440 | tf_op jit(solution)/shard_map/ppermute | solution.py:546
  63.2 14.5 %collective-permute-start.6 = (bf16[2,32,16,128]{3,2,1,0:T(8,128)(2,1)}, bf16[2,32,16,128]{3,2,1,0:T(8,128)(2,1)}, u32[]{:S(2)}, u32[]{:S(2)}) collective-permute-start(bf16[2,32,16,128]{3,2,1,0:T(8,128)(2,1)} %get-tuple-element.103), channel_id=1, source_target_pairs={{0,7},{1,0},{2,1},{3,2},{4,3},{5,4},{6,5},{7,6},{8,15},{9,8},{10,9... | collective-permute-start | bytes 786440 | tf_op jit(solution)/shard_map/ppermute | solution.py:546
  74.2 16.9 %collective-permute-start.21 = (bf16[2,32,32,128]{3,2,1,0:T(8,128)(2,1)}, bf16[2,32,32,128]{3,2,1,0:T(8,128)(2,1)}, u32[]{:S(2)}, u32[]{:S(2)}) collective-permute-start(bf16[2,32,32,128]{3,2,1,0:T(8,128)(2,1)} %get-tuple-element.125), channel_id=1, source_target_pairs={{0,1},{1,2},{2,3},{3,4},{4,5},{5,6},{6,7},{7,0},{8,9},{9,10},{10,1... | collective-permute-start | bytes 1572872 | tf_op jit(solution)/shard_map/ppermute | solution.py:546
  75.9 24.1 %collective-permute-start.22 = (bf16[2,32,32,128]{3,2,1,0:T(8,128)(2,1)}, bf16[2,32,32,128]{3,2,1,0:T(8,128)(2,1)}, u32[]{:S(2)}, u32[]{:S(2)}) collective-permute-start(bf16[2,32,32,128]{3,2,1,0:T(8,128)(2,1)} %get-tuple-element.126), channel_id=1, source_target_pairs={{0,2},{1,3},{2,4},{3,5},{4,6},{5,7},{6,0},{7,1},{8,10},{9,11},{10,... | collective-permute-start | bytes 1572872 | tf_op jit(solution)/shard_map/ppermute | solution.py:546
  77.0 34.1 %collective-permute-start.23 = (bf16[2,32,32,128]{3,2,1,0:T(8,128)(2,1)}, bf16[2,32,32,128]{3,2,1,0:T(8,128)(2,1)}, u32[]{:S(2)}, u32[]{:S(2)}) collective-permute-start(bf16[2,32,32,128]{3,2,1,0:T(8,128)(2,1)} %get-tuple-element.127), channel_id=1, source_target_pairs={{0,3},{1,4},{2,5},{3,6},{4,7},{5,0},{6,1},{7,2},{8,11},{9,12},{10,... | collective-permute-start | bytes 1572872 | tf_op jit(solution)/shard_map/ppermute | solution.py:546
  77.6 46.2 %collective-permute-start.24 = (bf16[2,32,32,128]{3,2,1,0:T(8,128)(2,1)}, bf16[2,32,32,128]{3,2,1,0:T(8,128)(2,1)}, u32[]{:S(2)}, u32[]{:S(2)}) collective-permute-start(bf16[2,32,32,128]{3,2,1,0:T(8,128)(2,1)} %get-tuple-element.128), channel_id=1, source_target_pairs={{0,4},{1,5},{2,6},{3,7},{4,0},{5,1},{6,2},{7,3},{8,12},{9,13},{10,... | collective-permute-start | bytes 1572872 | tf_op jit(solution)/shard_map/ppermute | solution.py:546
  77.8 46.2 %collective-permute-start.25 = (bf16[2,32,32,128]{3,2,1,0:T(8,128)(2,1)}, bf16[2,32,32,128]{3,2,1,0:T(8,128)(2,1)}, u32[]{:S(2)}, u32[]{:S(2)}) collective-permute-start(bf16[2,32,32,128]{3,2,1,0:T(8,128)(2,1)} %get-tuple-element.129), channel_id=1, source_target_pairs={{0,5},{1,6},{2,7},{3,0},{4,1},{5,2},{6,3},{7,4},{8,13},{9,14},{10,... | collective-permute-start | bytes 1572872 | tf_op jit(solution)/shard_map/ppermute | solution.py:546
  91.1 43.8 %collective-permute-start.26 = (bf16[2,32,32,128]{3,2,1,0:T(8,128)(2,1)}, bf16[2,32,32,128]{3,2,1,0:T(8,128)(2,1)}, u32[]{:S(2)}, u32[]{:S(2)}) collective-permute-start(bf16[2,32,32,128]{3,2,1,0:T(8,128)(2,1)} %get-tuple-element.130), channel_id=1, source_target_pairs={{0,6},{1,7},{2,0},{3,1},{4,2},{5,3},{6,4},{7,5},{8,14},{9,15},{10,... | collective-permute-start | bytes 1572872 | tf_op jit(solution)/shard_map/ppermute | solution.py:546
  100.1 36.2 %collective-permute-start.27 = (bf16[2,32,32,128]{3,2,1,0:T(8,128)(2,1)}, bf16[2,32,32,128]{3,2,1,0:T(8,128)(2,1)}, u32[]{:S(2)}, u32[]{:S(2)}) collective-permute-start(bf16[2,32,32,128]{3,2,1,0:T(8,128)(2,1)} %get-tuple-element.131), channel_id=1, source_target_pairs={{0,7},{1,0},{2,1},{3,2},{4,3},{5,4},{6,5},{7,6},{8,15},{9,8},{10,9... | collective-permute-start | bytes 1572872 | tf_op jit(solution)/shard_map/ppermute | solution.py:546
  111.1 28.1 %collective-permute-start.35 = (bf16[2,32,32,128]{3,2,1,0:T(8,128)(2,1)}, bf16[2,32,32,128]{3,2,1,0:T(8,128)(2,1)}, u32[]{:S(2)}, u32[]{:S(2)}) collective-permute-start(bf16[2,32,32,128]{3,2,1,0:T(8,128)(2,1)} %get-tuple-element.145), channel_id=1, source_target_pairs={{0,1},{1,2},{2,3},{3,4},{4,5},{5,6},{6,7},{7,0},{8,9},{9,10},{10,1... | collective-permute-start | bytes 1572872 | tf_op jit(solution)/shard_map/ppermute | solution.py:546
  123.8 21.2 %collective-permute-start.36 = (bf16[2,32,32,128]{3,2,1,0:T(8,128)(2,1)}, bf16[2,32,32,128]{3,2,1,0:T(8,128)(2,1)}, u32[]{:S(2)}, u32[]{:S(2)}) collective-permute-start(bf16[2,32,32,128]{3,2,1,0:T(8,128)(2,1)} %get-tuple-element.146), channel_id=1, source_target_pairs={{0,2},{1,3},{2,4},{3,5},{4,6},{5,7},{6,0},{7,1},{8,10},{9,11},{10,... | collective-permute-start | bytes 1572872 | tf_op jit(solution)/shard_map/ppermute | solution.py:546
  124.0 32.1 %collective-permute-start.37 = (bf16[2,32,32,128]{3,2,1,0:T(8,128)(2,1)}, bf16[2,32,32,128]{3,2,1,0:T(8,128)(2,1)}, u32[]{:S(2)}, u32[]{:S(2)}) collective-permute-start(bf16[2,32,32,128]{3,2,1,0:T(8,128)(2,1)} %get-tuple-element.147), channel_id=1, source_target_pairs={{0,3},{1,4},{2,5},{3,6},{4,7},{5,0},{6,1},{7,2},{8,11},{9,12},{10,... | collective-permute-start | bytes 1572872 | tf_op jit(solution)/shard_map/ppermute | solution.py:546
  134.9 33.9 %collective-permute-start.38 = (bf16[2,32,32,128]{3,2,1,0:T(8,128)(2,1)}, bf16[2,32,32,128]{3,2,1,0:T(8,128)(2,1)}, u32[]{:S(2)}, u32[]{:S(2)}) collective-permute-start(bf16[2,32,32,128]{3,2,1,0:T(8,128)(2,1)} %get-tuple-element.148), channel_id=1, source_target_pairs={{0,4},{1,5},{2,6},{3,7},{4,0},{5,1},{6,2},{7,3},{8,12},{9,13},{10,... | collective-permute-start | bytes 1572872 | tf_op jit(solution)/shard_map/ppermute | solution.py:546
  136.3 36.7 %collective-permute-start.39 = (bf16[2,32,32,128]{3,2,1,0:T(8,128)(2,1)}, bf16[2,32,32,128]{3,2,1,0:T(8,128)(2,1)}, u32[]{:S(2)}, u32[]{:S(2)}) collective-permute-start(bf16[2,32,32,128]{3,2,1,0:T(8,128)(2,1)} %get-tuple-element.149), channel_id=1, source_target_pairs={{0,5},{1,6},{2,7},{3,0},{4,1},{5,2},{6,3},{7,4},{8,13},{9,14},{10,... | collective-permute-start | bytes 1572872 | tf_op jit(solution)/shard_map/ppermute | solution.py:546
  139.2 35.6 %collective-permute-start.40 = (bf16[2,32,32,128]{3,2,1,0:T(8,128)(2,1)}, bf16[2,32,32,128]{3,2,1,0:T(8,128)(2,1)}, u32[]{:S(2)}, u32[]{:S(2)}) collective-permute-start(bf16[2,32,32,128]{3,2,1,0:T(8,128)(2,1)} %get-tuple-element.150), channel_id=1, source_target_pairs={{0,6},{1,7},{2,0},{3,1},{4,2},{5,3},{6,4},{7,5},{8,14},{9,15},{10,... | collective-permute-start | bytes 1572872 | tf_op jit(solution)/shard_map/ppermute | solution.py:546
  145.1 31.0 %collective-permute-start.41 = (bf16[2,32,32,128]{3,2,1,0:T(8,128)(2,1)}, bf16[2,32,32,128]{3,2,1,0:T(8,128)(2,1)}, u32[]{:S(2)}, u32[]{:S(2)}) collective-permute-start(bf16[2,32,32,128]{3,2,1,0:T(8,128)(2,1)} %get-tuple-element.151), channel_id=1, source_target_pairs={{0,7},{1,0},{2,1},{3,2},{4,3},{5,4},{6,5},{7,6},{8,15},{9,8},{10,9... | collective-permute-start | bytes 1572872 | tf_op jit(solution)/shard_map/ppermute | solution.py:546
  156.1 23.3 %collective-permute-start.42 = (bf16[2,32,32,128]{3,2,1,0:T(8,128)(2,1)}, bf16[2,32,32,128]{3,2,1,0:T(8,128)(2,1)}, u32[]{:S(2)}, u32[]{:S(2)}) collective-permute-start(bf16[2,32,32,128]{3,2,1,0:T(8,128)(2,1)} %get-tuple-element.162), channel_id=1, source_target_pairs={{0,1},{1,2},{2,3},{3,4},{4,5},{5,6},{6,7},{7,0},{8,9},{9,10},{10,1... | collective-permute-start | bytes 1572872 | tf_op jit(solution)/shard_map/ppermute | solution.py:546
  168.8 39.7 %collective-permute-start.43 = (bf16[2,32,32,128]{3,2,1,0:T(8,128)(2,1)}, bf16[2,32,32,128]{3,2,1,0:T(8,128)(2,1)}, u32[]{:S(2)}, u32[]{:S(2)}) collective-permute-start(bf16[2,32,32,128]{3,2,1,0:T(8,128)(2,1)} %get-tuple-element.163), channel_id=1, source_target_pairs={{0,2},{1,3},{2,4},{3,5},{4,6},{5,7},{6,0},{7,1},{8,10},{9,11},{10,... | collective-permute-start | bytes 1572872 | tf_op jit(solution)/shard_map/ppermute | solution.py:546
  172.9 35.6 %collective-permute-start.44 = (bf16[2,32,32,128]{3,2,1,0:T(8,128)(2,1)}, bf16[2,32,32,128]{3,2,1,0:T(8,128)(2,1)}, u32[]{:S(2)}, u32[]{:S(2)}) collective-permute-start(bf16[2,32,32,128]{3,2,1,0:T(8,128)(2,1)} %get-tuple-element.164), channel_id=1, source_target_pairs={{0,3},{1,4},{2,5},{3,6},{4,7},{5,0},{6,1},{7,2},{8,11},{9,12},{10,... | collective-permute-start | bytes 1572872 | tf_op jit(solution)/shard_map/ppermute | solution.py:546
  174.8 44.2 %collective-permute-start.45 = (bf16[2,32,32,128]{3,2,1,0:T(8,128)(2,1)}, bf16[2,32,32,128]{3,2,1,0:T(8,128)(2,1)}, u32[]{:S(2)}, u32[]{:S(2)}) collective-permute-start(bf16[2,32,32,128]{3,2,1,0:T(8,128)(2,1)} %get-tuple-element.165), channel_id=1, source_target_pairs={{0,4},{1,5},{2,6},{3,7},{4,0},{5,1},{6,2},{7,3},{8,12},{9,13},{10,... | collective-permute-start | bytes 1572872 | tf_op jit(solution)/shard_map/ppermute | solution.py:546
  176.0 49.2 %collective-permute-start.46 = (bf16[2,32,32,128]{3,2,1,0:T(8,128)(2,1)}, bf16[2,32,32,128]{3,2,1,0:T(8,128)(2,1)}, u32[]{:S(2)}, u32[]{:S(2)}) collective-permute-start(bf16[2,32,32,128]{3,2,1,0:T(8,128)(2,1)} %get-tuple-element.166), channel_id=1, source_target_pairs={{0,5},{1,6},{2,7},{3,0},{4,1},{5,2},{6,3},{7,4},{8,13},{9,14},{10,... | collective-permute-start | bytes 1572872 | tf_op jit(solution)/shard_map/ppermute | solution.py:546
  179.4 45.9 %collective-permute-start.47 = (bf16[2,32,32,128]{3,2,1,0:T(8,128)(2,1)}, bf16[2,32,32,128]{3,2,1,0:T(8,128)(2,1)}, u32[]{:S(2)}, u32[]{:S(2)}) collective-permute-start(bf16[2,32,32,128]{3,2,1,0:T(8,128)(2,1)} %get-tuple-element.167), channel_id=1, source_target_pairs={{0,6},{1,7},{2,0},{3,1},{4,2},{5,3},{6,4},{7,5},{8,14},{9,15},{10,... | collective-permute-start | bytes 1572872 | tf_op jit(solution)/shard_map/ppermute | solution.py:546
  208.5 44.7 %collective-permute-start.48 = (bf16[2,32,32,128]{3,2,1,0:T(8,128)(2,1)}, bf16[2,32,32,128]{3,2,1,0:T(8,128)(2,1)}, u32[]{:S(2)}, u32[]{:S(2)}) collective-permute-start(bf16[2,32,32,128]{3,2,1,0:T(8,128)(2,1)} %get-tuple-element.168), channel_id=1, source_target_pairs={{0,7},{1,0},{2,1},{3,2},{4,3},{5,4},{6,5},{7,6},{8,15},{9,8},{10,9... | collective-permute-start | bytes 1572872 | tf_op jit(solution)/shard_map/ppermute | solution.py:546
  208.5 47.5 %collective-permute-start.14 = (bf16[2,1024,128]{2,1,0:T(8,128)(2,1)}, bf16[2,1024,128]{2,1,0:T(8,128)(2,1)}, u32[]{:S(2)}, u32[]{:S(2)}) collective-permute-start(bf16[2,1024,128]{2,1,0:T(8,128)(2,1)} %get-tuple-element.114), channel_id=1, source_target_pairs={{0,1},{1,2},{2,3},{3,4},{4,5},{5,6},{6,7},{7,0},{8,9},{9,10},{10,1... | collective-permute-start | bytes 1572872 | tf_op jit(solution)/shard_map/ppermute | solution.py:546
  219.0 50.1 %collective-permute-start.15 = (bf16[2,1024,128]{2,1,0:T(8,128)(2,1)}, bf16[2,1024,128]{2,1,0:T(8,128)(2,1)}, u32[]{:S(2)}, u32[]{:S(2)}) collective-permute-start(bf16[2,1024,128]{2,1,0:T(8,128)(2,1)} %get-tuple-element.115), channel_id=1, source_target_pairs={{0,2},{1,3},{2,4},{3,5},{4,6},{5,7},{6,0},{7,1},{8,10},{9,11},{10,... | collective-permute-start | bytes 1572872 | tf_op jit(solution)/shard_map/ppermute | solution.py:546
  225.2 43.9 %collective-permute-start.16 = (bf16[2,1024,128]{2,1,0:T(8,128)(2,1)}, bf16[2,1024,128]{2,1,0:T(8,128)(2,1)}, u32[]{:S(2)}, u32[]{:S(2)}) collective-permute-start(bf16[2,1024,128]{2,1,0:T(8,128)(2,1)} %get-tuple-element.116), channel_id=1, source_target_pairs={{0,3},{1,4},{2,5},{3,6},{4,7},{5,0},{6,1},{7,2},{8,11},{9,12},{10,... | collective-permute-start | bytes 1572872 | tf_op jit(solution)/shard_map/ppermute | solution.py:546
  225.3 45.6 %collective-permute-start.17 = (bf16[2,1024,128]{2,1,0:T(8,128)(2,1)}, bf16[2,1024,128]{2,1,0:T(8,128)(2,1)}, u32[]{:S(2)}, u32[]{:S(2)}) collective-permute-start(bf16[2,1024,128]{2,1,0:T(8,128)(2,1)} %get-tuple-element.117), channel_id=1, source_target_pairs={{0,4},{1,5},{2,6},{3,7},{4,0},{5,1},{6,2},{7,3},{8,12},{9,13},{10,... | collective-permute-start | bytes 1572872 | tf_op jit(solution)/shard_map/ppermute | solution.py:546
  253.1 43.5 %collective-permute-start.18 = (bf16[2,1024,128]{2,1,0:T(8,128)(2,1)}, bf16[2,1024,128]{2,1,0:T(8,128)(2,1)}, u32[]{:S(2)}, u32[]{:S(2)}) collective-permute-start(bf16[2,1024,128]{2,1,0:T(8,128)(2,1)} %get-tuple-element.118), channel_id=1, source_target_pairs={{0,5},{1,6},{2,7},{3,0},{4,1},{5,2},{6,3},{7,4},{8,13},{9,14},{10,... | collective-permute-start | bytes 1572872 | tf_op jit(solution)/shard_map/ppermute | solution.py:546
  256.0 54.8 %collective-permute-start.19 = (bf16[2,1024,128]{2,1,0:T(8,128)(2,1)}, bf16[2,1024,128]{2,1,0:T(8,128)(2,1)}, u32[]{:S(2)}, u32[]{:S(2)}) collective-permute-start(bf16[2,1024,128]{2,1,0:T(8,128)(2,1)} %get-tuple-element.119), channel_id=1, source_target_pairs={{0,6},{1,7},{2,0},{3,1},{4,2},{5,3},{6,4},{7,5},{8,14},{9,15},{10,... | collective-permute-start | bytes 1572872 | tf_op jit(solution)/shard_map/ppermute | solution.py:546
  269.1 41.7 %collective-permute-start.20 = (bf16[2,1024,128]{2,1,0:T(8,128)(2,1)}, bf16[2,1024,128]{2,1,0:T(8,128)(2,1)}, u32[]{:S(2)}, u32[]{:S(2)}) collective-permute-start(bf16[2,1024,128]{2,1,0:T(8,128)(2,1)} %get-tuple-element.120), channel_id=1, source_target_pairs={{0,7},{1,0},{2,1},{3,2},{4,3},{5,4},{6,5},{7,6},{8,15},{9,8},{10,9... | collective-permute-start | bytes 1572872 | tf_op jit(solution)/shard_map/ppermute | solution.py:546
  269.1 41.8 %collective-permute-start.28 = (bf16[2,1024,128]{2,1,0:T(8,128)(2,1)}, bf16[2,1024,128]{2,1,0:T(8,128)(2,1)}, u32[]{:S(2)}, u32[]{:S(2)}) collective-permute-start(bf16[2,1024,128]{2,1,0:T(8,128)(2,1)} %get-tuple-element.134), channel_id=1, source_target_pairs={{0,1},{1,2},{2,3},{3,4},{4,5},{5,6},{6,7},{7,0},{8,9},{9,10},{10,1... | collective-permute-start | bytes 1572872 | tf_op jit(solution)/shard_map/ppermute | solution.py:546
  270.9 43.9 %collective-permute-start.29 = (bf16[2,1024,128]{2,1,0:T(8,128)(2,1)}, bf16[2,1024,128]{2,1,0:T(8,128)(2,1)}, u32[]{:S(2)}, u32[]{:S(2)}) collective-permute-start(bf16[2,1024,128]{2,1,0:T(8,128)(2,1)} %get-tuple-element.135), channel_id=1, source_target_pairs={{0,2},{1,3},{2,4},{3,5},{4,6},{5,7},{6,0},{7,1},{8,10},{9,11},{10,... | collective-permute-start | bytes 1572872 | tf_op jit(solution)/shard_map/ppermute | solution.py:546
  296.7 43.7 %collective-permute-start.30 = (bf16[2,1024,128]{2,1,0:T(8,128)(2,1)}, bf16[2,1024,128]{2,1,0:T(8,128)(2,1)}, u32[]{:S(2)}, u32[]{:S(2)}) collective-permute-start(bf16[2,1024,128]{2,1,0:T(8,128)(2,1)} %get-tuple-element.136), channel_id=1, source_target_pairs={{0,3},{1,4},{2,5},{3,6},{4,7},{5,0},{6,1},{7,2},{8,11},{9,12},{10,... | collective-permute-start | bytes 1572872 | tf_op jit(solution)/shard_map/ppermute | solution.py:546
  310.8 29.6 %collective-permute-start.31 = (bf16[2,1024,128]{2,1,0:T(8,128)(2,1)}, bf16[2,1024,128]{2,1,0:T(8,128)(2,1)}, u32[]{:S(2)}, u32[]{:S(2)}) collective-permute-start(bf16[2,1024,128]{2,1,0:T(8,128)(2,1)} %get-tuple-element.137), channel_id=1, source_target_pairs={{0,4},{1,5},{2,6},{3,7},{4,0},{5,1},{6,2},{7,3},{8,12},{9,13},{10,... | collective-permute-start | bytes 1572872 | tf_op jit(solution)/shard_map/ppermute | solution.py:546
  310.8 29.6 %collective-permute-start.32 = (bf16[2,1024,128]{2,1,0:T(8,128)(2,1)}, bf16[2,1024,128]{2,1,0:T(8,128)(2,1)}, u32[]{:S(2)}, u32[]{:S(2)}) collective-permute-start(bf16[2,1024,128]{2,1,0:T(8,128)(2,1)} %get-tuple-element.138), channel_id=1, source_target_pairs={{0,5},{1,6},{2,7},{3,0},{4,1},{5,2},{6,3},{7,4},{8,13},{9,14},{10,... | collective-permute-start | bytes 1572872 | tf_op jit(solution)/shard_map/ppermute | solution.py:546
  310.9 29.5 %collective-permute-start.33 = (bf16[2,1024,128]{2,1,0:T(8,128)(2,1)}, bf16[2,1024,128]{2,1,0:T(8,128)(2,1)}, u32[]{:S(2)}, u32[]{:S(2)}) collective-permute-start(bf16[2,1024,128]{2,1,0:T(8,128)(2,1)} %get-tuple-element.139), channel_id=1, source_target_pairs={{0,6},{1,7},{2,0},{3,1},{4,2},{5,3},{6,4},{7,5},{8,14},{9,15},{10,... | collective-permute-start | bytes 1572872 | tf_op jit(solution)/shard_map/ppermute | solution.py:546
  314.8 25.7 %collective-permute-start.34 = (bf16[2,1024,128]{2,1,0:T(8,128)(2,1)}, bf16[2,1024,128]{2,1,0:T(8,128)(2,1)}, u32[]{:S(2)}, u32[]{:S(2)}) collective-permute-start(bf16[2,1024,128]{2,1,0:T(8,128)(2,1)} %get-tuple-element.140), channel_id=1, source_target_pairs={{0,7},{1,0},{2,1},{3,2},{4,3},{5,4},{6,5},{7,6},{8,15},{9,8},{10,9... | collective-permute-start | bytes 1572872 | tf_op jit(solution)/shard_map/ppermute | solution.py:546

commit v3 on v2

--- a/solution.py
+++ b/solution.py
@@ -13,6 +13,7 @@
 penalty = 1.0
 threshold = 0.3
 VMEM_LIMIT = 67000000
+LAG = 3
 F32 = jnp.float32
 BF16 = jnp.bfloat16
 
@@ -33,8 +34,8 @@
 HBM = pl.BlockSpec(memory_space=pltpu.HBM)
 
 
-def params(**extra):
-    return pltpu.CompilerParams(vmem_limit_bytes=VMEM_LIMIT, **extra)
+def params(limit=VMEM_LIMIT, **extra):
+    return pltpu.CompilerParams(vmem_limit_bytes=limit, **extra)
 
 
 def once(shape):
@@ -85,7 +86,7 @@
             flat[where, :] = half[:, h * depth : (h + 1) * depth]
         return carry
 
-    lax.fori_loop(0, rows // 2, pair, 0)
+    lax.fori_loop(0, rows // 2, pair, 0, unroll=2)
 
     @pl.when(step == pl.num_programs(0) - 1)
     def last():
@@ -196,7 +197,7 @@
                 ]
         return carry
 
-    lax.fori_loop(0, kl // 2, to_kspace, 0)
+    lax.fori_loop(0, kl // 2, to_kspace, 0, unroll=2)
 
     def settle(i, carry):
         rows = pl.ds(pl.multiple_of(i * pitch(kl), 8), kl)
@@ -212,12 +213,15 @@
     cells = win * kl
     chunk = min(cells, 512)
 
-    def group(slot, carry):
-        first = offsets[0, slot]
-        start = pl.multiple_of(first * kl, kl)
+    def misfit_of(slot):
+        start = pl.multiple_of(offsets[0, slot] * kl, kl)
         window = kspace[pl.ds(start, cells), :].astype(BF16)
         predicted = jnp.dot(weights[slot], window, preferred_element_type=F32)
-        misfit = (predicted - samples[slot].astype(F32)).astype(BF16)
+        return (predicted - samples[slot].astype(F32)).astype(BF16)
+
+    def group(slot, misfit):
+        following = misfit_of(jnp.minimum(slot + 1, weights.shape[0] - 1))
+        first = offsets[0, slot]
         for c in range(0, cells, chunk):
             update = lax.dot_general(
                 weights[slot, :, c : c + chunk],
@@ -229,9 +233,9 @@
                 rows = pl.ds(pl.multiple_of((first + c // kl + k) * pitch(kl), 8), kl)
                 for p in range(2):
                     total[p, rows, :] += update[k * kl : (k + 1) * kl, p * depth : (p + 1) * depth]
-        return carry
-
-    lax.fori_loop(0, counts[0], group, 0)
+        return following
+
+    lax.fori_loop(0, counts[0], group, misfit_of(0))
 
     def to_rows(i, carry):
         columns = []
@@ -249,7 +253,7 @@
                 ]
         return carry
 
-    lax.fori_loop(0, kl // 2, to_rows, 0)
+    lax.fori_loop(0, kl // 2, to_rows, 0, unroll=2)
     for off in range(n):
         d = lax.rem(me + off, n)
         for p in range(2):
@@ -356,6 +360,22 @@
     for copy in copies:
         copy.wait()
 
+    def add_band(j, carry):
+        arrived = got.at[0 : shares - 1, :, pl.ds(j * rows, rows)]
+        pltpu.make_async_copy(arrived, arrived, grad_recv.at[j]).wait()
+
+        def line(i, carry):
+            x = j * rows + i
+            for p in range(2):
+                value = grad[mine, p, x].astype(F32)
+                for off in range(1, shares):
+                    value += got[lax.rem(mine + off, shares), p, x].astype(F32)
+                out[p, x] = value
+            return carry
+
+        lax.fori_loop(0, rows, line, 0)
+        return carry
+
     def do_band(j, carry):
         where = pl.ds(pl.multiple_of(j * band, band), band)
         arrived = landing.at[ready:coils, 0 : n - 1, :, where, :]
@@ -411,27 +431,15 @@
                 device_id={"coil": target},
                 device_id_type=pl.DeviceIdType.MESH,
             ).start()
+
+        @pl.when(j >= LAG)
+        def settled():
+            add_band(j - LAG, 0)
+
         return carry
 
     lax.fori_loop(0, chunks, do_band, 0)
-
-    def add_band(j, carry):
-        arrived = got.at[0 : shares - 1, :, pl.ds(j * rows, rows)]
-        pltpu.make_async_copy(arrived, arrived, grad_recv.at[j]).wait()
-
-        def line(i, carry):
-            x = j * rows + i
-            for p in range(2):
-                value = grad[mine, p, x].astype(F32)
-                for off in range(1, shares):
-                    value += got[lax.rem(mine + off, shares), p, x].astype(F32)
-                out[p, x] = value
-            return carry
-
-        lax.fori_loop(0, rows, line, 0)
-        return carry
-
-    lax.fori_loop(0, chunks, add_band, 0)
+    lax.fori_loop(max(chunks - LAG, 0), chunks, add_band, 0)
     gone = landing.at[ready:coils, 0 : n - 1]
     pltpu.make_async_copy(gone, gone, send).wait()
     gone = got.at[0 : shares - 1]
@@ -457,13 +465,14 @@
     ]
     if kl % 16:
         scratch.append(pltpu.VMEM((coils, n, 2, rows * kl, depth), F32))
+    limit = VMEM_LIMIT - 24 * xl * share * depth
     return pl.pallas_call(
         functools.partial(finish_kernel, n, shares, kl, xl, chunks, sent),
         in_specs=[vmem, HBM] + [HBM] * (coils * n),
         out_specs=vmem,
         out_shape=jax.ShapeDtypeStruct((2, xl, share, depth), F32),
         scratch_shapes=scratch,
-        compiler_params=params(collective_id=0, has_side_effects=True),
+        compiler_params=params(limit, collective_id=0, has_side_effects=True),
         name="finish",
     )(table, sensitivity, *[piece for back in backs for piece in back])
 
@@ -480,8 +489,7 @@
     return along(first + second), along(first - second)
 
 
-def update_kernel(where, image, gradient, auxiliary, dual, image_out, aux_out, dual_out):
-    del where
+def update_kernel(image, gradient, auxiliary, dual, image_out, aux_out, dual_out):
     rows = image.shape[1]
     for m in range(0, rows, 2):
         coeffs = []
@@ -509,24 +517,20 @@
                 dual_out[p, m + h] = value - kept
 
 
-def update_call(image, gradient, auxiliary, dual, position):
+def update_call(image, gradient, auxiliary, dual):
     _, xl, share, depth = auxiliary.shape
-    rows = 4 if xl % 4 == 0 else 2
-    block = (2, rows, share, depth)
-    plain = pl.BlockSpec(block, lambda i, w: (0, i, 0, 0))
+    rows = 8 if xl % 8 == 0 else 2
+    plain = pl.BlockSpec((2, rows, share, depth), lambda i: (0, i, 0, 0))
     shape = jax.ShapeDtypeStruct(auxiliary.shape, F32)
     return pl.pallas_call(
         update_kernel,
-        grid_spec=pltpu.PrefetchScalarGridSpec(
-            num_scalar_prefetch=1,
-            grid=(xl // rows,),
-            in_specs=[pl.BlockSpec(block, lambda i, w: (0, i, w[0], 0)), plain, plain, plain],
-            out_specs=[plain, plain, plain],
-        ),
+        grid=(xl // rows,),
+        in_specs=[plain, plain, plain, plain],
+        out_specs=[plain, plain, plain],
         out_shape=[shape, shape, shape],
-        compiler_params=params(),
+        compiler_params=params(VMEM_LIMIT - 24 * xl * share * depth),
         name="update",
-    )(position, image, gradient, auxiliary, dual)
+    )(image, gradient, auxiliary, dual)
 
 
 def body(image, sensitivity, blocks, samples, offsets, counts, auxiliary, scaled_dual):
@@ -549,6 +553,7 @@
     def tile_of(pieces, c):
         return tile_call(x_fwd, x_inv, pieces, blocks, sorted_samples, offsets, counts, c, n, kl, xl)
 
+    share = length_y // shares
     pieces, tiles, table = [], [], y_fwd
     for c in range(coils):
         parts = 2 if c == 0 and xl % 32 == 0 else 1
@@ -558,19 +563,19 @@
             table, half[0] = lax.optimization_barrier((table, half[0]))
             moved += swap(half)
         pieces.append(moved)
-    table, samples = lax.optimization_barrier((table, samples))
+    table, samples, source = lax.optimization_barrier((table, samples, image))
     sorted_samples = sort_call(samples)
+    current = lax.dynamic_slice_in_dim(source, lax.axis_index("coil") * share, share, 2)
     for c in range(coils):
         if c:
             pieces[c][0], tiles[-1][0] = lax.optimization_barrier((pieces[c][0], tiles[-1][0]))
         tiles.append(list(tile_of(pieces[c], c)))
-    early = max(coils - 2, 0)
+    early = max(coils - 3, 0)
     backs = list(tiles)
     for c in range(early):
         backs[c] = swap(tiles[c])
     gradient = finish_call(y_inv, backs, coils - early, sensitivity, shares, n, kl)
-    position = lax.axis_index("coil").astype(jnp.int32).reshape(1)
-    return tuple(update_call(image, gradient, auxiliary, scaled_dual, position))
+    return tuple(update_call(current, gradient, auxiliary, scaled_dual))
 
 
 def solution(mesh):

time: 472 us -> 456 us (0.966)
  waiting for transfers between devices: 83.6 us -> 61.9 us
  Pallas kernels: 285 us -> 296 us
  starting transfers between devices: 98.4 us -> 91.3 us
    pallas_call x1, Pallas kernels: 119 us -> 154 us  [finish_call(): pl.pallas_call(functools.partial(finish_kernel, n, shares, kl, xl, chunks...]
    ppermute x49 -> x42, waiting for transfers between devices: 83.6 us -> 61.9 us  [swap(): moved.append(lax.ppermute(parts[off], 'slab', ring))]
    pallas_call x4, Pallas kernels: 103 us -> 83.3 us  [tile_call(): pl.pallas_call(functools.partial(tile_kernel, n, kl, xl, cells // kl, par...]
    ppermute x49 -> x42, starting transfers between devices: 98.4 us -> 91.3 us  [swap(): moved.append(lax.ppermute(parts[off], 'slab', ring))]
  transfers between devices with their start and end apart: 49 -> 42, of which waited for: 12 -> 9; matrix products, arithmetic and copies ran while one was open for 0% -> 1% of each run, Pallas kernels for 31% -> 27%
where the time goes in v3:
time: 456 us; the launch traced here: 454 us
  Pallas kernels  296 us (65%)
  starting transfers between devices  91.3 us (20%)
  waiting for transfers between devices  61.9 us (14%)
    pallas_call x1, Pallas kernels, finish_call(): pl.pallas_call(functools.partial(finish_kernel, n, shares, kl, xl, chunks...  154 us
    ppermute x42, starting transfers between devices, swap(): moved.append(lax.ppermute(parts[off], 'slab', ring))  91.3 us
    pallas_call x4, Pallas kernels, tile_call(): pl.pallas_call(functools.partial(tile_kernel, n, kl, xl, cells // kl, par...  83.3 us
    ppermute x42, waiting for transfers between devices, swap(): moved.append(lax.ppermute(parts[off], 'slab', ring))  61.9 us
    pallas_call x5, Pallas kernels, forward_call(): pl.pallas_call(functools.partial(forward_kernel, n, kl, xp), grid=(steps,...  43.3 us
  transfers between devices with their start and end apart: 42, of which 9 were waited for; matrix products, arithmetic and copies ran while one was open for 1% of the time, Pallas kernels for 27%

profile of v3, /device:TPU:9, one launch (start us, length us, event | category | flops | bytes accessed | tf_op | source)
XLA Modules:
  0.0 453.9 jit_solution(835985539465235208)
XLA Ops:
  0.6 6.2 %forward.5 = (bf16[2,32,16,128]{3,2,1,0:T(8,128)(2,1)}, bf16[2,32,16,128]{3,2,1,0:T(8,128)(2,1)}, bf16[2,32,16,128]{3,2,1,0:T(8,128)(2,1)}, bf16[2,32,16,128]{3,...) custom-call(bf16[512,512]{1,0:T(8,128)(2,1)} %constant.22.table.fwd,, ...), custom_call_target="tpu_custom_call" | custom-call | flops 1073741824 | bytes 6291456 | tf_op jit(solution)/shard_map/forward/pallas_call | solution.py:111
  6.9 6.2 %forward.6 = (bf16[2,32,16,128]{3,2,1,0:T(8,128)(2,1)}, bf16[2,32,16,128]{3,2,1,0:T(8,128)(2,1)}, bf16[2,32,16,128]{3,2,1,0:T(8,128)(2,1)}, bf16[2,32,16,128]{3,...) custom-call(bf16[512,512]{1,0:T(8,128)(2,1)} %constant.22.table.fwd,, ...), custom_call_target="tpu_custom_call" | custom-call | flops 1073741824 | bytes 6291456 | tf_op jit(solution)/shard_map/forward/pallas_call | solution.py:111
  13.1 1.2 collective-permute-start.10
  14.3 2.0 collective-permute-start.11
  16.3 0.3 collective-permute-start.12
  16.6 0.8 collective-permute-start.13
  17.4 0.9 collective-permute-start.7
  18.3 2.3 collective-permute-done.10.refs_12_
  20.6 12.5 %collective-permute-start.8 = (bf16[2,32,16,128]{3,2,1,0:T(8,128)(2,1)}, bf16[2,32,16,128]{3,2,1,0:T(8,128)(2,1)}, u32[]{:S(2)}, u32[]{:S(2)}) collective-permute-start(bf16[2,32,16,128]{3,2,1,0:T(8,128)(2,1)} %get-tuple-element.110), channel_id=1, source_target_pairs={{0,2},{1,3},{2,4},{3,5},{4,6},{5,7},{6,0},{7,1},{8,10},{9,11},{10,... | collective-permute-start | bytes 786440 | tf_op jit(solution)/shard_map/ppermute | solution.py:550
  33.0 2.9 collective-permute-start.9
  36.0 0.3 collective-permute-start
  36.3 0.0 collective-permute-done.13.refs_15_
  36.3 3.1 collective-permute-start.1
  39.4 0.0 collective-permute-done.7.refs_9_
  39.4 0.0 collective-permute-start.2
  39.4 0.1 collective-permute-done.8.refs_10_
  39.5 0.2 collective-permute-start.3
  39.7 19.1 %collective-permute-done.9.refs_11_ = bf16[2,32,16,128]{3,2,1,0:T(8,128)(2,1)} collective-permute-done((bf16[2,32,16,128]{3,2,1,0:T(8,128)(2,1)}, bf16[2,32,16,128]{3,2,1,0:T(8,128)(2,1)}, u32[]{:S(2)}, u32[]{:S(2)}) %collective-permute-start.9) | collective-permute-done | bytes 262176 | tf_op jit(solution)/shard_map/ppermute | solution.py:550
  58.8 10.3 %forward.7 = (bf16[2,32,32,128]{3,2,1,0:T(8,128)(2,1)}, bf16[2,32,32,128]{3,2,1,0:T(8,128)(2,1)}, bf16[2,32,32,128]{3,2,1,0:T(8,128)(2,1)}, bf16[2,32,32,128]{3,...) custom-call(bf16[512,512]{1,0:T(8,128)(2,1)} %constant.22.table.fwd,, ...), custom_call_target="tpu_custom_call" | custom-call | flops 2147483648 | bytes 12582912 | tf_op jit(solution)/shard_map/forward/pallas_call | solution.py:111
  69.1 0.0 collective-permute-done.refs_1_
  69.1 0.1 collective-permute-start.21
  69.1 3.8 collective-permute-start.22
  72.9 0.8 collective-permute-start.23
  73.7 0.0 collective-permute-done.3.refs_4_
  73.7 0.7 collective-permute-start.5
  74.5 1.5 collective-permute-start.6
  75.9 10.2 %forward.8 = (bf16[2,32,32,128]{3,2,1,0:T(8,128)(2,1)}, bf16[2,32,32,128]{3,2,1,0:T(8,128)(2,1)}, bf16[2,32,32,128]{3,2,1,0:T(8,128)(2,1)}, bf16[2,32,32,128]{3,...) custom-call(bf16[512,512]{1,0:T(8,128)(2,1)} %constant.22.table.fwd,, ...), custom_call_target="tpu_custom_call" | custom-call | flops 2147483648 | bytes 12582912 | tf_op jit(solution)/shard_map/forward/pallas_call | solution.py:111
  86.2 15.6 %collective-permute-done.5.refs_6_ = bf16[2,32,16,128]{3,2,1,0:T(8,128)(2,1)} collective-permute-done((bf16[2,32,16,128]{3,2,1,0:T(8,128)(2,1)}, bf16[2,32,16,128]{3,2,1,0:T(8,128)(2,1)}, u32[]{:S(2)}, u32[]{:S(2)}) %collective-permute-start.5) | collective-permute-done | bytes 262176 | tf_op jit(solution)/shard_map/ppermute | solution.py:550
  101.8 1.2 collective-permute-start.24
  103.0 2.0 collective-permute-done.6.refs_7_
  105.0 0.7 collective-permute-start.25
  105.8 0.0 collective-permute-done.21.refs_1_
  105.8 0.0 collective-permute-start.26
  105.8 0.9 collective-permute-start.27
  106.7 1.6 collective-permute-start.28
  109.0 10.3 %forward.9 = (bf16[2,32,32,128]{3,2,1,0:T(8,128)(2,1)}, bf16[2,32,32,128]{3,2,1,0:T(8,128)(2,1)}, bf16[2,32,32,128]{3,2,1,0:T(8,128)(2,1)}, bf16[2,32,32,128]{3,...) custom-call(bf16[512,512]{1,0:T(8,128)(2,1)} %constant.22.table.fwd,, ...), custom_call_target="tpu_custom_call" | custom-call | flops 2147483648 | bytes 12582912 | tf_op jit(solution)/shard_map/forward/pallas_call | solution.py:111
  119.2 8.3 %sort.1.sorted_samples = bf16[4,24,128,256]{3,2,1,0:T(8,128)(2,1)} custom-call(bf16[24,1024,128]{2,1,0:T(8,128)(2,1)} %bitcast.1), custom_call_target="tpu_custom_call" | custom-call | flops 3145728 | bytes 12582912 | tf_op jit(solution)/shard_map/sort/pallas_call | solution.py:144
  127.6 3.2 constant_dynamic-slice_fusion.image
  130.8 5.5 %collective-permute-start.29 = (bf16[2,32,32,128]{3,2,1,0:T(8,128)(2,1)}, bf16[2,32,32,128]{3,2,1,0:T(8,128)(2,1)}, u32[]{:S(2)}, u32[]{:S(2)}) collective-permute-start(bf16[2,32,32,128]{3,2,1,0:T(8,128)(2,1)} %get-tuple-element.150), channel_id=1, source_target_pairs={{0,2},{1,3},{2,4},{3,5},{4,6},{5,7},{6,0},{7,1},{8,10},{9,11},{10,... | collective-permute-start | bytes 1572872 | tf_op jit(solution)/shard_map/ppermute | solution.py:550
  136.3 3.3 collective-permute-start.30
  139.6 0.2 collective-permute-start.31
  139.9 4.4 collective-permute-start.32
  144.2 2.4 collective-permute-start.33
  146.7 20.9 %tile.4 = (bf16[2,1024,128]{2,1,0:T(8,128)(2,1)}, bf16[2,1024,128]{2,1,0:T(8,128)(2,1)}, bf16[2,1024,128]{2,1,0:T(8,128)(2,1)}, bf16[2,1024,128]{2,1,0:T(8,128)(...) custom-call(s32[1,24]{1,0:T(1,128)} %offsets.7, ...), custom_call_target="tpu_custom_call" | custom-call | flops 10737418240 | bytes 20971520 | tf_op jit(solution)/shard_map/tile/pallas_call | solution.py:293
  167.6 0.1 collective-permute-start.34
  167.6 6.8 %collective-permute-start.35 = (bf16[2,32,32,128]{3,2,1,0:T(8,128)(2,1)}, bf16[2,32,32,128]{3,2,1,0:T(8,128)(2,1)}, u32[]{:S(2)}, u32[]{:S(2)}) collective-permute-start(bf16[2,32,32,128]{3,2,1,0:T(8,128)(2,1)} %get-tuple-element.166), channel_id=1, source_target_pairs={{0,1},{1,2},{2,3},{3,4},{4,5},{5,6},{6,7},{7,0},{8,9},{9,10},{10,1... | collective-permute-start | bytes 1572872 | tf_op jit(solution)/shard_map/ppermute | solution.py:550
  174.5 8.9 %collective-permute-done.31.refs_4_ = bf16[2,32,32,128]{3,2,1,0:T(8,128)(2,1)} collective-permute-done((bf16[2,32,32,128]{3,2,1,0:T(8,128)(2,1)}, bf16[2,32,32,128]{3,2,1,0:T(8,128)(2,1)}, u32[]{:S(2)}, u32[]{:S(2)}) %collective-permute-start.31) | collective-permute-done | bytes 524320 | tf_op jit(solution)/shard_map/ppermute | solution.py:550
  183.4 7.4 %collective-permute-start.36 = (bf16[2,32,32,128]{3,2,1,0:T(8,128)(2,1)}, bf16[2,32,32,128]{3,2,1,0:T(8,128)(2,1)}, u32[]{:S(2)}, u32[]{:S(2)}) collective-permute-start(bf16[2,32,32,128]{3,2,1,0:T(8,128)(2,1)} %get-tuple-element.167), channel_id=1, source_target_pairs={{0,2},{1,3},{2,4},{3,5},{4,6},{5,7},{6,0},{7,1},{8,10},{9,11},{10,... | collective-permute-start | bytes 1572872 | tf_op jit(solution)/shard_map/ppermute | solution.py:550
  190.8 0.6 collective-permute-start.38
  191.4 20.7 %tile.5 = (bf16[2,1024,128]{2,1,0:T(8,128)(2,1)}, bf16[2,1024,128]{2,1,0:T(8,128)(2,1)}, bf16[2,1024,128]{2,1,0:T(8,128)(2,1)}, bf16[2,1024,128]{2,1,0:T(8,128)(...) custom-call(s32[1,24]{1,0:T(1,128)} %offsets.7, ...), custom_call_target="tpu_custom_call" | custom-call | flops 10737418240 | bytes 20971520 | tf_op jit(solution)/shard_map/tile/pallas_call | solution.py:293
  212.1 2.9 collective-permute-start.39
  215.0 9.0 %collective-permute-start.40 = (bf16[2,32,32,128]{3,2,1,0:T(8,128)(2,1)}, bf16[2,32,32,128]{3,2,1,0:T(8,128)(2,1)}, u32[]{:S(2)}, u32[]{:S(2)}) collective-permute-start(bf16[2,32,32,128]{3,2,1,0:T(8,128)(2,1)} %get-tuple-element.171), channel_id=1, source_target_pairs={{0,6},{1,7},{2,0},{3,1},{4,2},{5,3},{6,4},{7,5},{8,14},{9,15},{10,... | collective-permute-start | bytes 1572872 | tf_op jit(solution)/shard_map/ppermute | solution.py:550
  224.0 1.7 collective-permute-start.14
  225.8 0.0 collective-permute-start.15
  225.8 20.8 %tile.6 = (bf16[2,1024,128]{2,1,0:T(8,128)(2,1)}, bf16[2,1024,128]{2,1,0:T(8,128)(2,1)}, bf16[2,1024,128]{2,1,0:T(8,128)(2,1)}, bf16[2,1024,128]{2,1,0:T(8,128)(...) custom-call(s32[1,24]{1,0:T(1,128)} %offsets.7, ...), custom_call_target="tpu_custom_call" | custom-call | flops 10737418240 | bytes 20971520 | tf_op jit(solution)/shard_map/tile/pallas_call | solution.py:293
  246.7 8.9 %collective-permute-start.16 = (bf16[2,1024,128]{2,1,0:T(8,128)(2,1)}, bf16[2,1024,128]{2,1,0:T(8,128)(2,1)}, u32[]{:S(2)}, u32[]{:S(2)}) collective-permute-start(bf16[2,1024,128]{2,1,0:T(8,128)(2,1)} %get-tuple-element.120), channel_id=1, source_target_pairs={{0,3},{1,4},{2,5},{3,6},{4,7},{5,0},{6,1},{7,2},{8,11},{9,12},{10,... | collective-permute-start | bytes 1572872 | tf_op jit(solution)/shard_map/ppermute | solution.py:550
  255.5 0.1 collective-permute-start.18
  255.6 2.3 collective-permute-start.19
  257.9 11.7 %collective-permute-done.15.refs_2_ = bf16[2,1024,128]{2,1,0:T(8,128)(2,1)} collective-permute-done((bf16[2,1024,128]{2,1,0:T(8,128)(2,1)}, bf16[2,1024,128]{2,1,0:T(8,128)(2,1)}, u32[]{:S(2)}, u32[]{:S(2)}) %collective-permute-start.15) | collective-permute-done | bytes 524320 | tf_op jit(solution)/shard_map/ppermute | solution.py:550
  269.7 20.8 %tile.7 = (bf16[2,1024,128]{2,1,0:T(8,128)(2,1)}, bf16[2,1024,128]{2,1,0:T(8,128)(2,1)}, bf16[2,1024,128]{2,1,0:T(8,128)(2,1)}, bf16[2,1024,128]{2,1,0:T(8,128)(...) custom-call(s32[1,24]{1,0:T(1,128)} %offsets.7, ...), custom_call_target="tpu_custom_call" | custom-call | flops 10737418240 | bytes 20971520 | tf_op jit(solution)/shard_map/tile/pallas_call | solution.py:293
  290.5 2.1 collective-permute-done.17.refs_4_
  292.6 0.1 collective-permute-done.18.refs_5_
  292.7 153.9 %finish.1.gradient = f32[2,32,64,128]{3,2,1,0:T(8,128)} custom-call(bf16[512,512]{1,0:T(8,128)(2,1)} %constant.21.inv.table, bf16[4,2,32,256,128]{4,3,2,1,0:T(8,128)(2,1)} %sens.11, bf16[2,1024,128]{2,1,0:T(8,128)(2,1)} %get-tuple-element.117.refs_0_, bf16[2,1024,128]{2,1,0:T(8,128)(2,1)} %collective-permute-done.14.refs_1_, ...), custom_call_target="tpu_custom_call" | custom-call | tf_op jit(solution)/shard_map/finish/pallas_call | solution.py:469
  446.6 7.3 %update.1 = (f32[2,32,64,128]{3,2,1,0:T(8,128)}, f32[2,32,64,128]{3,2,1,0:T(8,128)}, f32[2,32,64,128]{3,2,1,0:T(8,128)}) custom-call(f32[2,32,64,128]{3,2,1,0:T(8,128)} %constant_dynamic-slice_fusion.image, f32[2,32,64,128]{3,2,1,0:T(8,128)} %finish.1.gradient, f32[2,32,64,128]{3,2,1,0:T(8,128)} %auxiliary.1, f32[2,32,64,128]{3,2,1,0:T(8,128)} %dual.1), custom_call_target="tpu_custom_call" | custom-call | tf_op jit(solution)/shard_map/update/pallas_call | solution.py:525
  (33 shorter events, 0.1 us)
Async XLA Ops:
  13.1 7.5 %collective-permute-start.10 = (bf16[2,32,16,128]{3,2,1,0:T(8,128)(2,1)}, bf16[2,32,16,128]{3,2,1,0:T(8,128)(2,1)}, u32[]{:S(2)}, u32[]{:S(2)}) collective-permute-start(bf16[2,32,16,128]{3,2,1,0:T(8,128)(2,1)} %get-tuple-element.112), channel_id=1, source_target_pairs={{0,4},{1,5},{2,6},{3,7},{4,0},{5,1},{6,2},{7,3},{8,12},{9,13},{10,... | collective-permute-start | bytes 786440 | tf_op jit(solution)/shard_map/ppermute | solution.py:550
  14.3 18.7 %collective-permute-start.11 = (bf16[2,32,16,128]{3,2,1,0:T(8,128)(2,1)}, bf16[2,32,16,128]{3,2,1,0:T(8,128)(2,1)}, u32[]{:S(2)}, u32[]{:S(2)}) collective-permute-start(bf16[2,32,16,128]{3,2,1,0:T(8,128)(2,1)} %get-tuple-element.113), channel_id=1, source_target_pairs={{0,5},{1,6},{2,7},{3,0},{4,1},{5,2},{6,3},{7,4},{8,13},{9,14},{10,... | collective-permute-start | bytes 786440 | tf_op jit(solution)/shard_map/ppermute | solution.py:550
  16.3 19.7 %collective-permute-start.12 = (bf16[2,32,16,128]{3,2,1,0:T(8,128)(2,1)}, bf16[2,32,16,128]{3,2,1,0:T(8,128)(2,1)}, u32[]{:S(2)}, u32[]{:S(2)}) collective-permute-start(bf16[2,32,16,128]{3,2,1,0:T(8,128)(2,1)} %get-tuple-element.114), channel_id=1, source_target_pairs={{0,6},{1,7},{2,0},{3,1},{4,2},{5,3},{6,4},{7,5},{8,14},{9,15},{10,... | collective-permute-start | bytes 786440 | tf_op jit(solution)/shard_map/ppermute | solution.py:550
  16.6 19.7 %collective-permute-start.13 = (bf16[2,32,16,128]{3,2,1,0:T(8,128)(2,1)}, bf16[2,32,16,128]{3,2,1,0:T(8,128)(2,1)}, u32[]{:S(2)}, u32[]{:S(2)}) collective-permute-start(bf16[2,32,16,128]{3,2,1,0:T(8,128)(2,1)} %get-tuple-element.115), channel_id=1, source_target_pairs={{0,7},{1,0},{2,1},{3,2},{4,3},{5,4},{6,5},{7,6},{8,15},{9,8},{10,9... | collective-permute-start | bytes 786440 | tf_op jit(solution)/shard_map/ppermute | solution.py:550
  17.4 22.0 %collective-permute-start.7 = (bf16[2,32,16,128]{3,2,1,0:T(8,128)(2,1)}, bf16[2,32,16,128]{3,2,1,0:T(8,128)(2,1)}, u32[]{:S(2)}, u32[]{:S(2)}) collective-permute-start(bf16[2,32,16,128]{3,2,1,0:T(8,128)(2,1)} %get-tuple-element.109), channel_id=1, source_target_pairs={{0,1},{1,2},{2,3},{3,4},{4,5},{5,6},{6,7},{7,0},{8,9},{9,10},{10,1... | collective-permute-start | bytes 786440 | tf_op jit(solution)/shard_map/ppermute | solution.py:550
  20.6 18.9 %collective-permute-start.8 = (bf16[2,32,16,128]{3,2,1,0:T(8,128)(2,1)}, bf16[2,32,16,128]{3,2,1,0:T(8,128)(2,1)}, u32[]{:S(2)}, u32[]{:S(2)}) collective-permute-start(bf16[2,32,16,128]{3,2,1,0:T(8,128)(2,1)} %get-tuple-element.110), channel_id=1, source_target_pairs={{0,2},{1,3},{2,4},{3,5},{4,6},{5,7},{6,0},{7,1},{8,10},{9,11},{10,... | collective-permute-start | bytes 786440 | tf_op jit(solution)/shard_map/ppermute | solution.py:550
  33.0 25.7 %collective-permute-start.9 = (bf16[2,32,16,128]{3,2,1,0:T(8,128)(2,1)}, bf16[2,32,16,128]{3,2,1,0:T(8,128)(2,1)}, u32[]{:S(2)}, u32[]{:S(2)}) collective-permute-start(bf16[2,32,16,128]{3,2,1,0:T(8,128)(2,1)} %get-tuple-element.111), channel_id=1, source_target_pairs={{0,3},{1,4},{2,5},{3,6},{4,7},{5,0},{6,1},{7,2},{8,11},{9,12},{10,... | collective-permute-start | bytes 786440 | tf_op jit(solution)/shard_map/ppermute | solution.py:550
  36.0 33.1 %collective-permute-start = (bf16[2,32,16,128]{3,2,1,0:T(8,128)(2,1)}, bf16[2,32,16,128]{3,2,1,0:T(8,128)(2,1)}, u32[]{:S(2)}, u32[]{:S(2)}) collective-permute-start(bf16[2,32,16,128]{3,2,1,0:T(8,128)(2,1)} %get-tuple-element.101), channel_id=1, source_target_pairs={{0,1},{1,2},{2,3},{3,4},{4,5},{5,6},{6,7},{7,0},{8,9},{9,10},{10,1... | collective-permute-start | bytes 786440 | tf_op jit(solution)/shard_map/ppermute | solution.py:550
  36.3 32.8 %collective-permute-start.1 = (bf16[2,32,16,128]{3,2,1,0:T(8,128)(2,1)}, bf16[2,32,16,128]{3,2,1,0:T(8,128)(2,1)}, u32[]{:S(2)}, u32[]{:S(2)}) collective-permute-start(bf16[2,32,16,128]{3,2,1,0:T(8,128)(2,1)} %get-tuple-element.102), channel_id=1, source_target_pairs={{0,2},{1,3},{2,4},{3,5},{4,6},{5,7},{6,0},{7,1},{8,10},{9,11},{10,... | collective-permute-start | bytes 786440 | tf_op jit(solution)/shard_map/ppermute | solution.py:550
  39.4 33.5 %collective-permute-start.2 = (bf16[2,32,16,128]{3,2,1,0:T(8,128)(2,1)}, bf16[2,32,16,128]{3,2,1,0:T(8,128)(2,1)}, u32[]{:S(2)}, u32[]{:S(2)}) collective-permute-start(bf16[2,32,16,128]{3,2,1,0:T(8,128)(2,1)} %get-tuple-element.103), channel_id=1, source_target_pairs={{0,3},{1,4},{2,5},{3,6},{4,7},{5,0},{6,1},{7,2},{8,11},{9,12},{10,... | collective-permute-start | bytes 786440 | tf_op jit(solution)/shard_map/ppermute | solution.py:550
  39.5 34.3 %collective-permute-start.3 = (bf16[2,32,16,128]{3,2,1,0:T(8,128)(2,1)}, bf16[2,32,16,128]{3,2,1,0:T(8,128)(2,1)}, u32[]{:S(2)}, u32[]{:S(2)}) collective-permute-start(bf16[2,32,16,128]{3,2,1,0:T(8,128)(2,1)} %get-tuple-element.104), channel_id=1, source_target_pairs={{0,4},{1,5},{2,6},{3,7},{4,0},{5,1},{6,2},{7,3},{8,12},{9,13},{10,... | collective-permute-start | bytes 786440 | tf_op jit(solution)/shard_map/ppermute | solution.py:550
  58.8 15.7 %collective-permute-start.4 = (bf16[2,32,16,128]{3,2,1,0:T(8,128)(2,1)}, bf16[2,32,16,128]{3,2,1,0:T(8,128)(2,1)}, u32[]{:S(2)}, u32[]{:S(2)}) collective-permute-start(bf16[2,32,16,128]{3,2,1,0:T(8,128)(2,1)} %get-tuple-element.105), channel_id=1, source_target_pairs={{0,5},{1,6},{2,7},{3,0},{4,1},{5,2},{6,3},{7,4},{8,13},{9,14},{10,... | collective-permute-start | bytes 786440 | tf_op jit(solution)/shard_map/ppermute | solution.py:550
  69.1 36.7 %collective-permute-start.21 = (bf16[2,32,32,128]{3,2,1,0:T(8,128)(2,1)}, bf16[2,32,32,128]{3,2,1,0:T(8,128)(2,1)}, u32[]{:S(2)}, u32[]{:S(2)}) collective-permute-start(bf16[2,32,32,128]{3,2,1,0:T(8,128)(2,1)} %get-tuple-element.129), channel_id=1, source_target_pairs={{0,1},{1,2},{2,3},{3,4},{4,5},{5,6},{6,7},{7,0},{8,9},{9,10},{10,1... | collective-permute-start | bytes 1572872 | tf_op jit(solution)/shard_map/ppermute | solution.py:550
  69.1 36.6 %collective-permute-start.22 = (bf16[2,32,32,128]{3,2,1,0:T(8,128)(2,1)}, bf16[2,32,32,128]{3,2,1,0:T(8,128)(2,1)}, u32[]{:S(2)}, u32[]{:S(2)}) collective-permute-start(bf16[2,32,32,128]{3,2,1,0:T(8,128)(2,1)} %get-tuple-element.130), channel_id=1, source_target_pairs={{0,2},{1,3},{2,4},{3,5},{4,6},{5,7},{6,0},{7,1},{8,10},{9,11},{10,... | collective-permute-start | bytes 1572872 | tf_op jit(solution)/shard_map/ppermute | solution.py:550
  72.9 33.8 %collective-permute-start.23 = (bf16[2,32,32,128]{3,2,1,0:T(8,128)(2,1)}, bf16[2,32,32,128]{3,2,1,0:T(8,128)(2,1)}, u32[]{:S(2)}, u32[]{:S(2)}) collective-permute-start(bf16[2,32,32,128]{3,2,1,0:T(8,128)(2,1)} %get-tuple-element.131), channel_id=1, source_target_pairs={{0,3},{1,4},{2,5},{3,6},{4,7},{5,0},{6,1},{7,2},{8,11},{9,12},{10,... | collective-permute-start | bytes 1572872 | tf_op jit(solution)/shard_map/ppermute | solution.py:550
  73.7 28.1 %collective-permute-start.5 = (bf16[2,32,16,128]{3,2,1,0:T(8,128)(2,1)}, bf16[2,32,16,128]{3,2,1,0:T(8,128)(2,1)}, u32[]{:S(2)}, u32[]{:S(2)}) collective-permute-start(bf16[2,32,16,128]{3,2,1,0:T(8,128)(2,1)} %get-tuple-element.106), channel_id=1, source_target_pairs={{0,6},{1,7},{2,0},{3,1},{4,2},{5,3},{6,4},{7,5},{8,14},{9,15},{10,... | collective-permute-start | bytes 786440 | tf_op jit(solution)/shard_map/ppermute | solution.py:550
  74.5 30.6 %collective-permute-start.6 = (bf16[2,32,16,128]{3,2,1,0:T(8,128)(2,1)}, bf16[2,32,16,128]{3,2,1,0:T(8,128)(2,1)}, u32[]{:S(2)}, u32[]{:S(2)}) collective-permute-start(bf16[2,32,16,128]{3,2,1,0:T(8,128)(2,1)} %get-tuple-element.107), channel_id=1, source_target_pairs={{0,7},{1,0},{2,1},{3,2},{4,3},{5,4},{6,5},{7,6},{8,15},{9,8},{10,9... | collective-permute-start | bytes 786440 | tf_op jit(solution)/shard_map/ppermute | solution.py:550
  101.8 29.0 %collective-permute-start.24 = (bf16[2,32,32,128]{3,2,1,0:T(8,128)(2,1)}, bf16[2,32,32,128]{3,2,1,0:T(8,128)(2,1)}, u32[]{:S(2)}, u32[]{:S(2)}) collective-permute-start(bf16[2,32,32,128]{3,2,1,0:T(8,128)(2,1)} %get-tuple-element.132), channel_id=1, source_target_pairs={{0,4},{1,5},{2,6},{3,7},{4,0},{5,1},{6,2},{7,3},{8,12},{9,13},{10,... | collective-permute-start | bytes 1572872 | tf_op jit(solution)/shard_map/ppermute | solution.py:550
  105.0 31.2 %collective-permute-start.25 = (bf16[2,32,32,128]{3,2,1,0:T(8,128)(2,1)}, bf16[2,32,32,128]{3,2,1,0:T(8,128)(2,1)}, u32[]{:S(2)}, u32[]{:S(2)}) collective-permute-start(bf16[2,32,32,128]{3,2,1,0:T(8,128)(2,1)} %get-tuple-element.133), channel_id=1, source_target_pairs={{0,5},{1,6},{2,7},{3,0},{4,1},{5,2},{6,3},{7,4},{8,13},{9,14},{10,... | collective-permute-start | bytes 1572872 | tf_op jit(solution)/shard_map/ppermute | solution.py:550
  105.8 33.8 %collective-permute-start.26 = (bf16[2,32,32,128]{3,2,1,0:T(8,128)(2,1)}, bf16[2,32,32,128]{3,2,1,0:T(8,128)(2,1)}, u32[]{:S(2)}, u32[]{:S(2)}) collective-permute-start(bf16[2,32,32,128]{3,2,1,0:T(8,128)(2,1)} %get-tuple-element.134), channel_id=1, source_target_pairs={{0,6},{1,7},{2,0},{3,1},{4,2},{5,3},{6,4},{7,5},{8,14},{9,15},{10,... | collective-permute-start | bytes 1572872 | tf_op jit(solution)/shard_map/ppermute | solution.py:550
  105.8 34.1 %collective-permute-start.27 = (bf16[2,32,32,128]{3,2,1,0:T(8,128)(2,1)}, bf16[2,32,32,128]{3,2,1,0:T(8,128)(2,1)}, u32[]{:S(2)}, u32[]{:S(2)}) collective-permute-start(bf16[2,32,32,128]{3,2,1,0:T(8,128)(2,1)} %get-tuple-element.135), channel_id=1, source_target_pairs={{0,7},{1,0},{2,1},{3,2},{4,3},{5,4},{6,5},{7,6},{8,15},{9,8},{10,9... | collective-permute-start | bytes 1572872 | tf_op jit(solution)/shard_map/ppermute | solution.py:550
  106.7 37.5 %collective-permute-start.28 = (bf16[2,32,32,128]{3,2,1,0:T(8,128)(2,1)}, bf16[2,32,32,128]{3,2,1,0:T(8,128)(2,1)}, u32[]{:S(2)}, u32[]{:S(2)}) collective-permute-start(bf16[2,32,32,128]{3,2,1,0:T(8,128)(2,1)} %get-tuple-element.149), channel_id=1, source_target_pairs={{0,1},{1,2},{2,3},{3,4},{4,5},{5,6},{6,7},{7,0},{8,9},{9,10},{10,1... | collective-permute-start | bytes 1572872 | tf_op jit(solution)/shard_map/ppermute | solution.py:550
  130.8 36.8 %collective-permute-start.29 = (bf16[2,32,32,128]{3,2,1,0:T(8,128)(2,1)}, bf16[2,32,32,128]{3,2,1,0:T(8,128)(2,1)}, u32[]{:S(2)}, u32[]{:S(2)}) collective-permute-start(bf16[2,32,32,128]{3,2,1,0:T(8,128)(2,1)} %get-tuple-element.150), channel_id=1, source_target_pairs={{0,2},{1,3},{2,4},{3,5},{4,6},{5,7},{6,0},{7,1},{8,10},{9,11},{10,... | collective-permute-start | bytes 1572872 | tf_op jit(solution)/shard_map/ppermute | solution.py:550
  136.3 31.4 %collective-permute-start.30 = (bf16[2,32,32,128]{3,2,1,0:T(8,128)(2,1)}, bf16[2,32,32,128]{3,2,1,0:T(8,128)(2,1)}, u32[]{:S(2)}, u32[]{:S(2)}) collective-permute-start(bf16[2,32,32,128]{3,2,1,0:T(8,128)(2,1)} %get-tuple-element.151), channel_id=1, source_target_pairs={{0,3},{1,4},{2,5},{3,6},{4,7},{5,0},{6,1},{7,2},{8,11},{9,12},{10,... | collective-permute-start | bytes 1572872 | tf_op jit(solution)/shard_map/ppermute | solution.py:550
  139.6 43.8 %collective-permute-start.31 = (bf16[2,32,32,128]{3,2,1,0:T(8,128)(2,1)}, bf16[2,32,32,128]{3,2,1,0:T(8,128)(2,1)}, u32[]{:S(2)}, u32[]{:S(2)}) collective-permute-start(bf16[2,32,32,128]{3,2,1,0:T(8,128)(2,1)} %get-tuple-element.152), channel_id=1, source_target_pairs={{0,4},{1,5},{2,6},{3,7},{4,0},{5,1},{6,2},{7,3},{8,12},{9,13},{10,... | collective-permute-start | bytes 1572872 | tf_op jit(solution)/shard_map/ppermute | solution.py:550
  139.9 50.9 %collective-permute-start.32 = (bf16[2,32,32,128]{3,2,1,0:T(8,128)(2,1)}, bf16[2,32,32,128]{3,2,1,0:T(8,128)(2,1)}, u32[]{:S(2)}, u32[]{:S(2)}) collective-permute-start(bf16[2,32,32,128]{3,2,1,0:T(8,128)(2,1)} %get-tuple-element.153), channel_id=1, source_target_pairs={{0,5},{1,6},{2,7},{3,0},{4,1},{5,2},{6,3},{7,4},{8,13},{9,14},{10,... | collective-permute-start | bytes 1572872 | tf_op jit(solution)/shard_map/ppermute | solution.py:550
  144.2 46.5 %collective-permute-start.33 = (bf16[2,32,32,128]{3,2,1,0:T(8,128)(2,1)}, bf16[2,32,32,128]{3,2,1,0:T(8,128)(2,1)}, u32[]{:S(2)}, u32[]{:S(2)}) collective-permute-start(bf16[2,32,32,128]{3,2,1,0:T(8,128)(2,1)} %get-tuple-element.154), channel_id=1, source_target_pairs={{0,6},{1,7},{2,0},{3,1},{4,2},{5,3},{6,4},{7,5},{8,14},{9,15},{10,... | collective-permute-start | bytes 1572872 | tf_op jit(solution)/shard_map/ppermute | solution.py:550
  167.6 44.5 %collective-permute-start.34 = (bf16[2,32,32,128]{3,2,1,0:T(8,128)(2,1)}, bf16[2,32,32,128]{3,2,1,0:T(8,128)(2,1)}, u32[]{:S(2)}, u32[]{:S(2)}) collective-permute-start(bf16[2,32,32,128]{3,2,1,0:T(8,128)(2,1)} %get-tuple-element.155), channel_id=1, source_target_pairs={{0,7},{1,0},{2,1},{3,2},{4,3},{5,4},{6,5},{7,6},{8,15},{9,8},{10,9... | collective-permute-start | bytes 1572872 | tf_op jit(solution)/shard_map/ppermute | solution.py:550
  167.6 47.4 %collective-permute-start.35 = (bf16[2,32,32,128]{3,2,1,0:T(8,128)(2,1)}, bf16[2,32,32,128]{3,2,1,0:T(8,128)(2,1)}, u32[]{:S(2)}, u32[]{:S(2)}) collective-permute-start(bf16[2,32,32,128]{3,2,1,0:T(8,128)(2,1)} %get-tuple-element.166), channel_id=1, source_target_pairs={{0,1},{1,2},{2,3},{3,4},{4,5},{5,6},{6,7},{7,0},{8,9},{9,10},{10,1... | collective-permute-start | bytes 1572872 | tf_op jit(solution)/shard_map/ppermute | solution.py:550
  183.4 40.7 %collective-permute-start.36 = (bf16[2,32,32,128]{3,2,1,0:T(8,128)(2,1)}, bf16[2,32,32,128]{3,2,1,0:T(8,128)(2,1)}, u32[]{:S(2)}, u32[]{:S(2)}) collective-permute-start(bf16[2,32,32,128]{3,2,1,0:T(8,128)(2,1)} %get-tuple-element.167), channel_id=1, source_target_pairs={{0,2},{1,3},{2,4},{3,5},{4,6},{5,7},{6,0},{7,1},{8,10},{9,11},{10,... | collective-permute-start | bytes 1572872 | tf_op jit(solution)/shard_map/ppermute | solution.py:550
  190.7 33.3 %collective-permute-start.37 = (bf16[2,32,32,128]{3,2,1,0:T(8,128)(2,1)}, bf16[2,32,32,128]{3,2,1,0:T(8,128)(2,1)}, u32[]{:S(2)}, u32[]{:S(2)}) collective-permute-start(bf16[2,32,32,128]{3,2,1,0:T(8,128)(2,1)} %get-tuple-element.168), channel_id=1, source_target_pairs={{0,3},{1,4},{2,5},{3,6},{4,7},{5,0},{6,1},{7,2},{8,11},{9,12},{10,... | collective-permute-start | bytes 1572872 | tf_op jit(solution)/shard_map/ppermute | solution.py:550
  190.8 35.0 %collective-permute-start.38 = (bf16[2,32,32,128]{3,2,1,0:T(8,128)(2,1)}, bf16[2,32,32,128]{3,2,1,0:T(8,128)(2,1)}, u32[]{:S(2)}, u32[]{:S(2)}) collective-permute-start(bf16[2,32,32,128]{3,2,1,0:T(8,128)(2,1)} %get-tuple-element.169), channel_id=1, source_target_pairs={{0,4},{1,5},{2,6},{3,7},{4,0},{5,1},{6,2},{7,3},{8,12},{9,13},{10,... | collective-permute-start | bytes 1572872 | tf_op jit(solution)/shard_map/ppermute | solution.py:550
  212.1 34.5 %collective-permute-start.39 = (bf16[2,32,32,128]{3,2,1,0:T(8,128)(2,1)}, bf16[2,32,32,128]{3,2,1,0:T(8,128)(2,1)}, u32[]{:S(2)}, u32[]{:S(2)}) collective-permute-start(bf16[2,32,32,128]{3,2,1,0:T(8,128)(2,1)} %get-tuple-element.170), channel_id=1, source_target_pairs={{0,5},{1,6},{2,7},{3,0},{4,1},{5,2},{6,3},{7,4},{8,13},{9,14},{10,... | collective-permute-start | bytes 1572872 | tf_op jit(solution)/shard_map/ppermute | solution.py:550
  215.0 40.5 %collective-permute-start.40 = (bf16[2,32,32,128]{3,2,1,0:T(8,128)(2,1)}, bf16[2,32,32,128]{3,2,1,0:T(8,128)(2,1)}, u32[]{:S(2)}, u32[]{:S(2)}) collective-permute-start(bf16[2,32,32,128]{3,2,1,0:T(8,128)(2,1)} %get-tuple-element.171), channel_id=1, source_target_pairs={{0,6},{1,7},{2,0},{3,1},{4,2},{5,3},{6,4},{7,5},{8,14},{9,15},{10,... | collective-permute-start | bytes 1572872 | tf_op jit(solution)/shard_map/ppermute | solution.py:550
  224.0 31.5 %collective-permute-start.41 = (bf16[2,32,32,128]{3,2,1,0:T(8,128)(2,1)}, bf16[2,32,32,128]{3,2,1,0:T(8,128)(2,1)}, u32[]{:S(2)}, u32[]{:S(2)}) collective-permute-start(bf16[2,32,32,128]{3,2,1,0:T(8,128)(2,1)} %get-tuple-element.172), channel_id=1, source_target_pairs={{0,7},{1,0},{2,1},{3,2},{4,3},{5,4},{6,5},{7,6},{8,15},{9,8},{10,9... | collective-permute-start | bytes 1572872 | tf_op jit(solution)/shard_map/ppermute | solution.py:550
  224.0 31.6 %collective-permute-start.14 = (bf16[2,1024,128]{2,1,0:T(8,128)(2,1)}, bf16[2,1024,128]{2,1,0:T(8,128)(2,1)}, u32[]{:S(2)}, u32[]{:S(2)}) collective-permute-start(bf16[2,1024,128]{2,1,0:T(8,128)(2,1)} %get-tuple-element.118), channel_id=1, source_target_pairs={{0,1},{1,2},{2,3},{3,4},{4,5},{5,6},{6,7},{7,0},{8,9},{9,10},{10,1... | collective-permute-start | bytes 1572872 | tf_op jit(solution)/shard_map/ppermute | solution.py:550
  225.8 43.9 %collective-permute-start.15 = (bf16[2,1024,128]{2,1,0:T(8,128)(2,1)}, bf16[2,1024,128]{2,1,0:T(8,128)(2,1)}, u32[]{:S(2)}, u32[]{:S(2)}) collective-permute-start(bf16[2,1024,128]{2,1,0:T(8,128)(2,1)} %get-tuple-element.119), channel_id=1, source_target_pairs={{0,2},{1,3},{2,4},{3,5},{4,6},{5,7},{6,0},{7,1},{8,10},{9,11},{10,... | collective-permute-start | bytes 1572872 | tf_op jit(solution)/shard_map/ppermute | solution.py:550
  246.7 43.8 %collective-permute-start.16 = (bf16[2,1024,128]{2,1,0:T(8,128)(2,1)}, bf16[2,1024,128]{2,1,0:T(8,128)(2,1)}, u32[]{:S(2)}, u32[]{:S(2)}) collective-permute-start(bf16[2,1024,128]{2,1,0:T(8,128)(2,1)} %get-tuple-element.120), channel_id=1, source_target_pairs={{0,3},{1,4},{2,5},{3,6},{4,7},{5,0},{6,1},{7,2},{8,11},{9,12},{10,... | collective-permute-start | bytes 1572872 | tf_op jit(solution)/shard_map/ppermute | solution.py:550
  255.5 37.1 %collective-permute-start.17 = (bf16[2,1024,128]{2,1,0:T(8,128)(2,1)}, bf16[2,1024,128]{2,1,0:T(8,128)(2,1)}, u32[]{:S(2)}, u32[]{:S(2)}) collective-permute-start(bf16[2,1024,128]{2,1,0:T(8,128)(2,1)} %get-tuple-element.121), channel_id=1, source_target_pairs={{0,4},{1,5},{2,6},{3,7},{4,0},{5,1},{6,2},{7,3},{8,12},{9,13},{10,... | collective-permute-start | bytes 1572872 | tf_op jit(solution)/shard_map/ppermute | solution.py:550
  255.5 37.2 %collective-permute-start.18 = (bf16[2,1024,128]{2,1,0:T(8,128)(2,1)}, bf16[2,1024,128]{2,1,0:T(8,128)(2,1)}, u32[]{:S(2)}, u32[]{:S(2)}) collective-permute-start(bf16[2,1024,128]{2,1,0:T(8,128)(2,1)} %get-tuple-element.122), channel_id=1, source_target_pairs={{0,5},{1,6},{2,7},{3,0},{4,1},{5,2},{6,3},{7,4},{8,13},{9,14},{10,... | collective-permute-start | bytes 1572872 | tf_op jit(solution)/shard_map/ppermute | solution.py:550
  255.6 37.1 %collective-permute-start.19 = (bf16[2,1024,128]{2,1,0:T(8,128)(2,1)}, bf16[2,1024,128]{2,1,0:T(8,128)(2,1)}, u32[]{:S(2)}, u32[]{:S(2)}) collective-permute-start(bf16[2,1024,128]{2,1,0:T(8,128)(2,1)} %get-tuple-element.123), channel_id=1, source_target_pairs={{0,6},{1,7},{2,0},{3,1},{4,2},{5,3},{6,4},{7,5},{8,14},{9,15},{10,... | collective-permute-start | bytes 1572872 | tf_op jit(solution)/shard_map/ppermute | solution.py:550
  269.7 23.0 %collective-permute-start.20 = (bf16[2,1024,128]{2,1,0:T(8,128)(2,1)}, bf16[2,1024,128]{2,1,0:T(8,128)(2,1)}, u32[]{:S(2)}, u32[]{:S(2)}) collective-permute-start(bf16[2,1024,128]{2,1,0:T(8,128)(2,1)} %get-tuple-element.124), channel_id=1, source_target_pairs={{0,7},{1,0},{2,1},{3,2},{4,3},{5,4},{6,5},{7,6},{8,15},{9,8},{10,9... | collective-permute-start | bytes 1572872 | tf_op jit(solution)/shard_map/ppermute | solution.py:550

commit v4 on v3

--- a/solution.py
+++ b/solution.py
@@ -36,6 +36,19 @@
 
 def params(limit=VMEM_LIMIT, **extra):
     return pltpu.CompilerParams(vmem_limit_bytes=limit, **extra)
+
+
+def partner(me, off, n):
+    other, bit = me, 1
+    while bit < n:
+        if off & bit:
+            other = other + bit * (1 - 2 * (me // bit % 2))
+        bit *= 2
+    return other
+
+
+def turns(n):
+    return [*range(2, n, 2), *range(3, n, 2), 1]
 
 
 def once(shape):
@@ -91,7 +104,7 @@
     @pl.when(step == pl.num_programs(0) - 1)
     def last():
         for off in range(n):
-            d = lax.rem(me + off, n)
+            d = partner(me, off, n)
             for p in range(2):
 
                 def settle(k, carry):
@@ -103,18 +116,17 @@
                 lax.fori_loop(0, kl // 2, settle, 0, unroll=4)
 
 
-def forward_call(table, image, sensitivity, coil, part, parts, n, kl):
-    _, _, xl, length, depth = sensitivity.shape
-    xp = xl // parts
+def forward_call(table, image, sensitivity, coil, first, xp, n, kl):
+    _, _, _, length, depth = sensitivity.shape
     rows = 8 if xp % 8 == 0 else xp
-    steps = xp // rows
+    steps, skip = xp // rows, first // rows
     return pl.pallas_call(
         functools.partial(forward_kernel, n, kl, xp),
         grid=(steps,),
         in_specs=[
             once(table.shape),
-            pl.BlockSpec((2, rows, length, depth), lambda i: (0, part * steps + i, 0, 0)),
-            pl.BlockSpec((1, 2, rows, length, depth), lambda i: (coil, 0, part * steps + i, 0, 0)),
+            pl.BlockSpec((2, rows, length, depth), lambda i: (0, skip + i, 0, 0)),
+            pl.BlockSpec((1, 2, rows, length, depth), lambda i: (coil, 0, skip + i, 0, 0)),
         ],
         out_specs=[once((2, kl, xp, depth))] * n,
         out_shape=[jax.ShapeDtypeStruct((2, kl, xp, depth), BF16)] * n,
@@ -155,15 +167,14 @@
 
 
 def tile_kernel(n, kl, xl, win, parts, coil, offsets, counts, fwd, inv, blocks, sorted_samples, *refs):
-    pieces, outs, refs = refs[: n * parts], refs[n * parts : n * parts + n], refs[n * parts + n :]
+    count = n * len(parts)
+    pieces, outs, refs = refs[:count], refs[count : count + n], refs[count + n :]
     total, kspace, weights, piece, samples, leaving, sem, piece_sem, *wide = refs
     me = lax.axis_index("slab")
     copies = []
-    xp = xl // parts
     for off in range(n):
-        origin = lax.rem(me + n - off, n)
-        for h in range(parts):
-            target = piece.at[origin, :, :, pl.ds(h * xp, xp)]
+        for h, (start, size) in enumerate(parts):
+            target = piece.at[partner(me, off, n), :, :, pl.ds(start, size)]
             copies.append(pltpu.make_async_copy(pieces[h * n + off], target, piece_sem.at[h * n + off]))
     for copy in copies:
         copy.start()
@@ -255,7 +266,7 @@
 
     lax.fori_loop(0, kl // 2, to_rows, 0, unroll=2)
     for off in range(n):
-        d = lax.rem(me + off, n)
+        d = partner(me, off, n)
         for p in range(2):
 
             def leave(k, carry):
@@ -271,9 +282,8 @@
         pltpu.make_async_copy(leaving.at[off], outs[off], piece_sem.at[off]).wait()
 
 
-def tile_call(fwd, inv, pieces, blocks, samples, offsets, counts, coil, n, kl, xl):
+def tile_call(fwd, inv, pieces, parts, blocks, samples, offsets, counts, coil, n, kl, xl):
     depth = pieces[0].shape[-1]
-    parts = len(pieces) // n
     _, slots, psize, cells = blocks.shape
     length = n * xl
     narrow = kl % 16 == 0 and xl % 16 == 0
@@ -285,7 +295,7 @@
         pltpu.VMEM((slots, psize, 2 * depth), BF16),
         pltpu.VMEM((n, 2, xl * kl, depth), BF16),
         pltpu.SemaphoreType.DMA((2,)),
-        pltpu.SemaphoreType.DMA((n * parts,)),
+        pltpu.SemaphoreType.DMA((len(pieces),)),
     ]
     if not narrow:
         scratch.append(pltpu.VMEM((n, 2, kl, xl, depth), F32))
@@ -293,7 +303,7 @@
     return pl.pallas_call(
         functools.partial(tile_kernel, n, kl, xl, cells // kl, parts, coil),
         grid=(1,),
-        in_specs=[smem, smem, once(fwd.shape), once(inv.shape), HBM, HBM] + [HBM] * (n * parts),
+        in_specs=[smem, smem, once(fwd.shape), once(inv.shape), HBM, HBM] + [HBM] * len(pieces),
         out_specs=[HBM] * n,
         out_shape=[jax.ShapeDtypeStruct((2, xl * kl, depth), BF16)] * n,
         scratch_shapes=scratch,
@@ -316,6 +326,7 @@
     share = length // shares
     rows = xl // chunks
     band = rows * kl
+    group = min(rows, 2)
     me = lax.axis_index("slab")
     mine = lax.axis_index("coil")
 
@@ -337,13 +348,13 @@
     def send_band(j, carry):
         where = pl.ds(pl.multiple_of(j * band, band), band)
         for k in range(ready, coils):
-            for off in range(1, n):
+            for off in turns(n):
                 pltpu.make_async_remote_copy(
                     src_ref=backs[k][off].at[:, where, :],
                     dst_ref=landing.at[k, me, :, where, :],
                     send_sem=send,
                     recv_sem=recv.at[j],
-                    device_id={"slab": lax.rem(me + off, n)},
+                    device_id={"slab": partner(me, off, n)},
                     device_id_type=pl.DeviceIdType.MESH,
                 ).start()
         return carry
@@ -352,8 +363,8 @@
     copies = []
     for k in range(coils):
         for off in range(n if k < ready else 1):
-            origin = lax.rem(me + n - off, n)
-            copies.append(pltpu.make_async_copy(backs[k][off], landing.at[k, origin], local.at[k * n + off]))
+            origin = landing.at[k, partner(me, off, n)]
+            copies.append(pltpu.make_async_copy(backs[k][off], origin, local.at[k * n + off]))
         copies.append(pltpu.make_async_copy(sens.at[k], sens_v.at[k], local.at[coils * n + k]))
     for copy in copies:
         copy.start()
@@ -398,13 +409,13 @@
             return jnp.concatenate(pieces, axis=0).astype(BF16)
 
         def pair(i, carry):
-            total = [[None, None], [None, None]]
+            total = [[None, None]] * group
             for k in range(coils):
-                both = jnp.concatenate([columns_of(k, 2 * i), columns_of(k, 2 * i + 1)], axis=1)
+                both = jnp.concatenate([columns_of(k, group * i + h) for h in range(group)], axis=1)
                 adj = jnp.dot(table[...], both, preferred_element_type=F32)
                 adj = adj.astype(BF16).astype(F32)
-                for h in range(2):
-                    x = j * rows + 2 * i + h
+                for h in range(group):
+                    x = j * rows + group * i + h
                     ar = adj[:length, h * depth : (h + 1) * depth]
                     ai = adj[length:, h * depth : (h + 1) * depth]
                     sr = sens_v[k, 0, x].astype(F32)
@@ -412,14 +423,14 @@
                     re = sr * ar + si * ai
                     im = sr * ai - si * ar
                     total[h] = [re, im] if k == 0 else [total[h][0] + re, total[h][1] + im]
-            for h in range(2):
-                x = j * rows + 2 * i + h
+            for h in range(group):
+                x = j * rows + group * i + h
                 for p in range(2):
                     for q in range(shares):
                         grad[q, p, x] = total[h][p][q * share : (q + 1) * share].astype(BF16)
             return carry
 
-        lax.fori_loop(0, rows // 2, pair, 0)
+        lax.fori_loop(0, rows // group, pair, 0)
         lines = pl.ds(j * rows, rows)
         for off in range(1, shares):
             target = lax.rem(mine + off, shares)
@@ -448,7 +459,7 @@
 
 def finish_call(table, backs, sent, sensitivity, shares, n, kl):
     coils, _, xl, length, depth = sensitivity.shape
-    chunks = xl // 2 if xl % 2 == 0 else 1
+    chunks = xl
     rows = xl // chunks
     share = length // shares
     vmem = pl.BlockSpec(memory_space=pltpu.VMEM)
@@ -465,7 +476,7 @@
     ]
     if kl % 16:
         scratch.append(pltpu.VMEM((coils, n, 2, rows * kl, depth), F32))
-    limit = VMEM_LIMIT - 24 * xl * share * depth
+    limit = VMEM_LIMIT - 32 * xl * share * depth
     return pl.pallas_call(
         functools.partial(finish_kernel, n, shares, kl, xl, chunks, sent),
         in_specs=[vmem, HBM] + [HBM] * (coils * n),
@@ -528,7 +539,7 @@
         in_specs=[plain, plain, plain, plain],
         out_specs=[plain, plain, plain],
         out_shape=[shape, shape, shape],
-        compiler_params=params(VMEM_LIMIT - 24 * xl * share * depth),
+        compiler_params=params(VMEM_LIMIT - 128 * xl * share * depth),
         name="update",
     )(image, gradient, auxiliary, dual)
 
@@ -544,22 +555,25 @@
     x_inv = complex_table(n * xl, True)
 
     def swap(parts):
-        moved = [parts[0]]
-        for off in range(1, n):
-            ring = [(i, (i + off) % n) for i in range(n)]
-            moved.append(lax.ppermute(parts[off], "slab", ring))
+        moved = list(parts)
+        for off in turns(n):
+            moved[off] = lax.ppermute(parts[off], "slab", [(i, partner(i, off, n)) for i in range(n)])
         return moved
 
+    def parts_of(c):
+        if c == 0 and xl % 32 == 0:
+            return [(0, xl // 4), (xl // 4, xl // 4), (xl // 2, xl // 2)]
+        return [(0, xl)]
+
     def tile_of(pieces, c):
-        return tile_call(x_fwd, x_inv, pieces, blocks, sorted_samples, offsets, counts, c, n, kl, xl)
+        return tile_call(x_fwd, x_inv, pieces, parts_of(c), blocks, sorted_samples, offsets, counts, c, n, kl, xl)
 
     share = length_y // shares
     pieces, tiles, table = [], [], y_fwd
     for c in range(coils):
-        parts = 2 if c == 0 and xl % 32 == 0 else 1
         moved = []
-        for part in range(parts):
-            half = list(forward_call(table, image, sensitivity, c, part, parts, n, kl))
+        for first, size in parts_of(c):
+            half = list(forward_call(table, image, sensitivity, c, first, size, n, kl))
             table, half[0] = lax.optimization_barrier((table, half[0]))
             moved += swap(half)
         pieces.append(moved)

time: 456 us -> 453 us (level)
  starting transfers between devices: 91.3 us -> 73.3 us
  waiting for transfers between devices: 61.9 us -> 79.4 us
  Pallas kernels: 296 us -> 291 us
    ppermute x42 -> x49, starting transfers between devices: 91.3 us -> 73.3 us  [swap(): lax.ppermute(parts[off], 'slab', [(i, partner(i, off, n)) for i in range(...]
    ppermute x42 -> x49, waiting for transfers between devices: 61.9 us -> 79.4 us  [swap(): lax.ppermute(parts[off], 'slab', [(i, partner(i, off, n)) for i in range(...]
    pallas_call x1, Pallas kernels: 154 us -> 148 us  [finish_call(): pl.pallas_call(functools.partial(finish_kernel, n, shares, kl, xl, chunks...]
    pallas_call x5 -> x6, Pallas kernels: 43.3 us -> 46.4 us  [forward_call(): pl.pallas_call(functools.partial(forward_kernel, n, kl, xp), grid=(steps,...]
  transfers between devices with their start and end apart: 42 -> 49, of which waited for: 9 -> 9; matrix products, arithmetic and copies ran while one was open for 1% -> 1% of each run, Pallas kernels for 27% -> 29%
where the time goes in v4:
time: 453 us; the launch traced here: 450 us
  Pallas kernels  291 us (64%)
  waiting for transfers between devices  79.4 us (18%)
  starting transfers between devices  73.3 us (16%)
  local copies, waits for them, and re-layouts  4.77 us (1%)
    pallas_call x1, Pallas kernels, finish_call(): pl.pallas_call(functools.partial(finish_kernel, n, shares, kl, xl, chunks...  148 us
    pallas_call x4, Pallas kernels, tile_call(): pl.pallas_call(functools.partial(tile_kernel, n, kl, xl, cells // kl, par...  83.6 us
    ppermute x49, waiting for transfers between devices, swap(): lax.ppermute(parts[off], 'slab', [(i, partner(i, off, n)) for i in range(...  79.4 us
    ppermute x49, starting transfers between devices, swap(): lax.ppermute(parts[off], 'slab', [(i, partner(i, off, n)) for i in range(...  73.3 us
    pallas_call x6, Pallas kernels, forward_call(): pl.pallas_call(functools.partial(forward_kernel, n, kl, xp), grid=(steps,...  46.4 us
  transfers between devices with their start and end apart: 49, of which 9 were waited for; matrix products, arithmetic and copies ran while one was open for 1% of the time, Pallas kernels for 29%

profile of v4, /device:TPU:9, one launch (start us, length us, event | category | flops | bytes accessed | tf_op | source)
XLA Modules:
  0.0 450.2 jit_solution(11792396582590825113)
XLA Ops:
  0.6 4.6 %forward.6 = (bf16[2,32,8,128]{3,2,1,0:T(8,128)(2,1)}, bf16[2,32,8,128]{3,2,1,0:T(8,128)(2,1)}, bf16[2,32,8,128]{3,2,1,0:T(8,128)(2,1)}, bf16[2,32,8,128]{3,2,1,...) custom-call(bf16[512,512]{1,0:T(8,128)(2,1)} %constant.22.table.fwd,, ...), custom_call_target="tpu_custom_call" | custom-call | flops 536870912 | bytes 3145728 | tf_op jit(solution)/shard_map/forward/pallas_call | solution.py:123
  5.2 4.6 %forward.7 = (bf16[2,32,8,128]{3,2,1,0:T(8,128)(2,1)}, bf16[2,32,8,128]{3,2,1,0:T(8,128)(2,1)}, bf16[2,32,8,128]{3,2,1,0:T(8,128)(2,1)}, bf16[2,32,8,128]{3,2,1,...) custom-call(bf16[512,512]{1,0:T(8,128)(2,1)} %constant.22.table.fwd,, ...), custom_call_target="tpu_custom_call" | custom-call | flops 536870912 | bytes 3145728 | tf_op jit(solution)/shard_map/forward/pallas_call | solution.py:123
  9.8 1.2 collective-permute-start.10
  11.1 1.1 collective-permute-start.11
  12.2 2.2 collective-permute-start.12
  14.3 0.3 collective-permute-start.13
  14.6 0.3 collective-permute-start.7
  14.9 1.2 collective-permute-start.8
  16.1 7.7 %collective-permute-done.11.refs_13_ = bf16[2,32,8,128]{3,2,1,0:T(8,128)(2,1)} collective-permute-done((bf16[2,32,8,128]{3,2,1,0:T(8,128)(2,1)}, bf16[2,32,8,128]{3,2,1,0:T(8,128)(2,1)}, u32[]{:S(2)}, u32[]{:S(2)}) %collective-permute-start.11) | collective-permute-done | bytes 131104 | tf_op jit(solution)/shard_map/ppermute | solution.py:560
  23.8 1.1 collective-permute-start.9
  24.9 0.6 collective-permute-start
  25.4 0.3 collective-permute-start.1
  25.7 1.4 collective-permute-start.2
  27.1 1.2 collective-permute-start.3
  28.4 1.8 collective-permute-done.9.refs_11_
  30.2 2.2 collective-permute-start.4
  32.5 1.6 collective-permute-start.5
  34.1 3.1 collective-permute-start.6
  37.2 6.3 %forward.8 = (bf16[2,32,16,128]{3,2,1,0:T(8,128)(2,1)}, bf16[2,32,16,128]{3,2,1,0:T(8,128)(2,1)}, bf16[2,32,16,128]{3,2,1,0:T(8,128)(2,1)}, bf16[2,32,16,128]{3,...) custom-call(bf16[512,512]{1,0:T(8,128)(2,1)} %constant.22.table.fwd,, ...), custom_call_target="tpu_custom_call" | custom-call | flops 1073741824 | bytes 6291456 | tf_op jit(solution)/shard_map/forward/pallas_call | solution.py:123
  43.5 0.2 collective-permute-start.15
  43.7 1.9 collective-permute-start.16
  45.7 1.4 collective-permute-start.18
  47.1 10.3 %forward.9 = (bf16[2,32,32,128]{3,2,1,0:T(8,128)(2,1)}, bf16[2,32,32,128]{3,2,1,0:T(8,128)(2,1)}, bf16[2,32,32,128]{3,2,1,0:T(8,128)(2,1)}, bf16[2,32,32,128]{3,...) custom-call(bf16[512,512]{1,0:T(8,128)(2,1)} %constant.22.table.fwd,, ...), custom_call_target="tpu_custom_call" | custom-call | flops 2147483648 | bytes 12582912 | tf_op jit(solution)/shard_map/forward/pallas_call | solution.py:123
  57.4 0.5 collective-permute-start.28
  57.9 0.1 collective-permute-start.29
  58.0 1.6 collective-permute-start.30
  59.7 2.6 collective-permute-start.20
  62.3 10.3 %forward.10 = (bf16[2,32,32,128]{3,2,1,0:T(8,128)(2,1)}, bf16[2,32,32,128]{3,2,1,0:T(8,128)(2,1)}, bf16[2,32,32,128]{3,2,1,0:T(8,128)(2,1)}, bf16[2,32,32,128]{3...) custom-call(bf16[512,512]{1,0:T(8,128)(2,1)} %constant.22.table.fwd,, ...), custom_call_target="tpu_custom_call" | custom-call | flops 2147483648 | bytes 12582912 | tf_op jit(solution)/shard_map/forward/pallas_call | solution.py:123
  72.6 15.7 %collective-permute-done.19.refs_22_ = bf16[2,32,16,128]{3,2,1,0:T(8,128)(2,1)} collective-permute-done((bf16[2,32,16,128]{3,2,1,0:T(8,128)(2,1)}, bf16[2,32,16,128]{3,2,1,0:T(8,128)(2,1)}, u32[]{:S(2)}, u32[]{:S(2)}) %collective-permute-start.19) | collective-permute-done | bytes 262176 | tf_op jit(solution)/shard_map/ppermute | solution.py:560
  88.3 1.4 collective-permute-start.31
  89.7 4.6 %collective-permute-done.20.refs_23_ = bf16[2,32,16,128]{3,2,1,0:T(8,128)(2,1)} collective-permute-done((bf16[2,32,16,128]{3,2,1,0:T(8,128)(2,1)}, bf16[2,32,16,128]{3,2,1,0:T(8,128)(2,1)}, u32[]{:S(2)}, u32[]{:S(2)}) %collective-permute-start.20) | collective-permute-done | bytes 262176 | tf_op jit(solution)/shard_map/ppermute | solution.py:560
  94.2 1.4 collective-permute-start.32
  95.7 2.9 collective-permute-start.34
  99.2 10.3 %forward.11 = (bf16[2,32,32,128]{3,2,1,0:T(8,128)(2,1)}, bf16[2,32,32,128]{3,2,1,0:T(8,128)(2,1)}, bf16[2,32,32,128]{3,2,1,0:T(8,128)(2,1)}, bf16[2,32,32,128]{3...) custom-call(bf16[512,512]{1,0:T(8,128)(2,1)} %constant.22.table.fwd,, ...), custom_call_target="tpu_custom_call" | custom-call | flops 2147483648 | bytes 12582912 | tf_op jit(solution)/shard_map/forward/pallas_call | solution.py:123
  109.5 8.3 %sort.1.sorted_samples = bf16[4,24,128,256]{3,2,1,0:T(8,128)(2,1)} custom-call(bf16[24,1024,128]{2,1,0:T(8,128)(2,1)} %bitcast.1), custom_call_target="tpu_custom_call" | custom-call | flops 3145728 | bytes 12582912 | tf_op jit(solution)/shard_map/sort/pallas_call | solution.py:156
  117.9 3.2 constant_dynamic-slice_fusion.image
  121.0 7.0 %collective-permute-done.31.refs_4_ = bf16[2,32,32,128]{3,2,1,0:T(8,128)(2,1)} collective-permute-done((bf16[2,32,32,128]{3,2,1,0:T(8,128)(2,1)}, bf16[2,32,32,128]{3,2,1,0:T(8,128)(2,1)}, u32[]{:S(2)}, u32[]{:S(2)}) %collective-permute-start.31) | collective-permute-done | bytes 524320 | tf_op jit(solution)/shard_map/ppermute | solution.py:560
  128.0 0.1 collective-permute-start.36
  128.2 11.2 %collective-permute-done.32.refs_5_ = bf16[2,32,32,128]{3,2,1,0:T(8,128)(2,1)} collective-permute-done((bf16[2,32,32,128]{3,2,1,0:T(8,128)(2,1)}, bf16[2,32,32,128]{3,2,1,0:T(8,128)(2,1)}, u32[]{:S(2)}, u32[]{:S(2)}) %collective-permute-start.32) | collective-permute-done | bytes 524320 | tf_op jit(solution)/shard_map/ppermute | solution.py:560
  139.4 0.3 collective-permute-start.37
  139.7 1.4 collective-permute-start.38
  141.1 0.4 collective-permute-start.39
  141.5 2.5 collective-permute-start.40
  144.0 21.0 %tile.4 = (bf16[2,1024,128]{2,1,0:T(8,128)(2,1)}, bf16[2,1024,128]{2,1,0:T(8,128)(2,1)}, bf16[2,1024,128]{2,1,0:T(8,128)(2,1)}, bf16[2,1024,128]{2,1,0:T(8,128)(...) custom-call(s32[1,24]{1,0:T(1,128)} %offsets.7, ...), custom_call_target="tpu_custom_call" | custom-call | flops 10737418240 | bytes 20971520 | tf_op jit(solution)/shard_map/tile/pallas_call | solution.py:303
  165.0 0.3 collective-permute-start.41
  165.2 10.9 %collective-permute-start.43 = (bf16[2,32,32,128]{3,2,1,0:T(8,128)(2,1)}, bf16[2,32,32,128]{3,2,1,0:T(8,128)(2,1)}, u32[]{:S(2)}, u32[]{:S(2)}) collective-permute-start(bf16[2,32,32,128]{3,2,1,0:T(8,128)(2,1)} %get-tuple-element.187), channel_id=1, source_target_pairs={{0,2},{1,3},{2,0},{3,1},{4,6},{5,7},{6,4},{7,5},{8,10},{9,11},{10,... | collective-permute-start | bytes 1572872 | tf_op jit(solution)/shard_map/ppermute | solution.py:560
  176.1 11.5 %collective-permute-done.39.refs_5_ = bf16[2,32,32,128]{3,2,1,0:T(8,128)(2,1)} collective-permute-done((bf16[2,32,32,128]{3,2,1,0:T(8,128)(2,1)}, bf16[2,32,32,128]{3,2,1,0:T(8,128)(2,1)}, u32[]{:S(2)}, u32[]{:S(2)}) %collective-permute-start.39) | collective-permute-done | bytes 524320 | tf_op jit(solution)/shard_map/ppermute | solution.py:560
  187.6 0.9 collective-permute-start.44
  188.6 1.4 collective-permute-start.45
  190.0 21.0 %tile.5 = (bf16[2,1024,128]{2,1,0:T(8,128)(2,1)}, bf16[2,1024,128]{2,1,0:T(8,128)(2,1)}, bf16[2,1024,128]{2,1,0:T(8,128)(2,1)}, bf16[2,1024,128]{2,1,0:T(8,128)(...) custom-call(s32[1,24]{1,0:T(1,128)} %offsets.7, ...), custom_call_target="tpu_custom_call" | custom-call | flops 10737418240 | bytes 20971520 | tf_op jit(solution)/shard_map/tile/pallas_call | solution.py:303
  211.0 10.2 %collective-permute-start.46 = (bf16[2,32,32,128]{3,2,1,0:T(8,128)(2,1)}, bf16[2,32,32,128]{3,2,1,0:T(8,128)(2,1)}, u32[]{:S(2)}, u32[]{:S(2)}) collective-permute-start(bf16[2,32,32,128]{3,2,1,0:T(8,128)(2,1)} %get-tuple-element.190), channel_id=1, source_target_pairs={{0,5},{1,4},{2,7},{3,6},{4,1},{5,0},{6,3},{7,2},{8,13},{9,12},{10,... | collective-permute-start | bytes 1572872 | tf_op jit(solution)/shard_map/ppermute | solution.py:560
  221.3 0.1 collective-permute-start.48
  221.3 2.7 collective-permute-start.21
  224.0 20.8 %tile.6 = (bf16[2,1024,128]{2,1,0:T(8,128)(2,1)}, bf16[2,1024,128]{2,1,0:T(8,128)(2,1)}, bf16[2,1024,128]{2,1,0:T(8,128)(2,1)}, bf16[2,1024,128]{2,1,0:T(8,128)(...) custom-call(s32[1,24]{1,0:T(1,128)} %offsets.7, ...), custom_call_target="tpu_custom_call" | custom-call | flops 10737418240 | bytes 20971520 | tf_op jit(solution)/shard_map/tile/pallas_call | solution.py:303
  244.8 2.8 collective-permute-done.46.refs_5_
  247.6 0.6 collective-permute-start.24
  248.2 6.6 %collective-permute-start.25 = (bf16[2,1024,128]{2,1,0:T(8,128)(2,1)}, bf16[2,1024,128]{2,1,0:T(8,128)(2,1)}, u32[]{:S(2)}, u32[]{:S(2)}) collective-permute-start(bf16[2,1024,128]{2,1,0:T(8,128)(2,1)} %get-tuple-element.142), channel_id=1, source_target_pairs={{0,5},{1,4},{2,7},{3,6},{4,1},{5,0},{6,3},{7,2},{8,13},{9,12},{10,... | collective-permute-start | bytes 1572872 | tf_op jit(solution)/shard_map/ppermute | solution.py:560
  254.8 1.2 collective-permute-start.26
  256.0 1.7 collective-permute-start.27
  257.7 20.8 %tile.7 = (bf16[2,1024,128]{2,1,0:T(8,128)(2,1)}, bf16[2,1024,128]{2,1,0:T(8,128)(2,1)}, bf16[2,1024,128]{2,1,0:T(8,128)(2,1)}, bf16[2,1024,128]{2,1,0:T(8,128)(...) custom-call(s32[1,24]{1,0:T(1,128)} %offsets.7, ...), custom_call_target="tpu_custom_call" | custom-call | flops 10737418240 | bytes 20971520 | tf_op jit(solution)/shard_map/tile/pallas_call | solution.py:303
  278.6 17.0 %collective-permute-done.25.refs_5_ = bf16[2,1024,128]{2,1,0:T(8,128)(2,1)} collective-permute-done((bf16[2,1024,128]{2,1,0:T(8,128)(2,1)}, bf16[2,1024,128]{2,1,0:T(8,128)(2,1)}, u32[]{:S(2)}, u32[]{:S(2)}) %collective-permute-start.25) | collective-permute-done | bytes 524320 | tf_op jit(solution)/shard_map/ppermute | solution.py:560
  295.6 148.4 %finish.1.gradient = f32[2,32,64,128]{3,2,1,0:T(8,128)} custom-call(bf16[512,512]{1,0:T(8,128)(2,1)} %constant.21.inv.table, bf16[4,2,32,256,128]{4,3,2,1,0:T(8,128)(2,1)} %sens.13, bf16[2,1024,128]{2,1,0:T(8,128)(2,1)} %get-tuple-element.137.refs_0_, bf16[2,1024,128]{2,1,0:T(8,128)(2,1)} %collective-permute-done.21.refs_1_, ...), custom_call_target="tpu_custom_call" | custom-call | tf_op jit(solution)/shard_map/finish/pallas_call | solution.py:480
  444.1 1.6 copy-done
  445.6 4.6 %update.1 = (f32[2,32,64,128]{3,2,1,0:T(8,128)}, f32[2,32,64,128]{3,2,1,0:T(8,128)}, f32[2,32,64,128]{3,2,1,0:T(8,128)}) custom-call(f32[2,32,64,128]{3,2,1,0:T(8,128)S(1)} %copy-done.1, f32[2,32,64,128]{3,2,1,0:T(8,128)S(1)} %copy-done, f32[2,32,64,128]{3,2,1,0:T(8,128)S(1)} %copy-done.2, f32[2,32,64,128]{3,2,1,0:T(8,128)S(1)} %copy-done.3), custom_call_target="tpu_custom_call" | custom-call | tf_op jit(solution)/shard_map/update/pallas_call | solution.py:536
  (56 shorter events, 0.3 us)
Async XLA Ops:
  9.8 5.1 %collective-permute-start.10 = (bf16[2,32,8,128]{3,2,1,0:T(8,128)(2,1)}, bf16[2,32,8,128]{3,2,1,0:T(8,128)(2,1)}, u32[]{:S(2)}, u32[]{:S(2)}) collective-permute-start(bf16[2,32,8,128]{3,2,1,0:T(8,128)(2,1)} %get-tuple-element.124), channel_id=1, source_target_pairs={{0,4},{1,5},{2,6},{3,7},{4,0},{5,1},{6,2},{7,3},{8,12},{9,13},{10,... | collective-permute-start | bytes 393224 | tf_op jit(solution)/shard_map/ppermute | solution.py:560
  11.1 12.7 %collective-permute-start.11 = (bf16[2,32,8,128]{3,2,1,0:T(8,128)(2,1)}, bf16[2,32,8,128]{3,2,1,0:T(8,128)(2,1)}, u32[]{:S(2)}, u32[]{:S(2)}) collective-permute-start(bf16[2,32,8,128]{3,2,1,0:T(8,128)(2,1)} %get-tuple-element.125), channel_id=1, source_target_pairs={{0,5},{1,4},{2,7},{3,6},{4,1},{5,0},{6,3},{7,2},{8,13},{9,12},{10,... | collective-permute-start | bytes 393224 | tf_op jit(solution)/shard_map/ppermute | solution.py:560
  12.2 12.7 %collective-permute-start.12 = (bf16[2,32,8,128]{3,2,1,0:T(8,128)(2,1)}, bf16[2,32,8,128]{3,2,1,0:T(8,128)(2,1)}, u32[]{:S(2)}, u32[]{:S(2)}) collective-permute-start(bf16[2,32,8,128]{3,2,1,0:T(8,128)(2,1)} %get-tuple-element.126), channel_id=1, source_target_pairs={{0,6},{1,7},{2,4},{3,5},{4,2},{5,3},{6,0},{7,1},{8,14},{9,15},{10,... | collective-permute-start | bytes 393224 | tf_op jit(solution)/shard_map/ppermute | solution.py:560
  14.3 11.1 %collective-permute-start.13 = (bf16[2,32,8,128]{3,2,1,0:T(8,128)(2,1)}, bf16[2,32,8,128]{3,2,1,0:T(8,128)(2,1)}, u32[]{:S(2)}, u32[]{:S(2)}) collective-permute-start(bf16[2,32,8,128]{3,2,1,0:T(8,128)(2,1)} %get-tuple-element.127), channel_id=1, source_target_pairs={{0,7},{1,6},{2,5},{3,4},{4,3},{5,2},{6,1},{7,0},{8,15},{9,14},{10,... | collective-permute-start | bytes 393224 | tf_op jit(solution)/shard_map/ppermute | solution.py:560
  14.6 11.1 %collective-permute-start.7 = (bf16[2,32,8,128]{3,2,1,0:T(8,128)(2,1)}, bf16[2,32,8,128]{3,2,1,0:T(8,128)(2,1)}, u32[]{:S(2)}, u32[]{:S(2)}) collective-permute-start(bf16[2,32,8,128]{3,2,1,0:T(8,128)(2,1)} %get-tuple-element.121), channel_id=1, source_target_pairs={{0,1},{1,0},{2,3},{3,2},{4,5},{5,4},{6,7},{7,6},{8,9},{9,8},{10,11... | collective-permute-start | bytes 393224 | tf_op jit(solution)/shard_map/ppermute | solution.py:560
  14.9 12.2 %collective-permute-start.8 = (bf16[2,32,8,128]{3,2,1,0:T(8,128)(2,1)}, bf16[2,32,8,128]{3,2,1,0:T(8,128)(2,1)}, u32[]{:S(2)}, u32[]{:S(2)}) collective-permute-start(bf16[2,32,8,128]{3,2,1,0:T(8,128)(2,1)} %get-tuple-element.122), channel_id=1, source_target_pairs={{0,2},{1,3},{2,0},{3,1},{4,6},{5,7},{6,4},{7,5},{8,10},{9,11},{10,... | collective-permute-start | bytes 393224 | tf_op jit(solution)/shard_map/ppermute | solution.py:560
  23.8 6.4 %collective-permute-start.9 = (bf16[2,32,8,128]{3,2,1,0:T(8,128)(2,1)}, bf16[2,32,8,128]{3,2,1,0:T(8,128)(2,1)}, u32[]{:S(2)}, u32[]{:S(2)}) collective-permute-start(bf16[2,32,8,128]{3,2,1,0:T(8,128)(2,1)} %get-tuple-element.123), channel_id=1, source_target_pairs={{0,3},{1,2},{2,1},{3,0},{4,7},{5,6},{6,5},{7,4},{8,11},{9,10},{10,... | collective-permute-start | bytes 393224 | tf_op jit(solution)/shard_map/ppermute | solution.py:560
  24.9 7.6 %collective-permute-start = (bf16[2,32,8,128]{3,2,1,0:T(8,128)(2,1)}, bf16[2,32,8,128]{3,2,1,0:T(8,128)(2,1)}, u32[]{:S(2)}, u32[]{:S(2)}) collective-permute-start(bf16[2,32,8,128]{3,2,1,0:T(8,128)(2,1)} %get-tuple-element.113), channel_id=1, source_target_pairs={{0,1},{1,0},{2,3},{3,2},{4,5},{5,4},{6,7},{7,6},{8,9},{9,8},{10,11... | collective-permute-start | bytes 393224 | tf_op jit(solution)/shard_map/ppermute | solution.py:560
  25.4 8.7 %collective-permute-start.1 = (bf16[2,32,8,128]{3,2,1,0:T(8,128)(2,1)}, bf16[2,32,8,128]{3,2,1,0:T(8,128)(2,1)}, u32[]{:S(2)}, u32[]{:S(2)}) collective-permute-start(bf16[2,32,8,128]{3,2,1,0:T(8,128)(2,1)} %get-tuple-element.114), channel_id=1, source_target_pairs={{0,2},{1,3},{2,0},{3,1},{4,6},{5,7},{6,4},{7,5},{8,10},{9,11},{10,... | collective-permute-start | bytes 393224 | tf_op jit(solution)/shard_map/ppermute | solution.py:560
  25.7 17.8 %collective-permute-start.2 = (bf16[2,32,8,128]{3,2,1,0:T(8,128)(2,1)}, bf16[2,32,8,128]{3,2,1,0:T(8,128)(2,1)}, u32[]{:S(2)}, u32[]{:S(2)}) collective-permute-start(bf16[2,32,8,128]{3,2,1,0:T(8,128)(2,1)} %get-tuple-element.115), channel_id=1, source_target_pairs={{0,3},{1,2},{2,1},{3,0},{4,7},{5,6},{6,5},{7,4},{8,11},{9,10},{10,... | collective-permute-start | bytes 393224 | tf_op jit(solution)/shard_map/ppermute | solution.py:560
  27.1 16.4 %collective-permute-start.3 = (bf16[2,32,8,128]{3,2,1,0:T(8,128)(2,1)}, bf16[2,32,8,128]{3,2,1,0:T(8,128)(2,1)}, u32[]{:S(2)}, u32[]{:S(2)}) collective-permute-start(bf16[2,32,8,128]{3,2,1,0:T(8,128)(2,1)} %get-tuple-element.116), channel_id=1, source_target_pairs={{0,4},{1,5},{2,6},{3,7},{4,0},{5,1},{6,2},{7,3},{8,12},{9,13},{10,... | collective-permute-start | bytes 393224 | tf_op jit(solution)/shard_map/ppermute | solution.py:560
  30.2 13.5 %collective-permute-start.4 = (bf16[2,32,8,128]{3,2,1,0:T(8,128)(2,1)}, bf16[2,32,8,128]{3,2,1,0:T(8,128)(2,1)}, u32[]{:S(2)}, u32[]{:S(2)}) collective-permute-start(bf16[2,32,8,128]{3,2,1,0:T(8,128)(2,1)} %get-tuple-element.117), channel_id=1, source_target_pairs={{0,5},{1,4},{2,7},{3,6},{4,1},{5,0},{6,3},{7,2},{8,13},{9,12},{10,... | collective-permute-start | bytes 393224 | tf_op jit(solution)/shard_map/ppermute | solution.py:560
  32.5 13.2 %collective-permute-start.5 = (bf16[2,32,8,128]{3,2,1,0:T(8,128)(2,1)}, bf16[2,32,8,128]{3,2,1,0:T(8,128)(2,1)}, u32[]{:S(2)}, u32[]{:S(2)}) collective-permute-start(bf16[2,32,8,128]{3,2,1,0:T(8,128)(2,1)} %get-tuple-element.118), channel_id=1, source_target_pairs={{0,6},{1,7},{2,4},{3,5},{4,2},{5,3},{6,0},{7,1},{8,14},{9,15},{10,... | collective-permute-start | bytes 393224 | tf_op jit(solution)/shard_map/ppermute | solution.py:560
  34.1 11.6 %collective-permute-start.6 = (bf16[2,32,8,128]{3,2,1,0:T(8,128)(2,1)}, bf16[2,32,8,128]{3,2,1,0:T(8,128)(2,1)}, u32[]{:S(2)}, u32[]{:S(2)}) collective-permute-start(bf16[2,32,8,128]{3,2,1,0:T(8,128)(2,1)} %get-tuple-element.119), channel_id=1, source_target_pairs={{0,7},{1,6},{2,5},{3,4},{4,3},{5,2},{6,1},{7,0},{8,15},{9,14},{10,... | collective-permute-start | bytes 393224 | tf_op jit(solution)/shard_map/ppermute | solution.py:560
  43.4 14.0 %collective-permute-start.14 = (bf16[2,32,16,128]{3,2,1,0:T(8,128)(2,1)}, bf16[2,32,16,128]{3,2,1,0:T(8,128)(2,1)}, u32[]{:S(2)}, u32[]{:S(2)}) collective-permute-start(bf16[2,32,16,128]{3,2,1,0:T(8,128)(2,1)} %get-tuple-element.129), channel_id=1, source_target_pairs={{0,1},{1,0},{2,3},{3,2},{4,5},{5,4},{6,7},{7,6},{8,9},{9,8},{10,11... | collective-permute-start | bytes 786440 | tf_op jit(solution)/shard_map/ppermute | solution.py:560
  43.5 14.4 %collective-permute-start.15 = (bf16[2,32,16,128]{3,2,1,0:T(8,128)(2,1)}, bf16[2,32,16,128]{3,2,1,0:T(8,128)(2,1)}, u32[]{:S(2)}, u32[]{:S(2)}) collective-permute-start(bf16[2,32,16,128]{3,2,1,0:T(8,128)(2,1)} %get-tuple-element.130), channel_id=1, source_target_pairs={{0,2},{1,3},{2,0},{3,1},{4,6},{5,7},{6,4},{7,5},{8,10},{9,11},{10,... | collective-permute-start | bytes 786440 | tf_op jit(solution)/shard_map/ppermute | solution.py:560
  43.7 14.3 %collective-permute-start.16 = (bf16[2,32,16,128]{3,2,1,0:T(8,128)(2,1)}, bf16[2,32,16,128]{3,2,1,0:T(8,128)(2,1)}, u32[]{:S(2)}, u32[]{:S(2)}) collective-permute-start(bf16[2,32,16,128]{3,2,1,0:T(8,128)(2,1)} %get-tuple-element.131), channel_id=1, source_target_pairs={{0,3},{1,2},{2,1},{3,0},{4,7},{5,6},{6,5},{7,4},{8,11},{9,10},{10,... | collective-permute-start | bytes 786440 | tf_op jit(solution)/shard_map/ppermute | solution.py:560
  45.7 14.0 %collective-permute-start.17 = (bf16[2,32,16,128]{3,2,1,0:T(8,128)(2,1)}, bf16[2,32,16,128]{3,2,1,0:T(8,128)(2,1)}, u32[]{:S(2)}, u32[]{:S(2)}) collective-permute-start(bf16[2,32,16,128]{3,2,1,0:T(8,128)(2,1)} %get-tuple-element.132), channel_id=1, source_target_pairs={{0,4},{1,5},{2,6},{3,7},{4,0},{5,1},{6,2},{7,3},{8,12},{9,13},{10,... | collective-permute-start | bytes 786440 | tf_op jit(solution)/shard_map/ppermute | solution.py:560
  45.7 14.0 %collective-permute-start.18 = (bf16[2,32,16,128]{3,2,1,0:T(8,128)(2,1)}, bf16[2,32,16,128]{3,2,1,0:T(8,128)(2,1)}, u32[]{:S(2)}, u32[]{:S(2)}) collective-permute-start(bf16[2,32,16,128]{3,2,1,0:T(8,128)(2,1)} %get-tuple-element.133), channel_id=1, source_target_pairs={{0,5},{1,4},{2,7},{3,6},{4,1},{5,0},{6,3},{7,2},{8,13},{9,12},{10,... | collective-permute-start | bytes 786440 | tf_op jit(solution)/shard_map/ppermute | solution.py:560
  57.4 38.2 %collective-permute-start.28 = (bf16[2,32,32,128]{3,2,1,0:T(8,128)(2,1)}, bf16[2,32,32,128]{3,2,1,0:T(8,128)(2,1)}, u32[]{:S(2)}, u32[]{:S(2)}) collective-permute-start(bf16[2,32,32,128]{3,2,1,0:T(8,128)(2,1)} %get-tuple-element.149), channel_id=1, source_target_pairs={{0,1},{1,0},{2,3},{3,2},{4,5},{5,4},{6,7},{7,6},{8,9},{9,8},{10,11... | collective-permute-start | bytes 1572872 | tf_op jit(solution)/shard_map/ppermute | solution.py:560
  57.9 37.8 %collective-permute-start.29 = (bf16[2,32,32,128]{3,2,1,0:T(8,128)(2,1)}, bf16[2,32,32,128]{3,2,1,0:T(8,128)(2,1)}, u32[]{:S(2)}, u32[]{:S(2)}) collective-permute-start(bf16[2,32,32,128]{3,2,1,0:T(8,128)(2,1)} %get-tuple-element.150), channel_id=1, source_target_pairs={{0,2},{1,3},{2,0},{3,1},{4,6},{5,7},{6,4},{7,5},{8,10},{9,11},{10,... | collective-permute-start | bytes 1572872 | tf_op jit(solution)/shard_map/ppermute | solution.py:560
  58.0 40.5 %collective-permute-start.30 = (bf16[2,32,32,128]{3,2,1,0:T(8,128)(2,1)}, bf16[2,32,32,128]{3,2,1,0:T(8,128)(2,1)}, u32[]{:S(2)}, u32[]{:S(2)}) collective-permute-start(bf16[2,32,32,128]{3,2,1,0:T(8,128)(2,1)} %get-tuple-element.151), channel_id=1, source_target_pairs={{0,3},{1,2},{2,1},{3,0},{4,7},{5,6},{6,5},{7,4},{8,11},{9,10},{10,... | collective-permute-start | bytes 1572872 | tf_op jit(solution)/shard_map/ppermute | solution.py:560
  59.6 28.6 %collective-permute-start.19 = (bf16[2,32,16,128]{3,2,1,0:T(8,128)(2,1)}, bf16[2,32,16,128]{3,2,1,0:T(8,128)(2,1)}, u32[]{:S(2)}, u32[]{:S(2)}) collective-permute-start(bf16[2,32,16,128]{3,2,1,0:T(8,128)(2,1)} %get-tuple-element.134), channel_id=1, source_target_pairs={{0,6},{1,7},{2,4},{3,5},{4,2},{5,3},{6,0},{7,1},{8,14},{9,15},{10,... | collective-permute-start | bytes 786440 | tf_op jit(solution)/shard_map/ppermute | solution.py:560
  59.7 34.5 %collective-permute-start.20 = (bf16[2,32,16,128]{3,2,1,0:T(8,128)(2,1)}, bf16[2,32,16,128]{3,2,1,0:T(8,128)(2,1)}, u32[]{:S(2)}, u32[]{:S(2)}) collective-permute-start(bf16[2,32,16,128]{3,2,1,0:T(8,128)(2,1)} %get-tuple-element.135), channel_id=1, source_target_pairs={{0,7},{1,6},{2,5},{3,4},{4,3},{5,2},{6,1},{7,0},{8,15},{9,14},{10,... | collective-permute-start | bytes 786440 | tf_op jit(solution)/shard_map/ppermute | solution.py:560
  88.3 39.8 %collective-permute-start.31 = (bf16[2,32,32,128]{3,2,1,0:T(8,128)(2,1)}, bf16[2,32,32,128]{3,2,1,0:T(8,128)(2,1)}, u32[]{:S(2)}, u32[]{:S(2)}) collective-permute-start(bf16[2,32,32,128]{3,2,1,0:T(8,128)(2,1)} %get-tuple-element.152), channel_id=1, source_target_pairs={{0,4},{1,5},{2,6},{3,7},{4,0},{5,1},{6,2},{7,3},{8,12},{9,13},{10,... | collective-permute-start | bytes 1572872 | tf_op jit(solution)/shard_map/ppermute | solution.py:560
  94.2 45.1 %collective-permute-start.32 = (bf16[2,32,32,128]{3,2,1,0:T(8,128)(2,1)}, bf16[2,32,32,128]{3,2,1,0:T(8,128)(2,1)}, u32[]{:S(2)}, u32[]{:S(2)}) collective-permute-start(bf16[2,32,32,128]{3,2,1,0:T(8,128)(2,1)} %get-tuple-element.153), channel_id=1, source_target_pairs={{0,5},{1,4},{2,7},{3,6},{4,1},{5,0},{6,3},{7,2},{8,13},{9,12},{10,... | collective-permute-start | bytes 1572872 | tf_op jit(solution)/shard_map/ppermute | solution.py:560
  95.7 44.0 %collective-permute-start.33 = (bf16[2,32,32,128]{3,2,1,0:T(8,128)(2,1)}, bf16[2,32,32,128]{3,2,1,0:T(8,128)(2,1)}, u32[]{:S(2)}, u32[]{:S(2)}) collective-permute-start(bf16[2,32,32,128]{3,2,1,0:T(8,128)(2,1)} %get-tuple-element.154), channel_id=1, source_target_pairs={{0,6},{1,7},{2,4},{3,5},{4,2},{5,3},{6,0},{7,1},{8,14},{9,15},{10,... | collective-permute-start | bytes 1572872 | tf_op jit(solution)/shard_map/ppermute | solution.py:560
  95.7 45.4 %collective-permute-start.34 = (bf16[2,32,32,128]{3,2,1,0:T(8,128)(2,1)}, bf16[2,32,32,128]{3,2,1,0:T(8,128)(2,1)}, u32[]{:S(2)}, u32[]{:S(2)}) collective-permute-start(bf16[2,32,32,128]{3,2,1,0:T(8,128)(2,1)} %get-tuple-element.155), channel_id=1, source_target_pairs={{0,7},{1,6},{2,5},{3,4},{4,3},{5,2},{6,1},{7,0},{8,15},{9,14},{10,... | collective-permute-start | bytes 1572872 | tf_op jit(solution)/shard_map/ppermute | solution.py:560
  98.6 43.0 %collective-permute-start.35 = (bf16[2,32,32,128]{3,2,1,0:T(8,128)(2,1)}, bf16[2,32,32,128]{3,2,1,0:T(8,128)(2,1)}, u32[]{:S(2)}, u32[]{:S(2)}) collective-permute-start(bf16[2,32,32,128]{3,2,1,0:T(8,128)(2,1)} %get-tuple-element.169), channel_id=1, source_target_pairs={{0,1},{1,0},{2,3},{3,2},{4,5},{5,4},{6,7},{7,6},{8,9},{9,8},{10,11... | collective-permute-start | bytes 1572872 | tf_op jit(solution)/shard_map/ppermute | solution.py:560
  128.0 36.9 %collective-permute-start.36 = (bf16[2,32,32,128]{3,2,1,0:T(8,128)(2,1)}, bf16[2,32,32,128]{3,2,1,0:T(8,128)(2,1)}, u32[]{:S(2)}, u32[]{:S(2)}) collective-permute-start(bf16[2,32,32,128]{3,2,1,0:T(8,128)(2,1)} %get-tuple-element.170), channel_id=1, source_target_pairs={{0,2},{1,3},{2,0},{3,1},{4,6},{5,7},{6,4},{7,5},{8,10},{9,11},{10,... | collective-permute-start | bytes 1572872 | tf_op jit(solution)/shard_map/ppermute | solution.py:560
  139.4 25.9 %collective-permute-start.37 = (bf16[2,32,32,128]{3,2,1,0:T(8,128)(2,1)}, bf16[2,32,32,128]{3,2,1,0:T(8,128)(2,1)}, u32[]{:S(2)}, u32[]{:S(2)}) collective-permute-start(bf16[2,32,32,128]{3,2,1,0:T(8,128)(2,1)} %get-tuple-element.171), channel_id=1, source_target_pairs={{0,3},{1,2},{2,1},{3,0},{4,7},{5,6},{6,5},{7,4},{8,11},{9,10},{10,... | collective-permute-start | bytes 1572872 | tf_op jit(solution)/shard_map/ppermute | solution.py:560
  139.7 25.6 %collective-permute-start.38 = (bf16[2,32,32,128]{3,2,1,0:T(8,128)(2,1)}, bf16[2,32,32,128]{3,2,1,0:T(8,128)(2,1)}, u32[]{:S(2)}, u32[]{:S(2)}) collective-permute-start(bf16[2,32,32,128]{3,2,1,0:T(8,128)(2,1)} %get-tuple-element.172), channel_id=1, source_target_pairs={{0,4},{1,5},{2,6},{3,7},{4,0},{5,1},{6,2},{7,3},{8,12},{9,13},{10,... | collective-permute-start | bytes 1572872 | tf_op jit(solution)/shard_map/ppermute | solution.py:560
  141.1 46.6 %collective-permute-start.39 = (bf16[2,32,32,128]{3,2,1,0:T(8,128)(2,1)}, bf16[2,32,32,128]{3,2,1,0:T(8,128)(2,1)}, u32[]{:S(2)}, u32[]{:S(2)}) collective-permute-start(bf16[2,32,32,128]{3,2,1,0:T(8,128)(2,1)} %get-tuple-element.173), channel_id=1, source_target_pairs={{0,5},{1,4},{2,7},{3,6},{4,1},{5,0},{6,3},{7,2},{8,13},{9,12},{10,... | collective-permute-start | bytes 1572872 | tf_op jit(solution)/shard_map/ppermute | solution.py:560
  141.5 47.1 %collective-permute-start.40 = (bf16[2,32,32,128]{3,2,1,0:T(8,128)(2,1)}, bf16[2,32,32,128]{3,2,1,0:T(8,128)(2,1)}, u32[]{:S(2)}, u32[]{:S(2)}) collective-permute-start(bf16[2,32,32,128]{3,2,1,0:T(8,128)(2,1)} %get-tuple-element.174), channel_id=1, source_target_pairs={{0,6},{1,7},{2,4},{3,5},{4,2},{5,3},{6,0},{7,1},{8,14},{9,15},{10,... | collective-permute-start | bytes 1572872 | tf_op jit(solution)/shard_map/ppermute | solution.py:560
  165.0 46.0 %collective-permute-start.41 = (bf16[2,32,32,128]{3,2,1,0:T(8,128)(2,1)}, bf16[2,32,32,128]{3,2,1,0:T(8,128)(2,1)}, u32[]{:S(2)}, u32[]{:S(2)}) collective-permute-start(bf16[2,32,32,128]{3,2,1,0:T(8,128)(2,1)} %get-tuple-element.175), channel_id=1, source_target_pairs={{0,7},{1,6},{2,5},{3,4},{4,3},{5,2},{6,1},{7,0},{8,15},{9,14},{10,... | collective-permute-start | bytes 1572872 | tf_op jit(solution)/shard_map/ppermute | solution.py:560
  165.2 56.0 %collective-permute-start.42 = (bf16[2,32,32,128]{3,2,1,0:T(8,128)(2,1)}, bf16[2,32,32,128]{3,2,1,0:T(8,128)(2,1)}, u32[]{:S(2)}, u32[]{:S(2)}) collective-permute-start(bf16[2,32,32,128]{3,2,1,0:T(8,128)(2,1)} %get-tuple-element.186), channel_id=1, source_target_pairs={{0,1},{1,0},{2,3},{3,2},{4,5},{5,4},{6,7},{7,6},{8,9},{9,8},{10,11... | collective-permute-start | bytes 1572872 | tf_op jit(solution)/shard_map/ppermute | solution.py:560
  165.2 56.0 %collective-permute-start.43 = (bf16[2,32,32,128]{3,2,1,0:T(8,128)(2,1)}, bf16[2,32,32,128]{3,2,1,0:T(8,128)(2,1)}, u32[]{:S(2)}, u32[]{:S(2)}) collective-permute-start(bf16[2,32,32,128]{3,2,1,0:T(8,128)(2,1)} %get-tuple-element.187), channel_id=1, source_target_pairs={{0,2},{1,3},{2,0},{3,1},{4,6},{5,7},{6,4},{7,5},{8,10},{9,11},{10,... | collective-permute-start | bytes 1572872 | tf_op jit(solution)/shard_map/ppermute | solution.py:560
  187.6 33.7 %collective-permute-start.44 = (bf16[2,32,32,128]{3,2,1,0:T(8,128)(2,1)}, bf16[2,32,32,128]{3,2,1,0:T(8,128)(2,1)}, u32[]{:S(2)}, u32[]{:S(2)}) collective-permute-start(bf16[2,32,32,128]{3,2,1,0:T(8,128)(2,1)} %get-tuple-element.188), channel_id=1, source_target_pairs={{0,3},{1,2},{2,1},{3,0},{4,7},{5,6},{6,5},{7,4},{8,11},{9,10},{10,... | collective-permute-start | bytes 1572872 | tf_op jit(solution)/shard_map/ppermute | solution.py:560
  188.6 35.4 %collective-permute-start.45 = (bf16[2,32,32,128]{3,2,1,0:T(8,128)(2,1)}, bf16[2,32,32,128]{3,2,1,0:T(8,128)(2,1)}, u32[]{:S(2)}, u32[]{:S(2)}) collective-permute-start(bf16[2,32,32,128]{3,2,1,0:T(8,128)(2,1)} %get-tuple-element.189), channel_id=1, source_target_pairs={{0,4},{1,5},{2,6},{3,7},{4,0},{5,1},{6,2},{7,3},{8,12},{9,13},{10,... | collective-permute-start | bytes 1572872 | tf_op jit(solution)/shard_map/ppermute | solution.py:560
  211.0 36.6 %collective-permute-start.46 = (bf16[2,32,32,128]{3,2,1,0:T(8,128)(2,1)}, bf16[2,32,32,128]{3,2,1,0:T(8,128)(2,1)}, u32[]{:S(2)}, u32[]{:S(2)}) collective-permute-start(bf16[2,32,32,128]{3,2,1,0:T(8,128)(2,1)} %get-tuple-element.190), channel_id=1, source_target_pairs={{0,5},{1,4},{2,7},{3,6},{4,1},{5,0},{6,3},{7,2},{8,13},{9,12},{10,... | collective-permute-start | bytes 1572872 | tf_op jit(solution)/shard_map/ppermute | solution.py:560
  221.2 26.4 %collective-permute-start.47 = (bf16[2,32,32,128]{3,2,1,0:T(8,128)(2,1)}, bf16[2,32,32,128]{3,2,1,0:T(8,128)(2,1)}, u32[]{:S(2)}, u32[]{:S(2)}) collective-permute-start(bf16[2,32,32,128]{3,2,1,0:T(8,128)(2,1)} %get-tuple-element.191), channel_id=1, source_target_pairs={{0,6},{1,7},{2,4},{3,5},{4,2},{5,3},{6,0},{7,1},{8,14},{9,15},{10,... | collective-permute-start | bytes 1572872 | tf_op jit(solution)/shard_map/ppermute | solution.py:560
  221.3 27.0 %collective-permute-start.48 = (bf16[2,32,32,128]{3,2,1,0:T(8,128)(2,1)}, bf16[2,32,32,128]{3,2,1,0:T(8,128)(2,1)}, u32[]{:S(2)}, u32[]{:S(2)}) collective-permute-start(bf16[2,32,32,128]{3,2,1,0:T(8,128)(2,1)} %get-tuple-element.192), channel_id=1, source_target_pairs={{0,7},{1,6},{2,5},{3,4},{4,3},{5,2},{6,1},{7,0},{8,15},{9,14},{10,... | collective-permute-start | bytes 1572872 | tf_op jit(solution)/shard_map/ppermute | solution.py:560
  221.3 33.5 %collective-permute-start.21 = (bf16[2,1024,128]{2,1,0:T(8,128)(2,1)}, bf16[2,1024,128]{2,1,0:T(8,128)(2,1)}, u32[]{:S(2)}, u32[]{:S(2)}) collective-permute-start(bf16[2,1024,128]{2,1,0:T(8,128)(2,1)} %get-tuple-element.138), channel_id=1, source_target_pairs={{0,1},{1,0},{2,3},{3,2},{4,5},{5,4},{6,7},{7,6},{8,9},{9,8},{10,11... | collective-permute-start | bytes 1572872 | tf_op jit(solution)/shard_map/ppermute | solution.py:560
  224.0 32.0 %collective-permute-start.22 = (bf16[2,1024,128]{2,1,0:T(8,128)(2,1)}, bf16[2,1024,128]{2,1,0:T(8,128)(2,1)}, u32[]{:S(2)}, u32[]{:S(2)}) collective-permute-start(bf16[2,1024,128]{2,1,0:T(8,128)(2,1)} %get-tuple-element.139), channel_id=1, source_target_pairs={{0,2},{1,3},{2,0},{3,1},{4,6},{5,7},{6,4},{7,5},{8,10},{9,11},{10,... | collective-permute-start | bytes 1572872 | tf_op jit(solution)/shard_map/ppermute | solution.py:560
  247.6 31.0 %collective-permute-start.23 = (bf16[2,1024,128]{2,1,0:T(8,128)(2,1)}, bf16[2,1024,128]{2,1,0:T(8,128)(2,1)}, u32[]{:S(2)}, u32[]{:S(2)}) collective-permute-start(bf16[2,1024,128]{2,1,0:T(8,128)(2,1)} %get-tuple-element.140), channel_id=1, source_target_pairs={{0,3},{1,2},{2,1},{3,0},{4,7},{5,6},{6,5},{7,4},{8,11},{9,10},{10,... | collective-permute-start | bytes 1572872 | tf_op jit(solution)/shard_map/ppermute | solution.py:560
  247.6 31.0 %collective-permute-start.24 = (bf16[2,1024,128]{2,1,0:T(8,128)(2,1)}, bf16[2,1024,128]{2,1,0:T(8,128)(2,1)}, u32[]{:S(2)}, u32[]{:S(2)}) collective-permute-start(bf16[2,1024,128]{2,1,0:T(8,128)(2,1)} %get-tuple-element.141), channel_id=1, source_target_pairs={{0,4},{1,5},{2,6},{3,7},{4,0},{5,1},{6,2},{7,3},{8,12},{9,13},{10,... | collective-permute-start | bytes 1572872 | tf_op jit(solution)/shard_map/ppermute | solution.py:560
  248.2 47.4 %collective-permute-start.25 = (bf16[2,1024,128]{2,1,0:T(8,128)(2,1)}, bf16[2,1024,128]{2,1,0:T(8,128)(2,1)}, u32[]{:S(2)}, u32[]{:S(2)}) collective-permute-start(bf16[2,1024,128]{2,1,0:T(8,128)(2,1)} %get-tuple-element.142), channel_id=1, source_target_pairs={{0,5},{1,4},{2,7},{3,6},{4,1},{5,0},{6,3},{7,2},{8,13},{9,12},{10,... | collective-permute-start | bytes 1572872 | tf_op jit(solution)/shard_map/ppermute | solution.py:560
  254.8 40.8 %collective-permute-start.26 = (bf16[2,1024,128]{2,1,0:T(8,128)(2,1)}, bf16[2,1024,128]{2,1,0:T(8,128)(2,1)}, u32[]{:S(2)}, u32[]{:S(2)}) collective-permute-start(bf16[2,1024,128]{2,1,0:T(8,128)(2,1)} %get-tuple-element.143), channel_id=1, source_target_pairs={{0,6},{1,7},{2,4},{3,5},{4,2},{5,3},{6,0},{7,1},{8,14},{9,15},{10,... | collective-permute-start | bytes 1572872 | tf_op jit(solution)/shard_map/ppermute | solution.py:560
  256.0 39.6 %collective-permute-start.27 = (bf16[2,1024,128]{2,1,0:T(8,128)(2,1)}, bf16[2,1024,128]{2,1,0:T(8,128)(2,1)}, u32[]{:S(2)}, u32[]{:S(2)}) collective-permute-start(bf16[2,1024,128]{2,1,0:T(8,128)(2,1)} %get-tuple-element.144), channel_id=1, source_target_pairs={{0,7},{1,6},{2,5},{3,4},{4,3},{5,2},{6,1},{7,0},{8,15},{9,14},{10,... | collective-permute-start | bytes 1572872 | tf_op jit(solution)/shard_map/ppermute | solution.py:560
  295.6 148.4 %copy-start.1 = (f32[2,32,64,128]{3,2,1,0:T(8,128)S(1)}, f32[2,32,64,128]{3,2,1,0:T(8,128)}, u32[]{:S(2)}) copy-start(f32[2,32,64,128]{3,2,1,0:T(8,128)} %constant_dynamic-slice_fusion.image) | copy-start | bytes 6291460
  295.6 148.4 %copy-start.2 = (f32[2,32,64,128]{3,2,1,0:T(8,128)S(1)}, f32[2,32,64,128]{3,2,1,0:T(8,128)}, u32[]{:S(2)}) copy-start(f32[2,32,64,128]{3,2,1,0:T(8,128)} %auxiliary.1) | copy-start | bytes 6291460
  295.6 148.4 %copy-start.3 = (f32[2,32,64,128]{3,2,1,0:T(8,128)S(1)}, f32[2,32,64,128]{3,2,1,0:T(8,128)}, u32[]{:S(2)}) copy-start(f32[2,32,64,128]{3,2,1,0:T(8,128)} %dual.1) | copy-start | bytes 6291460
  444.0 1.6 copy-start

commit v5 on v4

--- a/solution.py
+++ b/solution.py
@@ -38,13 +38,12 @@
     return pltpu.CompilerParams(vmem_limit_bytes=limit, **extra)
 
 
-def partner(me, off, n):
-    other, bit = me, 1
-    while bit < n:
-        if off & bit:
-            other = other + bit * (1 - 2 * (me // bit % 2))
-        bit *= 2
-    return other
+def ahead(me, off, n):
+    return (me + off) % n
+
+
+def behind(me, off, n):
+    return (me + n - off) % n
 
 
 def turns(n):
@@ -76,7 +75,7 @@
     outs, flat = refs[:n], refs[n]
     rows, length = image.shape[1], image.shape[2]
     me = lax.axis_index("slab")
-    step = pl.program_id(0)
+    coil, step = pl.program_id(0), pl.program_id(1)
 
     def pair(i, carry):
         columns = []
@@ -101,38 +100,39 @@
 
     lax.fori_loop(0, rows // 2, pair, 0, unroll=2)
 
-    @pl.when(step == pl.num_programs(0) - 1)
+    @pl.when(step == pl.num_programs(1) - 1)
     def last():
         for off in range(n):
-            d = partner(me, off, n)
+            d = ahead(me, off, n)
             for p in range(2):
 
                 def settle(k, carry):
                     base = pl.multiple_of(((p * n + d) * kl + 2 * k) * pitch(xp), 8)
                     for h in range(2):
-                        outs[off][p, 2 * k + h] = flat[pl.ds(base + h * pitch(xp), xp), :].astype(BF16)
+                        outs[off][coil, p, 2 * k + h] = flat[pl.ds(base + h * pitch(xp), xp), :].astype(BF16)
                     return carry
 
                 lax.fori_loop(0, kl // 2, settle, 0, unroll=4)
 
 
-def forward_call(table, image, sensitivity, coil, first, xp, n, kl):
+def forward_call(table, image, sensitivity, batch, first, xp, n, kl):
     _, _, _, length, depth = sensitivity.shape
     rows = 8 if xp % 8 == 0 else xp
     steps, skip = xp // rows, first // rows
+    shape = (len(batch), 2, kl, xp, depth)
     return pl.pallas_call(
         functools.partial(forward_kernel, n, kl, xp),
-        grid=(steps,),
+        grid=(len(batch), steps),
         in_specs=[
             once(table.shape),
-            pl.BlockSpec((2, rows, length, depth), lambda i: (0, skip + i, 0, 0)),
-            pl.BlockSpec((1, 2, rows, length, depth), lambda i: (coil, 0, skip + i, 0, 0)),
+            pl.BlockSpec((2, rows, length, depth), lambda c, i: (0, skip + i, 0, 0)),
+            pl.BlockSpec((1, 2, rows, length, depth), lambda c, i: (batch[0] + c, 0, skip + i, 0, 0)),
         ],
-        out_specs=[once((2, kl, xp, depth))] * n,
-        out_shape=[jax.ShapeDtypeStruct((2, kl, xp, depth), BF16)] * n,
+        out_specs=[once(shape)] * n,
+        out_shape=[jax.ShapeDtypeStruct(shape, BF16)] * n,
         scratch_shapes=[pltpu.VMEM(((2 * length + 1) * pitch(xp), depth), F32)],
         compiler_params=params(),
-        cost_estimate=cost(8 * length * length * xp * depth, 12 * xp * length * depth),
+        cost_estimate=cost(8 * len(batch) * length * length * xp * depth, 12 * len(batch) * xp * length * depth),
         name="forward",
     )(table, image, sensitivity)
 
@@ -166,7 +166,7 @@
     )(samples.reshape(slots, lines, depth))
 
 
-def tile_kernel(n, kl, xl, win, parts, coil, offsets, counts, fwd, inv, blocks, sorted_samples, *refs):
+def tile_kernel(n, kl, xl, win, parts, coil, place, offsets, counts, fwd, inv, blocks, sorted_samples, *refs):
     count = n * len(parts)
     pieces, outs, refs = refs[:count], refs[count : count + n], refs[count + n :]
     total, kspace, weights, piece, samples, leaving, sem, piece_sem, *wide = refs
@@ -174,8 +174,8 @@
     copies = []
     for off in range(n):
         for h, (start, size) in enumerate(parts):
-            target = piece.at[partner(me, off, n), :, :, pl.ds(start, size)]
-            copies.append(pltpu.make_async_copy(pieces[h * n + off], target, piece_sem.at[h * n + off]))
+            target = piece.at[behind(me, off, n), :, :, pl.ds(start, size)]
+            copies.append(pltpu.make_async_copy(pieces[h * n + off].at[place], target, piece_sem.at[h * n + off]))
     for copy in copies:
         copy.start()
     for copy in copies:
@@ -266,7 +266,7 @@
 
     lax.fori_loop(0, kl // 2, to_rows, 0, unroll=2)
     for off in range(n):
-        d = partner(me, off, n)
+        d = ahead(me, off, n)
         for p in range(2):
 
             def leave(k, carry):
@@ -282,7 +282,7 @@
         pltpu.make_async_copy(leaving.at[off], outs[off], piece_sem.at[off]).wait()
 
 
-def tile_call(fwd, inv, pieces, parts, blocks, samples, offsets, counts, coil, n, kl, xl):
+def tile_call(fwd, inv, pieces, parts, place, blocks, samples, offsets, counts, coil, n, kl, xl):
     depth = pieces[0].shape[-1]
     _, slots, psize, cells = blocks.shape
     length = n * xl
@@ -301,7 +301,7 @@
         scratch.append(pltpu.VMEM((n, 2, kl, xl, depth), F32))
     smem = pl.BlockSpec(memory_space=pltpu.SMEM)
     return pl.pallas_call(
-        functools.partial(tile_kernel, n, kl, xl, cells // kl, parts, coil),
+        functools.partial(tile_kernel, n, kl, xl, cells // kl, parts, coil, place),
         grid=(1,),
         in_specs=[smem, smem, once(fwd.shape), once(inv.shape), HBM, HBM] + [HBM] * len(pieces),
         out_specs=[HBM] * n,
@@ -316,10 +316,10 @@
     )(offsets, counts, fwd, inv, blocks, samples, *pieces)
 
 
-def finish_kernel(n, shares, kl, xl, chunks, sent, table, sens, *refs):
+def finish_kernel(n, shares, kl, xl, chunks, sent, table_ref, sens, *refs):
     coils = sens.shape[0]
     backs, refs = [refs[k * n : (k + 1) * n] for k in range(coils)], refs[coils * n :]
-    out, landing, sens_v, grad, got, recv, send, local, grad_recv, grad_send, *wide = refs
+    out, table, landing, sens_v, grad, got, recv, send, local, grad_recv, grad_send, *wide = refs
     ready = coils - sent
     length = n * kl
     depth = landing.shape[-1]
@@ -354,16 +354,16 @@
                     dst_ref=landing.at[k, me, :, where, :],
                     send_sem=send,
                     recv_sem=recv.at[j],
-                    device_id={"slab": partner(me, off, n)},
+                    device_id={"slab": ahead(me, off, n)},
                     device_id_type=pl.DeviceIdType.MESH,
                 ).start()
         return carry
 
     lax.fori_loop(0, chunks, send_band, 0)
-    copies = []
+    copies = [pltpu.make_async_copy(table_ref, table, local.at[coils * n + coils])]
     for k in range(coils):
         for off in range(n if k < ready else 1):
-            origin = landing.at[k, partner(me, off, n)]
+            origin = landing.at[k, behind(me, off, n)]
             copies.append(pltpu.make_async_copy(backs[k][off], origin, local.at[k * n + off]))
         copies.append(pltpu.make_async_copy(sens.at[k], sens_v.at[k], local.at[coils * n + k]))
     for copy in copies:
@@ -464,13 +464,14 @@
     share = length // shares
     vmem = pl.BlockSpec(memory_space=pltpu.VMEM)
     scratch = [
+        pltpu.VMEM(table.shape, BF16),
         pltpu.VMEM((coils, n, 2, xl * kl, depth), BF16),
         pltpu.VMEM(sensitivity.shape, BF16),
         pltpu.VMEM((shares, 2, xl, share, depth), BF16),
         pltpu.VMEM((shares, 2, xl, share, depth), BF16),
         pltpu.SemaphoreType.DMA((chunks,)),
         pltpu.SemaphoreType.DMA,
-        pltpu.SemaphoreType.DMA((coils * n + coils,)),
+        pltpu.SemaphoreType.DMA((coils * n + coils + 1,)),
         pltpu.SemaphoreType.DMA((chunks,)),
         pltpu.SemaphoreType.DMA,
     ]
@@ -479,9 +480,9 @@
     limit = VMEM_LIMIT - 32 * xl * share * depth
     return pl.pallas_call(
         functools.partial(finish_kernel, n, shares, kl, xl, chunks, sent),
-        in_specs=[vmem, HBM] + [HBM] * (coils * n),
+        in_specs=[HBM] * (2 + coils * n),
         out_specs=vmem,
-        out_shape=jax.ShapeDtypeStruct((2, xl, share, depth), F32),
+        out_shape=pltpu.VMEM((2, xl, share, depth), F32),
         scratch_shapes=scratch,
         compiler_params=params(limit, collective_id=0, has_side_effects=True),
         name="finish",
@@ -557,33 +558,42 @@
     def swap(parts):
         moved = list(parts)
         for off in turns(n):
-            moved[off] = lax.ppermute(parts[off], "slab", [(i, partner(i, off, n)) for i in range(n)])
+            moved[off] = lax.ppermute(parts[off], "slab", [(i, ahead(i, off, n)) for i in range(n)])
         return moved
+
+    batches = [[c] for c in range(min(coils, 2))] + [
+        list(range(c, min(c + 2, coils))) for c in range(2, coils, 2)
+    ]
 
     def parts_of(c):
         if c == 0 and xl % 32 == 0:
             return [(0, xl // 4), (xl // 4, xl // 4), (xl // 2, xl // 2)]
         return [(0, xl)]
 
-    def tile_of(pieces, c):
-        return tile_call(x_fwd, x_inv, pieces, parts_of(c), blocks, sorted_samples, offsets, counts, c, n, kl, xl)
+    def tile_of(pieces, place, c):
+        return tile_call(
+            x_fwd, x_inv, pieces, parts_of(c), place, blocks, sorted_samples, offsets, counts, c, n, kl, xl
+        )
 
     share = length_y // shares
     pieces, tiles, table = [], [], y_fwd
-    for c in range(coils):
+    for batch in batches:
+        c = batch[0]
         moved = []
         for first, size in parts_of(c):
-            half = list(forward_call(table, image, sensitivity, c, first, size, n, kl))
+            half = list(forward_call(table, image, sensitivity, batch, first, size, n, kl))
             table, half[0] = lax.optimization_barrier((table, half[0]))
             moved += swap(half)
-        pieces.append(moved)
+        pieces += [(moved, place) for place in range(len(batch))]
     table, samples, source = lax.optimization_barrier((table, samples, image))
     sorted_samples = sort_call(samples)
     current = lax.dynamic_slice_in_dim(source, lax.axis_index("coil") * share, share, 2)
     for c in range(coils):
+        arrived, place = pieces[c]
         if c:
-            pieces[c][0], tiles[-1][0] = lax.optimization_barrier((pieces[c][0], tiles[-1][0]))
-        tiles.append(list(tile_of(pieces[c], c)))
+            arrived = list(arrived)
+            arrived[0], tiles[-1][0] = lax.optimization_barrier((arrived[0], tiles[-1][0]))
+        tiles.append(list(tile_of(arrived, place, c)))
     early = max(coils - 3, 0)
     backs = list(tiles)
     for c in range(early):

time: 453 us -> 465 us (1.026)
  starting transfers between devices: 73.3 us -> 93.3 us
  waiting for transfers between devices: 79.4 us -> 62.6 us
  Pallas kernels: 291 us -> 302 us
    ppermute x49 -> x42, starting transfers between devices: 73.3 us -> 93.3 us  [swap(): lax.ppermute(parts[off], 'slab', [(i, ahead(i, off, n)) for i in range(n)])]
    ppermute x49 -> x42, waiting for transfers between devices: 79.4 us -> 62.6 us  [swap(): lax.ppermute(parts[off], 'slab', [(i, ahead(i, off, n)) for i in range(n)])]
    pallas_call x1, Pallas kernels: 148 us -> 162 us  [finish_call(): pl.pallas_call(functools.partial(finish_kernel, n, shares, kl, xl, chunks...]
    pallas_call x6 -> x5, Pallas kernels: 46.4 us -> 44.3 us  [forward_call(): pl.pallas_call(functools.partial(forward_kernel, n, kl, xp), grid=(len(ba...]
  transfers between devices with their start and end apart: 49 -> 42, of which waited for: 9 -> 5; matrix products, arithmetic and copies ran while one was open for 1% -> 1% of each run, Pallas kernels for 29% -> 27%
where the time goes in v5:
time: 465 us; the launch traced here: 463 us
  Pallas kernels  302 us (65%)
  starting transfers between devices  93.3 us (20%)
  waiting for transfers between devices  62.6 us (13%)
    pallas_call x1, Pallas kernels, finish_call(): pl.pallas_call(functools.partial(finish_kernel, n, shares, kl, xl, chunks...  162 us
    ppermute x42, starting transfers between devices, swap(): lax.ppermute(parts[off], 'slab', [(i, ahead(i, off, n)) for i in range(n)])  93.3 us
    pallas_call x4, Pallas kernels, tile_call(): pl.pallas_call(functools.partial(tile_kernel, n, kl, xl, cells // kl, par...  83.4 us
    ppermute x42, waiting for transfers between devices, swap(): lax.ppermute(parts[off], 'slab', [(i, ahead(i, off, n)) for i in range(n)])  62.6 us
    pallas_call x5, Pallas kernels, forward_call(): pl.pallas_call(functools.partial(forward_kernel, n, kl, xp), grid=(len(ba...  44.3 us
  transfers between devices with their start and end apart: 42, of which 5 were waited for; matrix products, arithmetic and copies ran while one was open for 1% of the time, Pallas kernels for 27%

profile of v5, /device:TPU:9, one launch (start us, length us, event | category | flops | bytes accessed | tf_op | source)
XLA Modules:
  0.0 463.0 jit_solution(11690500246953159370)
XLA Ops:
  0.6 4.6 forward.5
  5.2 4.6 forward.6
  9.8 1.2 collective-permute-start.10
  11.1 2.0 collective-permute-start.11
  13.1 0.3 collective-permute-start.12
  13.3 0.8 collective-permute-start.13
  14.1 0.9 collective-permute-start.7
  15.1 2.1 collective-permute-start.8
  17.2 6.7 %collective-permute-start.9 = (bf16[1,2,32,8,128]{4,3,2,1,0:T(8,128)(2,1)}, bf16[1,2,32,8,128]{4,3,2,1,0:T(8,128)(2,1)}, u32[]{:S(2)}, u32[]{:S(2)}) collective-permute-start(bf16[1,2,32,8,128]{4,3,2,1,0:T(8,128)(2,1)} %get-tuple-element.113), channel_id=1, source_target_pairs={{0,3},{1,4},{2,5},{3,6},{4,7},{5,0},{6,1},{7,2},{8,11},{9,12},{10,... | collective-permute-start | bytes 393224 | tf_op jit(solution)/shard_map/ppermute | solution.py:561
  23.9 0.0 collective-permute-done.12.refs_14_
  23.9 2.4 collective-permute-start.1
  26.3 6.2 %forward.7 = (bf16[1,2,32,16,128]{4,3,2,1,0:T(8,128)(2,1)}, bf16[1,2,32,16,128]{4,3,2,1,0:T(8,128)(2,1)}, bf16[1,2,32,16,128]{4,3,2,1,0:T(8,128)(2,1)}, bf16[1,2...) custom-call(bf16[512,512]{1,0:T(8,128)(2,1)} %constant.22.table.fwd,, ...), custom_call_target="tpu_custom_call" | custom-call | flops 1073741824 | bytes 6291456 | tf_op jit(solution)/shard_map/forward/pallas_call | solution.py:123
  32.5 1.7 collective-permute-start.14
  34.2 0.0 collective-permute-done.9.refs_11_
  34.3 1.2 collective-permute-start.3
  35.5 0.3 collective-permute-start.4
  35.8 1.8 collective-permute-start.5
  37.6 0.0 collective-permute-done.2.refs_3_
  37.6 0.0 collective-permute-start.6
  37.6 4.7 %collective-permute-done.3.refs_4_ = bf16[1,2,32,8,128]{4,3,2,1,0:T(8,128)(2,1)} collective-permute-done((bf16[1,2,32,8,128]{4,3,2,1,0:T(8,128)(2,1)}, bf16[1,2,32,8,128]{4,3,2,1,0:T(8,128)(2,1)}, u32[]{:S(2)}, u32[]{:S(2)}) %collective-permute-start.3) | collective-permute-done | bytes 131104 | tf_op jit(solution)/shard_map/ppermute | solution.py:561
  42.3 1.2 collective-permute-done.4.refs_5_
  43.5 3.7 collective-permute-start.16
  47.3 0.0 collective-permute-done.5.refs_6_
  47.3 0.0 collective-permute-start.17
  47.3 0.0 collective-permute-done.6.refs_7_
  47.3 0.7 collective-permute-start.18
  48.0 2.4 collective-permute-start.19
  50.4 10.3 %forward.8 = (bf16[1,2,32,32,128]{4,3,2,1,0:T(8,128)(2,1)}, bf16[1,2,32,32,128]{4,3,2,1,0:T(8,128)(2,1)}, bf16[1,2,32,32,128]{4,3,2,1,0:T(8,128)(2,1)}, bf16[1,2...) custom-call(bf16[512,512]{1,0:T(8,128)(2,1)} %constant.22.table.fwd,, ...), custom_call_target="tpu_custom_call" | custom-call | flops 2147483648 | bytes 12582912 | tf_op jit(solution)/shard_map/forward/pallas_call | solution.py:123
  60.7 0.0 collective-permute-done.15.refs_18_
  60.7 0.4 collective-permute-start.28
  61.2 0.1 collective-permute-start.20
  61.3 5.0 %collective-permute-done.17.refs_20_ = bf16[1,2,32,16,128]{4,3,2,1,0:T(8,128)(2,1)} collective-permute-done((bf16[1,2,32,16,128]{4,3,2,1,0:T(8,128)(2,1)}, bf16[1,2,32,16,128]{4,3,2,1,0:T(8,128)(2,1)}, u32[]{:S(2)}, u32[]{:S(2)}) %collective-permute-start.17) | collective-permute-done | bytes 262176 | tf_op jit(solution)/shard_map/ppermute | solution.py:561
  66.3 5.0 %collective-permute-start.29 = (bf16[1,2,32,32,128]{4,3,2,1,0:T(8,128)(2,1)}, bf16[1,2,32,32,128]{4,3,2,1,0:T(8,128)(2,1)}, u32[]{:S(2)}, u32[]{:S(2)}) collective-permute-start(bf16[1,2,32,32,128]{4,3,2,1,0:T(8,128)(2,1)} %get-tuple-element.140), channel_id=1, source_target_pairs={{0,2},{1,3},{2,4},{3,5},{4,6},{5,7},{6,0},{7,1},{8,10},{9,11},{10,... | collective-permute-start | bytes 1572872 | tf_op jit(solution)/shard_map/ppermute | solution.py:561
  71.4 0.0 collective-permute-done.18.refs_21_
  71.4 0.0 collective-permute-start.30
  71.4 0.1 collective-permute-start.31
  71.4 18.5 %forward.9 = (bf16[2,2,32,32,128]{4,3,2,1,0:T(8,128)(2,1)}, bf16[2,2,32,32,128]{4,3,2,1,0:T(8,128)(2,1)}, bf16[2,2,32,32,128]{4,3,2,1,0:T(8,128)(2,1)}, bf16[2,2...) custom-call(bf16[512,512]{1,0:T(8,128)(2,1)} %constant.22.table.fwd,, ...), custom_call_target="tpu_custom_call" | custom-call | flops 4294967296 | bytes 25165824 | tf_op jit(solution)/shard_map/forward/pallas_call | solution.py:123
  90.0 3.1 collective-permute-start.35
  93.1 0.8 collective-permute-start.36
  93.9 0.2 collective-permute-start.32
  94.1 38.7 %collective-permute-done.30.refs_3_ = bf16[1,2,32,32,128]{4,3,2,1,0:T(8,128)(2,1)} collective-permute-done((bf16[1,2,32,32,128]{4,3,2,1,0:T(8,128)(2,1)}, bf16[1,2,32,32,128]{4,3,2,1,0:T(8,128)(2,1)}, u32[]{:S(2)}, u32[]{:S(2)}) %collective-permute-start.30) | collective-permute-done | bytes 524320 | tf_op jit(solution)/shard_map/ppermute | solution.py:561
  132.8 12.9 %collective-permute-done.31.refs_4_ = bf16[1,2,32,32,128]{4,3,2,1,0:T(8,128)(2,1)} collective-permute-done((bf16[1,2,32,32,128]{4,3,2,1,0:T(8,128)(2,1)}, bf16[1,2,32,32,128]{4,3,2,1,0:T(8,128)(2,1)}, u32[]{:S(2)}, u32[]{:S(2)}) %collective-permute-start.31) | collective-permute-done | bytes 524320 | tf_op jit(solution)/shard_map/ppermute | solution.py:561
  146.3 8.3 %sort.1.sorted_samples = bf16[4,24,128,256]{3,2,1,0:T(8,128)(2,1)} custom-call(bf16[24,1024,128]{2,1,0:T(8,128)(2,1)} %bitcast.1), custom_call_target="tpu_custom_call" | custom-call | flops 3145728 | bytes 12582912 | tf_op jit(solution)/shard_map/sort/pallas_call | solution.py:156
  154.6 3.2 constant_dynamic-slice_fusion.image
  157.8 0.6 collective-permute-start.38
  158.4 2.9 collective-permute-start.39
  161.3 0.1 collective-permute-start.40
  161.3 1.5 collective-permute-start.41
  162.9 21.0 %tile.4 = (bf16[2,1024,128]{2,1,0:T(8,128)(2,1)}, bf16[2,1024,128]{2,1,0:T(8,128)(2,1)}, bf16[2,1024,128]{2,1,0:T(8,128)(2,1)}, bf16[2,1024,128]{2,1,0:T(8,128)(...) custom-call(s32[1,24]{1,0:T(1,128)} %offsets.7, ...), custom_call_target="tpu_custom_call" | custom-call | flops 10737418240 | bytes 20971520 | tf_op jit(solution)/shard_map/tile/pallas_call | solution.py:303
  183.8 20.9 %tile.5 = (bf16[2,1024,128]{2,1,0:T(8,128)(2,1)}, bf16[2,1024,128]{2,1,0:T(8,128)(2,1)}, bf16[2,1024,128]{2,1,0:T(8,128)(2,1)}, bf16[2,1024,128]{2,1,0:T(8,128)(...) custom-call(s32[1,24]{1,0:T(1,128)} %offsets.7, ...), custom_call_target="tpu_custom_call" | custom-call | flops 10737418240 | bytes 20971520 | tf_op jit(solution)/shard_map/tile/pallas_call | solution.py:303
  204.8 24.6 %collective-permute-start.21 = (bf16[2,1024,128]{2,1,0:T(8,128)(2,1)}, bf16[2,1024,128]{2,1,0:T(8,128)(2,1)}, u32[]{:S(2)}, u32[]{:S(2)}) collective-permute-start(bf16[2,1024,128]{2,1,0:T(8,128)(2,1)} %get-tuple-element.128), channel_id=1, source_target_pairs={{0,1},{1,2},{2,3},{3,4},{4,5},{5,6},{6,7},{7,0},{8,9},{9,10},{10,1... | collective-permute-start | bytes 1572872 | tf_op jit(solution)/shard_map/ppermute | solution.py:561
  229.4 21.9 %collective-permute-start.22 = (bf16[2,1024,128]{2,1,0:T(8,128)(2,1)}, bf16[2,1024,128]{2,1,0:T(8,128)(2,1)}, u32[]{:S(2)}, u32[]{:S(2)}) collective-permute-start(bf16[2,1024,128]{2,1,0:T(8,128)(2,1)} %get-tuple-element.129), channel_id=1, source_target_pairs={{0,2},{1,3},{2,4},{3,5},{4,6},{5,7},{6,0},{7,1},{8,10},{9,11},{10,... | collective-permute-start | bytes 1572872 | tf_op jit(solution)/shard_map/ppermute | solution.py:561
  251.3 0.0 collective-permute-start.23
  251.3 0.3 collective-permute-start.24
  251.6 2.9 collective-permute-start.25
  254.4 20.8 %tile.6 = (bf16[2,1024,128]{2,1,0:T(8,128)(2,1)}, bf16[2,1024,128]{2,1,0:T(8,128)(2,1)}, bf16[2,1024,128]{2,1,0:T(8,128)(2,1)}, bf16[2,1024,128]{2,1,0:T(8,128)(...) custom-call(s32[1,24]{1,0:T(1,128)} %offsets.7, ...), custom_call_target="tpu_custom_call" | custom-call | flops 10737418240 | bytes 20971520 | tf_op jit(solution)/shard_map/tile/pallas_call | solution.py:303
  275.2 0.1 collective-permute-start.26
  275.3 0.4 collective-permute-start.27
  275.7 20.8 %tile.7 = (bf16[2,1024,128]{2,1,0:T(8,128)(2,1)}, bf16[2,1024,128]{2,1,0:T(8,128)(2,1)}, bf16[2,1024,128]{2,1,0:T(8,128)(2,1)}, bf16[2,1024,128]{2,1,0:T(8,128)(...) custom-call(s32[1,24]{1,0:T(1,128)} %offsets.7, ...), custom_call_target="tpu_custom_call" | custom-call | flops 10737418240 | bytes 20971520 | tf_op jit(solution)/shard_map/tile/pallas_call | solution.py:303
  296.5 0.0 copy-start
  296.5 0.0 copy-start.1
  296.6 0.0 copy-start.2
  296.6 161.8 %finish.1.gradient = f32[2,32,64,128]{3,2,1,0:T(8,128)S(1)} custom-call(bf16[512,512]{1,0:T(8,128)(2,1)} %constant.21.inv.table_ref, bf16[4,2,32,256,128]{4,3,2,1,0:T(8,128)(2,1)} %sens.11, bf16[2,1024,128]{2,1,0:T(8,128)(2,1)} %get-tuple-element.127.refs_0_, bf16[2,1024,128]{2,1,0:T(8,128)(2,1)} %collective-permute-done.21.refs_1_, ...), custom_call_target="tpu_custom_call" | custom-call | tf_op jit(solution)/shard_map/finish/pallas_call | solution.py:481
  458.4 4.6 update.1
  (39 shorter events, 0.1 us)
Async XLA Ops:
  9.8 5.2 %collective-permute-start.10 = (bf16[1,2,32,8,128]{4,3,2,1,0:T(8,128)(2,1)}, bf16[1,2,32,8,128]{4,3,2,1,0:T(8,128)(2,1)}, u32[]{:S(2)}, u32[]{:S(2)}) collective-permute-start(bf16[1,2,32,8,128]{4,3,2,1,0:T(8,128)(2,1)} %get-tuple-element.114), channel_id=1, source_target_pairs={{0,4},{1,5},{2,6},{3,7},{4,0},{5,1},{6,2},{7,3},{8,12},{9,13},{10,... | collective-permute-start | bytes 393224 | tf_op jit(solution)/shard_map/ppermute | solution.py:561
  11.1 6.1 %collective-permute-start.11 = (bf16[1,2,32,8,128]{4,3,2,1,0:T(8,128)(2,1)}, bf16[1,2,32,8,128]{4,3,2,1,0:T(8,128)(2,1)}, u32[]{:S(2)}, u32[]{:S(2)}) collective-permute-start(bf16[1,2,32,8,128]{4,3,2,1,0:T(8,128)(2,1)} %get-tuple-element.115), channel_id=1, source_target_pairs={{0,5},{1,6},{2,7},{3,0},{4,1},{5,2},{6,3},{7,4},{8,13},{9,14},{10,... | collective-permute-start | bytes 393224 | tf_op jit(solution)/shard_map/ppermute | solution.py:561
  13.1 10.8 %collective-permute-start.12 = (bf16[1,2,32,8,128]{4,3,2,1,0:T(8,128)(2,1)}, bf16[1,2,32,8,128]{4,3,2,1,0:T(8,128)(2,1)}, u32[]{:S(2)}, u32[]{:S(2)}) collective-permute-start(bf16[1,2,32,8,128]{4,3,2,1,0:T(8,128)(2,1)} %get-tuple-element.116), channel_id=1, source_target_pairs={{0,6},{1,7},{2,0},{3,1},{4,2},{5,3},{6,4},{7,5},{8,14},{9,15},{10,... | collective-permute-start | bytes 393224 | tf_op jit(solution)/shard_map/ppermute | solution.py:561
  13.3 10.6 %collective-permute-start.13 = (bf16[1,2,32,8,128]{4,3,2,1,0:T(8,128)(2,1)}, bf16[1,2,32,8,128]{4,3,2,1,0:T(8,128)(2,1)}, u32[]{:S(2)}, u32[]{:S(2)}) collective-permute-start(bf16[1,2,32,8,128]{4,3,2,1,0:T(8,128)(2,1)} %get-tuple-element.117), channel_id=1, source_target_pairs={{0,7},{1,0},{2,1},{3,2},{4,3},{5,4},{6,5},{7,6},{8,15},{9,8},{10,9... | collective-permute-start | bytes 393224 | tf_op jit(solution)/shard_map/ppermute | solution.py:561
  14.1 12.2 %collective-permute-start.7 = (bf16[1,2,32,8,128]{4,3,2,1,0:T(8,128)(2,1)}, bf16[1,2,32,8,128]{4,3,2,1,0:T(8,128)(2,1)}, u32[]{:S(2)}, u32[]{:S(2)}) collective-permute-start(bf16[1,2,32,8,128]{4,3,2,1,0:T(8,128)(2,1)} %get-tuple-element.111), channel_id=1, source_target_pairs={{0,1},{1,2},{2,3},{3,4},{4,5},{5,6},{6,7},{7,0},{8,9},{9,10},{10,1... | collective-permute-start | bytes 393224 | tf_op jit(solution)/shard_map/ppermute | solution.py:561
  15.1 17.5 %collective-permute-start.8 = (bf16[1,2,32,8,128]{4,3,2,1,0:T(8,128)(2,1)}, bf16[1,2,32,8,128]{4,3,2,1,0:T(8,128)(2,1)}, u32[]{:S(2)}, u32[]{:S(2)}) collective-permute-start(bf16[1,2,32,8,128]{4,3,2,1,0:T(8,128)(2,1)} %get-tuple-element.112), channel_id=1, source_target_pairs={{0,2},{1,3},{2,4},{3,5},{4,6},{5,7},{6,0},{7,1},{8,10},{9,11},{10,... | collective-permute-start | bytes 393224 | tf_op jit(solution)/shard_map/ppermute | solution.py:561
  17.2 17.1 %collective-permute-start.9 = (bf16[1,2,32,8,128]{4,3,2,1,0:T(8,128)(2,1)}, bf16[1,2,32,8,128]{4,3,2,1,0:T(8,128)(2,1)}, u32[]{:S(2)}, u32[]{:S(2)}) collective-permute-start(bf16[1,2,32,8,128]{4,3,2,1,0:T(8,128)(2,1)} %get-tuple-element.113), channel_id=1, source_target_pairs={{0,3},{1,4},{2,5},{3,6},{4,7},{5,0},{6,1},{7,2},{8,11},{9,12},{10,... | collective-permute-start | bytes 393224 | tf_op jit(solution)/shard_map/ppermute | solution.py:561
  23.9 11.6 %collective-permute-start = (bf16[1,2,32,8,128]{4,3,2,1,0:T(8,128)(2,1)}, bf16[1,2,32,8,128]{4,3,2,1,0:T(8,128)(2,1)}, u32[]{:S(2)}, u32[]{:S(2)}) collective-permute-start(bf16[1,2,32,8,128]{4,3,2,1,0:T(8,128)(2,1)} %get-tuple-element.103), channel_id=1, source_target_pairs={{0,1},{1,2},{2,3},{3,4},{4,5},{5,6},{6,7},{7,0},{8,9},{9,10},{10,1... | collective-permute-start | bytes 393224 | tf_op jit(solution)/shard_map/ppermute | solution.py:561
  23.9 11.9 %collective-permute-start.1 = (bf16[1,2,32,8,128]{4,3,2,1,0:T(8,128)(2,1)}, bf16[1,2,32,8,128]{4,3,2,1,0:T(8,128)(2,1)}, u32[]{:S(2)}, u32[]{:S(2)}) collective-permute-start(bf16[1,2,32,8,128]{4,3,2,1,0:T(8,128)(2,1)} %get-tuple-element.104), channel_id=1, source_target_pairs={{0,2},{1,3},{2,4},{3,5},{4,6},{5,7},{6,0},{7,1},{8,10},{9,11},{10,... | collective-permute-start | bytes 393224 | tf_op jit(solution)/shard_map/ppermute | solution.py:561
  26.3 11.3 %collective-permute-start.2 = (bf16[1,2,32,8,128]{4,3,2,1,0:T(8,128)(2,1)}, bf16[1,2,32,8,128]{4,3,2,1,0:T(8,128)(2,1)}, u32[]{:S(2)}, u32[]{:S(2)}) collective-permute-start(bf16[1,2,32,8,128]{4,3,2,1,0:T(8,128)(2,1)} %get-tuple-element.105), channel_id=1, source_target_pairs={{0,3},{1,4},{2,5},{3,6},{4,7},{5,0},{6,1},{7,2},{8,11},{9,12},{10,... | collective-permute-start | bytes 393224 | tf_op jit(solution)/shard_map/ppermute | solution.py:561
  32.5 15.4 %collective-permute-start.14 = (bf16[1,2,32,16,128]{4,3,2,1,0:T(8,128)(2,1)}, bf16[1,2,32,16,128]{4,3,2,1,0:T(8,128)(2,1)}, u32[]{:S(2)}, u32[]{:S(2)}) collective-permute-start(bf16[1,2,32,16,128]{4,3,2,1,0:T(8,128)(2,1)} %get-tuple-element.119), channel_id=1, source_target_pairs={{0,1},{1,2},{2,3},{3,4},{4,5},{5,6},{6,7},{7,0},{8,9},{9,10},{10,1... | collective-permute-start | bytes 786440 | tf_op jit(solution)/shard_map/ppermute | solution.py:561
  34.3 8.1 %collective-permute-start.3 = (bf16[1,2,32,8,128]{4,3,2,1,0:T(8,128)(2,1)}, bf16[1,2,32,8,128]{4,3,2,1,0:T(8,128)(2,1)}, u32[]{:S(2)}, u32[]{:S(2)}) collective-permute-start(bf16[1,2,32,8,128]{4,3,2,1,0:T(8,128)(2,1)} %get-tuple-element.106), channel_id=1, source_target_pairs={{0,4},{1,5},{2,6},{3,7},{4,0},{5,1},{6,2},{7,3},{8,12},{9,13},{10,... | collective-permute-start | bytes 393224 | tf_op jit(solution)/shard_map/ppermute | solution.py:561
  35.5 8.1 %collective-permute-start.4 = (bf16[1,2,32,8,128]{4,3,2,1,0:T(8,128)(2,1)}, bf16[1,2,32,8,128]{4,3,2,1,0:T(8,128)(2,1)}, u32[]{:S(2)}, u32[]{:S(2)}) collective-permute-start(bf16[1,2,32,8,128]{4,3,2,1,0:T(8,128)(2,1)} %get-tuple-element.107), channel_id=1, source_target_pairs={{0,5},{1,6},{2,7},{3,0},{4,1},{5,2},{6,3},{7,4},{8,13},{9,14},{10,... | collective-permute-start | bytes 393224 | tf_op jit(solution)/shard_map/ppermute | solution.py:561
  35.8 11.5 %collective-permute-start.5 = (bf16[1,2,32,8,128]{4,3,2,1,0:T(8,128)(2,1)}, bf16[1,2,32,8,128]{4,3,2,1,0:T(8,128)(2,1)}, u32[]{:S(2)}, u32[]{:S(2)}) collective-permute-start(bf16[1,2,32,8,128]{4,3,2,1,0:T(8,128)(2,1)} %get-tuple-element.108), channel_id=1, source_target_pairs={{0,6},{1,7},{2,0},{3,1},{4,2},{5,3},{6,4},{7,5},{8,14},{9,15},{10,... | collective-permute-start | bytes 393224 | tf_op jit(solution)/shard_map/ppermute | solution.py:561
  37.6 9.7 %collective-permute-start.6 = (bf16[1,2,32,8,128]{4,3,2,1,0:T(8,128)(2,1)}, bf16[1,2,32,8,128]{4,3,2,1,0:T(8,128)(2,1)}, u32[]{:S(2)}, u32[]{:S(2)}) collective-permute-start(bf16[1,2,32,8,128]{4,3,2,1,0:T(8,128)(2,1)} %get-tuple-element.109), channel_id=1, source_target_pairs={{0,7},{1,0},{2,1},{3,2},{4,3},{5,4},{6,5},{7,6},{8,15},{9,8},{10,9... | collective-permute-start | bytes 393224 | tf_op jit(solution)/shard_map/ppermute | solution.py:561
  42.3 18.4 %collective-permute-start.15 = (bf16[1,2,32,16,128]{4,3,2,1,0:T(8,128)(2,1)}, bf16[1,2,32,16,128]{4,3,2,1,0:T(8,128)(2,1)}, u32[]{:S(2)}, u32[]{:S(2)}) collective-permute-start(bf16[1,2,32,16,128]{4,3,2,1,0:T(8,128)(2,1)} %get-tuple-element.120), channel_id=1, source_target_pairs={{0,2},{1,3},{2,4},{3,5},{4,6},{5,7},{6,0},{7,1},{8,10},{9,11},{10,... | collective-permute-start | bytes 786440 | tf_op jit(solution)/shard_map/ppermute | solution.py:561
  43.5 17.6 %collective-permute-start.16 = (bf16[1,2,32,16,128]{4,3,2,1,0:T(8,128)(2,1)}, bf16[1,2,32,16,128]{4,3,2,1,0:T(8,128)(2,1)}, u32[]{:S(2)}, u32[]{:S(2)}) collective-permute-start(bf16[1,2,32,16,128]{4,3,2,1,0:T(8,128)(2,1)} %get-tuple-element.121), channel_id=1, source_target_pairs={{0,3},{1,4},{2,5},{3,6},{4,7},{5,0},{6,1},{7,2},{8,11},{9,12},{10,... | collective-permute-start | bytes 786440 | tf_op jit(solution)/shard_map/ppermute | solution.py:561
  47.3 19.1 %collective-permute-start.17 = (bf16[1,2,32,16,128]{4,3,2,1,0:T(8,128)(2,1)}, bf16[1,2,32,16,128]{4,3,2,1,0:T(8,128)(2,1)}, u32[]{:S(2)}, u32[]{:S(2)}) collective-permute-start(bf16[1,2,32,16,128]{4,3,2,1,0:T(8,128)(2,1)} %get-tuple-element.122), channel_id=1, source_target_pairs={{0,4},{1,5},{2,6},{3,7},{4,0},{5,1},{6,2},{7,3},{8,12},{9,13},{10,... | collective-permute-start | bytes 786440 | tf_op jit(solution)/shard_map/ppermute | solution.py:561
  47.3 24.1 %collective-permute-start.18 = (bf16[1,2,32,16,128]{4,3,2,1,0:T(8,128)(2,1)}, bf16[1,2,32,16,128]{4,3,2,1,0:T(8,128)(2,1)}, u32[]{:S(2)}, u32[]{:S(2)}) collective-permute-start(bf16[1,2,32,16,128]{4,3,2,1,0:T(8,128)(2,1)} %get-tuple-element.123), channel_id=1, source_target_pairs={{0,5},{1,6},{2,7},{3,0},{4,1},{5,2},{6,3},{7,4},{8,13},{9,14},{10,... | collective-permute-start | bytes 786440 | tf_op jit(solution)/shard_map/ppermute | solution.py:561
  48.0 23.4 %collective-permute-start.19 = (bf16[1,2,32,16,128]{4,3,2,1,0:T(8,128)(2,1)}, bf16[1,2,32,16,128]{4,3,2,1,0:T(8,128)(2,1)}, u32[]{:S(2)}, u32[]{:S(2)}) collective-permute-start(bf16[1,2,32,16,128]{4,3,2,1,0:T(8,128)(2,1)} %get-tuple-element.124), channel_id=1, source_target_pairs={{0,6},{1,7},{2,0},{3,1},{4,2},{5,3},{6,4},{7,5},{8,14},{9,15},{10,... | collective-permute-start | bytes 786440 | tf_op jit(solution)/shard_map/ppermute | solution.py:561
  60.7 32.4 %collective-permute-start.28 = (bf16[1,2,32,32,128]{4,3,2,1,0:T(8,128)(2,1)}, bf16[1,2,32,32,128]{4,3,2,1,0:T(8,128)(2,1)}, u32[]{:S(2)}, u32[]{:S(2)}) collective-permute-start(bf16[1,2,32,32,128]{4,3,2,1,0:T(8,128)(2,1)} %get-tuple-element.139), channel_id=1, source_target_pairs={{0,1},{1,2},{2,3},{3,4},{4,5},{5,6},{6,7},{7,0},{8,9},{9,10},{10,1... | collective-permute-start | bytes 1572872 | tf_op jit(solution)/shard_map/ppermute | solution.py:561
  61.2 28.8 %collective-permute-start.20 = (bf16[1,2,32,16,128]{4,3,2,1,0:T(8,128)(2,1)}, bf16[1,2,32,16,128]{4,3,2,1,0:T(8,128)(2,1)}, u32[]{:S(2)}, u32[]{:S(2)}) collective-permute-start(bf16[1,2,32,16,128]{4,3,2,1,0:T(8,128)(2,1)} %get-tuple-element.125), channel_id=1, source_target_pairs={{0,7},{1,0},{2,1},{3,2},{4,3},{5,4},{6,5},{7,6},{8,15},{9,8},{10,9... | collective-permute-start | bytes 786440 | tf_op jit(solution)/shard_map/ppermute | solution.py:561
  66.3 27.6 %collective-permute-start.29 = (bf16[1,2,32,32,128]{4,3,2,1,0:T(8,128)(2,1)}, bf16[1,2,32,32,128]{4,3,2,1,0:T(8,128)(2,1)}, u32[]{:S(2)}, u32[]{:S(2)}) collective-permute-start(bf16[1,2,32,32,128]{4,3,2,1,0:T(8,128)(2,1)} %get-tuple-element.140), channel_id=1, source_target_pairs={{0,2},{1,3},{2,4},{3,5},{4,6},{5,7},{6,0},{7,1},{8,10},{9,11},{10,... | collective-permute-start | bytes 1572872 | tf_op jit(solution)/shard_map/ppermute | solution.py:561
  71.4 61.4 %collective-permute-start.30 = (bf16[1,2,32,32,128]{4,3,2,1,0:T(8,128)(2,1)}, bf16[1,2,32,32,128]{4,3,2,1,0:T(8,128)(2,1)}, u32[]{:S(2)}, u32[]{:S(2)}) collective-permute-start(bf16[1,2,32,32,128]{4,3,2,1,0:T(8,128)(2,1)} %get-tuple-element.141), channel_id=1, source_target_pairs={{0,3},{1,4},{2,5},{3,6},{4,7},{5,0},{6,1},{7,2},{8,11},{9,12},{10,... | collective-permute-start | bytes 1572872 | tf_op jit(solution)/shard_map/ppermute | solution.py:561
  71.4 74.3 %collective-permute-start.31 = (bf16[1,2,32,32,128]{4,3,2,1,0:T(8,128)(2,1)}, bf16[1,2,32,32,128]{4,3,2,1,0:T(8,128)(2,1)}, u32[]{:S(2)}, u32[]{:S(2)}) collective-permute-start(bf16[1,2,32,32,128]{4,3,2,1,0:T(8,128)(2,1)} %get-tuple-element.142), channel_id=1, source_target_pairs={{0,4},{1,5},{2,6},{3,7},{4,0},{5,1},{6,2},{7,3},{8,12},{9,13},{10,... | collective-permute-start | bytes 1572872 | tf_op jit(solution)/shard_map/ppermute | solution.py:561
  90.0 71.3 %collective-permute-start.35 = (bf16[2,2,32,32,128]{4,3,2,1,0:T(8,128)(2,1)}, bf16[2,2,32,32,128]{4,3,2,1,0:T(8,128)(2,1)}, u32[]{:S(2)}, u32[]{:S(2)}) collective-permute-start(bf16[2,2,32,32,128]{4,3,2,1,0:T(8,128)(2,1)} %get-tuple-element.156), channel_id=1, source_target_pairs={{0,1},{1,2},{2,3},{3,4},{4,5},{5,6},{6,7},{7,0},{8,9},{9,10},{10,1... | collective-permute-start | bytes 3145736 | tf_op jit(solution)/shard_map/ppermute | solution.py:561
  93.1 68.2 %collective-permute-start.36 = (bf16[2,2,32,32,128]{4,3,2,1,0:T(8,128)(2,1)}, bf16[2,2,32,32,128]{4,3,2,1,0:T(8,128)(2,1)}, u32[]{:S(2)}, u32[]{:S(2)}) collective-permute-start(bf16[2,2,32,32,128]{4,3,2,1,0:T(8,128)(2,1)} %get-tuple-element.157), channel_id=1, source_target_pairs={{0,2},{1,3},{2,4},{3,5},{4,6},{5,7},{6,0},{7,1},{8,10},{9,11},{10,... | collective-permute-start | bytes 3145736 | tf_op jit(solution)/shard_map/ppermute | solution.py:561
  93.9 63.9 %collective-permute-start.32 = (bf16[1,2,32,32,128]{4,3,2,1,0:T(8,128)(2,1)}, bf16[1,2,32,32,128]{4,3,2,1,0:T(8,128)(2,1)}, u32[]{:S(2)}, u32[]{:S(2)}) collective-permute-start(bf16[1,2,32,32,128]{4,3,2,1,0:T(8,128)(2,1)} %get-tuple-element.143), channel_id=1, source_target_pairs={{0,5},{1,6},{2,7},{3,0},{4,1},{5,2},{6,3},{7,4},{8,13},{9,14},{10,... | collective-permute-start | bytes 1572872 | tf_op jit(solution)/shard_map/ppermute | solution.py:561
  132.8 25.0 %collective-permute-start.33 = (bf16[1,2,32,32,128]{4,3,2,1,0:T(8,128)(2,1)}, bf16[1,2,32,32,128]{4,3,2,1,0:T(8,128)(2,1)}, u32[]{:S(2)}, u32[]{:S(2)}) collective-permute-start(bf16[1,2,32,32,128]{4,3,2,1,0:T(8,128)(2,1)} %get-tuple-element.144), channel_id=1, source_target_pairs={{0,6},{1,7},{2,0},{3,1},{4,2},{5,3},{6,4},{7,5},{8,14},{9,15},{10,... | collective-permute-start | bytes 1572872 | tf_op jit(solution)/shard_map/ppermute | solution.py:561
  145.7 12.8 %collective-permute-start.34 = (bf16[1,2,32,32,128]{4,3,2,1,0:T(8,128)(2,1)}, bf16[1,2,32,32,128]{4,3,2,1,0:T(8,128)(2,1)}, u32[]{:S(2)}, u32[]{:S(2)}) collective-permute-start(bf16[1,2,32,32,128]{4,3,2,1,0:T(8,128)(2,1)} %get-tuple-element.145), channel_id=1, source_target_pairs={{0,7},{1,0},{2,1},{3,2},{4,3},{5,4},{6,5},{7,6},{8,15},{9,8},{10,9... | collective-permute-start | bytes 1572872 | tf_op jit(solution)/shard_map/ppermute | solution.py:561
  157.8 47.0 %collective-permute-start.37 = (bf16[2,2,32,32,128]{4,3,2,1,0:T(8,128)(2,1)}, bf16[2,2,32,32,128]{4,3,2,1,0:T(8,128)(2,1)}, u32[]{:S(2)}, u32[]{:S(2)}) collective-permute-start(bf16[2,2,32,32,128]{4,3,2,1,0:T(8,128)(2,1)} %get-tuple-element.158), channel_id=1, source_target_pairs={{0,3},{1,4},{2,5},{3,6},{4,7},{5,0},{6,1},{7,2},{8,11},{9,12},{10,... | collective-permute-start | bytes 3145736 | tf_op jit(solution)/shard_map/ppermute | solution.py:561
  157.8 71.6 %collective-permute-start.38 = (bf16[2,2,32,32,128]{4,3,2,1,0:T(8,128)(2,1)}, bf16[2,2,32,32,128]{4,3,2,1,0:T(8,128)(2,1)}, u32[]{:S(2)}, u32[]{:S(2)}) collective-permute-start(bf16[2,2,32,32,128]{4,3,2,1,0:T(8,128)(2,1)} %get-tuple-element.159), channel_id=1, source_target_pairs={{0,4},{1,5},{2,6},{3,7},{4,0},{5,1},{6,2},{7,3},{8,12},{9,13},{10,... | collective-permute-start | bytes 3145736 | tf_op jit(solution)/shard_map/ppermute | solution.py:561
  158.4 92.9 %collective-permute-start.39 = (bf16[2,2,32,32,128]{4,3,2,1,0:T(8,128)(2,1)}, bf16[2,2,32,32,128]{4,3,2,1,0:T(8,128)(2,1)}, u32[]{:S(2)}, u32[]{:S(2)}) collective-permute-start(bf16[2,2,32,32,128]{4,3,2,1,0:T(8,128)(2,1)} %get-tuple-element.160), channel_id=1, source_target_pairs={{0,5},{1,6},{2,7},{3,0},{4,1},{5,2},{6,3},{7,4},{8,13},{9,14},{10,... | collective-permute-start | bytes 3145736 | tf_op jit(solution)/shard_map/ppermute | solution.py:561
  161.3 90.0 %collective-permute-start.40 = (bf16[2,2,32,32,128]{4,3,2,1,0:T(8,128)(2,1)}, bf16[2,2,32,32,128]{4,3,2,1,0:T(8,128)(2,1)}, u32[]{:S(2)}, u32[]{:S(2)}) collective-permute-start(bf16[2,2,32,32,128]{4,3,2,1,0:T(8,128)(2,1)} %get-tuple-element.161), channel_id=1, source_target_pairs={{0,6},{1,7},{2,0},{3,1},{4,2},{5,3},{6,4},{7,5},{8,14},{9,15},{10,... | collective-permute-start | bytes 3145736 | tf_op jit(solution)/shard_map/ppermute | solution.py:561
  161.3 90.2 %collective-permute-start.41 = (bf16[2,2,32,32,128]{4,3,2,1,0:T(8,128)(2,1)}, bf16[2,2,32,32,128]{4,3,2,1,0:T(8,128)(2,1)}, u32[]{:S(2)}, u32[]{:S(2)}) collective-permute-start(bf16[2,2,32,32,128]{4,3,2,1,0:T(8,128)(2,1)} %get-tuple-element.162), channel_id=1, source_target_pairs={{0,7},{1,0},{2,1},{3,2},{4,3},{5,4},{6,5},{7,6},{8,15},{9,8},{10,9... | collective-permute-start | bytes 3145736 | tf_op jit(solution)/shard_map/ppermute | solution.py:561
  204.8 70.4 %collective-permute-start.21 = (bf16[2,1024,128]{2,1,0:T(8,128)(2,1)}, bf16[2,1024,128]{2,1,0:T(8,128)(2,1)}, u32[]{:S(2)}, u32[]{:S(2)}) collective-permute-start(bf16[2,1024,128]{2,1,0:T(8,128)(2,1)} %get-tuple-element.128), channel_id=1, source_target_pairs={{0,1},{1,2},{2,3},{3,4},{4,5},{5,6},{6,7},{7,0},{8,9},{9,10},{10,1... | collective-permute-start | bytes 1572872 | tf_op jit(solution)/shard_map/ppermute | solution.py:561
  229.4 45.9 %collective-permute-start.22 = (bf16[2,1024,128]{2,1,0:T(8,128)(2,1)}, bf16[2,1024,128]{2,1,0:T(8,128)(2,1)}, u32[]{:S(2)}, u32[]{:S(2)}) collective-permute-start(bf16[2,1024,128]{2,1,0:T(8,128)(2,1)} %get-tuple-element.129), channel_id=1, source_target_pairs={{0,2},{1,3},{2,4},{3,5},{4,6},{5,7},{6,0},{7,1},{8,10},{9,11},{10,... | collective-permute-start | bytes 1572872 | tf_op jit(solution)/shard_map/ppermute | solution.py:561
  251.3 45.2 %collective-permute-start.23 = (bf16[2,1024,128]{2,1,0:T(8,128)(2,1)}, bf16[2,1024,128]{2,1,0:T(8,128)(2,1)}, u32[]{:S(2)}, u32[]{:S(2)}) collective-permute-start(bf16[2,1024,128]{2,1,0:T(8,128)(2,1)} %get-tuple-element.130), channel_id=1, source_target_pairs={{0,3},{1,4},{2,5},{3,6},{4,7},{5,0},{6,1},{7,2},{8,11},{9,12},{10,... | collective-permute-start | bytes 1572872 | tf_op jit(solution)/shard_map/ppermute | solution.py:561
  251.3 45.2 %collective-permute-start.24 = (bf16[2,1024,128]{2,1,0:T(8,128)(2,1)}, bf16[2,1024,128]{2,1,0:T(8,128)(2,1)}, u32[]{:S(2)}, u32[]{:S(2)}) collective-permute-start(bf16[2,1024,128]{2,1,0:T(8,128)(2,1)} %get-tuple-element.131), channel_id=1, source_target_pairs={{0,4},{1,5},{2,6},{3,7},{4,0},{5,1},{6,2},{7,3},{8,12},{9,13},{10,... | collective-permute-start | bytes 1572872 | tf_op jit(solution)/shard_map/ppermute | solution.py:561
  251.6 44.9 %collective-permute-start.25 = (bf16[2,1024,128]{2,1,0:T(8,128)(2,1)}, bf16[2,1024,128]{2,1,0:T(8,128)(2,1)}, u32[]{:S(2)}, u32[]{:S(2)}) collective-permute-start(bf16[2,1024,128]{2,1,0:T(8,128)(2,1)} %get-tuple-element.132), channel_id=1, source_target_pairs={{0,5},{1,6},{2,7},{3,0},{4,1},{5,2},{6,3},{7,4},{8,13},{9,14},{10,... | collective-permute-start | bytes 1572872 | tf_op jit(solution)/shard_map/ppermute | solution.py:561
  275.2 21.3 %collective-permute-start.26 = (bf16[2,1024,128]{2,1,0:T(8,128)(2,1)}, bf16[2,1024,128]{2,1,0:T(8,128)(2,1)}, u32[]{:S(2)}, u32[]{:S(2)}) collective-permute-start(bf16[2,1024,128]{2,1,0:T(8,128)(2,1)} %get-tuple-element.133), channel_id=1, source_target_pairs={{0,6},{1,7},{2,0},{3,1},{4,2},{5,3},{6,4},{7,5},{8,14},{9,15},{10,... | collective-permute-start | bytes 1572872 | tf_op jit(solution)/shard_map/ppermute | solution.py:561
  275.3 21.2 %collective-permute-start.27 = (bf16[2,1024,128]{2,1,0:T(8,128)(2,1)}, bf16[2,1024,128]{2,1,0:T(8,128)(2,1)}, u32[]{:S(2)}, u32[]{:S(2)}) collective-permute-start(bf16[2,1024,128]{2,1,0:T(8,128)(2,1)} %get-tuple-element.134), channel_id=1, source_target_pairs={{0,7},{1,0},{2,1},{3,2},{4,3},{5,4},{6,5},{7,6},{8,15},{9,8},{10,9... | collective-permute-start | bytes 1572872 | tf_op jit(solution)/shard_map/ppermute | solution.py:561
  296.5 161.9 %copy-start = (f32[2,32,64,128]{3,2,1,0:T(8,128)S(1)}, f32[2,32,64,128]{3,2,1,0:T(8,128)}, u32[]{:S(2)}) copy-start(f32[2,32,64,128]{3,2,1,0:T(8,128)} %constant_dynamic-slice_fusion.image) | copy-start | bytes 6291460
  296.5 161.9 %copy-start.1 = (f32[2,32,64,128]{3,2,1,0:T(8,128)S(1)}, f32[2,32,64,128]{3,2,1,0:T(8,128)}, u32[]{:S(2)}) copy-start(f32[2,32,64,128]{3,2,1,0:T(8,128)} %auxiliary.1) | copy-start | bytes 6291460
  296.6 161.9 %copy-start.2 = (f32[2,32,64,128]{3,2,1,0:T(8,128)S(1)}, f32[2,32,64,128]{3,2,1,0:T(8,128)}, u32[]{:S(2)}) copy-start(f32[2,32,64,128]{3,2,1,0:T(8,128)} %dual.1) | copy-start | bytes 6291460

commit v6 on v5

--- a/solution.py
+++ b/solution.py
@@ -561,13 +561,11 @@
             moved[off] = lax.ppermute(parts[off], "slab", [(i, ahead(i, off, n)) for i in range(n)])
         return moved
 
-    batches = [[c] for c in range(min(coils, 2))] + [
-        list(range(c, min(c + 2, coils))) for c in range(2, coils, 2)
-    ]
+    batches = [[c] for c in range(coils)]
 
     def parts_of(c):
         if c == 0 and xl % 32 == 0:
-            return [(0, xl // 4), (xl // 4, xl // 4), (xl // 2, xl // 2)]
+            return [(0, xl // 2), (xl // 2, xl // 2)]
         return [(0, xl)]
 
     def tile_of(pieces, place, c):

time: 465 us -> 449 us (0.966)
  Pallas kernels: 302 us -> 288 us
    pallas_call x1, Pallas kernels: 162 us -> 148 us  [finish_call(): pl.pallas_call(functools.partial(finish_kernel, n, shares, kl, xl, chunks...]
  transfers between devices with their start and end apart: 42 -> 42, of which waited for: 5 -> 9; matrix products, arithmetic and copies ran while one was open for 1% -> 1% of each run, Pallas kernels for 27% -> 27%
where the time goes in v6:
time: 449 us; the launch traced here: 446 us
  Pallas kernels  288 us (64%)
  starting transfers between devices  91.4 us (20%)
  waiting for transfers between devices  61.9 us (14%)
    pallas_call x1, Pallas kernels, finish_call(): pl.pallas_call(functools.partial(finish_kernel, n, shares, kl, xl, chunks...  148 us
    ppermute x42, starting transfers between devices, swap(): lax.ppermute(parts[off], 'slab', [(i, ahead(i, off, n)) for i in range(n)])  91.4 us
    pallas_call x4, Pallas kernels, tile_call(): pl.pallas_call(functools.partial(tile_kernel, n, kl, xl, cells // kl, par...  83.2 us
    ppermute x42, waiting for transfers between devices, swap(): lax.ppermute(parts[off], 'slab', [(i, ahead(i, off, n)) for i in range(n)])  61.9 us
    pallas_call x5, Pallas kernels, forward_call(): pl.pallas_call(functools.partial(forward_kernel, n, kl, xp), grid=(len(ba...  43.4 us
  transfers between devices with their start and end apart: 42, of which 9 were waited for; matrix products, arithmetic and copies ran while one was open for 1% of the time, Pallas kernels for 27%

profile of v6, /device:TPU:9, one launch (start us, length us, event | category | flops | bytes accessed | tf_op | source)
XLA Modules:
  0.0 445.8 jit_solution(9983375322797817497)
XLA Ops:
  0.6 6.2 %forward.5 = (bf16[1,2,32,16,128]{4,3,2,1,0:T(8,128)(2,1)}, bf16[1,2,32,16,128]{4,3,2,1,0:T(8,128)(2,1)}, bf16[1,2,32,16,128]{4,3,2,1,0:T(8,128)(2,1)}, bf16[1,2...) custom-call(bf16[512,512]{1,0:T(8,128)(2,1)} %constant.22.table.fwd,, ...), custom_call_target="tpu_custom_call" | custom-call | flops 1073741824 | bytes 6291456 | tf_op jit(solution)/shard_map/forward/pallas_call | solution.py:123
  6.9 6.2 %forward.6 = (bf16[1,2,32,16,128]{4,3,2,1,0:T(8,128)(2,1)}, bf16[1,2,32,16,128]{4,3,2,1,0:T(8,128)(2,1)}, bf16[1,2,32,16,128]{4,3,2,1,0:T(8,128)(2,1)}, bf16[1,2...) custom-call(bf16[512,512]{1,0:T(8,128)(2,1)} %constant.22.table.fwd,, ...), custom_call_target="tpu_custom_call" | custom-call | flops 1073741824 | bytes 6291456 | tf_op jit(solution)/shard_map/forward/pallas_call | solution.py:123
  13.1 1.2 collective-permute-start.10
  14.3 2.0 collective-permute-start.11
  16.3 0.3 collective-permute-start.12
  16.6 0.8 collective-permute-start.13
  17.4 0.9 collective-permute-start.7
  18.3 2.3 collective-permute-done.10.refs_12_
  20.6 12.5 %collective-permute-start.8 = (bf16[1,2,32,16,128]{4,3,2,1,0:T(8,128)(2,1)}, bf16[1,2,32,16,128]{4,3,2,1,0:T(8,128)(2,1)}, u32[]{:S(2)}, u32[]{:S(2)}) collective-permute-start(bf16[1,2,32,16,128]{4,3,2,1,0:T(8,128)(2,1)} %get-tuple-element.110), channel_id=1, source_target_pairs={{0,2},{1,3},{2,4},{3,5},{4,6},{5,7},{6,0},{7,1},{8,10},{9,11},{10,... | collective-permute-start | bytes 786440 | tf_op jit(solution)/shard_map/ppermute | solution.py:561
  33.0 2.9 collective-permute-start.9
  36.0 0.3 collective-permute-start
  36.3 0.0 collective-permute-done.13.refs_15_
  36.3 3.1 collective-permute-start.1
  39.4 0.0 collective-permute-done.7.refs_9_
  39.4 0.0 collective-permute-start.2
  39.4 0.1 collective-permute-done.8.refs_10_
  39.5 0.2 collective-permute-start.3
  39.7 19.1 %collective-permute-done.9.refs_11_ = bf16[1,2,32,16,128]{4,3,2,1,0:T(8,128)(2,1)} collective-permute-done((bf16[1,2,32,16,128]{4,3,2,1,0:T(8,128)(2,1)}, bf16[1,2,32,16,128]{4,3,2,1,0:T(8,128)(2,1)}, u32[]{:S(2)}, u32[]{:S(2)}) %collective-permute-start.9) | collective-permute-done | bytes 262176 | tf_op jit(solution)/shard_map/ppermute | solution.py:561
  58.8 10.3 %forward.7 = (bf16[1,2,32,32,128]{4,3,2,1,0:T(8,128)(2,1)}, bf16[1,2,32,32,128]{4,3,2,1,0:T(8,128)(2,1)}, bf16[1,2,32,32,128]{4,3,2,1,0:T(8,128)(2,1)}, bf16[1,2...) custom-call(bf16[512,512]{1,0:T(8,128)(2,1)} %constant.22.table.fwd,, ...), custom_call_target="tpu_custom_call" | custom-call | flops 2147483648 | bytes 12582912 | tf_op jit(solution)/shard_map/forward/pallas_call | solution.py:123
  69.1 0.1 collective-permute-start.21
  69.1 0.0 collective-permute-done.1.refs_2_
  69.1 3.7 collective-permute-start.22
  72.9 0.0 collective-permute-done.2.refs_3_
  72.9 0.8 collective-permute-start.23
  73.7 0.7 collective-permute-start.5
  74.5 1.5 collective-permute-start.6
  75.9 10.3 %forward.8 = (bf16[1,2,32,32,128]{4,3,2,1,0:T(8,128)(2,1)}, bf16[1,2,32,32,128]{4,3,2,1,0:T(8,128)(2,1)}, bf16[1,2,32,32,128]{4,3,2,1,0:T(8,128)(2,1)}, bf16[1,2...) custom-call(bf16[512,512]{1,0:T(8,128)(2,1)} %constant.22.table.fwd,, ...), custom_call_target="tpu_custom_call" | custom-call | flops 2147483648 | bytes 12582912 | tf_op jit(solution)/shard_map/forward/pallas_call | solution.py:123
  86.2 15.6 %collective-permute-done.5.refs_6_ = bf16[1,2,32,16,128]{4,3,2,1,0:T(8,128)(2,1)} collective-permute-done((bf16[1,2,32,16,128]{4,3,2,1,0:T(8,128)(2,1)}, bf16[1,2,32,16,128]{4,3,2,1,0:T(8,128)(2,1)}, u32[]{:S(2)}, u32[]{:S(2)}) %collective-permute-start.5) | collective-permute-done | bytes 262176 | tf_op jit(solution)/shard_map/ppermute | solution.py:561
  101.8 1.2 collective-permute-start.24
  103.1 2.0 collective-permute-done.6.refs_7_
  105.0 0.7 collective-permute-start.25
  105.8 0.9 collective-permute-start.27
  106.7 1.6 collective-permute-start.28
  109.0 10.4 %forward.9 = (bf16[1,2,32,32,128]{4,3,2,1,0:T(8,128)(2,1)}, bf16[1,2,32,32,128]{4,3,2,1,0:T(8,128)(2,1)}, bf16[1,2,32,32,128]{4,3,2,1,0:T(8,128)(2,1)}, bf16[1,2...) custom-call(bf16[512,512]{1,0:T(8,128)(2,1)} %constant.22.table.fwd,, ...), custom_call_target="tpu_custom_call" | custom-call | flops 2147483648 | bytes 12582912 | tf_op jit(solution)/shard_map/forward/pallas_call | solution.py:123
  119.3 8.3 %sort.1.sorted_samples = bf16[4,24,128,256]{3,2,1,0:T(8,128)(2,1)} custom-call(bf16[24,1024,128]{2,1,0:T(8,128)(2,1)} %bitcast.1), custom_call_target="tpu_custom_call" | custom-call | flops 3145728 | bytes 12582912 | tf_op jit(solution)/shard_map/sort/pallas_call | solution.py:156
  127.6 3.2 constant_dynamic-slice_fusion.image
  130.8 5.5 %collective-permute-start.29 = (bf16[1,2,32,32,128]{4,3,2,1,0:T(8,128)(2,1)}, bf16[1,2,32,32,128]{4,3,2,1,0:T(8,128)(2,1)}, u32[]{:S(2)}, u32[]{:S(2)}) collective-permute-start(bf16[1,2,32,32,128]{4,3,2,1,0:T(8,128)(2,1)} %get-tuple-element.150), channel_id=1, source_target_pairs={{0,2},{1,3},{2,4},{3,5},{4,6},{5,7},{6,0},{7,1},{8,10},{9,11},{10,... | collective-permute-start | bytes 1572872 | tf_op jit(solution)/shard_map/ppermute | solution.py:561
  136.3 3.3 collective-permute-start.30
  139.6 0.2 collective-permute-start.31
  139.9 4.4 collective-permute-start.32
  144.2 2.4 collective-permute-start.33
  146.7 20.8 %tile.4 = (bf16[2,1024,128]{2,1,0:T(8,128)(2,1)}, bf16[2,1024,128]{2,1,0:T(8,128)(2,1)}, bf16[2,1024,128]{2,1,0:T(8,128)(2,1)}, bf16[2,1024,128]{2,1,0:T(8,128)(...) custom-call(s32[1,24]{1,0:T(1,128)} %offsets.7, ...), custom_call_target="tpu_custom_call" | custom-call | flops 10737418240 | bytes 20971520 | tf_op jit(solution)/shard_map/tile/pallas_call | solution.py:303
  167.5 0.1 collective-permute-start.34
  167.6 6.9 %collective-permute-start.35 = (bf16[1,2,32,32,128]{4,3,2,1,0:T(8,128)(2,1)}, bf16[1,2,32,32,128]{4,3,2,1,0:T(8,128)(2,1)}, u32[]{:S(2)}, u32[]{:S(2)}) collective-permute-start(bf16[1,2,32,32,128]{4,3,2,1,0:T(8,128)(2,1)} %get-tuple-element.166), channel_id=1, source_target_pairs={{0,1},{1,2},{2,3},{3,4},{4,5},{5,6},{6,7},{7,0},{8,9},{9,10},{10,1... | collective-permute-start | bytes 1572872 | tf_op jit(solution)/shard_map/ppermute | solution.py:561
  174.5 8.9 %collective-permute-done.31.refs_4_ = bf16[1,2,32,32,128]{4,3,2,1,0:T(8,128)(2,1)} collective-permute-done((bf16[1,2,32,32,128]{4,3,2,1,0:T(8,128)(2,1)}, bf16[1,2,32,32,128]{4,3,2,1,0:T(8,128)(2,1)}, u32[]{:S(2)}, u32[]{:S(2)}) %collective-permute-start.31) | collective-permute-done | bytes 524320 | tf_op jit(solution)/shard_map/ppermute | solution.py:561
  183.4 7.4 %collective-permute-start.36 = (bf16[1,2,32,32,128]{4,3,2,1,0:T(8,128)(2,1)}, bf16[1,2,32,32,128]{4,3,2,1,0:T(8,128)(2,1)}, u32[]{:S(2)}, u32[]{:S(2)}) collective-permute-start(bf16[1,2,32,32,128]{4,3,2,1,0:T(8,128)(2,1)} %get-tuple-element.167), channel_id=1, source_target_pairs={{0,2},{1,3},{2,4},{3,5},{4,6},{5,7},{6,0},{7,1},{8,10},{9,11},{10,... | collective-permute-start | bytes 1572872 | tf_op jit(solution)/shard_map/ppermute | solution.py:561
  190.8 0.6 collective-permute-start.38
  191.4 20.8 %tile.5 = (bf16[2,1024,128]{2,1,0:T(8,128)(2,1)}, bf16[2,1024,128]{2,1,0:T(8,128)(2,1)}, bf16[2,1024,128]{2,1,0:T(8,128)(2,1)}, bf16[2,1024,128]{2,1,0:T(8,128)(...) custom-call(s32[1,24]{1,0:T(1,128)} %offsets.7, ...), custom_call_target="tpu_custom_call" | custom-call | flops 10737418240 | bytes 20971520 | tf_op jit(solution)/shard_map/tile/pallas_call | solution.py:303
  212.2 2.9 collective-permute-start.39
  215.1 9.0 %collective-permute-start.40 = (bf16[1,2,32,32,128]{4,3,2,1,0:T(8,128)(2,1)}, bf16[1,2,32,32,128]{4,3,2,1,0:T(8,128)(2,1)}, u32[]{:S(2)}, u32[]{:S(2)}) collective-permute-start(bf16[1,2,32,32,128]{4,3,2,1,0:T(8,128)(2,1)} %get-tuple-element.171), channel_id=1, source_target_pairs={{0,6},{1,7},{2,0},{3,1},{4,2},{5,3},{6,4},{7,5},{8,14},{9,15},{10,... | collective-permute-start | bytes 1572872 | tf_op jit(solution)/shard_map/ppermute | solution.py:561
  224.1 1.7 collective-permute-start.14
  225.9 0.0 collective-permute-start.15
  225.9 20.8 %tile.6 = (bf16[2,1024,128]{2,1,0:T(8,128)(2,1)}, bf16[2,1024,128]{2,1,0:T(8,128)(2,1)}, bf16[2,1024,128]{2,1,0:T(8,128)(2,1)}, bf16[2,1024,128]{2,1,0:T(8,128)(...) custom-call(s32[1,24]{1,0:T(1,128)} %offsets.7, ...), custom_call_target="tpu_custom_call" | custom-call | flops 10737418240 | bytes 20971520 | tf_op jit(solution)/shard_map/tile/pallas_call | solution.py:303
  246.7 8.9 %collective-permute-start.16 = (bf16[2,1024,128]{2,1,0:T(8,128)(2,1)}, bf16[2,1024,128]{2,1,0:T(8,128)(2,1)}, u32[]{:S(2)}, u32[]{:S(2)}) collective-permute-start(bf16[2,1024,128]{2,1,0:T(8,128)(2,1)} %get-tuple-element.120), channel_id=1, source_target_pairs={{0,3},{1,4},{2,5},{3,6},{4,7},{5,0},{6,1},{7,2},{8,11},{9,12},{10,... | collective-permute-start | bytes 1572872 | tf_op jit(solution)/shard_map/ppermute | solution.py:561
  255.6 0.1 collective-permute-start.18
  255.7 2.4 collective-permute-start.19
  258.0 11.7 %collective-permute-done.15.refs_2_ = bf16[2,1024,128]{2,1,0:T(8,128)(2,1)} collective-permute-done((bf16[2,1024,128]{2,1,0:T(8,128)(2,1)}, bf16[2,1024,128]{2,1,0:T(8,128)(2,1)}, u32[]{:S(2)}, u32[]{:S(2)}) %collective-permute-start.15) | collective-permute-done | bytes 524320 | tf_op jit(solution)/shard_map/ppermute | solution.py:561
  269.8 20.8 %tile.7 = (bf16[2,1024,128]{2,1,0:T(8,128)(2,1)}, bf16[2,1024,128]{2,1,0:T(8,128)(2,1)}, bf16[2,1024,128]{2,1,0:T(8,128)(2,1)}, bf16[2,1024,128]{2,1,0:T(8,128)(...) custom-call(s32[1,24]{1,0:T(1,128)} %offsets.7, ...), custom_call_target="tpu_custom_call" | custom-call | flops 10737418240 | bytes 20971520 | tf_op jit(solution)/shard_map/tile/pallas_call | solution.py:303
  290.6 2.1 collective-permute-done.17.refs_4_
  292.7 0.1 collective-permute-done.18.refs_5_
  292.8 0.0 copy-start.1
  292.8 0.0 copy-start.2
  292.8 148.3 %finish.1.gradient = f32[2,32,64,128]{3,2,1,0:T(8,128)S(1)} custom-call(bf16[512,512]{1,0:T(8,128)(2,1)} %constant.21.inv.table_ref, bf16[4,2,32,256,128]{4,3,2,1,0:T(8,128)(2,1)} %sens.11, bf16[2,1024,128]{2,1,0:T(8,128)(2,1)} %get-tuple-element.117.refs_0_, bf16[2,1024,128]{2,1,0:T(8,128)(2,1)} %collective-permute-done.14.refs_1_, ...), custom_call_target="tpu_custom_call" | custom-call | tf_op jit(solution)/shard_map/finish/pallas_call | solution.py:481
  441.2 4.6 %update.1 = (f32[2,32,64,128]{3,2,1,0:T(8,128)}, f32[2,32,64,128]{3,2,1,0:T(8,128)}, f32[2,32,64,128]{3,2,1,0:T(8,128)}) custom-call(f32[2,32,64,128]{3,2,1,0:T(8,128)S(1)} %copy-done, f32[2,32,64,128]{3,2,1,0:T(8,128)S(1)} %finish.1.gradient, f32[2,32,64,128]{3,2,1,0:T(8,128)S(1)} %copy-done.1, f32[2,32,64,128]{3,2,1,0:T(8,128)S(1)} %copy-done.2), custom_call_target="tpu_custom_call" | custom-call | tf_op jit(solution)/shard_map/update/pallas_call | solution.py:537
  (39 shorter events, 0.1 us)
Async XLA Ops:
  13.1 7.5 %collective-permute-start.10 = (bf16[1,2,32,16,128]{4,3,2,1,0:T(8,128)(2,1)}, bf16[1,2,32,16,128]{4,3,2,1,0:T(8,128)(2,1)}, u32[]{:S(2)}, u32[]{:S(2)}) collective-permute-start(bf16[1,2,32,16,128]{4,3,2,1,0:T(8,128)(2,1)} %get-tuple-element.112), channel_id=1, source_target_pairs={{0,4},{1,5},{2,6},{3,7},{4,0},{5,1},{6,2},{7,3},{8,12},{9,13},{10,... | collective-permute-start | bytes 786440 | tf_op jit(solution)/shard_map/ppermute | solution.py:561
  14.3 18.7 %collective-permute-start.11 = (bf16[1,2,32,16,128]{4,3,2,1,0:T(8,128)(2,1)}, bf16[1,2,32,16,128]{4,3,2,1,0:T(8,128)(2,1)}, u32[]{:S(2)}, u32[]{:S(2)}) collective-permute-start(bf16[1,2,32,16,128]{4,3,2,1,0:T(8,128)(2,1)} %get-tuple-element.113), channel_id=1, source_target_pairs={{0,5},{1,6},{2,7},{3,0},{4,1},{5,2},{6,3},{7,4},{8,13},{9,14},{10,... | collective-permute-start | bytes 786440 | tf_op jit(solution)/shard_map/ppermute | solution.py:561
  16.3 19.7 %collective-permute-start.12 = (bf16[1,2,32,16,128]{4,3,2,1,0:T(8,128)(2,1)}, bf16[1,2,32,16,128]{4,3,2,1,0:T(8,128)(2,1)}, u32[]{:S(2)}, u32[]{:S(2)}) collective-permute-start(bf16[1,2,32,16,128]{4,3,2,1,0:T(8,128)(2,1)} %get-tuple-element.114), channel_id=1, source_target_pairs={{0,6},{1,7},{2,0},{3,1},{4,2},{5,3},{6,4},{7,5},{8,14},{9,15},{10,... | collective-permute-start | bytes 786440 | tf_op jit(solution)/shard_map/ppermute | solution.py:561
  16.6 19.7 %collective-permute-start.13 = (bf16[1,2,32,16,128]{4,3,2,1,0:T(8,128)(2,1)}, bf16[1,2,32,16,128]{4,3,2,1,0:T(8,128)(2,1)}, u32[]{:S(2)}, u32[]{:S(2)}) collective-permute-start(bf16[1,2,32,16,128]{4,3,2,1,0:T(8,128)(2,1)} %get-tuple-element.115), channel_id=1, source_target_pairs={{0,7},{1,0},{2,1},{3,2},{4,3},{5,4},{6,5},{7,6},{8,15},{9,8},{10,9... | collective-permute-start | bytes 786440 | tf_op jit(solution)/shard_map/ppermute | solution.py:561
  17.4 22.0 %collective-permute-start.7 = (bf16[1,2,32,16,128]{4,3,2,1,0:T(8,128)(2,1)}, bf16[1,2,32,16,128]{4,3,2,1,0:T(8,128)(2,1)}, u32[]{:S(2)}, u32[]{:S(2)}) collective-permute-start(bf16[1,2,32,16,128]{4,3,2,1,0:T(8,128)(2,1)} %get-tuple-element.109), channel_id=1, source_target_pairs={{0,1},{1,2},{2,3},{3,4},{4,5},{5,6},{6,7},{7,0},{8,9},{9,10},{10,1... | collective-permute-start | bytes 786440 | tf_op jit(solution)/shard_map/ppermute | solution.py:561
  20.6 18.9 %collective-permute-start.8 = (bf16[1,2,32,16,128]{4,3,2,1,0:T(8,128)(2,1)}, bf16[1,2,32,16,128]{4,3,2,1,0:T(8,128)(2,1)}, u32[]{:S(2)}, u32[]{:S(2)}) collective-permute-start(bf16[1,2,32,16,128]{4,3,2,1,0:T(8,128)(2,1)} %get-tuple-element.110), channel_id=1, source_target_pairs={{0,2},{1,3},{2,4},{3,5},{4,6},{5,7},{6,0},{7,1},{8,10},{9,11},{10,... | collective-permute-start | bytes 786440 | tf_op jit(solution)/shard_map/ppermute | solution.py:561
  33.0 25.7 %collective-permute-start.9 = (bf16[1,2,32,16,128]{4,3,2,1,0:T(8,128)(2,1)}, bf16[1,2,32,16,128]{4,3,2,1,0:T(8,128)(2,1)}, u32[]{:S(2)}, u32[]{:S(2)}) collective-permute-start(bf16[1,2,32,16,128]{4,3,2,1,0:T(8,128)(2,1)} %get-tuple-element.111), channel_id=1, source_target_pairs={{0,3},{1,4},{2,5},{3,6},{4,7},{5,0},{6,1},{7,2},{8,11},{9,12},{10,... | collective-permute-start | bytes 786440 | tf_op jit(solution)/shard_map/ppermute | solution.py:561
  36.0 33.1 %collective-permute-start = (bf16[1,2,32,16,128]{4,3,2,1,0:T(8,128)(2,1)}, bf16[1,2,32,16,128]{4,3,2,1,0:T(8,128)(2,1)}, u32[]{:S(2)}, u32[]{:S(2)}) collective-permute-start(bf16[1,2,32,16,128]{4,3,2,1,0:T(8,128)(2,1)} %get-tuple-element.101), channel_id=1, source_target_pairs={{0,1},{1,2},{2,3},{3,4},{4,5},{5,6},{6,7},{7,0},{8,9},{9,10},{10,1... | collective-permute-start | bytes 786440 | tf_op jit(solution)/shard_map/ppermute | solution.py:561
  36.3 32.8 %collective-permute-start.1 = (bf16[1,2,32,16,128]{4,3,2,1,0:T(8,128)(2,1)}, bf16[1,2,32,16,128]{4,3,2,1,0:T(8,128)(2,1)}, u32[]{:S(2)}, u32[]{:S(2)}) collective-permute-start(bf16[1,2,32,16,128]{4,3,2,1,0:T(8,128)(2,1)} %get-tuple-element.102), channel_id=1, source_target_pairs={{0,2},{1,3},{2,4},{3,5},{4,6},{5,7},{6,0},{7,1},{8,10},{9,11},{10,... | collective-permute-start | bytes 786440 | tf_op jit(solution)/shard_map/ppermute | solution.py:561
  39.4 33.5 %collective-permute-start.2 = (bf16[1,2,32,16,128]{4,3,2,1,0:T(8,128)(2,1)}, bf16[1,2,32,16,128]{4,3,2,1,0:T(8,128)(2,1)}, u32[]{:S(2)}, u32[]{:S(2)}) collective-permute-start(bf16[1,2,32,16,128]{4,3,2,1,0:T(8,128)(2,1)} %get-tuple-element.103), channel_id=1, source_target_pairs={{0,3},{1,4},{2,5},{3,6},{4,7},{5,0},{6,1},{7,2},{8,11},{9,12},{10,... | collective-permute-start | bytes 786440 | tf_op jit(solution)/shard_map/ppermute | solution.py:561
  39.5 34.3 %collective-permute-start.3 = (bf16[1,2,32,16,128]{4,3,2,1,0:T(8,128)(2,1)}, bf16[1,2,32,16,128]{4,3,2,1,0:T(8,128)(2,1)}, u32[]{:S(2)}, u32[]{:S(2)}) collective-permute-start(bf16[1,2,32,16,128]{4,3,2,1,0:T(8,128)(2,1)} %get-tuple-element.104), channel_id=1, source_target_pairs={{0,4},{1,5},{2,6},{3,7},{4,0},{5,1},{6,2},{7,3},{8,12},{9,13},{10,... | collective-permute-start | bytes 786440 | tf_op jit(solution)/shard_map/ppermute | solution.py:561
  58.8 15.7 %collective-permute-start.4 = (bf16[1,2,32,16,128]{4,3,2,1,0:T(8,128)(2,1)}, bf16[1,2,32,16,128]{4,3,2,1,0:T(8,128)(2,1)}, u32[]{:S(2)}, u32[]{:S(2)}) collective-permute-start(bf16[1,2,32,16,128]{4,3,2,1,0:T(8,128)(2,1)} %get-tuple-element.105), channel_id=1, source_target_pairs={{0,5},{1,6},{2,7},{3,0},{4,1},{5,2},{6,3},{7,4},{8,13},{9,14},{10,... | collective-permute-start | bytes 786440 | tf_op jit(solution)/shard_map/ppermute | solution.py:561
  69.1 36.7 %collective-permute-start.21 = (bf16[1,2,32,32,128]{4,3,2,1,0:T(8,128)(2,1)}, bf16[1,2,32,32,128]{4,3,2,1,0:T(8,128)(2,1)}, u32[]{:S(2)}, u32[]{:S(2)}) collective-permute-start(bf16[1,2,32,32,128]{4,3,2,1,0:T(8,128)(2,1)} %get-tuple-element.129), channel_id=1, source_target_pairs={{0,1},{1,2},{2,3},{3,4},{4,5},{5,6},{6,7},{7,0},{8,9},{9,10},{10,1... | collective-permute-start | bytes 1572872 | tf_op jit(solution)/shard_map/ppermute | solution.py:561
  69.1 36.6 %collective-permute-start.22 = (bf16[1,2,32,32,128]{4,3,2,1,0:T(8,128)(2,1)}, bf16[1,2,32,32,128]{4,3,2,1,0:T(8,128)(2,1)}, u32[]{:S(2)}, u32[]{:S(2)}) collective-permute-start(bf16[1,2,32,32,128]{4,3,2,1,0:T(8,128)(2,1)} %get-tuple-element.130), channel_id=1, source_target_pairs={{0,2},{1,3},{2,4},{3,5},{4,6},{5,7},{6,0},{7,1},{8,10},{9,11},{10,... | collective-permute-start | bytes 1572872 | tf_op jit(solution)/shard_map/ppermute | solution.py:561
  72.9 33.8 %collective-permute-start.23 = (bf16[1,2,32,32,128]{4,3,2,1,0:T(8,128)(2,1)}, bf16[1,2,32,32,128]{4,3,2,1,0:T(8,128)(2,1)}, u32[]{:S(2)}, u32[]{:S(2)}) collective-permute-start(bf16[1,2,32,32,128]{4,3,2,1,0:T(8,128)(2,1)} %get-tuple-element.131), channel_id=1, source_target_pairs={{0,3},{1,4},{2,5},{3,6},{4,7},{5,0},{6,1},{7,2},{8,11},{9,12},{10,... | collective-permute-start | bytes 1572872 | tf_op jit(solution)/shard_map/ppermute | solution.py:561
  73.7 28.1 %collective-permute-start.5 = (bf16[1,2,32,16,128]{4,3,2,1,0:T(8,128)(2,1)}, bf16[1,2,32,16,128]{4,3,2,1,0:T(8,128)(2,1)}, u32[]{:S(2)}, u32[]{:S(2)}) collective-permute-start(bf16[1,2,32,16,128]{4,3,2,1,0:T(8,128)(2,1)} %get-tuple-element.106), channel_id=1, source_target_pairs={{0,6},{1,7},{2,0},{3,1},{4,2},{5,3},{6,4},{7,5},{8,14},{9,15},{10,... | collective-permute-start | bytes 786440 | tf_op jit(solution)/shard_map/ppermute | solution.py:561
  74.5 30.6 %collective-permute-start.6 = (bf16[1,2,32,16,128]{4,3,2,1,0:T(8,128)(2,1)}, bf16[1,2,32,16,128]{4,3,2,1,0:T(8,128)(2,1)}, u32[]{:S(2)}, u32[]{:S(2)}) collective-permute-start(bf16[1,2,32,16,128]{4,3,2,1,0:T(8,128)(2,1)} %get-tuple-element.107), channel_id=1, source_target_pairs={{0,7},{1,0},{2,1},{3,2},{4,3},{5,4},{6,5},{7,6},{8,15},{9,8},{10,9... | collective-permute-start | bytes 786440 | tf_op jit(solution)/shard_map/ppermute | solution.py:561
  101.8 29.0 %collective-permute-start.24 = (bf16[1,2,32,32,128]{4,3,2,1,0:T(8,128)(2,1)}, bf16[1,2,32,32,128]{4,3,2,1,0:T(8,128)(2,1)}, u32[]{:S(2)}, u32[]{:S(2)}) collective-permute-start(bf16[1,2,32,32,128]{4,3,2,1,0:T(8,128)(2,1)} %get-tuple-element.132), channel_id=1, source_target_pairs={{0,4},{1,5},{2,6},{3,7},{4,0},{5,1},{6,2},{7,3},{8,12},{9,13},{10,... | collective-permute-start | bytes 1572872 | tf_op jit(solution)/shard_map/ppermute | solution.py:561
  105.0 31.2 %collective-permute-start.25 = (bf16[1,2,32,32,128]{4,3,2,1,0:T(8,128)(2,1)}, bf16[1,2,32,32,128]{4,3,2,1,0:T(8,128)(2,1)}, u32[]{:S(2)}, u32[]{:S(2)}) collective-permute-start(bf16[1,2,32,32,128]{4,3,2,1,0:T(8,128)(2,1)} %get-tuple-element.133), channel_id=1, source_target_pairs={{0,5},{1,6},{2,7},{3,0},{4,1},{5,2},{6,3},{7,4},{8,13},{9,14},{10,... | collective-permute-start | bytes 1572872 | tf_op jit(solution)/shard_map/ppermute | solution.py:561
  105.8 33.8 %collective-permute-start.26 = (bf16[1,2,32,32,128]{4,3,2,1,0:T(8,128)(2,1)}, bf16[1,2,32,32,128]{4,3,2,1,0:T(8,128)(2,1)}, u32[]{:S(2)}, u32[]{:S(2)}) collective-permute-start(bf16[1,2,32,32,128]{4,3,2,1,0:T(8,128)(2,1)} %get-tuple-element.134), channel_id=1, source_target_pairs={{0,6},{1,7},{2,0},{3,1},{4,2},{5,3},{6,4},{7,5},{8,14},{9,15},{10,... | collective-permute-start | bytes 1572872 | tf_op jit(solution)/shard_map/ppermute | solution.py:561
  105.8 34.1 %collective-permute-start.27 = (bf16[1,2,32,32,128]{4,3,2,1,0:T(8,128)(2,1)}, bf16[1,2,32,32,128]{4,3,2,1,0:T(8,128)(2,1)}, u32[]{:S(2)}, u32[]{:S(2)}) collective-permute-start(bf16[1,2,32,32,128]{4,3,2,1,0:T(8,128)(2,1)} %get-tuple-element.135), channel_id=1, source_target_pairs={{0,7},{1,0},{2,1},{3,2},{4,3},{5,4},{6,5},{7,6},{8,15},{9,8},{10,9... | collective-permute-start | bytes 1572872 | tf_op jit(solution)/shard_map/ppermute | solution.py:561
  106.7 37.5 %collective-permute-start.28 = (bf16[1,2,32,32,128]{4,3,2,1,0:T(8,128)(2,1)}, bf16[1,2,32,32,128]{4,3,2,1,0:T(8,128)(2,1)}, u32[]{:S(2)}, u32[]{:S(2)}) collective-permute-start(bf16[1,2,32,32,128]{4,3,2,1,0:T(8,128)(2,1)} %get-tuple-element.149), channel_id=1, source_target_pairs={{0,1},{1,2},{2,3},{3,4},{4,5},{5,6},{6,7},{7,0},{8,9},{9,10},{10,1... | collective-permute-start | bytes 1572872 | tf_op jit(solution)/shard_map/ppermute | solution.py:561
  130.8 36.7 %collective-permute-start.29 = (bf16[1,2,32,32,128]{4,3,2,1,0:T(8,128)(2,1)}, bf16[1,2,32,32,128]{4,3,2,1,0:T(8,128)(2,1)}, u32[]{:S(2)}, u32[]{:S(2)}) collective-permute-start(bf16[1,2,32,32,128]{4,3,2,1,0:T(8,128)(2,1)} %get-tuple-element.150), channel_id=1, source_target_pairs={{0,2},{1,3},{2,4},{3,5},{4,6},{5,7},{6,0},{7,1},{8,10},{9,11},{10,... | collective-permute-start | bytes 1572872 | tf_op jit(solution)/shard_map/ppermute | solution.py:561
  136.3 31.3 %collective-permute-start.30 = (bf16[1,2,32,32,128]{4,3,2,1,0:T(8,128)(2,1)}, bf16[1,2,32,32,128]{4,3,2,1,0:T(8,128)(2,1)}, u32[]{:S(2)}, u32[]{:S(2)}) collective-permute-start(bf16[1,2,32,32,128]{4,3,2,1,0:T(8,128)(2,1)} %get-tuple-element.151), channel_id=1, source_target_pairs={{0,3},{1,4},{2,5},{3,6},{4,7},{5,0},{6,1},{7,2},{8,11},{9,12},{10,... | collective-permute-start | bytes 1572872 | tf_op jit(solution)/shard_map/ppermute | solution.py:561
  139.6 43.8 %collective-permute-start.31 = (bf16[1,2,32,32,128]{4,3,2,1,0:T(8,128)(2,1)}, bf16[1,2,32,32,128]{4,3,2,1,0:T(8,128)(2,1)}, u32[]{:S(2)}, u32[]{:S(2)}) collective-permute-start(bf16[1,2,32,32,128]{4,3,2,1,0:T(8,128)(2,1)} %get-tuple-element.152), channel_id=1, source_target_pairs={{0,4},{1,5},{2,6},{3,7},{4,0},{5,1},{6,2},{7,3},{8,12},{9,13},{10,... | collective-permute-start | bytes 1572872 | tf_op jit(solution)/shard_map/ppermute | solution.py:561
  139.9 50.9 %collective-permute-start.32 = (bf16[1,2,32,32,128]{4,3,2,1,0:T(8,128)(2,1)}, bf16[1,2,32,32,128]{4,3,2,1,0:T(8,128)(2,1)}, u32[]{:S(2)}, u32[]{:S(2)}) collective-permute-start(bf16[1,2,32,32,128]{4,3,2,1,0:T(8,128)(2,1)} %get-tuple-element.153), channel_id=1, source_target_pairs={{0,5},{1,6},{2,7},{3,0},{4,1},{5,2},{6,3},{7,4},{8,13},{9,14},{10,... | collective-permute-start | bytes 1572872 | tf_op jit(solution)/shard_map/ppermute | solution.py:561
  144.2 46.5 %collective-permute-start.33 = (bf16[1,2,32,32,128]{4,3,2,1,0:T(8,128)(2,1)}, bf16[1,2,32,32,128]{4,3,2,1,0:T(8,128)(2,1)}, u32[]{:S(2)}, u32[]{:S(2)}) collective-permute-start(bf16[1,2,32,32,128]{4,3,2,1,0:T(8,128)(2,1)} %get-tuple-element.154), channel_id=1, source_target_pairs={{0,6},{1,7},{2,0},{3,1},{4,2},{5,3},{6,4},{7,5},{8,14},{9,15},{10,... | collective-permute-start | bytes 1572872 | tf_op jit(solution)/shard_map/ppermute | solution.py:561
  167.5 44.7 %collective-permute-start.34 = (bf16[1,2,32,32,128]{4,3,2,1,0:T(8,128)(2,1)}, bf16[1,2,32,32,128]{4,3,2,1,0:T(8,128)(2,1)}, u32[]{:S(2)}, u32[]{:S(2)}) collective-permute-start(bf16[1,2,32,32,128]{4,3,2,1,0:T(8,128)(2,1)} %get-tuple-element.155), channel_id=1, source_target_pairs={{0,7},{1,0},{2,1},{3,2},{4,3},{5,4},{6,5},{7,6},{8,15},{9,8},{10,9... | collective-permute-start | bytes 1572872 | tf_op jit(solution)/shard_map/ppermute | solution.py:561
  167.6 47.5 %collective-permute-start.35 = (bf16[1,2,32,32,128]{4,3,2,1,0:T(8,128)(2,1)}, bf16[1,2,32,32,128]{4,3,2,1,0:T(8,128)(2,1)}, u32[]{:S(2)}, u32[]{:S(2)}) collective-permute-start(bf16[1,2,32,32,128]{4,3,2,1,0:T(8,128)(2,1)} %get-tuple-element.166), channel_id=1, source_target_pairs={{0,1},{1,2},{2,3},{3,4},{4,5},{5,6},{6,7},{7,0},{8,9},{9,10},{10,1... | collective-permute-start | bytes 1572872 | tf_op jit(solution)/shard_map/ppermute | solution.py:561
  183.4 40.8 %collective-permute-start.36 = (bf16[1,2,32,32,128]{4,3,2,1,0:T(8,128)(2,1)}, bf16[1,2,32,32,128]{4,3,2,1,0:T(8,128)(2,1)}, u32[]{:S(2)}, u32[]{:S(2)}) collective-permute-start(bf16[1,2,32,32,128]{4,3,2,1,0:T(8,128)(2,1)} %get-tuple-element.167), channel_id=1, source_target_pairs={{0,2},{1,3},{2,4},{3,5},{4,6},{5,7},{6,0},{7,1},{8,10},{9,11},{10,... | collective-permute-start | bytes 1572872 | tf_op jit(solution)/shard_map/ppermute | solution.py:561
  190.8 33.4 %collective-permute-start.37 = (bf16[1,2,32,32,128]{4,3,2,1,0:T(8,128)(2,1)}, bf16[1,2,32,32,128]{4,3,2,1,0:T(8,128)(2,1)}, u32[]{:S(2)}, u32[]{:S(2)}) collective-permute-start(bf16[1,2,32,32,128]{4,3,2,1,0:T(8,128)(2,1)} %get-tuple-element.168), channel_id=1, source_target_pairs={{0,3},{1,4},{2,5},{3,6},{4,7},{5,0},{6,1},{7,2},{8,11},{9,12},{10,... | collective-permute-start | bytes 1572872 | tf_op jit(solution)/shard_map/ppermute | solution.py:561
  190.8 35.1 %collective-permute-start.38 = (bf16[1,2,32,32,128]{4,3,2,1,0:T(8,128)(2,1)}, bf16[1,2,32,32,128]{4,3,2,1,0:T(8,128)(2,1)}, u32[]{:S(2)}, u32[]{:S(2)}) collective-permute-start(bf16[1,2,32,32,128]{4,3,2,1,0:T(8,128)(2,1)} %get-tuple-element.169), channel_id=1, source_target_pairs={{0,4},{1,5},{2,6},{3,7},{4,0},{5,1},{6,2},{7,3},{8,12},{9,13},{10,... | collective-permute-start | bytes 1572872 | tf_op jit(solution)/shard_map/ppermute | solution.py:561
  212.2 34.5 %collective-permute-start.39 = (bf16[1,2,32,32,128]{4,3,2,1,0:T(8,128)(2,1)}, bf16[1,2,32,32,128]{4,3,2,1,0:T(8,128)(2,1)}, u32[]{:S(2)}, u32[]{:S(2)}) collective-permute-start(bf16[1,2,32,32,128]{4,3,2,1,0:T(8,128)(2,1)} %get-tuple-element.170), channel_id=1, source_target_pairs={{0,5},{1,6},{2,7},{3,0},{4,1},{5,2},{6,3},{7,4},{8,13},{9,14},{10,... | collective-permute-start | bytes 1572872 | tf_op jit(solution)/shard_map/ppermute | solution.py:561
  215.1 40.5 %collective-permute-start.40 = (bf16[1,2,32,32,128]{4,3,2,1,0:T(8,128)(2,1)}, bf16[1,2,32,32,128]{4,3,2,1,0:T(8,128)(2,1)}, u32[]{:S(2)}, u32[]{:S(2)}) collective-permute-start(bf16[1,2,32,32,128]{4,3,2,1,0:T(8,128)(2,1)} %get-tuple-element.171), channel_id=1, source_target_pairs={{0,6},{1,7},{2,0},{3,1},{4,2},{5,3},{6,4},{7,5},{8,14},{9,15},{10,... | collective-permute-start | bytes 1572872 | tf_op jit(solution)/shard_map/ppermute | solution.py:561
  224.1 31.5 %collective-permute-start.41 = (bf16[1,2,32,32,128]{4,3,2,1,0:T(8,128)(2,1)}, bf16[1,2,32,32,128]{4,3,2,1,0:T(8,128)(2,1)}, u32[]{:S(2)}, u32[]{:S(2)}) collective-permute-start(bf16[1,2,32,32,128]{4,3,2,1,0:T(8,128)(2,1)} %get-tuple-element.172), channel_id=1, source_target_pairs={{0,7},{1,0},{2,1},{3,2},{4,3},{5,4},{6,5},{7,6},{8,15},{9,8},{10,9... | collective-permute-start | bytes 1572872 | tf_op jit(solution)/shard_map/ppermute | solution.py:561
  224.1 31.5 %collective-permute-start.14 = (bf16[2,1024,128]{2,1,0:T(8,128)(2,1)}, bf16[2,1024,128]{2,1,0:T(8,128)(2,1)}, u32[]{:S(2)}, u32[]{:S(2)}) collective-permute-start(bf16[2,1024,128]{2,1,0:T(8,128)(2,1)} %get-tuple-element.118), channel_id=1, source_target_pairs={{0,1},{1,2},{2,3},{3,4},{4,5},{5,6},{6,7},{7,0},{8,9},{9,10},{10,1... | collective-permute-start | bytes 1572872 | tf_op jit(solution)/shard_map/ppermute | solution.py:561
  225.9 43.9 %collective-permute-start.15 = (bf16[2,1024,128]{2,1,0:T(8,128)(2,1)}, bf16[2,1024,128]{2,1,0:T(8,128)(2,1)}, u32[]{:S(2)}, u32[]{:S(2)}) collective-permute-start(bf16[2,1024,128]{2,1,0:T(8,128)(2,1)} %get-tuple-element.119), channel_id=1, source_target_pairs={{0,2},{1,3},{2,4},{3,5},{4,6},{5,7},{6,0},{7,1},{8,10},{9,11},{10,... | collective-permute-start | bytes 1572872 | tf_op jit(solution)/shard_map/ppermute | solution.py:561
  246.7 43.9 %collective-permute-start.16 = (bf16[2,1024,128]{2,1,0:T(8,128)(2,1)}, bf16[2,1024,128]{2,1,0:T(8,128)(2,1)}, u32[]{:S(2)}, u32[]{:S(2)}) collective-permute-start(bf16[2,1024,128]{2,1,0:T(8,128)(2,1)} %get-tuple-element.120), channel_id=1, source_target_pairs={{0,3},{1,4},{2,5},{3,6},{4,7},{5,0},{6,1},{7,2},{8,11},{9,12},{10,... | collective-permute-start | bytes 1572872 | tf_op jit(solution)/shard_map/ppermute | solution.py:561
  255.6 37.1 %collective-permute-start.17 = (bf16[2,1024,128]{2,1,0:T(8,128)(2,1)}, bf16[2,1024,128]{2,1,0:T(8,128)(2,1)}, u32[]{:S(2)}, u32[]{:S(2)}) collective-permute-start(bf16[2,1024,128]{2,1,0:T(8,128)(2,1)} %get-tuple-element.121), channel_id=1, source_target_pairs={{0,4},{1,5},{2,6},{3,7},{4,0},{5,1},{6,2},{7,3},{8,12},{9,13},{10,... | collective-permute-start | bytes 1572872 | tf_op jit(solution)/shard_map/ppermute | solution.py:561
  255.6 37.2 %collective-permute-start.18 = (bf16[2,1024,128]{2,1,0:T(8,128)(2,1)}, bf16[2,1024,128]{2,1,0:T(8,128)(2,1)}, u32[]{:S(2)}, u32[]{:S(2)}) collective-permute-start(bf16[2,1024,128]{2,1,0:T(8,128)(2,1)} %get-tuple-element.122), channel_id=1, source_target_pairs={{0,5},{1,6},{2,7},{3,0},{4,1},{5,2},{6,3},{7,4},{8,13},{9,14},{10,... | collective-permute-start | bytes 1572872 | tf_op jit(solution)/shard_map/ppermute | solution.py:561
  255.7 37.1 %collective-permute-start.19 = (bf16[2,1024,128]{2,1,0:T(8,128)(2,1)}, bf16[2,1024,128]{2,1,0:T(8,128)(2,1)}, u32[]{:S(2)}, u32[]{:S(2)}) collective-permute-start(bf16[2,1024,128]{2,1,0:T(8,128)(2,1)} %get-tuple-element.123), channel_id=1, source_target_pairs={{0,6},{1,7},{2,0},{3,1},{4,2},{5,3},{6,4},{7,5},{8,14},{9,15},{10,... | collective-permute-start | bytes 1572872 | tf_op jit(solution)/shard_map/ppermute | solution.py:561
  269.8 23.0 %collective-permute-start.20 = (bf16[2,1024,128]{2,1,0:T(8,128)(2,1)}, bf16[2,1024,128]{2,1,0:T(8,128)(2,1)}, u32[]{:S(2)}, u32[]{:S(2)}) collective-permute-start(bf16[2,1024,128]{2,1,0:T(8,128)(2,1)} %get-tuple-element.124), channel_id=1, source_target_pairs={{0,7},{1,0},{2,1},{3,2},{4,3},{5,4},{6,5},{7,6},{8,15},{9,8},{10,9... | collective-permute-start | bytes 1572872 | tf_op jit(solution)/shard_map/ppermute | solution.py:561
  292.8 148.4 %copy-start = (f32[2,32,64,128]{3,2,1,0:T(8,128)S(1)}, f32[2,32,64,128]{3,2,1,0:T(8,128)}, u32[]{:S(2)}) copy-start(f32[2,32,64,128]{3,2,1,0:T(8,128)} %constant_dynamic-slice_fusion.image) | copy-start | bytes 6291460
  292.8 148.4 %copy-start.1 = (f32[2,32,64,128]{3,2,1,0:T(8,128)S(1)}, f32[2,32,64,128]{3,2,1,0:T(8,128)}, u32[]{:S(2)}) copy-start(f32[2,32,64,128]{3,2,1,0:T(8,128)} %auxiliary.1) | copy-start | bytes 6291460
  292.8 148.4 %copy-start.2 = (f32[2,32,64,128]{3,2,1,0:T(8,128)S(1)}, f32[2,32,64,128]{3,2,1,0:T(8,128)}, u32[]{:S(2)}) copy-start(f32[2,32,64,128]{3,2,1,0:T(8,128)} %dual.1) | copy-start | bytes 6291460

commit v7 on v6

--- a/solution.py
+++ b/solution.py
@@ -13,7 +13,6 @@
 penalty = 1.0
 threshold = 0.3
 VMEM_LIMIT = 67000000
-LAG = 3
 F32 = jnp.float32
 BF16 = jnp.bfloat16
 
@@ -112,12 +111,12 @@
                         outs[off][coil, p, 2 * k + h] = flat[pl.ds(base + h * pitch(xp), xp), :].astype(BF16)
                     return carry
 
-                lax.fori_loop(0, kl // 2, settle, 0, unroll=4)
+                lax.fori_loop(0, kl // 2, settle, 0, unroll=8)
 
 
 def forward_call(table, image, sensitivity, batch, first, xp, n, kl):
     _, _, _, length, depth = sensitivity.shape
-    rows = 8 if xp % 8 == 0 else xp
+    rows = 4 if xp % 4 == 0 else xp
     steps, skip = xp // rows, first // rows
     shape = (len(batch), 2, kl, xp, depth)
     return pl.pallas_call(
@@ -316,10 +315,70 @@
     )(offsets, counts, fwd, inv, blocks, samples, *pieces)
 
 
-def finish_kernel(n, shares, kl, xl, chunks, sent, table_ref, sens, *refs):
+def haar_rows(first, second):
+    even = lax.broadcasted_iota(jnp.int32, first.shape, 0) % 2 == 0
+    rows = first.shape[0]
+
+    def along(v):
+        after = pltpu.roll(v, rows - 1, 0)
+        ahead = pltpu.roll(v, 1, 0)
+        return jnp.where(even, v + after, ahead - v) * 0.5
+
+    return along(first + second), along(first - second)
+
+
+def update_pair(m, image, gradient, auxiliary, dual, image_out, aux_out, dual_out):
+    coeffs = []
+    for p in range(2):
+        target = haar_rows(auxiliary[p, m] - dual[p, m], auxiliary[p, m + 1] - dual[p, m + 1])
+        following = []
+        for h in range(2):
+            current = image[p, m + h]
+            value = current - step_size * (gradient[p, m + h] + penalty * (current - target[h]))
+            following.append(value)
+        for h in range(2):
+            image_out[p, m + h] = following[h]
+        spread = haar_rows(*following)
+        coeffs.append([spread[h] + dual[p, m + h] for h in range(2)])
+    for h in range(2):
+        re, im = coeffs[0][h], coeffs[1][h]
+        magnitude = jnp.sqrt(re * re + im * im)
+        factor = jnp.maximum(1.0 - threshold / jnp.maximum(magnitude, threshold), 0.0)
+        for p, value in enumerate((re, im)):
+            kept = value * factor
+            aux_out[p, m + h] = kept
+            dual_out[p, m + h] = value - kept
+
+
+def store_kernel(*refs):
+    count = len(refs) // 2
+    copies = [
+        pltpu.make_async_copy(refs[k].at[p], refs[count + k].at[p], refs[-1].at[k, p])
+        for k in range(count)
+        for p in range(2)
+    ]
+    for copy in copies:
+        copy.start()
+    for copy in copies:
+        copy.wait()
+
+
+def store_call(*values):
+    return pl.pallas_call(
+        store_kernel,
+        in_specs=[pl.BlockSpec(memory_space=pltpu.VMEM)] * len(values),
+        out_specs=[HBM] * len(values),
+        out_shape=[jax.ShapeDtypeStruct(value.shape, value.dtype) for value in values],
+        scratch_shapes=[pltpu.SemaphoreType.DMA((len(values), 2))],
+        compiler_params=params(2**24),
+        name="store",
+    )(*values)
+
+
+def finish_kernel(n, shares, kl, xl, chunks, sent, table_ref, sens, image, auxiliary, dual, *refs):
     coils = sens.shape[0]
     backs, refs = [refs[k * n : (k + 1) * n] for k in range(coils)], refs[coils * n :]
-    out, table, landing, sens_v, grad, got, recv, send, local, grad_recv, grad_send, *wide = refs
+    image_out, aux_out, dual_out, table, held, landing, sens_v, grad, got, recv, send, local, grad_recv, grad_send, *wide = refs
     ready = coils - sent
     length = n * kl
     depth = landing.shape[-1]
@@ -360,7 +419,10 @@
         return carry
 
     lax.fori_loop(0, chunks, send_band, 0)
+    columns = pl.ds(pl.multiple_of(mine * share, share), share)
     copies = [pltpu.make_async_copy(table_ref, table, local.at[coils * n + coils])]
+    for k, source in enumerate((image.at[:, :, columns], auxiliary, dual)):
+        copies.append(pltpu.make_async_copy(source, held.at[k], local.at[coils * n + coils + 1 + k]))
     for k in range(coils):
         for off in range(n if k < ready else 1):
             origin = landing.at[k, behind(me, off, n)]
@@ -371,21 +433,21 @@
     for copy in copies:
         copy.wait()
 
-    def add_band(j, carry):
+    def add_band(j):
         arrived = got.at[0 : shares - 1, :, pl.ds(j * rows, rows)]
         pltpu.make_async_copy(arrived, arrived, grad_recv.at[j]).wait()
-
-        def line(i, carry):
+        for i in range(rows):
             x = j * rows + i
             for p in range(2):
                 value = grad[mine, p, x].astype(F32)
                 for off in range(1, shares):
                     value += got[lax.rem(mine + off, shares), p, x].astype(F32)
-                out[p, x] = value
-            return carry
-
-        lax.fori_loop(0, rows, line, 0)
-        return carry
+                image_out[p, x] = value
+
+    def settle(m):
+        for k in range(2 // rows):
+            add_band(2 // rows * m + k)
+        update_pair(2 * m, held.at[0], image_out, held.at[1], held.at[2], image_out, aux_out, dual_out)
 
     def do_band(j, carry):
         where = pl.ds(pl.multiple_of(j * band, band), band)
@@ -443,21 +505,21 @@
                 device_id_type=pl.DeviceIdType.MESH,
             ).start()
 
-        @pl.when(j >= LAG)
+        @pl.when((j % 2 == 1) & (j >= 3))
         def settled():
-            add_band(j - LAG, 0)
+            settle((j - 3) // 2)
 
         return carry
 
     lax.fori_loop(0, chunks, do_band, 0)
-    lax.fori_loop(max(chunks - LAG, 0), chunks, add_band, 0)
+    settle(chunks // 2 - 1)
     gone = landing.at[ready:coils, 0 : n - 1]
     pltpu.make_async_copy(gone, gone, send).wait()
     gone = got.at[0 : shares - 1]
     pltpu.make_async_copy(gone, gone, grad_send).wait()
 
 
-def finish_call(table, backs, sent, sensitivity, shares, n, kl):
+def finish_call(table, backs, sent, sensitivity, image, auxiliary, dual, shares, n, kl):
     coils, _, xl, length, depth = sensitivity.shape
     chunks = xl
     rows = xl // chunks
@@ -465,84 +527,29 @@
     vmem = pl.BlockSpec(memory_space=pltpu.VMEM)
     scratch = [
         pltpu.VMEM(table.shape, BF16),
+        pltpu.VMEM((3, 2, xl, share, depth), F32),
         pltpu.VMEM((coils, n, 2, xl * kl, depth), BF16),
         pltpu.VMEM(sensitivity.shape, BF16),
         pltpu.VMEM((shares, 2, xl, share, depth), BF16),
         pltpu.VMEM((shares, 2, xl, share, depth), BF16),
         pltpu.SemaphoreType.DMA((chunks,)),
         pltpu.SemaphoreType.DMA,
-        pltpu.SemaphoreType.DMA((coils * n + coils + 1,)),
+        pltpu.SemaphoreType.DMA((coils * n + coils + 4,)),
         pltpu.SemaphoreType.DMA((chunks,)),
         pltpu.SemaphoreType.DMA,
     ]
     if kl % 16:
         scratch.append(pltpu.VMEM((coils, n, 2, rows * kl, depth), F32))
-    limit = VMEM_LIMIT - 32 * xl * share * depth
+    limit = VMEM_LIMIT - 26 * xl * share * depth
     return pl.pallas_call(
         functools.partial(finish_kernel, n, shares, kl, xl, chunks, sent),
-        in_specs=[HBM] * (2 + coils * n),
-        out_specs=vmem,
-        out_shape=pltpu.VMEM((2, xl, share, depth), F32),
+        in_specs=[HBM] * (5 + coils * n),
+        out_specs=[vmem] * 3,
+        out_shape=[pltpu.VMEM((2, xl, share, depth), F32)] * 3,
         scratch_shapes=scratch,
         compiler_params=params(limit, collective_id=0, has_side_effects=True),
         name="finish",
-    )(table, sensitivity, *[piece for back in backs for piece in back])
-
-
-def haar_rows(first, second):
-    even = lax.broadcasted_iota(jnp.int32, first.shape, 0) % 2 == 0
-    rows = first.shape[0]
-
-    def along(v):
-        after = pltpu.roll(v, rows - 1, 0)
-        ahead = pltpu.roll(v, 1, 0)
-        return jnp.where(even, v + after, ahead - v) * 0.5
-
-    return along(first + second), along(first - second)
-
-
-def update_kernel(image, gradient, auxiliary, dual, image_out, aux_out, dual_out):
-    rows = image.shape[1]
-    for m in range(0, rows, 2):
-        coeffs = []
-        for p in range(2):
-            target = haar_rows(
-                auxiliary[p, m] - dual[p, m], auxiliary[p, m + 1] - dual[p, m + 1]
-            )
-            following = []
-            for h in range(2):
-                current = image[p, m + h]
-                value = current - step_size * (
-                    gradient[p, m + h].astype(F32) + penalty * (current - target[h])
-                )
-                image_out[p, m + h] = value
-                following.append(value)
-            spread = haar_rows(*following)
-            coeffs.append([spread[h] + dual[p, m + h] for h in range(2)])
-        for h in range(2):
-            re, im = coeffs[0][h], coeffs[1][h]
-            magnitude = jnp.sqrt(re * re + im * im)
-            factor = jnp.maximum(1.0 - threshold / jnp.maximum(magnitude, threshold), 0.0)
-            for p, value in enumerate((re, im)):
-                kept = value * factor
-                aux_out[p, m + h] = kept
-                dual_out[p, m + h] = value - kept
-
-
-def update_call(image, gradient, auxiliary, dual):
-    _, xl, share, depth = auxiliary.shape
-    rows = 8 if xl % 8 == 0 else 2
-    plain = pl.BlockSpec((2, rows, share, depth), lambda i: (0, i, 0, 0))
-    shape = jax.ShapeDtypeStruct(auxiliary.shape, F32)
-    return pl.pallas_call(
-        update_kernel,
-        grid=(xl // rows,),
-        in_specs=[plain, plain, plain, plain],
-        out_specs=[plain, plain, plain],
-        out_shape=[shape, shape, shape],
-        compiler_params=params(VMEM_LIMIT - 128 * xl * share * depth),
-        name="update",
-    )(image, gradient, auxiliary, dual)
+    )(table, sensitivity, image, auxiliary, dual, *[piece for back in backs for piece in back])
 
 
 def body(image, sensitivity, blocks, samples, offsets, counts, auxiliary, scaled_dual):
@@ -573,7 +580,6 @@
             x_fwd, x_inv, pieces, parts_of(c), place, blocks, sorted_samples, offsets, counts, c, n, kl, xl
         )
 
-    share = length_y // shares
     pieces, tiles, table = [], [], y_fwd
     for batch in batches:
         c = batch[0]
@@ -583,9 +589,8 @@
             table, half[0] = lax.optimization_barrier((table, half[0]))
             moved += swap(half)
         pieces += [(moved, place) for place in range(len(batch))]
-    table, samples, source = lax.optimization_barrier((table, samples, image))
+    table, samples = lax.optimization_barrier((table, samples))
     sorted_samples = sort_call(samples)
-    current = lax.dynamic_slice_in_dim(source, lax.axis_index("coil") * share, share, 2)
     for c in range(coils):
         arrived, place = pieces[c]
         if c:
@@ -596,8 +601,10 @@
     backs = list(tiles)
     for c in range(early):
         backs[c] = swap(tiles[c])
-    gradient = finish_call(y_inv, backs, coils - early, sensitivity, shares, n, kl)
-    return tuple(update_call(current, gradient, auxiliary, scaled_dual))
+    results = finish_call(
+        y_inv, backs, coils - early, sensitivity, image, auxiliary, scaled_dual, shares, n, kl
+    )
+    return tuple(store_call(*results))
 
 
 def solution(mesh):

time: 449 us -> 438 us (0.976)
  starting transfers between devices: 91.4 us -> 77.2 us
    ppermute x42, starting transfers between devices: 91.4 us -> 77.2 us  [swap(): lax.ppermute(parts[off], 'slab', [(i, ahead(i, off, n)) for i in range(n)])]
  transfers between devices with their start and end apart: 42 -> 42, of which waited for: 9 -> 10; matrix products, arithmetic and copies ran while one was open for 1% -> 0% of each run, Pallas kernels for 27% -> 30%
where the time goes in v7:
time: 438 us; the launch traced here: 435 us
  Pallas kernels  290 us (66%)
  starting transfers between devices  77.2 us (18%)
  waiting for transfers between devices  65.8 us (15%)
    pallas_call x1, Pallas kernels, finish_call(): pl.pallas_call(functools.partial(finish_kernel, n, shares, kl, xl, chunks...  149 us
    pallas_call x4, Pallas kernels, tile_call(): pl.pallas_call(functools.partial(tile_kernel, n, kl, xl, cells // kl, par...  83.2 us
    ppermute x42, starting transfers between devices, swap(): lax.ppermute(parts[off], 'slab', [(i, ahead(i, off, n)) for i in range(n)])  77.2 us
    ppermute x42, waiting for transfers between devices, swap(): lax.ppermute(parts[off], 'slab', [(i, ahead(i, off, n)) for i in range(n)])  65.8 us
    pallas_call x5, Pallas kernels, forward_call(): pl.pallas_call(functools.partial(forward_kernel, n, kl, xp), grid=(len(ba...  47.5 us
  transfers between devices with their start and end apart: 42, of which 10 were waited for; matrix products, arithmetic and copies ran while one was open for 0% of the time, Pallas kernels for 30%

profile of v7, /device:TPU:9, one launch (start us, length us, event | category | flops | bytes accessed | tf_op | source)
XLA Modules:
  0.0 434.9 jit_solution(12515872481905772543)
XLA Ops:
  0.6 6.5 %forward.5 = (bf16[1,2,32,16,128]{4,3,2,1,0:T(8,128)(2,1)}, bf16[1,2,32,16,128]{4,3,2,1,0:T(8,128)(2,1)}, bf16[1,2,32,16,128]{4,3,2,1,0:T(8,128)(2,1)}, bf16[1,2...) custom-call(bf16[512,512]{1,0:T(8,128)(2,1)} %constant.11.table.fwd,, ...), custom_call_target="tpu_custom_call" | custom-call | flops 1073741824 | bytes 6291456 | tf_op jit(solution)/shard_map/forward/pallas_call | solution.py:122
  7.1 1.8 collective-permute-start
  8.9 1.2 collective-permute-start.1
  10.1 0.4 collective-permute-start.2
  10.4 0.2 collective-permute-start.3
  10.7 2.6 collective-permute-start.4
  13.2 1.4 collective-permute-done.refs_1_
  14.7 1.2 collective-permute-start.5
  15.9 6.1 %collective-permute-done.1.refs_2_ = bf16[1,2,32,16,128]{4,3,2,1,0:T(8,128)(2,1)} collective-permute-done((bf16[1,2,32,16,128]{4,3,2,1,0:T(8,128)(2,1)}, bf16[1,2,32,16,128]{4,3,2,1,0:T(8,128)(2,1)}, u32[]{:S(2)}, u32[]{:S(2)}) %collective-permute-start.1) | collective-permute-done | bytes 262176 | tf_op jit(solution)/shard_map/ppermute | solution.py:568
  22.0 6.5 %forward.6 = (bf16[1,2,32,16,128]{4,3,2,1,0:T(8,128)(2,1)}, bf16[1,2,32,16,128]{4,3,2,1,0:T(8,128)(2,1)}, bf16[1,2,32,16,128]{4,3,2,1,0:T(8,128)(2,1)}, bf16[1,2...) custom-call(bf16[512,512]{1,0:T(8,128)(2,1)} %constant.11.table.fwd,, ...), custom_call_target="tpu_custom_call" | custom-call | flops 1073741824 | bytes 6291456 | tf_op jit(solution)/shard_map/forward/pallas_call | solution.py:122
  28.5 1.8 collective-permute-start.7
  30.3 3.4 collective-permute-done.3.refs_4_
  33.7 0.1 collective-permute-done.4.refs_5_
  33.8 0.0 collective-permute-start.9
  33.8 2.1 collective-permute-start.10
  35.9 0.0 collective-permute-done.6.refs_7_
  35.9 2.9 collective-permute-start.11
  38.8 11.5 %forward.7 = (bf16[1,2,32,32,128]{4,3,2,1,0:T(8,128)(2,1)}, bf16[1,2,32,32,128]{4,3,2,1,0:T(8,128)(2,1)}, bf16[1,2,32,32,128]{4,3,2,1,0:T(8,128)(2,1)}, bf16[1,2...) custom-call(bf16[512,512]{1,0:T(8,128)(2,1)} %constant.11.table.fwd,, ...), custom_call_target="tpu_custom_call" | custom-call | flops 2147483648 | bytes 12582912 | tf_op jit(solution)/shard_map/forward/pallas_call | solution.py:122
  50.3 0.1 collective-permute-start.21
  50.4 0.0 collective-permute-done.8.refs_10_
  50.4 1.3 collective-permute-start.22
  51.6 0.9 collective-permute-start.23
  52.6 26.2 %collective-permute-done.10.refs_12_ = bf16[1,2,32,16,128]{4,3,2,1,0:T(8,128)(2,1)} collective-permute-done((bf16[1,2,32,16,128]{4,3,2,1,0:T(8,128)(2,1)}, bf16[1,2,32,16,128]{4,3,2,1,0:T(8,128)(2,1)}, u32[]{:S(2)}, u32[]{:S(2)}) %collective-permute-start.10) | collective-permute-done | bytes 262176 | tf_op jit(solution)/shard_map/ppermute | solution.py:568
  78.8 0.0 collective-permute-start.12
  78.8 0.5 collective-permute-done.11.refs_13_
  79.3 11.5 %forward.8 = (bf16[1,2,32,32,128]{4,3,2,1,0:T(8,128)(2,1)}, bf16[1,2,32,32,128]{4,3,2,1,0:T(8,128)(2,1)}, bf16[1,2,32,32,128]{4,3,2,1,0:T(8,128)(2,1)}, bf16[1,2...) custom-call(bf16[512,512]{1,0:T(8,128)(2,1)} %constant.11.table.fwd,, ...), custom_call_target="tpu_custom_call" | custom-call | flops 2147483648 | bytes 12582912 | tf_op jit(solution)/shard_map/forward/pallas_call | solution.py:122
  90.8 1.2 collective-permute-start.24
  91.9 0.0 collective-permute-done.13.refs_15_
  91.9 2.1 collective-permute-start.25
  94.0 0.0 collective-permute-done.21.refs_1_
  94.0 1.8 collective-permute-start.26
  95.8 0.0 collective-permute-done.22.refs_2_
  95.8 0.0 collective-permute-start.27
  95.9 1.7 collective-permute-start.28
  98.2 11.5 %forward.9 = (bf16[1,2,32,32,128]{4,3,2,1,0:T(8,128)(2,1)}, bf16[1,2,32,32,128]{4,3,2,1,0:T(8,128)(2,1)}, bf16[1,2,32,32,128]{4,3,2,1,0:T(8,128)(2,1)}, bf16[1,2...) custom-call(bf16[512,512]{1,0:T(8,128)(2,1)} %constant.11.table.fwd,, ...), custom_call_target="tpu_custom_call" | custom-call | flops 2147483648 | bytes 12582912 | tf_op jit(solution)/shard_map/forward/pallas_call | solution.py:122
  109.8 8.3 %sort.1.sorted_samples = bf16[4,24,128,256]{3,2,1,0:T(8,128)(2,1)} custom-call(bf16[24,1024,128]{2,1,0:T(8,128)(2,1)} %bitcast.1), custom_call_target="tpu_custom_call" | custom-call | flops 3145728 | bytes 12582912 | tf_op jit(solution)/shard_map/sort/pallas_call | solution.py:155
  118.1 9.2 %collective-permute-start.29 = (bf16[1,2,32,32,128]{4,3,2,1,0:T(8,128)(2,1)}, bf16[1,2,32,32,128]{4,3,2,1,0:T(8,128)(2,1)}, u32[]{:S(2)}, u32[]{:S(2)}) collective-permute-start(bf16[1,2,32,32,128]{4,3,2,1,0:T(8,128)(2,1)} %get-tuple-element.149), channel_id=1, source_target_pairs={{0,2},{1,3},{2,4},{3,5},{4,6},{5,7},{6,0},{7,1},{8,10},{9,11},{10,... | collective-permute-start | bytes 1572872 | tf_op jit(solution)/shard_map/ppermute | solution.py:568
  127.2 3.0 collective-permute-start.30
  130.2 0.4 collective-permute-start.31
  130.6 0.0 collective-permute-done.27.refs_7_
  130.6 4.2 collective-permute-start.32
  134.8 0.0 collective-permute-done.28.refs_1_
  134.8 2.6 collective-permute-start.33
  137.4 20.9 %tile.4 = (bf16[2,1024,128]{2,1,0:T(8,128)(2,1)}, bf16[2,1024,128]{2,1,0:T(8,128)(2,1)}, bf16[2,1024,128]{2,1,0:T(8,128)(2,1)}, bf16[2,1024,128]{2,1,0:T(8,128)(...) custom-call(s32[1,24]{1,0:T(1,128)} %offsets.7, ...), custom_call_target="tpu_custom_call" | custom-call | flops 10737418240 | bytes 20971520 | tf_op jit(solution)/shard_map/tile/pallas_call | solution.py:302
  158.2 0.0 collective-permute-done.29.refs_2_
  158.3 0.1 collective-permute-start.34
  158.3 1.7 collective-permute-start.35
  160.1 14.1 %collective-permute-done.31.refs_4_ = bf16[1,2,32,32,128]{4,3,2,1,0:T(8,128)(2,1)} collective-permute-done((bf16[1,2,32,32,128]{4,3,2,1,0:T(8,128)(2,1)}, bf16[1,2,32,32,128]{4,3,2,1,0:T(8,128)(2,1)}, u32[]{:S(2)}, u32[]{:S(2)}) %collective-permute-start.31) | collective-permute-done | bytes 524320 | tf_op jit(solution)/shard_map/ppermute | solution.py:568
  174.1 7.1 %collective-permute-start.36 = (bf16[1,2,32,32,128]{4,3,2,1,0:T(8,128)(2,1)}, bf16[1,2,32,32,128]{4,3,2,1,0:T(8,128)(2,1)}, u32[]{:S(2)}, u32[]{:S(2)}) collective-permute-start(bf16[1,2,32,32,128]{4,3,2,1,0:T(8,128)(2,1)} %get-tuple-element.166), channel_id=1, source_target_pairs={{0,2},{1,3},{2,4},{3,5},{4,6},{5,7},{6,0},{7,1},{8,10},{9,11},{10,... | collective-permute-start | bytes 1572872 | tf_op jit(solution)/shard_map/ppermute | solution.py:568
  181.2 0.9 collective-permute-start.38
  182.1 20.8 %tile.5 = (bf16[2,1024,128]{2,1,0:T(8,128)(2,1)}, bf16[2,1024,128]{2,1,0:T(8,128)(2,1)}, bf16[2,1024,128]{2,1,0:T(8,128)(2,1)}, bf16[2,1024,128]{2,1,0:T(8,128)(...) custom-call(s32[1,24]{1,0:T(1,128)} %offsets.7, ...), custom_call_target="tpu_custom_call" | custom-call | flops 10737418240 | bytes 20971520 | tf_op jit(solution)/shard_map/tile/pallas_call | solution.py:302
  202.9 2.9 collective-permute-start.39
  205.8 8.9 %collective-permute-start.40 = (bf16[1,2,32,32,128]{4,3,2,1,0:T(8,128)(2,1)}, bf16[1,2,32,32,128]{4,3,2,1,0:T(8,128)(2,1)}, u32[]{:S(2)}, u32[]{:S(2)}) collective-permute-start(bf16[1,2,32,32,128]{4,3,2,1,0:T(8,128)(2,1)} %get-tuple-element.170), channel_id=1, source_target_pairs={{0,6},{1,7},{2,0},{3,1},{4,2},{5,3},{6,4},{7,5},{8,14},{9,15},{10,... | collective-permute-start | bytes 1572872 | tf_op jit(solution)/shard_map/ppermute | solution.py:568
  214.8 1.7 collective-permute-start.14
  216.5 20.8 %tile.6 = (bf16[2,1024,128]{2,1,0:T(8,128)(2,1)}, bf16[2,1024,128]{2,1,0:T(8,128)(2,1)}, bf16[2,1024,128]{2,1,0:T(8,128)(2,1)}, bf16[2,1024,128]{2,1,0:T(8,128)(...) custom-call(s32[1,24]{1,0:T(1,128)} %offsets.7, ...), custom_call_target="tpu_custom_call" | custom-call | flops 10737418240 | bytes 20971520 | tf_op jit(solution)/shard_map/tile/pallas_call | solution.py:302
  237.3 8.9 %collective-permute-start.16 = (bf16[2,1024,128]{2,1,0:T(8,128)(2,1)}, bf16[2,1024,128]{2,1,0:T(8,128)(2,1)}, u32[]{:S(2)}, u32[]{:S(2)}) collective-permute-start(bf16[2,1024,128]{2,1,0:T(8,128)(2,1)} %get-tuple-element.119), channel_id=1, source_target_pairs={{0,3},{1,4},{2,5},{3,6},{4,7},{5,0},{6,1},{7,2},{8,11},{9,12},{10,... | collective-permute-start | bytes 1572872 | tf_op jit(solution)/shard_map/ppermute | solution.py:568
  246.2 0.1 collective-permute-start.18
  246.2 2.4 collective-permute-start.19
  248.7 11.7 %collective-permute-done.15.refs_2_ = bf16[2,1024,128]{2,1,0:T(8,128)(2,1)} collective-permute-done((bf16[2,1024,128]{2,1,0:T(8,128)(2,1)}, bf16[2,1024,128]{2,1,0:T(8,128)(2,1)}, u32[]{:S(2)}, u32[]{:S(2)}) %collective-permute-start.15) | collective-permute-done | bytes 524320 | tf_op jit(solution)/shard_map/ppermute | solution.py:568
  260.4 20.8 %tile.7 = (bf16[2,1024,128]{2,1,0:T(8,128)(2,1)}, bf16[2,1024,128]{2,1,0:T(8,128)(2,1)}, bf16[2,1024,128]{2,1,0:T(8,128)(2,1)}, bf16[2,1024,128]{2,1,0:T(8,128)(...) custom-call(s32[1,24]{1,0:T(1,128)} %offsets.7, ...), custom_call_target="tpu_custom_call" | custom-call | flops 10737418240 | bytes 20971520 | tf_op jit(solution)/shard_map/tile/pallas_call | solution.py:302
  281.2 2.1 collective-permute-done.17.refs_4_
  283.3 0.1 collective-permute-done.18.refs_5_
  283.4 148.5 %finish.1 = (f32[2,32,64,128]{3,2,1,0:T(8,128)S(1)}, f32[2,32,64,128]{3,2,1,0:T(8,128)S(1)}, f32[2,32,64,128]{3,2,1,0:T(8,128)S(1)}) custom-call(bf16[512,512]{1,0:T(8,128)(2,1)} %constant.10.inv.table_ref, bf16[4,2,32,256,128]{4,3,2,1,0:T(8,128)(2,1)} %sens.11, f32[2,32,256,128]{3,2,1,0:T(8,128)} %image.11, f32[2,32,64,128]{3,2,1,0:T(8,128)} %auxiliary.1, ...), custom_call_target="tpu_custom_call" | custom-call | tf_op jit(solution)/shard_map/finish/pallas_call | solution.py:544
  432.0 2.7 store.1
  (32 shorter events, 0.1 us)
Async XLA Ops:
  7.1 7.6 %collective-permute-start = (bf16[1,2,32,16,128]{4,3,2,1,0:T(8,128)(2,1)}, bf16[1,2,32,16,128]{4,3,2,1,0:T(8,128)(2,1)}, u32[]{:S(2)}, u32[]{:S(2)}) collective-permute-start(bf16[1,2,32,16,128]{4,3,2,1,0:T(8,128)(2,1)} %get-tuple-element.100), channel_id=1, source_target_pairs={{0,1},{1,2},{2,3},{3,4},{4,5},{5,6},{6,7},{7,0},{8,9},{9,10},{10,1... | collective-permute-start | bytes 786440 | tf_op jit(solution)/shard_map/ppermute | solution.py:568
  8.9 13.1 %collective-permute-start.1 = (bf16[1,2,32,16,128]{4,3,2,1,0:T(8,128)(2,1)}, bf16[1,2,32,16,128]{4,3,2,1,0:T(8,128)(2,1)}, u32[]{:S(2)}, u32[]{:S(2)}) collective-permute-start(bf16[1,2,32,16,128]{4,3,2,1,0:T(8,128)(2,1)} %get-tuple-element.101), channel_id=1, source_target_pairs={{0,2},{1,3},{2,4},{3,5},{4,6},{5,7},{6,0},{7,1},{8,10},{9,11},{10,... | collective-permute-start | bytes 786440 | tf_op jit(solution)/shard_map/ppermute | solution.py:568
  10.1 18.5 %collective-permute-start.2 = (bf16[1,2,32,16,128]{4,3,2,1,0:T(8,128)(2,1)}, bf16[1,2,32,16,128]{4,3,2,1,0:T(8,128)(2,1)}, u32[]{:S(2)}, u32[]{:S(2)}) collective-permute-start(bf16[1,2,32,16,128]{4,3,2,1,0:T(8,128)(2,1)} %get-tuple-element.102), channel_id=1, source_target_pairs={{0,3},{1,4},{2,5},{3,6},{4,7},{5,0},{6,1},{7,2},{8,11},{9,12},{10,... | collective-permute-start | bytes 786440 | tf_op jit(solution)/shard_map/ppermute | solution.py:568
  10.4 23.2 %collective-permute-start.3 = (bf16[1,2,32,16,128]{4,3,2,1,0:T(8,128)(2,1)}, bf16[1,2,32,16,128]{4,3,2,1,0:T(8,128)(2,1)}, u32[]{:S(2)}, u32[]{:S(2)}) collective-permute-start(bf16[1,2,32,16,128]{4,3,2,1,0:T(8,128)(2,1)} %get-tuple-element.103), channel_id=1, source_target_pairs={{0,4},{1,5},{2,6},{3,7},{4,0},{5,1},{6,2},{7,3},{8,12},{9,13},{10,... | collective-permute-start | bytes 786440 | tf_op jit(solution)/shard_map/ppermute | solution.py:568
  10.7 23.1 %collective-permute-start.4 = (bf16[1,2,32,16,128]{4,3,2,1,0:T(8,128)(2,1)}, bf16[1,2,32,16,128]{4,3,2,1,0:T(8,128)(2,1)}, u32[]{:S(2)}, u32[]{:S(2)}) collective-permute-start(bf16[1,2,32,16,128]{4,3,2,1,0:T(8,128)(2,1)} %get-tuple-element.104), channel_id=1, source_target_pairs={{0,5},{1,6},{2,7},{3,0},{4,1},{5,2},{6,3},{7,4},{8,13},{9,14},{10,... | collective-permute-start | bytes 786440 | tf_op jit(solution)/shard_map/ppermute | solution.py:568
  14.7 19.1 %collective-permute-start.5 = (bf16[1,2,32,16,128]{4,3,2,1,0:T(8,128)(2,1)}, bf16[1,2,32,16,128]{4,3,2,1,0:T(8,128)(2,1)}, u32[]{:S(2)}, u32[]{:S(2)}) collective-permute-start(bf16[1,2,32,16,128]{4,3,2,1,0:T(8,128)(2,1)} %get-tuple-element.105), channel_id=1, source_target_pairs={{0,6},{1,7},{2,0},{3,1},{4,2},{5,3},{6,4},{7,5},{8,14},{9,15},{10,... | collective-permute-start | bytes 786440 | tf_op jit(solution)/shard_map/ppermute | solution.py:568
  22.0 13.9 %collective-permute-start.6 = (bf16[1,2,32,16,128]{4,3,2,1,0:T(8,128)(2,1)}, bf16[1,2,32,16,128]{4,3,2,1,0:T(8,128)(2,1)}, u32[]{:S(2)}, u32[]{:S(2)}) collective-permute-start(bf16[1,2,32,16,128]{4,3,2,1,0:T(8,128)(2,1)} %get-tuple-element.106), channel_id=1, source_target_pairs={{0,7},{1,0},{2,1},{3,2},{4,3},{5,4},{6,5},{7,6},{8,15},{9,8},{10,9... | collective-permute-start | bytes 786440 | tf_op jit(solution)/shard_map/ppermute | solution.py:568
  28.5 21.8 %collective-permute-start.7 = (bf16[1,2,32,16,128]{4,3,2,1,0:T(8,128)(2,1)}, bf16[1,2,32,16,128]{4,3,2,1,0:T(8,128)(2,1)}, u32[]{:S(2)}, u32[]{:S(2)}) collective-permute-start(bf16[1,2,32,16,128]{4,3,2,1,0:T(8,128)(2,1)} %get-tuple-element.108), channel_id=1, source_target_pairs={{0,1},{1,2},{2,3},{3,4},{4,5},{5,6},{6,7},{7,0},{8,9},{9,10},{10,1... | collective-permute-start | bytes 786440 | tf_op jit(solution)/shard_map/ppermute | solution.py:568
  33.7 16.7 %collective-permute-start.8 = (bf16[1,2,32,16,128]{4,3,2,1,0:T(8,128)(2,1)}, bf16[1,2,32,16,128]{4,3,2,1,0:T(8,128)(2,1)}, u32[]{:S(2)}, u32[]{:S(2)}) collective-permute-start(bf16[1,2,32,16,128]{4,3,2,1,0:T(8,128)(2,1)} %get-tuple-element.109), channel_id=1, source_target_pairs={{0,2},{1,3},{2,4},{3,5},{4,6},{5,7},{6,0},{7,1},{8,10},{9,11},{10,... | collective-permute-start | bytes 786440 | tf_op jit(solution)/shard_map/ppermute | solution.py:568
  33.8 17.9 %collective-permute-start.9 = (bf16[1,2,32,16,128]{4,3,2,1,0:T(8,128)(2,1)}, bf16[1,2,32,16,128]{4,3,2,1,0:T(8,128)(2,1)}, u32[]{:S(2)}, u32[]{:S(2)}) collective-permute-start(bf16[1,2,32,16,128]{4,3,2,1,0:T(8,128)(2,1)} %get-tuple-element.110), channel_id=1, source_target_pairs={{0,3},{1,4},{2,5},{3,6},{4,7},{5,0},{6,1},{7,2},{8,11},{9,12},{10,... | collective-permute-start | bytes 786440 | tf_op jit(solution)/shard_map/ppermute | solution.py:568
  33.8 45.0 %collective-permute-start.10 = (bf16[1,2,32,16,128]{4,3,2,1,0:T(8,128)(2,1)}, bf16[1,2,32,16,128]{4,3,2,1,0:T(8,128)(2,1)}, u32[]{:S(2)}, u32[]{:S(2)}) collective-permute-start(bf16[1,2,32,16,128]{4,3,2,1,0:T(8,128)(2,1)} %get-tuple-element.111), channel_id=1, source_target_pairs={{0,4},{1,5},{2,6},{3,7},{4,0},{5,1},{6,2},{7,3},{8,12},{9,13},{10,... | collective-permute-start | bytes 786440 | tf_op jit(solution)/shard_map/ppermute | solution.py:568
  35.9 43.4 %collective-permute-start.11 = (bf16[1,2,32,16,128]{4,3,2,1,0:T(8,128)(2,1)}, bf16[1,2,32,16,128]{4,3,2,1,0:T(8,128)(2,1)}, u32[]{:S(2)}, u32[]{:S(2)}) collective-permute-start(bf16[1,2,32,16,128]{4,3,2,1,0:T(8,128)(2,1)} %get-tuple-element.112), channel_id=1, source_target_pairs={{0,5},{1,6},{2,7},{3,0},{4,1},{5,2},{6,3},{7,4},{8,13},{9,14},{10,... | collective-permute-start | bytes 786440 | tf_op jit(solution)/shard_map/ppermute | solution.py:568
  50.3 43.7 %collective-permute-start.21 = (bf16[1,2,32,32,128]{4,3,2,1,0:T(8,128)(2,1)}, bf16[1,2,32,32,128]{4,3,2,1,0:T(8,128)(2,1)}, u32[]{:S(2)}, u32[]{:S(2)}) collective-permute-start(bf16[1,2,32,32,128]{4,3,2,1,0:T(8,128)(2,1)} %get-tuple-element.128), channel_id=1, source_target_pairs={{0,1},{1,2},{2,3},{3,4},{4,5},{5,6},{6,7},{7,0},{8,9},{9,10},{10,1... | collective-permute-start | bytes 1572872 | tf_op jit(solution)/shard_map/ppermute | solution.py:568
  50.4 45.5 %collective-permute-start.22 = (bf16[1,2,32,32,128]{4,3,2,1,0:T(8,128)(2,1)}, bf16[1,2,32,32,128]{4,3,2,1,0:T(8,128)(2,1)}, u32[]{:S(2)}, u32[]{:S(2)}) collective-permute-start(bf16[1,2,32,32,128]{4,3,2,1,0:T(8,128)(2,1)} %get-tuple-element.129), channel_id=1, source_target_pairs={{0,2},{1,3},{2,4},{3,5},{4,6},{5,7},{6,0},{7,1},{8,10},{9,11},{10,... | collective-permute-start | bytes 1572872 | tf_op jit(solution)/shard_map/ppermute | solution.py:568
  51.6 44.2 %collective-permute-start.23 = (bf16[1,2,32,32,128]{4,3,2,1,0:T(8,128)(2,1)}, bf16[1,2,32,32,128]{4,3,2,1,0:T(8,128)(2,1)}, u32[]{:S(2)}, u32[]{:S(2)}) collective-permute-start(bf16[1,2,32,32,128]{4,3,2,1,0:T(8,128)(2,1)} %get-tuple-element.130), channel_id=1, source_target_pairs={{0,3},{1,4},{2,5},{3,6},{4,7},{5,0},{6,1},{7,2},{8,11},{9,12},{10,... | collective-permute-start | bytes 1572872 | tf_op jit(solution)/shard_map/ppermute | solution.py:568
  78.8 12.0 %collective-permute-start.12 = (bf16[1,2,32,16,128]{4,3,2,1,0:T(8,128)(2,1)}, bf16[1,2,32,16,128]{4,3,2,1,0:T(8,128)(2,1)}, u32[]{:S(2)}, u32[]{:S(2)}) collective-permute-start(bf16[1,2,32,16,128]{4,3,2,1,0:T(8,128)(2,1)} %get-tuple-element.113), channel_id=1, source_target_pairs={{0,6},{1,7},{2,0},{3,1},{4,2},{5,3},{6,4},{7,5},{8,14},{9,15},{10,... | collective-permute-start | bytes 786440 | tf_op jit(solution)/shard_map/ppermute | solution.py:568
  79.3 12.7 %collective-permute-start.13 = (bf16[1,2,32,16,128]{4,3,2,1,0:T(8,128)(2,1)}, bf16[1,2,32,16,128]{4,3,2,1,0:T(8,128)(2,1)}, u32[]{:S(2)}, u32[]{:S(2)}) collective-permute-start(bf16[1,2,32,16,128]{4,3,2,1,0:T(8,128)(2,1)} %get-tuple-element.114), channel_id=1, source_target_pairs={{0,7},{1,0},{2,1},{3,2},{4,3},{5,4},{6,5},{7,6},{8,15},{9,8},{10,9... | collective-permute-start | bytes 786440 | tf_op jit(solution)/shard_map/ppermute | solution.py:568
  90.8 27.3 %collective-permute-start.24 = (bf16[1,2,32,32,128]{4,3,2,1,0:T(8,128)(2,1)}, bf16[1,2,32,32,128]{4,3,2,1,0:T(8,128)(2,1)}, u32[]{:S(2)}, u32[]{:S(2)}) collective-permute-start(bf16[1,2,32,32,128]{4,3,2,1,0:T(8,128)(2,1)} %get-tuple-element.131), channel_id=1, source_target_pairs={{0,4},{1,5},{2,6},{3,7},{4,0},{5,1},{6,2},{7,3},{8,12},{9,13},{10,... | collective-permute-start | bytes 1572872 | tf_op jit(solution)/shard_map/ppermute | solution.py:568
  91.9 35.3 %collective-permute-start.25 = (bf16[1,2,32,32,128]{4,3,2,1,0:T(8,128)(2,1)}, bf16[1,2,32,32,128]{4,3,2,1,0:T(8,128)(2,1)}, u32[]{:S(2)}, u32[]{:S(2)}) collective-permute-start(bf16[1,2,32,32,128]{4,3,2,1,0:T(8,128)(2,1)} %get-tuple-element.132), channel_id=1, source_target_pairs={{0,5},{1,6},{2,7},{3,0},{4,1},{5,2},{6,3},{7,4},{8,13},{9,14},{10,... | collective-permute-start | bytes 1572872 | tf_op jit(solution)/shard_map/ppermute | solution.py:568
  94.0 36.2 %collective-permute-start.26 = (bf16[1,2,32,32,128]{4,3,2,1,0:T(8,128)(2,1)}, bf16[1,2,32,32,128]{4,3,2,1,0:T(8,128)(2,1)}, u32[]{:S(2)}, u32[]{:S(2)}) collective-permute-start(bf16[1,2,32,32,128]{4,3,2,1,0:T(8,128)(2,1)} %get-tuple-element.133), channel_id=1, source_target_pairs={{0,6},{1,7},{2,0},{3,1},{4,2},{5,3},{6,4},{7,5},{8,14},{9,15},{10,... | collective-permute-start | bytes 1572872 | tf_op jit(solution)/shard_map/ppermute | solution.py:568
  95.8 34.7 %collective-permute-start.27 = (bf16[1,2,32,32,128]{4,3,2,1,0:T(8,128)(2,1)}, bf16[1,2,32,32,128]{4,3,2,1,0:T(8,128)(2,1)}, u32[]{:S(2)}, u32[]{:S(2)}) collective-permute-start(bf16[1,2,32,32,128]{4,3,2,1,0:T(8,128)(2,1)} %get-tuple-element.134), channel_id=1, source_target_pairs={{0,7},{1,0},{2,1},{3,2},{4,3},{5,4},{6,5},{7,6},{8,15},{9,8},{10,9... | collective-permute-start | bytes 1572872 | tf_op jit(solution)/shard_map/ppermute | solution.py:568
  95.9 39.0 %collective-permute-start.28 = (bf16[1,2,32,32,128]{4,3,2,1,0:T(8,128)(2,1)}, bf16[1,2,32,32,128]{4,3,2,1,0:T(8,128)(2,1)}, u32[]{:S(2)}, u32[]{:S(2)}) collective-permute-start(bf16[1,2,32,32,128]{4,3,2,1,0:T(8,128)(2,1)} %get-tuple-element.148), channel_id=1, source_target_pairs={{0,1},{1,2},{2,3},{3,4},{4,5},{5,6},{6,7},{7,0},{8,9},{9,10},{10,1... | collective-permute-start | bytes 1572872 | tf_op jit(solution)/shard_map/ppermute | solution.py:568
  118.1 40.2 %collective-permute-start.29 = (bf16[1,2,32,32,128]{4,3,2,1,0:T(8,128)(2,1)}, bf16[1,2,32,32,128]{4,3,2,1,0:T(8,128)(2,1)}, u32[]{:S(2)}, u32[]{:S(2)}) collective-permute-start(bf16[1,2,32,32,128]{4,3,2,1,0:T(8,128)(2,1)} %get-tuple-element.149), channel_id=1, source_target_pairs={{0,2},{1,3},{2,4},{3,5},{4,6},{5,7},{6,0},{7,1},{8,10},{9,11},{10,... | collective-permute-start | bytes 1572872 | tf_op jit(solution)/shard_map/ppermute | solution.py:568
  127.2 31.1 %collective-permute-start.30 = (bf16[1,2,32,32,128]{4,3,2,1,0:T(8,128)(2,1)}, bf16[1,2,32,32,128]{4,3,2,1,0:T(8,128)(2,1)}, u32[]{:S(2)}, u32[]{:S(2)}) collective-permute-start(bf16[1,2,32,32,128]{4,3,2,1,0:T(8,128)(2,1)} %get-tuple-element.150), channel_id=1, source_target_pairs={{0,3},{1,4},{2,5},{3,6},{4,7},{5,0},{6,1},{7,2},{8,11},{9,12},{10,... | collective-permute-start | bytes 1572872 | tf_op jit(solution)/shard_map/ppermute | solution.py:568
  130.2 43.9 %collective-permute-start.31 = (bf16[1,2,32,32,128]{4,3,2,1,0:T(8,128)(2,1)}, bf16[1,2,32,32,128]{4,3,2,1,0:T(8,128)(2,1)}, u32[]{:S(2)}, u32[]{:S(2)}) collective-permute-start(bf16[1,2,32,32,128]{4,3,2,1,0:T(8,128)(2,1)} %get-tuple-element.151), channel_id=1, source_target_pairs={{0,4},{1,5},{2,6},{3,7},{4,0},{5,1},{6,2},{7,3},{8,12},{9,13},{10,... | collective-permute-start | bytes 1572872 | tf_op jit(solution)/shard_map/ppermute | solution.py:568
  130.6 50.6 %collective-permute-start.32 = (bf16[1,2,32,32,128]{4,3,2,1,0:T(8,128)(2,1)}, bf16[1,2,32,32,128]{4,3,2,1,0:T(8,128)(2,1)}, u32[]{:S(2)}, u32[]{:S(2)}) collective-permute-start(bf16[1,2,32,32,128]{4,3,2,1,0:T(8,128)(2,1)} %get-tuple-element.152), channel_id=1, source_target_pairs={{0,5},{1,6},{2,7},{3,0},{4,1},{5,2},{6,3},{7,4},{8,13},{9,14},{10,... | collective-permute-start | bytes 1572872 | tf_op jit(solution)/shard_map/ppermute | solution.py:568
  134.8 46.4 %collective-permute-start.33 = (bf16[1,2,32,32,128]{4,3,2,1,0:T(8,128)(2,1)}, bf16[1,2,32,32,128]{4,3,2,1,0:T(8,128)(2,1)}, u32[]{:S(2)}, u32[]{:S(2)}) collective-permute-start(bf16[1,2,32,32,128]{4,3,2,1,0:T(8,128)(2,1)} %get-tuple-element.153), channel_id=1, source_target_pairs={{0,6},{1,7},{2,0},{3,1},{4,2},{5,3},{6,4},{7,5},{8,14},{9,15},{10,... | collective-permute-start | bytes 1572872 | tf_op jit(solution)/shard_map/ppermute | solution.py:568
  158.3 44.7 %collective-permute-start.34 = (bf16[1,2,32,32,128]{4,3,2,1,0:T(8,128)(2,1)}, bf16[1,2,32,32,128]{4,3,2,1,0:T(8,128)(2,1)}, u32[]{:S(2)}, u32[]{:S(2)}) collective-permute-start(bf16[1,2,32,32,128]{4,3,2,1,0:T(8,128)(2,1)} %get-tuple-element.154), channel_id=1, source_target_pairs={{0,7},{1,0},{2,1},{3,2},{4,3},{5,4},{6,5},{7,6},{8,15},{9,8},{10,9... | collective-permute-start | bytes 1572872 | tf_op jit(solution)/shard_map/ppermute | solution.py:568
  158.3 47.5 %collective-permute-start.35 = (bf16[1,2,32,32,128]{4,3,2,1,0:T(8,128)(2,1)}, bf16[1,2,32,32,128]{4,3,2,1,0:T(8,128)(2,1)}, u32[]{:S(2)}, u32[]{:S(2)}) collective-permute-start(bf16[1,2,32,32,128]{4,3,2,1,0:T(8,128)(2,1)} %get-tuple-element.165), channel_id=1, source_target_pairs={{0,1},{1,2},{2,3},{3,4},{4,5},{5,6},{6,7},{7,0},{8,9},{9,10},{10,1... | collective-permute-start | bytes 1572872 | tf_op jit(solution)/shard_map/ppermute | solution.py:568
  174.1 40.6 %collective-permute-start.36 = (bf16[1,2,32,32,128]{4,3,2,1,0:T(8,128)(2,1)}, bf16[1,2,32,32,128]{4,3,2,1,0:T(8,128)(2,1)}, u32[]{:S(2)}, u32[]{:S(2)}) collective-permute-start(bf16[1,2,32,32,128]{4,3,2,1,0:T(8,128)(2,1)} %get-tuple-element.166), channel_id=1, source_target_pairs={{0,2},{1,3},{2,4},{3,5},{4,6},{5,7},{6,0},{7,1},{8,10},{9,11},{10,... | collective-permute-start | bytes 1572872 | tf_op jit(solution)/shard_map/ppermute | solution.py:568
  181.2 33.6 %collective-permute-start.37 = (bf16[1,2,32,32,128]{4,3,2,1,0:T(8,128)(2,1)}, bf16[1,2,32,32,128]{4,3,2,1,0:T(8,128)(2,1)}, u32[]{:S(2)}, u32[]{:S(2)}) collective-permute-start(bf16[1,2,32,32,128]{4,3,2,1,0:T(8,128)(2,1)} %get-tuple-element.167), channel_id=1, source_target_pairs={{0,3},{1,4},{2,5},{3,6},{4,7},{5,0},{6,1},{7,2},{8,11},{9,12},{10,... | collective-permute-start | bytes 1572872 | tf_op jit(solution)/shard_map/ppermute | solution.py:568
  181.2 35.3 %collective-permute-start.38 = (bf16[1,2,32,32,128]{4,3,2,1,0:T(8,128)(2,1)}, bf16[1,2,32,32,128]{4,3,2,1,0:T(8,128)(2,1)}, u32[]{:S(2)}, u32[]{:S(2)}) collective-permute-start(bf16[1,2,32,32,128]{4,3,2,1,0:T(8,128)(2,1)} %get-tuple-element.168), channel_id=1, source_target_pairs={{0,4},{1,5},{2,6},{3,7},{4,0},{5,1},{6,2},{7,3},{8,12},{9,13},{10,... | collective-permute-start | bytes 1572872 | tf_op jit(solution)/shard_map/ppermute | solution.py:568
  202.9 34.3 %collective-permute-start.39 = (bf16[1,2,32,32,128]{4,3,2,1,0:T(8,128)(2,1)}, bf16[1,2,32,32,128]{4,3,2,1,0:T(8,128)(2,1)}, u32[]{:S(2)}, u32[]{:S(2)}) collective-permute-start(bf16[1,2,32,32,128]{4,3,2,1,0:T(8,128)(2,1)} %get-tuple-element.169), channel_id=1, source_target_pairs={{0,5},{1,6},{2,7},{3,0},{4,1},{5,2},{6,3},{7,4},{8,13},{9,14},{10,... | collective-permute-start | bytes 1572872 | tf_op jit(solution)/shard_map/ppermute | solution.py:568
  205.8 40.3 %collective-permute-start.40 = (bf16[1,2,32,32,128]{4,3,2,1,0:T(8,128)(2,1)}, bf16[1,2,32,32,128]{4,3,2,1,0:T(8,128)(2,1)}, u32[]{:S(2)}, u32[]{:S(2)}) collective-permute-start(bf16[1,2,32,32,128]{4,3,2,1,0:T(8,128)(2,1)} %get-tuple-element.170), channel_id=1, source_target_pairs={{0,6},{1,7},{2,0},{3,1},{4,2},{5,3},{6,4},{7,5},{8,14},{9,15},{10,... | collective-permute-start | bytes 1572872 | tf_op jit(solution)/shard_map/ppermute | solution.py:568
  214.7 31.4 %collective-permute-start.41 = (bf16[1,2,32,32,128]{4,3,2,1,0:T(8,128)(2,1)}, bf16[1,2,32,32,128]{4,3,2,1,0:T(8,128)(2,1)}, u32[]{:S(2)}, u32[]{:S(2)}) collective-permute-start(bf16[1,2,32,32,128]{4,3,2,1,0:T(8,128)(2,1)} %get-tuple-element.171), channel_id=1, source_target_pairs={{0,7},{1,0},{2,1},{3,2},{4,3},{5,4},{6,5},{7,6},{8,15},{9,8},{10,9... | collective-permute-start | bytes 1572872 | tf_op jit(solution)/shard_map/ppermute | solution.py:568
  214.8 31.5 %collective-permute-start.14 = (bf16[2,1024,128]{2,1,0:T(8,128)(2,1)}, bf16[2,1024,128]{2,1,0:T(8,128)(2,1)}, u32[]{:S(2)}, u32[]{:S(2)}) collective-permute-start(bf16[2,1024,128]{2,1,0:T(8,128)(2,1)} %get-tuple-element.117), channel_id=1, source_target_pairs={{0,1},{1,2},{2,3},{3,4},{4,5},{5,6},{6,7},{7,0},{8,9},{9,10},{10,1... | collective-permute-start | bytes 1572872 | tf_op jit(solution)/shard_map/ppermute | solution.py:568
  216.5 43.9 %collective-permute-start.15 = (bf16[2,1024,128]{2,1,0:T(8,128)(2,1)}, bf16[2,1024,128]{2,1,0:T(8,128)(2,1)}, u32[]{:S(2)}, u32[]{:S(2)}) collective-permute-start(bf16[2,1024,128]{2,1,0:T(8,128)(2,1)} %get-tuple-element.118), channel_id=1, source_target_pairs={{0,2},{1,3},{2,4},{3,5},{4,6},{5,7},{6,0},{7,1},{8,10},{9,11},{10,... | collective-permute-start | bytes 1572872 | tf_op jit(solution)/shard_map/ppermute | solution.py:568
  237.3 43.9 %collective-permute-start.16 = (bf16[2,1024,128]{2,1,0:T(8,128)(2,1)}, bf16[2,1024,128]{2,1,0:T(8,128)(2,1)}, u32[]{:S(2)}, u32[]{:S(2)}) collective-permute-start(bf16[2,1024,128]{2,1,0:T(8,128)(2,1)} %get-tuple-element.119), channel_id=1, source_target_pairs={{0,3},{1,4},{2,5},{3,6},{4,7},{5,0},{6,1},{7,2},{8,11},{9,12},{10,... | collective-permute-start | bytes 1572872 | tf_op jit(solution)/shard_map/ppermute | solution.py:568
  246.2 37.2 %collective-permute-start.17 = (bf16[2,1024,128]{2,1,0:T(8,128)(2,1)}, bf16[2,1024,128]{2,1,0:T(8,128)(2,1)}, u32[]{:S(2)}, u32[]{:S(2)}) collective-permute-start(bf16[2,1024,128]{2,1,0:T(8,128)(2,1)} %get-tuple-element.120), channel_id=1, source_target_pairs={{0,4},{1,5},{2,6},{3,7},{4,0},{5,1},{6,2},{7,3},{8,12},{9,13},{10,... | collective-permute-start | bytes 1572872 | tf_op jit(solution)/shard_map/ppermute | solution.py:568
  246.2 37.3 %collective-permute-start.18 = (bf16[2,1024,128]{2,1,0:T(8,128)(2,1)}, bf16[2,1024,128]{2,1,0:T(8,128)(2,1)}, u32[]{:S(2)}, u32[]{:S(2)}) collective-permute-start(bf16[2,1024,128]{2,1,0:T(8,128)(2,1)} %get-tuple-element.121), channel_id=1, source_target_pairs={{0,5},{1,6},{2,7},{3,0},{4,1},{5,2},{6,3},{7,4},{8,13},{9,14},{10,... | collective-permute-start | bytes 1572872 | tf_op jit(solution)/shard_map/ppermute | solution.py:568
  246.2 37.2 %collective-permute-start.19 = (bf16[2,1024,128]{2,1,0:T(8,128)(2,1)}, bf16[2,1024,128]{2,1,0:T(8,128)(2,1)}, u32[]{:S(2)}, u32[]{:S(2)}) collective-permute-start(bf16[2,1024,128]{2,1,0:T(8,128)(2,1)} %get-tuple-element.122), channel_id=1, source_target_pairs={{0,6},{1,7},{2,0},{3,1},{4,2},{5,3},{6,4},{7,5},{8,14},{9,15},{10,... | collective-permute-start | bytes 1572872 | tf_op jit(solution)/shard_map/ppermute | solution.py:568
  260.4 23.0 %collective-permute-start.20 = (bf16[2,1024,128]{2,1,0:T(8,128)(2,1)}, bf16[2,1024,128]{2,1,0:T(8,128)(2,1)}, u32[]{:S(2)}, u32[]{:S(2)}) collective-permute-start(bf16[2,1024,128]{2,1,0:T(8,128)(2,1)} %get-tuple-element.123), channel_id=1, source_target_pairs={{0,7},{1,0},{2,1},{3,2},{4,3},{5,4},{6,5},{7,6},{8,15},{9,8},{10,9... | collective-permute-start | bytes 1572872 | tf_op jit(solution)/shard_map/ppermute | solution.py:568

commit v8 on v7

--- a/solution.py
+++ b/solution.py
@@ -13,6 +13,7 @@
 penalty = 1.0
 threshold = 0.3
 VMEM_LIMIT = 67000000
+SPLIT = 4
 F32 = jnp.float32
 BF16 = jnp.bfloat16
 
@@ -70,11 +71,22 @@
     return jnp.concatenate(pieces, axis=0)
 
 
-def forward_kernel(n, kl, xp, table, image, sens, *refs):
-    outs, flat = refs[:n], refs[n]
+def forward_kernel(n, kl, xp, offs, table, image, sens, *refs):
+    outs, flat = refs[: len(offs)], refs[len(offs)]
     rows, length = image.shape[1], image.shape[2]
     me = lax.axis_index("slab")
     coil, step = pl.program_id(0), pl.program_id(1)
+    lines = 2 * length
+    if len(offs) < n:
+        whole, table = table, refs[len(offs) + 1]
+        lines = table.shape[0]
+
+        @pl.when((coil == 0) & (step == 0))
+        def gather():
+            for p in range(2):
+                for i, off in enumerate(offs):
+                    source = pl.ds(pl.multiple_of(p * length + ahead(me, off, n) * kl, kl), kl)
+                    table[(p * len(offs) + i) * kl : (p * len(offs) + i + 1) * kl, :] = whole[source, :]
 
     def pair(i, carry):
         columns = []
@@ -93,7 +105,7 @@
         half = jnp.dot(table[...], both, preferred_element_type=F32)
         depth = half.shape[1] // 2
         for h in range(2):
-            where = pl.ds(step * rows + 2 * i + h, 2 * length, stride=pitch(xp))
+            where = pl.ds(step * rows + 2 * i + h, lines, stride=pitch(xp))
             flat[where, :] = half[:, h * depth : (h + 1) * depth]
         return carry
 
@@ -101,35 +113,36 @@
 
     @pl.when(step == pl.num_programs(1) - 1)
     def last():
-        for off in range(n):
-            d = ahead(me, off, n)
+        for i, off in enumerate(offs):
+            d = ahead(me, off, n) if len(offs) == n else i
             for p in range(2):
 
                 def settle(k, carry):
-                    base = pl.multiple_of(((p * n + d) * kl + 2 * k) * pitch(xp), 8)
+                    base = pl.multiple_of(((p * len(offs) + d) * kl + 2 * k) * pitch(xp), 8)
                     for h in range(2):
-                        outs[off][coil, p, 2 * k + h] = flat[pl.ds(base + h * pitch(xp), xp), :].astype(BF16)
+                        outs[i][coil, p, 2 * k + h] = flat[pl.ds(base + h * pitch(xp), xp), :].astype(BF16)
                     return carry
 
-                lax.fori_loop(0, kl // 2, settle, 0, unroll=8)
-
-
-def forward_call(table, image, sensitivity, batch, first, xp, n, kl):
+                lax.fori_loop(0, kl // 2, settle, 0, unroll=4)
+
+
+def forward_call(table, image, sensitivity, batch, first, xp, offs, n, kl):
     _, _, _, length, depth = sensitivity.shape
-    rows = 4 if xp % 4 == 0 else xp
+    rows = 8 if xp % 8 == 0 else xp
     steps, skip = xp // rows, first // rows
     shape = (len(batch), 2, kl, xp, depth)
     return pl.pallas_call(
-        functools.partial(forward_kernel, n, kl, xp),
+        functools.partial(forward_kernel, n, kl, xp, offs),
         grid=(len(batch), steps),
         in_specs=[
             once(table.shape),
             pl.BlockSpec((2, rows, length, depth), lambda c, i: (0, skip + i, 0, 0)),
             pl.BlockSpec((1, 2, rows, length, depth), lambda c, i: (batch[0] + c, 0, skip + i, 0, 0)),
         ],
-        out_specs=[once(shape)] * n,
-        out_shape=[jax.ShapeDtypeStruct(shape, BF16)] * n,
-        scratch_shapes=[pltpu.VMEM(((2 * length + 1) * pitch(xp), depth), F32)],
+        out_specs=[once(shape)] * len(offs),
+        out_shape=[jax.ShapeDtypeStruct(shape, BF16)] * len(offs),
+        scratch_shapes=[pltpu.VMEM(((2 * len(offs) * kl + 1) * pitch(xp), depth), F32)]
+        + ([pltpu.VMEM((2 * len(offs) * kl, table.shape[1]), BF16)] if len(offs) < n else []),
         compiler_params=params(),
         cost_estimate=cost(8 * len(batch) * length * length * xp * depth, 12 * len(batch) * xp * length * depth),
         name="forward",
@@ -352,10 +365,14 @@
 
 def store_kernel(*refs):
     count = len(refs) // 2
+    rows = refs[0].shape[1] // SPLIT
     copies = [
-        pltpu.make_async_copy(refs[k].at[p], refs[count + k].at[p], refs[-1].at[k, p])
+        pltpu.make_async_copy(
+            refs[k].at[p, pl.ds(q * rows, rows)], refs[count + k].at[p, pl.ds(q * rows, rows)], refs[-1].at[k, p, q]
+        )
         for k in range(count)
         for p in range(2)
+        for q in range(SPLIT)
     ]
     for copy in copies:
         copy.start()
@@ -369,7 +386,7 @@
         in_specs=[pl.BlockSpec(memory_space=pltpu.VMEM)] * len(values),
         out_specs=[HBM] * len(values),
         out_shape=[jax.ShapeDtypeStruct(value.shape, value.dtype) for value in values],
-        scratch_shapes=[pltpu.SemaphoreType.DMA((len(values), 2))],
+        scratch_shapes=[pltpu.SemaphoreType.DMA((len(values), 2, SPLIT))],
         compiler_params=params(2**24),
         name="store",
     )(*values)
@@ -562,10 +579,11 @@
     x_fwd = complex_table(n * xl, False)
     x_inv = complex_table(n * xl, True)
 
-    def swap(parts):
+    def swap(parts, offs):
         moved = list(parts)
-        for off in turns(n):
-            moved[off] = lax.ppermute(parts[off], "slab", [(i, ahead(i, off, n)) for i in range(n)])
+        for turn, off in enumerate(offs):
+            if off:
+                moved[turn] = lax.ppermute(parts[turn], "slab", [(i, ahead(i, off, n)) for i in range(n)])
         return moved
 
     batches = [[c] for c in range(coils)]
@@ -583,11 +601,20 @@
     pieces, tiles, table = [], [], y_fwd
     for batch in batches:
         c = batch[0]
+        everyone = [*turns(n), 0]
         moved = []
-        for first, size in parts_of(c):
-            half = list(forward_call(table, image, sensitivity, batch, first, size, n, kl))
-            table, half[0] = lax.optimization_barrier((table, half[0]))
-            moved += swap(half)
+        jobs = [(first, size, everyone) for first, size in parts_of(c)]
+        if len(jobs) > 1 and n >= 4 and kl % 16 == 0:
+            first, size, _ = jobs[0]
+            jobs[:1] = [(first, size, everyone[: n // 2]), (first, size, everyone[n // 2 :])]
+        for first, size, offs in jobs:
+            half = list(forward_call(table, image, sensitivity, batch, first, size, offs, n, kl))
+            table, half[-1] = lax.optimization_barrier((table, half[-1]))
+            moved += swap(half, offs)
+        ordered = []
+        for h in range(len(parts_of(c))):
+            ordered += [moved[h * n + everyone.index(off)] for off in range(n)]
+        moved = ordered
         pieces += [(moved, place) for place in range(len(batch))]
     table, samples = lax.optimization_barrier((table, samples))
     sorted_samples = sort_call(samples)
@@ -600,7 +627,7 @@
     early = max(coils - 3, 0)
     backs = list(tiles)
     for c in range(early):
-        backs[c] = swap(tiles[c])
+        backs[c] = swap(tiles[c], range(n))
     results = finish_call(
         y_inv, backs, coils - early, sensitivity, image, auxiliary, scaled_dual, shares, n, kl
     )

time: 438 us -> 438 us (level)
    pallas_call x5 -> x6, Pallas kernels: 47.5 us -> 47.3 us  [forward_call(): pl.pallas_call(functools.partial(forward_kernel, n, kl, xp, offs), grid=(...]
  transfers between devices with their start and end apart: 42 -> 42, of which waited for: 10 -> 9; matrix products, arithmetic and copies ran while one was open for 0% -> 0% of each run, Pallas kernels for 30% -> 31%
where the time goes in v8:
time: 438 us; the launch traced here: 434 us
  Pallas kernels  290 us (66%)
  starting transfers between devices  77.9 us (18%)
  waiting for transfers between devices  65 us (15%)
    pallas_call x1, Pallas kernels, finish_call(): pl.pallas_call(functools.partial(finish_kernel, n, shares, kl, xl, chunks...  148 us
    pallas_call x4, Pallas kernels, tile_call(): pl.pallas_call(functools.partial(tile_kernel, n, kl, xl, cells // kl, par...  83.2 us
    ppermute x42, starting transfers between devices, swap(): lax.ppermute(parts[turn], 'slab', [(i, ahead(i, off, n)) for i in range(n)])  77.9 us
    ppermute x42, waiting for transfers between devices, swap(): lax.ppermute(parts[turn], 'slab', [(i, ahead(i, off, n)) for i in range(n)])  65 us
    pallas_call x6, Pallas kernels, forward_call(): pl.pallas_call(functools.partial(forward_kernel, n, kl, xp, offs), grid=(...  47.3 us
  transfers between devices with their start and end apart: 42, of which 9 were waited for; matrix products, arithmetic and copies ran while one was open for 0% of the time, Pallas kernels for 31%

profile of v8, /device:TPU:9, one launch (start us, length us, event | category | flops | bytes accessed | tf_op | source)
XLA Modules:
  0.0 434.5 jit_solution(10902913718266254412)
XLA Ops:
  0.6 5.1 %forward.6 = (bf16[1,2,32,16,128]{4,3,2,1,0:T(8,128)(2,1)}, bf16[1,2,32,16,128]{4,3,2,1,0:T(8,128)(2,1)}, bf16[1,2,32,16,128]{4,3,2,1,0:T(8,128)(2,1)}, bf16[1,2,32,16,128]{4,3,2,1,0:T(8,128)(2,1)}) custom-call(bf16[512,512]{1,0:T(8,128)(2,1)} %constant.11.table.fwd, f32[2,32,256,128]{3,2,1,0:T(8,128)} %image.13, bf16[4,2,32,256,128]{4,3,2,1,0:T(8,128)(2,1)} %sens.13), custom_call_target="tpu_custom_call" | custom-call | flops 1073741824 | bytes 6291456 | tf_op jit(solution)/shard_map/forward/pallas_call | solution.py:134
  5.7 1.8 collective-permute-start.2
  7.5 1.2 collective-permute-start.1
  8.7 0.2 collective-permute-start.3
  8.9 1.2 collective-permute-start.5
  10.1 5.0 %forward.7 = (bf16[1,2,32,16,128]{4,3,2,1,0:T(8,128)(2,1)}, bf16[1,2,32,16,128]{4,3,2,1,0:T(8,128)(2,1)}, bf16[1,2,32,16,128]{4,3,2,1,0:T(8,128)(2,1)}, bf16[1,2,32,16,128]{4,3,2,1,0:T(8,128)(2,1)}) custom-call(bf16[512,512]{1,0:T(8,128)(2,1)} %constant.11.table.fwd, f32[2,32,256,128]{3,2,1,0:T(8,128)} %image.13, bf16[4,2,32,256,128]{4,3,2,1,0:T(8,128)(2,1)} %sens.13), custom_call_target="tpu_custom_call" | custom-call | flops 1073741824 | bytes 6291456 | tf_op jit(solution)/shard_map/forward/pallas_call | solution.py:134
  15.1 0.9 collective-permute-start
  16.0 5.5 %collective-permute-done.2.refs_3_ = bf16[1,2,32,16,128]{4,3,2,1,0:T(8,128)(2,1)} collective-permute-done((bf16[1,2,32,16,128]{4,3,2,1,0:T(8,128)(2,1)}, bf16[1,2,32,16,128]{4,3,2,1,0:T(8,128)(2,1)}, u32[]{:S(2)}, u32[]{:S(2)}) %collective-permute-start.2) | collective-permute-done | bytes 262176 | tf_op jit(solution)/shard_map/ppermute | solution.py:586
  21.5 0.0 collective-permute-start.4
  21.5 0.0 collective-permute-done.1.refs_2_
  21.5 1.1 collective-permute-start.6
  22.6 6.3 %forward.8 = (bf16[1,2,32,16,128]{4,3,2,1,0:T(8,128)(2,1)}, bf16[1,2,32,16,128]{4,3,2,1,0:T(8,128)(2,1)}, bf16[1,2,32,16,128]{4,3,2,1,0:T(8,128)(2,1)}, bf16[1,2...) custom-call(bf16[512,512]{1,0:T(8,128)(2,1)} %constant.11.table.fwd,, ...), custom_call_target="tpu_custom_call" | custom-call | flops 1073741824 | bytes 6291456 | tf_op jit(solution)/shard_map/forward/pallas_call | solution.py:134
  28.9 1.7 collective-permute-done.3.refs_4_
  30.6 0.0 collective-permute-start.7
  30.6 0.0 collective-permute-done.5.refs_6_
  30.6 2.3 collective-permute-start.8
  32.9 0.0 collective-permute-done.refs_1_
  32.9 0.0 collective-permute-start.9
  32.9 0.0 collective-permute-done.4.refs_5_
  32.9 2.0 collective-permute-start.10
  35.0 0.0 collective-permute-done.6.refs_7_
  35.0 2.9 collective-permute-start.11
  37.8 10.3 %forward.9 = (bf16[1,2,32,32,128]{4,3,2,1,0:T(8,128)(2,1)}, bf16[1,2,32,32,128]{4,3,2,1,0:T(8,128)(2,1)}, bf16[1,2,32,32,128]{4,3,2,1,0:T(8,128)(2,1)}, bf16[1,2...) custom-call(bf16[512,512]{1,0:T(8,128)(2,1)} %constant.11.table.fwd,, ...), custom_call_target="tpu_custom_call" | custom-call | flops 2147483648 | bytes 12582912 | tf_op jit(solution)/shard_map/forward/pallas_call | solution.py:134
  48.1 0.0 collective-permute-done.7.refs_9_
  48.1 0.1 collective-permute-start.21
  48.2 0.0 collective-permute-done.8.refs_10_
  48.2 0.1 collective-permute-start.22
  48.3 18.8 %collective-permute-done.9.refs_11_ = bf16[1,2,32,16,128]{4,3,2,1,0:T(8,128)(2,1)} collective-permute-done((bf16[1,2,32,16,128]{4,3,2,1,0:T(8,128)(2,1)}, bf16[1,2,32,16,128]{4,3,2,1,0:T(8,128)(2,1)}, u32[]{:S(2)}, u32[]{:S(2)}) %collective-permute-start.9) | collective-permute-done | bytes 262176 | tf_op jit(solution)/shard_map/ppermute | solution.py:586
  67.1 2.5 collective-permute-start.23
  69.6 11.3 %collective-permute-done.10.refs_12_ = bf16[1,2,32,16,128]{4,3,2,1,0:T(8,128)(2,1)} collective-permute-done((bf16[1,2,32,16,128]{4,3,2,1,0:T(8,128)(2,1)}, bf16[1,2,32,16,128]{4,3,2,1,0:T(8,128)(2,1)}, u32[]{:S(2)}, u32[]{:S(2)}) %collective-permute-start.10) | collective-permute-done | bytes 262176 | tf_op jit(solution)/shard_map/ppermute | solution.py:586
  80.9 0.3 collective-permute-done.11.refs_13_
  81.2 10.3 %forward.10 = (bf16[1,2,32,32,128]{4,3,2,1,0:T(8,128)(2,1)}, bf16[1,2,32,32,128]{4,3,2,1,0:T(8,128)(2,1)}, bf16[1,2,32,32,128]{4,3,2,1,0:T(8,128)(2,1)}, bf16[1,...) custom-call(bf16[512,512]{1,0:T(8,128)(2,1)} %constant.11.table.fwd,, ...), custom_call_target="tpu_custom_call" | custom-call | flops 2147483648 | bytes 12582912 | tf_op jit(solution)/shard_map/forward/pallas_call | solution.py:134
  91.5 0.1 collective-permute-start.24
  91.5 3.2 collective-permute-start.25
  94.7 0.7 collective-permute-start.26
  95.4 1.7 collective-permute-start.28
  97.8 10.3 %forward.11 = (bf16[1,2,32,32,128]{4,3,2,1,0:T(8,128)(2,1)}, bf16[1,2,32,32,128]{4,3,2,1,0:T(8,128)(2,1)}, bf16[1,2,32,32,128]{4,3,2,1,0:T(8,128)(2,1)}, bf16[1,...) custom-call(bf16[512,512]{1,0:T(8,128)(2,1)} %constant.11.table.fwd,, ...), custom_call_target="tpu_custom_call" | custom-call | flops 2147483648 | bytes 12582912 | tf_op jit(solution)/shard_map/forward/pallas_call | solution.py:134
  108.1 8.3 %sort.1.sorted_samples = bf16[4,24,128,256]{3,2,1,0:T(8,128)(2,1)} custom-call(bf16[24,1024,128]{2,1,0:T(8,128)(2,1)} %bitcast.1), custom_call_target="tpu_custom_call" | custom-call | flops 3145728 | bytes 12582912 | tf_op jit(solution)/shard_map/sort/pallas_call | solution.py:168
  116.4 11.8 %collective-permute-start.29 = (bf16[1,2,32,32,128]{4,3,2,1,0:T(8,128)(2,1)}, bf16[1,2,32,32,128]{4,3,2,1,0:T(8,128)(2,1)}, u32[]{:S(2)}, u32[]{:S(2)}) collective-permute-start(bf16[1,2,32,32,128]{4,3,2,1,0:T(8,128)(2,1)} %get-tuple-element.153), channel_id=1, source_target_pairs={{0,2},{1,3},{2,4},{3,5},{4,6},{5,7},{6,0},{7,1},{8,10},{9,11},{10,... | collective-permute-start | bytes 1572872 | tf_op jit(solution)/shard_map/ppermute | solution.py:586
  128.3 1.7 collective-permute-start.30
  130.0 1.5 collective-permute-start.31
  131.5 3.1 collective-permute-start.32
  134.6 3.7 collective-permute-start.33
  138.3 20.9 %tile.4 = (bf16[2,1024,128]{2,1,0:T(8,128)(2,1)}, bf16[2,1024,128]{2,1,0:T(8,128)(2,1)}, bf16[2,1024,128]{2,1,0:T(8,128)(2,1)}, bf16[2,1024,128]{2,1,0:T(8,128)(...) custom-call(s32[1,24]{1,0:T(1,128)} %offsets.7, ...), custom_call_target="tpu_custom_call" | custom-call | flops 10737418240 | bytes 20971520 | tf_op jit(solution)/shard_map/tile/pallas_call | solution.py:315
  159.1 0.1 collective-permute-start.34
  159.2 1.7 collective-permute-start.35
  160.9 13.5 %collective-permute-done.31.refs_4_ = bf16[1,2,32,32,128]{4,3,2,1,0:T(8,128)(2,1)} collective-permute-done((bf16[1,2,32,32,128]{4,3,2,1,0:T(8,128)(2,1)}, bf16[1,2,32,32,128]{4,3,2,1,0:T(8,128)(2,1)}, u32[]{:S(2)}, u32[]{:S(2)}) %collective-permute-start.31) | collective-permute-done | bytes 524320 | tf_op jit(solution)/shard_map/ppermute | solution.py:586
  174.4 6.3 %collective-permute-start.36 = (bf16[1,2,32,32,128]{4,3,2,1,0:T(8,128)(2,1)}, bf16[1,2,32,32,128]{4,3,2,1,0:T(8,128)(2,1)}, u32[]{:S(2)}, u32[]{:S(2)}) collective-permute-start(bf16[1,2,32,32,128]{4,3,2,1,0:T(8,128)(2,1)} %get-tuple-element.170), channel_id=1, source_target_pairs={{0,2},{1,3},{2,4},{3,5},{4,6},{5,7},{6,0},{7,1},{8,10},{9,11},{10,... | collective-permute-start | bytes 1572872 | tf_op jit(solution)/shard_map/ppermute | solution.py:586
  180.7 2.3 collective-permute-start.38
  183.0 20.8 %tile.5 = (bf16[2,1024,128]{2,1,0:T(8,128)(2,1)}, bf16[2,1024,128]{2,1,0:T(8,128)(2,1)}, bf16[2,1024,128]{2,1,0:T(8,128)(2,1)}, bf16[2,1024,128]{2,1,0:T(8,128)(...) custom-call(s32[1,24]{1,0:T(1,128)} %offsets.7, ...), custom_call_target="tpu_custom_call" | custom-call | flops 10737418240 | bytes 20971520 | tf_op jit(solution)/shard_map/tile/pallas_call | solution.py:315
  203.8 2.9 collective-permute-start.39
  206.7 7.8 %collective-permute-start.40 = (bf16[1,2,32,32,128]{4,3,2,1,0:T(8,128)(2,1)}, bf16[1,2,32,32,128]{4,3,2,1,0:T(8,128)(2,1)}, u32[]{:S(2)}, u32[]{:S(2)}) collective-permute-start(bf16[1,2,32,32,128]{4,3,2,1,0:T(8,128)(2,1)} %get-tuple-element.174), channel_id=1, source_target_pairs={{0,6},{1,7},{2,0},{3,1},{4,2},{5,3},{6,4},{7,5},{8,14},{9,15},{10,... | collective-permute-start | bytes 1572872 | tf_op jit(solution)/shard_map/ppermute | solution.py:586
  214.5 1.7 collective-permute-start.14
  216.3 0.0 collective-permute-start.15
  216.3 20.7 %tile.6 = (bf16[2,1024,128]{2,1,0:T(8,128)(2,1)}, bf16[2,1024,128]{2,1,0:T(8,128)(2,1)}, bf16[2,1024,128]{2,1,0:T(8,128)(2,1)}, bf16[2,1024,128]{2,1,0:T(8,128)(...) custom-call(s32[1,24]{1,0:T(1,128)} %offsets.7, ...), custom_call_target="tpu_custom_call" | custom-call | flops 10737418240 | bytes 20971520 | tf_op jit(solution)/shard_map/tile/pallas_call | solution.py:315
  237.0 8.9 %collective-permute-start.16 = (bf16[2,1024,128]{2,1,0:T(8,128)(2,1)}, bf16[2,1024,128]{2,1,0:T(8,128)(2,1)}, u32[]{:S(2)}, u32[]{:S(2)}) collective-permute-start(bf16[2,1024,128]{2,1,0:T(8,128)(2,1)} %get-tuple-element.123), channel_id=1, source_target_pairs={{0,3},{1,4},{2,5},{3,6},{4,7},{5,0},{6,1},{7,2},{8,11},{9,12},{10,... | collective-permute-start | bytes 1572872 | tf_op jit(solution)/shard_map/ppermute | solution.py:586
  245.9 0.1 collective-permute-start.18
  246.0 2.5 collective-permute-start.19
  248.4 11.7 %collective-permute-done.15.refs_2_ = bf16[2,1024,128]{2,1,0:T(8,128)(2,1)} collective-permute-done((bf16[2,1024,128]{2,1,0:T(8,128)(2,1)}, bf16[2,1024,128]{2,1,0:T(8,128)(2,1)}, u32[]{:S(2)}, u32[]{:S(2)}) %collective-permute-start.15) | collective-permute-done | bytes 524320 | tf_op jit(solution)/shard_map/ppermute | solution.py:586
  260.1 20.8 %tile.7 = (bf16[2,1024,128]{2,1,0:T(8,128)(2,1)}, bf16[2,1024,128]{2,1,0:T(8,128)(2,1)}, bf16[2,1024,128]{2,1,0:T(8,128)(2,1)}, bf16[2,1024,128]{2,1,0:T(8,128)(...) custom-call(s32[1,24]{1,0:T(1,128)} %offsets.7, ...), custom_call_target="tpu_custom_call" | custom-call | flops 10737418240 | bytes 20971520 | tf_op jit(solution)/shard_map/tile/pallas_call | solution.py:315
  281.0 2.1 collective-permute-done.17.refs_4_
  283.1 0.1 collective-permute-done.18.refs_5_
  283.2 148.3 %finish.1 = (f32[2,32,64,128]{3,2,1,0:T(8,128)S(1)}, f32[2,32,64,128]{3,2,1,0:T(8,128)S(1)}, f32[2,32,64,128]{3,2,1,0:T(8,128)S(1)}) custom-call(bf16[512,512]{1,0:T(8,128)(2,1)} %constant.10.inv.table_ref, bf16[4,2,32,256,128]{4,3,2,1,0:T(8,128)(2,1)} %sens.13, f32[2,32,256,128]{3,2,1,0:T(8,128)} %image.13, f32[2,32,64,128]{3,2,1,0:T(8,128)} %auxiliary.1, ...), custom_call_target="tpu_custom_call" | custom-call | tf_op jit(solution)/shard_map/finish/pallas_call | solution.py:561
  431.4 2.8 store.1
  (33 shorter events, 0.1 us)
Async XLA Ops:
  5.7 15.8 %collective-permute-start.2 = (bf16[1,2,32,16,128]{4,3,2,1,0:T(8,128)(2,1)}, bf16[1,2,32,16,128]{4,3,2,1,0:T(8,128)(2,1)}, u32[]{:S(2)}, u32[]{:S(2)}) collective-permute-start(bf16[1,2,32,16,128]{4,3,2,1,0:T(8,128)(2,1)} %get-tuple-element.106), channel_id=1, source_target_pairs={{0,3},{1,4},{2,5},{3,6},{4,7},{5,0},{6,1},{7,2},{8,11},{9,12},{10,... | collective-permute-start | bytes 786440 | tf_op jit(solution)/shard_map/ppermute | solution.py:586
  7.5 14.0 %collective-permute-start.1 = (bf16[1,2,32,16,128]{4,3,2,1,0:T(8,128)(2,1)}, bf16[1,2,32,16,128]{4,3,2,1,0:T(8,128)(2,1)}, u32[]{:S(2)}, u32[]{:S(2)}) collective-permute-start(bf16[1,2,32,16,128]{4,3,2,1,0:T(8,128)(2,1)} %get-tuple-element.105), channel_id=1, source_target_pairs={{0,2},{1,3},{2,4},{3,5},{4,6},{5,7},{6,0},{7,1},{8,10},{9,11},{10,... | collective-permute-start | bytes 786440 | tf_op jit(solution)/shard_map/ppermute | solution.py:586
  8.7 21.9 %collective-permute-start.3 = (bf16[1,2,32,16,128]{4,3,2,1,0:T(8,128)(2,1)}, bf16[1,2,32,16,128]{4,3,2,1,0:T(8,128)(2,1)}, u32[]{:S(2)}, u32[]{:S(2)}) collective-permute-start(bf16[1,2,32,16,128]{4,3,2,1,0:T(8,128)(2,1)} %get-tuple-element.107), channel_id=1, source_target_pairs={{0,4},{1,5},{2,6},{3,7},{4,0},{5,1},{6,2},{7,3},{8,12},{9,13},{10,... | collective-permute-start | bytes 786440 | tf_op jit(solution)/shard_map/ppermute | solution.py:586
  8.9 21.7 %collective-permute-start.5 = (bf16[1,2,32,16,128]{4,3,2,1,0:T(8,128)(2,1)}, bf16[1,2,32,16,128]{4,3,2,1,0:T(8,128)(2,1)}, u32[]{:S(2)}, u32[]{:S(2)}) collective-permute-start(bf16[1,2,32,16,128]{4,3,2,1,0:T(8,128)(2,1)} %get-tuple-element.109), channel_id=1, source_target_pairs={{0,6},{1,7},{2,0},{3,1},{4,2},{5,3},{6,4},{7,5},{8,14},{9,15},{10,... | collective-permute-start | bytes 786440 | tf_op jit(solution)/shard_map/ppermute | solution.py:586
  15.1 17.9 %collective-permute-start = (bf16[1,2,32,16,128]{4,3,2,1,0:T(8,128)(2,1)}, bf16[1,2,32,16,128]{4,3,2,1,0:T(8,128)(2,1)}, u32[]{:S(2)}, u32[]{:S(2)}) collective-permute-start(bf16[1,2,32,16,128]{4,3,2,1,0:T(8,128)(2,1)} %get-tuple-element.104), channel_id=1, source_target_pairs={{0,1},{1,2},{2,3},{3,4},{4,5},{5,6},{6,7},{7,0},{8,9},{9,10},{10,1... | collective-permute-start | bytes 786440 | tf_op jit(solution)/shard_map/ppermute | solution.py:586
  21.5 11.5 %collective-permute-start.4 = (bf16[1,2,32,16,128]{4,3,2,1,0:T(8,128)(2,1)}, bf16[1,2,32,16,128]{4,3,2,1,0:T(8,128)(2,1)}, u32[]{:S(2)}, u32[]{:S(2)}) collective-permute-start(bf16[1,2,32,16,128]{4,3,2,1,0:T(8,128)(2,1)} %get-tuple-element.108), channel_id=1, source_target_pairs={{0,5},{1,6},{2,7},{3,0},{4,1},{5,2},{6,3},{7,4},{8,13},{9,14},{10,... | collective-permute-start | bytes 786440 | tf_op jit(solution)/shard_map/ppermute | solution.py:586
  21.5 13.5 %collective-permute-start.6 = (bf16[1,2,32,16,128]{4,3,2,1,0:T(8,128)(2,1)}, bf16[1,2,32,16,128]{4,3,2,1,0:T(8,128)(2,1)}, u32[]{:S(2)}, u32[]{:S(2)}) collective-permute-start(bf16[1,2,32,16,128]{4,3,2,1,0:T(8,128)(2,1)} %get-tuple-element.110), channel_id=1, source_target_pairs={{0,7},{1,0},{2,1},{3,2},{4,3},{5,4},{6,5},{7,6},{8,15},{9,8},{10,9... | collective-permute-start | bytes 786440 | tf_op jit(solution)/shard_map/ppermute | solution.py:586
  30.6 17.6 %collective-permute-start.7 = (bf16[1,2,32,16,128]{4,3,2,1,0:T(8,128)(2,1)}, bf16[1,2,32,16,128]{4,3,2,1,0:T(8,128)(2,1)}, u32[]{:S(2)}, u32[]{:S(2)}) collective-permute-start(bf16[1,2,32,16,128]{4,3,2,1,0:T(8,128)(2,1)} %get-tuple-element.112), channel_id=1, source_target_pairs={{0,1},{1,2},{2,3},{3,4},{4,5},{5,6},{6,7},{7,0},{8,9},{9,10},{10,1... | collective-permute-start | bytes 786440 | tf_op jit(solution)/shard_map/ppermute | solution.py:586
  30.6 17.6 %collective-permute-start.8 = (bf16[1,2,32,16,128]{4,3,2,1,0:T(8,128)(2,1)}, bf16[1,2,32,16,128]{4,3,2,1,0:T(8,128)(2,1)}, u32[]{:S(2)}, u32[]{:S(2)}) collective-permute-start(bf16[1,2,32,16,128]{4,3,2,1,0:T(8,128)(2,1)} %get-tuple-element.113), channel_id=1, source_target_pairs={{0,2},{1,3},{2,4},{3,5},{4,6},{5,7},{6,0},{7,1},{8,10},{9,11},{10,... | collective-permute-start | bytes 786440 | tf_op jit(solution)/shard_map/ppermute | solution.py:586
  32.9 34.1 %collective-permute-start.9 = (bf16[1,2,32,16,128]{4,3,2,1,0:T(8,128)(2,1)}, bf16[1,2,32,16,128]{4,3,2,1,0:T(8,128)(2,1)}, u32[]{:S(2)}, u32[]{:S(2)}) collective-permute-start(bf16[1,2,32,16,128]{4,3,2,1,0:T(8,128)(2,1)} %get-tuple-element.114), channel_id=1, source_target_pairs={{0,3},{1,4},{2,5},{3,6},{4,7},{5,0},{6,1},{7,2},{8,11},{9,12},{10,... | collective-permute-start | bytes 786440 | tf_op jit(solution)/shard_map/ppermute | solution.py:586
  32.9 47.9 %collective-permute-start.10 = (bf16[1,2,32,16,128]{4,3,2,1,0:T(8,128)(2,1)}, bf16[1,2,32,16,128]{4,3,2,1,0:T(8,128)(2,1)}, u32[]{:S(2)}, u32[]{:S(2)}) collective-permute-start(bf16[1,2,32,16,128]{4,3,2,1,0:T(8,128)(2,1)} %get-tuple-element.115), channel_id=1, source_target_pairs={{0,4},{1,5},{2,6},{3,7},{4,0},{5,1},{6,2},{7,3},{8,12},{9,13},{10,... | collective-permute-start | bytes 786440 | tf_op jit(solution)/shard_map/ppermute | solution.py:586
  35.0 46.2 %collective-permute-start.11 = (bf16[1,2,32,16,128]{4,3,2,1,0:T(8,128)(2,1)}, bf16[1,2,32,16,128]{4,3,2,1,0:T(8,128)(2,1)}, u32[]{:S(2)}, u32[]{:S(2)}) collective-permute-start(bf16[1,2,32,16,128]{4,3,2,1,0:T(8,128)(2,1)} %get-tuple-element.116), channel_id=1, source_target_pairs={{0,5},{1,6},{2,7},{3,0},{4,1},{5,2},{6,3},{7,4},{8,13},{9,14},{10,... | collective-permute-start | bytes 786440 | tf_op jit(solution)/shard_map/ppermute | solution.py:586
  48.1 46.6 %collective-permute-start.21 = (bf16[1,2,32,32,128]{4,3,2,1,0:T(8,128)(2,1)}, bf16[1,2,32,32,128]{4,3,2,1,0:T(8,128)(2,1)}, u32[]{:S(2)}, u32[]{:S(2)}) collective-permute-start(bf16[1,2,32,32,128]{4,3,2,1,0:T(8,128)(2,1)} %get-tuple-element.132), channel_id=1, source_target_pairs={{0,1},{1,2},{2,3},{3,4},{4,5},{5,6},{6,7},{7,0},{8,9},{9,10},{10,1... | collective-permute-start | bytes 1572872 | tf_op jit(solution)/shard_map/ppermute | solution.py:586
  48.2 47.2 %collective-permute-start.22 = (bf16[1,2,32,32,128]{4,3,2,1,0:T(8,128)(2,1)}, bf16[1,2,32,32,128]{4,3,2,1,0:T(8,128)(2,1)}, u32[]{:S(2)}, u32[]{:S(2)}) collective-permute-start(bf16[1,2,32,32,128]{4,3,2,1,0:T(8,128)(2,1)} %get-tuple-element.133), channel_id=1, source_target_pairs={{0,2},{1,3},{2,4},{3,5},{4,6},{5,7},{6,0},{7,1},{8,10},{9,11},{10,... | collective-permute-start | bytes 1572872 | tf_op jit(solution)/shard_map/ppermute | solution.py:586
  67.1 28.3 %collective-permute-start.23 = (bf16[1,2,32,32,128]{4,3,2,1,0:T(8,128)(2,1)}, bf16[1,2,32,32,128]{4,3,2,1,0:T(8,128)(2,1)}, u32[]{:S(2)}, u32[]{:S(2)}) collective-permute-start(bf16[1,2,32,32,128]{4,3,2,1,0:T(8,128)(2,1)} %get-tuple-element.134), channel_id=1, source_target_pairs={{0,3},{1,4},{2,5},{3,6},{4,7},{5,0},{6,1},{7,2},{8,11},{9,12},{10,... | collective-permute-start | bytes 1572872 | tf_op jit(solution)/shard_map/ppermute | solution.py:586
  80.9 10.6 %collective-permute-start.12 = (bf16[1,2,32,16,128]{4,3,2,1,0:T(8,128)(2,1)}, bf16[1,2,32,16,128]{4,3,2,1,0:T(8,128)(2,1)}, u32[]{:S(2)}, u32[]{:S(2)}) collective-permute-start(bf16[1,2,32,16,128]{4,3,2,1,0:T(8,128)(2,1)} %get-tuple-element.117), channel_id=1, source_target_pairs={{0,6},{1,7},{2,0},{3,1},{4,2},{5,3},{6,4},{7,5},{8,14},{9,15},{10,... | collective-permute-start | bytes 786440 | tf_op jit(solution)/shard_map/ppermute | solution.py:586
  81.2 10.4 %collective-permute-start.13 = (bf16[1,2,32,16,128]{4,3,2,1,0:T(8,128)(2,1)}, bf16[1,2,32,16,128]{4,3,2,1,0:T(8,128)(2,1)}, u32[]{:S(2)}, u32[]{:S(2)}) collective-permute-start(bf16[1,2,32,16,128]{4,3,2,1,0:T(8,128)(2,1)} %get-tuple-element.118), channel_id=1, source_target_pairs={{0,7},{1,0},{2,1},{3,2},{4,3},{5,4},{6,5},{7,6},{8,15},{9,8},{10,9... | collective-permute-start | bytes 786440 | tf_op jit(solution)/shard_map/ppermute | solution.py:586
  91.5 25.0 %collective-permute-start.24 = (bf16[1,2,32,32,128]{4,3,2,1,0:T(8,128)(2,1)}, bf16[1,2,32,32,128]{4,3,2,1,0:T(8,128)(2,1)}, u32[]{:S(2)}, u32[]{:S(2)}) collective-permute-start(bf16[1,2,32,32,128]{4,3,2,1,0:T(8,128)(2,1)} %get-tuple-element.135), channel_id=1, source_target_pairs={{0,4},{1,5},{2,6},{3,7},{4,0},{5,1},{6,2},{7,3},{8,12},{9,13},{10,... | collective-permute-start | bytes 1572872 | tf_op jit(solution)/shard_map/ppermute | solution.py:586
  91.5 36.8 %collective-permute-start.25 = (bf16[1,2,32,32,128]{4,3,2,1,0:T(8,128)(2,1)}, bf16[1,2,32,32,128]{4,3,2,1,0:T(8,128)(2,1)}, u32[]{:S(2)}, u32[]{:S(2)}) collective-permute-start(bf16[1,2,32,32,128]{4,3,2,1,0:T(8,128)(2,1)} %get-tuple-element.136), channel_id=1, source_target_pairs={{0,5},{1,6},{2,7},{3,0},{4,1},{5,2},{6,3},{7,4},{8,13},{9,14},{10,... | collective-permute-start | bytes 1572872 | tf_op jit(solution)/shard_map/ppermute | solution.py:586
  94.7 35.3 %collective-permute-start.26 = (bf16[1,2,32,32,128]{4,3,2,1,0:T(8,128)(2,1)}, bf16[1,2,32,32,128]{4,3,2,1,0:T(8,128)(2,1)}, u32[]{:S(2)}, u32[]{:S(2)}) collective-permute-start(bf16[1,2,32,32,128]{4,3,2,1,0:T(8,128)(2,1)} %get-tuple-element.137), channel_id=1, source_target_pairs={{0,6},{1,7},{2,0},{3,1},{4,2},{5,3},{6,4},{7,5},{8,14},{9,15},{10,... | collective-permute-start | bytes 1572872 | tf_op jit(solution)/shard_map/ppermute | solution.py:586
  95.4 36.1 %collective-permute-start.27 = (bf16[1,2,32,32,128]{4,3,2,1,0:T(8,128)(2,1)}, bf16[1,2,32,32,128]{4,3,2,1,0:T(8,128)(2,1)}, u32[]{:S(2)}, u32[]{:S(2)}) collective-permute-start(bf16[1,2,32,32,128]{4,3,2,1,0:T(8,128)(2,1)} %get-tuple-element.138), channel_id=1, source_target_pairs={{0,7},{1,0},{2,1},{3,2},{4,3},{5,4},{6,5},{7,6},{8,15},{9,8},{10,9... | collective-permute-start | bytes 1572872 | tf_op jit(solution)/shard_map/ppermute | solution.py:586
  95.4 39.2 %collective-permute-start.28 = (bf16[1,2,32,32,128]{4,3,2,1,0:T(8,128)(2,1)}, bf16[1,2,32,32,128]{4,3,2,1,0:T(8,128)(2,1)}, u32[]{:S(2)}, u32[]{:S(2)}) collective-permute-start(bf16[1,2,32,32,128]{4,3,2,1,0:T(8,128)(2,1)} %get-tuple-element.152), channel_id=1, source_target_pairs={{0,1},{1,2},{2,3},{3,4},{4,5},{5,6},{6,7},{7,0},{8,9},{9,10},{10,1... | collective-permute-start | bytes 1572872 | tf_op jit(solution)/shard_map/ppermute | solution.py:586
  116.4 42.7 %collective-permute-start.29 = (bf16[1,2,32,32,128]{4,3,2,1,0:T(8,128)(2,1)}, bf16[1,2,32,32,128]{4,3,2,1,0:T(8,128)(2,1)}, u32[]{:S(2)}, u32[]{:S(2)}) collective-permute-start(bf16[1,2,32,32,128]{4,3,2,1,0:T(8,128)(2,1)} %get-tuple-element.153), channel_id=1, source_target_pairs={{0,2},{1,3},{2,4},{3,5},{4,6},{5,7},{6,0},{7,1},{8,10},{9,11},{10,... | collective-permute-start | bytes 1572872 | tf_op jit(solution)/shard_map/ppermute | solution.py:586
  128.3 30.9 %collective-permute-start.30 = (bf16[1,2,32,32,128]{4,3,2,1,0:T(8,128)(2,1)}, bf16[1,2,32,32,128]{4,3,2,1,0:T(8,128)(2,1)}, u32[]{:S(2)}, u32[]{:S(2)}) collective-permute-start(bf16[1,2,32,32,128]{4,3,2,1,0:T(8,128)(2,1)} %get-tuple-element.154), channel_id=1, source_target_pairs={{0,3},{1,4},{2,5},{3,6},{4,7},{5,0},{6,1},{7,2},{8,11},{9,12},{10,... | collective-permute-start | bytes 1572872 | tf_op jit(solution)/shard_map/ppermute | solution.py:586
  130.0 44.4 %collective-permute-start.31 = (bf16[1,2,32,32,128]{4,3,2,1,0:T(8,128)(2,1)}, bf16[1,2,32,32,128]{4,3,2,1,0:T(8,128)(2,1)}, u32[]{:S(2)}, u32[]{:S(2)}) collective-permute-start(bf16[1,2,32,32,128]{4,3,2,1,0:T(8,128)(2,1)} %get-tuple-element.155), channel_id=1, source_target_pairs={{0,4},{1,5},{2,6},{3,7},{4,0},{5,1},{6,2},{7,3},{8,12},{9,13},{10,... | collective-permute-start | bytes 1572872 | tf_op jit(solution)/shard_map/ppermute | solution.py:586
  131.5 49.2 %collective-permute-start.32 = (bf16[1,2,32,32,128]{4,3,2,1,0:T(8,128)(2,1)}, bf16[1,2,32,32,128]{4,3,2,1,0:T(8,128)(2,1)}, u32[]{:S(2)}, u32[]{:S(2)}) collective-permute-start(bf16[1,2,32,32,128]{4,3,2,1,0:T(8,128)(2,1)} %get-tuple-element.156), channel_id=1, source_target_pairs={{0,5},{1,6},{2,7},{3,0},{4,1},{5,2},{6,3},{7,4},{8,13},{9,14},{10,... | collective-permute-start | bytes 1572872 | tf_op jit(solution)/shard_map/ppermute | solution.py:586
  134.6 46.1 %collective-permute-start.33 = (bf16[1,2,32,32,128]{4,3,2,1,0:T(8,128)(2,1)}, bf16[1,2,32,32,128]{4,3,2,1,0:T(8,128)(2,1)}, u32[]{:S(2)}, u32[]{:S(2)}) collective-permute-start(bf16[1,2,32,32,128]{4,3,2,1,0:T(8,128)(2,1)} %get-tuple-element.157), channel_id=1, source_target_pairs={{0,6},{1,7},{2,0},{3,1},{4,2},{5,3},{6,4},{7,5},{8,14},{9,15},{10,... | collective-permute-start | bytes 1572872 | tf_op jit(solution)/shard_map/ppermute | solution.py:586
  159.1 44.6 %collective-permute-start.34 = (bf16[1,2,32,32,128]{4,3,2,1,0:T(8,128)(2,1)}, bf16[1,2,32,32,128]{4,3,2,1,0:T(8,128)(2,1)}, u32[]{:S(2)}, u32[]{:S(2)}) collective-permute-start(bf16[1,2,32,32,128]{4,3,2,1,0:T(8,128)(2,1)} %get-tuple-element.158), channel_id=1, source_target_pairs={{0,7},{1,0},{2,1},{3,2},{4,3},{5,4},{6,5},{7,6},{8,15},{9,8},{10,9... | collective-permute-start | bytes 1572872 | tf_op jit(solution)/shard_map/ppermute | solution.py:586
  159.2 47.5 %collective-permute-start.35 = (bf16[1,2,32,32,128]{4,3,2,1,0:T(8,128)(2,1)}, bf16[1,2,32,32,128]{4,3,2,1,0:T(8,128)(2,1)}, u32[]{:S(2)}, u32[]{:S(2)}) collective-permute-start(bf16[1,2,32,32,128]{4,3,2,1,0:T(8,128)(2,1)} %get-tuple-element.169), channel_id=1, source_target_pairs={{0,1},{1,2},{2,3},{3,4},{4,5},{5,6},{6,7},{7,0},{8,9},{9,10},{10,1... | collective-permute-start | bytes 1572872 | tf_op jit(solution)/shard_map/ppermute | solution.py:586
  174.4 40.1 %collective-permute-start.36 = (bf16[1,2,32,32,128]{4,3,2,1,0:T(8,128)(2,1)}, bf16[1,2,32,32,128]{4,3,2,1,0:T(8,128)(2,1)}, u32[]{:S(2)}, u32[]{:S(2)}) collective-permute-start(bf16[1,2,32,32,128]{4,3,2,1,0:T(8,128)(2,1)} %get-tuple-element.170), channel_id=1, source_target_pairs={{0,2},{1,3},{2,4},{3,5},{4,6},{5,7},{6,0},{7,1},{8,10},{9,11},{10,... | collective-permute-start | bytes 1572872 | tf_op jit(solution)/shard_map/ppermute | solution.py:586
  180.7 33.8 %collective-permute-start.37 = (bf16[1,2,32,32,128]{4,3,2,1,0:T(8,128)(2,1)}, bf16[1,2,32,32,128]{4,3,2,1,0:T(8,128)(2,1)}, u32[]{:S(2)}, u32[]{:S(2)}) collective-permute-start(bf16[1,2,32,32,128]{4,3,2,1,0:T(8,128)(2,1)} %get-tuple-element.171), channel_id=1, source_target_pairs={{0,3},{1,4},{2,5},{3,6},{4,7},{5,0},{6,1},{7,2},{8,11},{9,12},{10,... | collective-permute-start | bytes 1572872 | tf_op jit(solution)/shard_map/ppermute | solution.py:586
  180.7 35.6 %collective-permute-start.38 = (bf16[1,2,32,32,128]{4,3,2,1,0:T(8,128)(2,1)}, bf16[1,2,32,32,128]{4,3,2,1,0:T(8,128)(2,1)}, u32[]{:S(2)}, u32[]{:S(2)}) collective-permute-start(bf16[1,2,32,32,128]{4,3,2,1,0:T(8,128)(2,1)} %get-tuple-element.172), channel_id=1, source_target_pairs={{0,4},{1,5},{2,6},{3,7},{4,0},{5,1},{6,2},{7,3},{8,12},{9,13},{10,... | collective-permute-start | bytes 1572872 | tf_op jit(solution)/shard_map/ppermute | solution.py:586
  203.8 33.2 %collective-permute-start.39 = (bf16[1,2,32,32,128]{4,3,2,1,0:T(8,128)(2,1)}, bf16[1,2,32,32,128]{4,3,2,1,0:T(8,128)(2,1)}, u32[]{:S(2)}, u32[]{:S(2)}) collective-permute-start(bf16[1,2,32,32,128]{4,3,2,1,0:T(8,128)(2,1)} %get-tuple-element.173), channel_id=1, source_target_pairs={{0,5},{1,6},{2,7},{3,0},{4,1},{5,2},{6,3},{7,4},{8,13},{9,14},{10,... | collective-permute-start | bytes 1572872 | tf_op jit(solution)/shard_map/ppermute | solution.py:586
  206.7 39.2 %collective-permute-start.40 = (bf16[1,2,32,32,128]{4,3,2,1,0:T(8,128)(2,1)}, bf16[1,2,32,32,128]{4,3,2,1,0:T(8,128)(2,1)}, u32[]{:S(2)}, u32[]{:S(2)}) collective-permute-start(bf16[1,2,32,32,128]{4,3,2,1,0:T(8,128)(2,1)} %get-tuple-element.174), channel_id=1, source_target_pairs={{0,6},{1,7},{2,0},{3,1},{4,2},{5,3},{6,4},{7,5},{8,14},{9,15},{10,... | collective-permute-start | bytes 1572872 | tf_op jit(solution)/shard_map/ppermute | solution.py:586
  214.5 31.4 %collective-permute-start.41 = (bf16[1,2,32,32,128]{4,3,2,1,0:T(8,128)(2,1)}, bf16[1,2,32,32,128]{4,3,2,1,0:T(8,128)(2,1)}, u32[]{:S(2)}, u32[]{:S(2)}) collective-permute-start(bf16[1,2,32,32,128]{4,3,2,1,0:T(8,128)(2,1)} %get-tuple-element.175), channel_id=1, source_target_pairs={{0,7},{1,0},{2,1},{3,2},{4,3},{5,4},{6,5},{7,6},{8,15},{9,8},{10,9... | collective-permute-start | bytes 1572872 | tf_op jit(solution)/shard_map/ppermute | solution.py:586
  214.5 31.4 %collective-permute-start.14 = (bf16[2,1024,128]{2,1,0:T(8,128)(2,1)}, bf16[2,1024,128]{2,1,0:T(8,128)(2,1)}, u32[]{:S(2)}, u32[]{:S(2)}) collective-permute-start(bf16[2,1024,128]{2,1,0:T(8,128)(2,1)} %get-tuple-element.121), channel_id=1, source_target_pairs={{0,1},{1,2},{2,3},{3,4},{4,5},{5,6},{6,7},{7,0},{8,9},{9,10},{10,1... | collective-permute-start | bytes 1572872 | tf_op jit(solution)/shard_map/ppermute | solution.py:586
  216.3 43.9 %collective-permute-start.15 = (bf16[2,1024,128]{2,1,0:T(8,128)(2,1)}, bf16[2,1024,128]{2,1,0:T(8,128)(2,1)}, u32[]{:S(2)}, u32[]{:S(2)}) collective-permute-start(bf16[2,1024,128]{2,1,0:T(8,128)(2,1)} %get-tuple-element.122), channel_id=1, source_target_pairs={{0,2},{1,3},{2,4},{3,5},{4,6},{5,7},{6,0},{7,1},{8,10},{9,11},{10,... | collective-permute-start | bytes 1572872 | tf_op jit(solution)/shard_map/ppermute | solution.py:586
  237.0 44.0 %collective-permute-start.16 = (bf16[2,1024,128]{2,1,0:T(8,128)(2,1)}, bf16[2,1024,128]{2,1,0:T(8,128)(2,1)}, u32[]{:S(2)}, u32[]{:S(2)}) collective-permute-start(bf16[2,1024,128]{2,1,0:T(8,128)(2,1)} %get-tuple-element.123), channel_id=1, source_target_pairs={{0,3},{1,4},{2,5},{3,6},{4,7},{5,0},{6,1},{7,2},{8,11},{9,12},{10,... | collective-permute-start | bytes 1572872 | tf_op jit(solution)/shard_map/ppermute | solution.py:586
  245.9 37.2 %collective-permute-start.17 = (bf16[2,1024,128]{2,1,0:T(8,128)(2,1)}, bf16[2,1024,128]{2,1,0:T(8,128)(2,1)}, u32[]{:S(2)}, u32[]{:S(2)}) collective-permute-start(bf16[2,1024,128]{2,1,0:T(8,128)(2,1)} %get-tuple-element.124), channel_id=1, source_target_pairs={{0,4},{1,5},{2,6},{3,7},{4,0},{5,1},{6,2},{7,3},{8,12},{9,13},{10,... | collective-permute-start | bytes 1572872 | tf_op jit(solution)/shard_map/ppermute | solution.py:586
  245.9 37.3 %collective-permute-start.18 = (bf16[2,1024,128]{2,1,0:T(8,128)(2,1)}, bf16[2,1024,128]{2,1,0:T(8,128)(2,1)}, u32[]{:S(2)}, u32[]{:S(2)}) collective-permute-start(bf16[2,1024,128]{2,1,0:T(8,128)(2,1)} %get-tuple-element.125), channel_id=1, source_target_pairs={{0,5},{1,6},{2,7},{3,0},{4,1},{5,2},{6,3},{7,4},{8,13},{9,14},{10,... | collective-permute-start | bytes 1572872 | tf_op jit(solution)/shard_map/ppermute | solution.py:586
  246.0 37.2 %collective-permute-start.19 = (bf16[2,1024,128]{2,1,0:T(8,128)(2,1)}, bf16[2,1024,128]{2,1,0:T(8,128)(2,1)}, u32[]{:S(2)}, u32[]{:S(2)}) collective-permute-start(bf16[2,1024,128]{2,1,0:T(8,128)(2,1)} %get-tuple-element.126), channel_id=1, source_target_pairs={{0,6},{1,7},{2,0},{3,1},{4,2},{5,3},{6,4},{7,5},{8,14},{9,15},{10,... | collective-permute-start | bytes 1572872 | tf_op jit(solution)/shard_map/ppermute | solution.py:586
  260.1 23.0 %collective-permute-start.20 = (bf16[2,1024,128]{2,1,0:T(8,128)(2,1)}, bf16[2,1024,128]{2,1,0:T(8,128)(2,1)}, u32[]{:S(2)}, u32[]{:S(2)}) collective-permute-start(bf16[2,1024,128]{2,1,0:T(8,128)(2,1)} %get-tuple-element.127), channel_id=1, source_target_pairs={{0,7},{1,0},{2,1},{3,2},{4,3},{5,4},{6,5},{7,6},{8,15},{9,8},{10,9... | collective-permute-start | bytes 1572872 | tf_op jit(solution)/shard_map/ppermute | solution.py:586

commit v9 on v8

--- a/solution.py
+++ b/solution.py
@@ -392,17 +392,14 @@
     )(*values)
 
 
-def finish_kernel(n, shares, kl, xl, chunks, sent, table_ref, sens, image, auxiliary, dual, *refs):
+def finish_kernel(n, shares, kl, xl, sent, table_ref, sens, image, auxiliary, dual, *refs):
     coils = sens.shape[0]
     backs, refs = [refs[k * n : (k + 1) * n] for k in range(coils)], refs[coils * n :]
     image_out, aux_out, dual_out, table, held, landing, sens_v, grad, got, recv, send, local, grad_recv, grad_send, *wide = refs
     ready = coils - sent
     length = n * kl
-    depth = landing.shape[-1]
     share = length // shares
-    rows = xl // chunks
-    band = rows * kl
-    group = min(rows, 2)
+    band = kl
     me = lax.axis_index("slab")
     mine = lax.axis_index("coil")
 
@@ -429,13 +426,13 @@
                     src_ref=backs[k][off].at[:, where, :],
                     dst_ref=landing.at[k, me, :, where, :],
                     send_sem=send,
-                    recv_sem=recv.at[j],
+                    recv_sem=recv.at[j, k - ready],
                     device_id={"slab": ahead(me, off, n)},
                     device_id_type=pl.DeviceIdType.MESH,
                 ).start()
         return carry
 
-    lax.fori_loop(0, chunks, send_band, 0)
+    lax.fori_loop(0, xl, send_band, 0)
     columns = pl.ds(pl.multiple_of(mine * share, share), share)
     copies = [pltpu.make_async_copy(table_ref, table, local.at[coils * n + coils])]
     for k, source in enumerate((image.at[:, :, columns], auxiliary, dual)):
@@ -450,72 +447,55 @@
     for copy in copies:
         copy.wait()
 
-    def add_band(j):
-        arrived = got.at[0 : shares - 1, :, pl.ds(j * rows, rows)]
-        pltpu.make_async_copy(arrived, arrived, grad_recv.at[j]).wait()
-        for i in range(rows):
-            x = j * rows + i
-            for p in range(2):
-                value = grad[mine, p, x].astype(F32)
-                for off in range(1, shares):
-                    value += got[lax.rem(mine + off, shares), p, x].astype(F32)
-                image_out[p, x] = value
+    def add_band(x):
+        arrived = got.at[0 : shares - 1, :, x]
+        pltpu.make_async_copy(arrived, arrived, grad_recv.at[x]).wait()
+        for p in range(2):
+            value = grad[mine, p, x].astype(F32)
+            for off in range(1, shares):
+                value += got[lax.rem(mine + off, shares), p, x].astype(F32)
+            image_out[p, x] = value
 
     def settle(m):
-        for k in range(2 // rows):
-            add_band(2 // rows * m + k)
+        for h in range(2):
+            add_band(2 * m + h)
         update_pair(2 * m, held.at[0], image_out, held.at[1], held.at[2], image_out, aux_out, dual_out)
+
+    def farthest(turn):
+        upper = mine // max(shares // 2, 1)
+        down = shares - 2 - turn + (2 * shares - 2 - turn - mine) // shares
+        up = turn + 1 - (shares + mine - turn - 1) // shares
+        return down * (1 - upper) + up * upper
 
     def do_band(j, carry):
         where = pl.ds(pl.multiple_of(j * band, band), band)
-        arrived = landing.at[ready:coils, 0 : n - 1, :, where, :]
-        pltpu.make_async_copy(arrived, arrived, recv.at[j]).wait()
-        if wide:
-            for k in range(coils):
-                for s in range(n):
-                    for p in range(2):
-                        wide[0][k, s, p] = landing[k, s, p, where, :].astype(F32)
-
-        def columns_of(k, i):
-            pieces = []
-            for p in range(2):
-                for s in range(n):
-                    if wide:
-                        pieces.append(wide[0][k, s, p, pl.ds(pl.multiple_of(i * kl, kl), kl), :])
-                    else:
-                        row = pl.multiple_of((j * rows + i) * kl, kl)
-                        pieces.append(landing[k, s, p, pl.ds(row, kl), :])
-            return jnp.concatenate(pieces, axis=0).astype(BF16)
-
-        def pair(i, carry):
-            total = [[None, None]] * group
-            for k in range(coils):
-                both = jnp.concatenate([columns_of(k, group * i + h) for h in range(group)], axis=1)
-                adj = jnp.dot(table[...], both, preferred_element_type=F32)
-                adj = adj.astype(BF16).astype(F32)
-                for h in range(group):
-                    x = j * rows + group * i + h
-                    ar = adj[:length, h * depth : (h + 1) * depth]
-                    ai = adj[length:, h * depth : (h + 1) * depth]
-                    sr = sens_v[k, 0, x].astype(F32)
-                    si = sens_v[k, 1, x].astype(F32)
-                    re = sr * ar + si * ai
-                    im = sr * ai - si * ar
-                    total[h] = [re, im] if k == 0 else [total[h][0] + re, total[h][1] + im]
-            for h in range(group):
-                x = j * rows + group * i + h
-                for p in range(2):
-                    for q in range(shares):
-                        grad[q, p, x] = total[h][p][q * share : (q + 1) * share].astype(BF16)
-            return carry
-
-        lax.fori_loop(0, rows // group, pair, 0)
-        lines = pl.ds(j * rows, rows)
-        for off in range(1, shares):
-            target = lax.rem(mine + off, shares)
+        re = im = None
+        for k in range(coils):
+            if k >= ready:
+                arrived = landing.at[k, 0 : n - 1, :, where, :]
+                pltpu.make_async_copy(arrived, arrived, recv.at[j, k - ready]).wait()
+            pieces = [landing[k, s, p, where, :] for p in range(2) for s in range(n)]
+            if wide:
+                for i, piece in enumerate(pieces):
+                    wide[0][i * kl : (i + 1) * kl, :] = piece.astype(F32)
+                both = wide[0][...].astype(BF16)
+            else:
+                both = jnp.concatenate(pieces, axis=0)
+            adj = jnp.dot(table[...], both, preferred_element_type=F32)
+            adj = adj.astype(BF16).astype(F32)
+            ar, ai = adj[:length], adj[length:]
+            sr = sens_v[k, 0, j].astype(F32)
+            si = sens_v[k, 1, j].astype(F32)
+            re = sr * ar + si * ai if k == 0 else re + (sr * ar + si * ai)
+            im = sr * ai - si * ar if k == 0 else im + (sr * ai - si * ar)
+        for p, value in enumerate((re, im)):
+            for q in range(shares):
+                grad[q, p, j] = value[q * share : (q + 1) * share].astype(BF16)
+        for turn in range(shares - 1):
+            target = farthest(turn)
             pltpu.make_async_remote_copy(
-                src_ref=grad.at[target, :, lines],
-                dst_ref=got.at[mine, :, lines],
+                src_ref=grad.at[target, :, j],
+                dst_ref=got.at[mine, :, j],
                 send_sem=grad_send,
                 recv_sem=grad_recv.at[j],
                 device_id={"coil": target},
@@ -528,8 +508,8 @@
 
         return carry
 
-    lax.fori_loop(0, chunks, do_band, 0)
-    settle(chunks // 2 - 1)
+    lax.fori_loop(0, xl, do_band, 0)
+    settle(xl // 2 - 1)
     gone = landing.at[ready:coils, 0 : n - 1]
     pltpu.make_async_copy(gone, gone, send).wait()
     gone = got.at[0 : shares - 1]
@@ -538,8 +518,6 @@
 
 def finish_call(table, backs, sent, sensitivity, image, auxiliary, dual, shares, n, kl):
     coils, _, xl, length, depth = sensitivity.shape
-    chunks = xl
-    rows = xl // chunks
     share = length // shares
     vmem = pl.BlockSpec(memory_space=pltpu.VMEM)
     scratch = [
@@ -549,17 +527,17 @@
         pltpu.VMEM(sensitivity.shape, BF16),
         pltpu.VMEM((shares, 2, xl, share, depth), BF16),
         pltpu.VMEM((shares, 2, xl, share, depth), BF16),
-        pltpu.SemaphoreType.DMA((chunks,)),
+        pltpu.SemaphoreType.DMA((xl, sent)),
         pltpu.SemaphoreType.DMA,
         pltpu.SemaphoreType.DMA((coils * n + coils + 4,)),
-        pltpu.SemaphoreType.DMA((chunks,)),
+        pltpu.SemaphoreType.DMA((xl,)),
         pltpu.SemaphoreType.DMA,
     ]
     if kl % 16:
-        scratch.append(pltpu.VMEM((coils, n, 2, rows * kl, depth), F32))
+        scratch.append(pltpu.VMEM((2 * length, depth), F32))
     limit = VMEM_LIMIT - 26 * xl * share * depth
     return pl.pallas_call(
-        functools.partial(finish_kernel, n, shares, kl, xl, chunks, sent),
+        functools.partial(finish_kernel, n, shares, kl, xl, sent),
         in_specs=[HBM] * (5 + coils * n),
         out_specs=[vmem] * 3,
         out_shape=[pltpu.VMEM((2, xl, share, depth), F32)] * 3,

time: 438 us -> 437 us (level)
  no operation moved by 1% of the time
where the time goes in v9:
time: 437 us; the launch traced here: 434 us
  Pallas kernels  289 us (66%)
  starting transfers between devices  77.9 us (18%)
  waiting for transfers between devices  65 us (15%)
    pallas_call x1, Pallas kernels, finish_call(): pl.pallas_call(functools.partial(finish_kernel, n, shares, kl, xl, sent),...  148 us
    pallas_call x4, Pallas kernels, tile_call(): pl.pallas_call(functools.partial(tile_kernel, n, kl, xl, cells // kl, par...  83.2 us
    ppermute x42, starting transfers between devices, swap(): lax.ppermute(parts[turn], 'slab', [(i, ahead(i, off, n)) for i in range(n)])  77.9 us
    ppermute x42, waiting for transfers between devices, swap(): lax.ppermute(parts[turn], 'slab', [(i, ahead(i, off, n)) for i in range(n)])  65 us
    pallas_call x6, Pallas kernels, forward_call(): pl.pallas_call(functools.partial(forward_kernel, n, kl, xp, offs), grid=(...  47.3 us
  transfers between devices with their start and end apart: 42, of which 9 were waited for; matrix products, arithmetic and copies ran while one was open for 0% of the time, Pallas kernels for 31%

profile of v9, /device:TPU:9, one launch (start us, length us, event | category | flops | bytes accessed | tf_op | source)
XLA Modules:
  0.0 433.9 jit_solution(15247054338760173303)
XLA Ops:
  0.6 5.1 %forward.6 = (bf16[1,2,32,16,128]{4,3,2,1,0:T(8,128)(2,1)}, bf16[1,2,32,16,128]{4,3,2,1,0:T(8,128)(2,1)}, bf16[1,2,32,16,128]{4,3,2,1,0:T(8,128)(2,1)}, bf16[1,2,32,16,128]{4,3,2,1,0:T(8,128)(2,1)}) custom-call(bf16[512,512]{1,0:T(8,128)(2,1)} %constant.11.table.fwd, f32[2,32,256,128]{3,2,1,0:T(8,128)} %image.13, bf16[4,2,32,256,128]{4,3,2,1,0:T(8,128)(2,1)} %sens.13), custom_call_target="tpu_custom_call" | custom-call | flops 1073741824 | bytes 6291456 | tf_op jit(solution)/shard_map/forward/pallas_call | solution.py:134
  5.7 1.8 collective-permute-start.2
  7.5 1.2 collective-permute-start.1
  8.7 0.2 collective-permute-start.3
  8.9 1.2 collective-permute-start.5
  10.1 5.0 %forward.7 = (bf16[1,2,32,16,128]{4,3,2,1,0:T(8,128)(2,1)}, bf16[1,2,32,16,128]{4,3,2,1,0:T(8,128)(2,1)}, bf16[1,2,32,16,128]{4,3,2,1,0:T(8,128)(2,1)}, bf16[1,2,32,16,128]{4,3,2,1,0:T(8,128)(2,1)}) custom-call(bf16[512,512]{1,0:T(8,128)(2,1)} %constant.11.table.fwd, f32[2,32,256,128]{3,2,1,0:T(8,128)} %image.13, bf16[4,2,32,256,128]{4,3,2,1,0:T(8,128)(2,1)} %sens.13), custom_call_target="tpu_custom_call" | custom-call | flops 1073741824 | bytes 6291456 | tf_op jit(solution)/shard_map/forward/pallas_call | solution.py:134
  15.1 0.9 collective-permute-start
  16.0 5.5 %collective-permute-done.2.refs_3_ = bf16[1,2,32,16,128]{4,3,2,1,0:T(8,128)(2,1)} collective-permute-done((bf16[1,2,32,16,128]{4,3,2,1,0:T(8,128)(2,1)}, bf16[1,2,32,16,128]{4,3,2,1,0:T(8,128)(2,1)}, u32[]{:S(2)}, u32[]{:S(2)}) %collective-permute-start.2) | collective-permute-done | bytes 262176 | tf_op jit(solution)/shard_map/ppermute | solution.py:564
  21.5 0.0 collective-permute-start.4
  21.5 0.0 collective-permute-done.1.refs_2_
  21.5 1.1 collective-permute-start.6
  22.6 6.3 %forward.8 = (bf16[1,2,32,16,128]{4,3,2,1,0:T(8,128)(2,1)}, bf16[1,2,32,16,128]{4,3,2,1,0:T(8,128)(2,1)}, bf16[1,2,32,16,128]{4,3,2,1,0:T(8,128)(2,1)}, bf16[1,2...) custom-call(bf16[512,512]{1,0:T(8,128)(2,1)} %constant.11.table.fwd,, ...), custom_call_target="tpu_custom_call" | custom-call | flops 1073741824 | bytes 6291456 | tf_op jit(solution)/shard_map/forward/pallas_call | solution.py:134
  28.9 1.7 collective-permute-done.3.refs_4_
  30.6 0.0 collective-permute-start.7
  30.6 0.0 collective-permute-done.5.refs_6_
  30.6 2.3 collective-permute-start.8
  32.9 0.0 collective-permute-done.refs_1_
  32.9 0.0 collective-permute-start.9
  32.9 0.0 collective-permute-done.4.refs_5_
  32.9 2.0 collective-permute-start.10
  35.0 0.0 collective-permute-done.6.refs_7_
  35.0 2.9 collective-permute-start.11
  37.8 10.3 %forward.9 = (bf16[1,2,32,32,128]{4,3,2,1,0:T(8,128)(2,1)}, bf16[1,2,32,32,128]{4,3,2,1,0:T(8,128)(2,1)}, bf16[1,2,32,32,128]{4,3,2,1,0:T(8,128)(2,1)}, bf16[1,2...) custom-call(bf16[512,512]{1,0:T(8,128)(2,1)} %constant.11.table.fwd,, ...), custom_call_target="tpu_custom_call" | custom-call | flops 2147483648 | bytes 12582912 | tf_op jit(solution)/shard_map/forward/pallas_call | solution.py:134
  48.1 0.0 collective-permute-done.7.refs_9_
  48.1 0.1 collective-permute-start.21
  48.2 0.0 collective-permute-done.8.refs_10_
  48.2 0.1 collective-permute-start.22
  48.3 18.8 %collective-permute-done.9.refs_11_ = bf16[1,2,32,16,128]{4,3,2,1,0:T(8,128)(2,1)} collective-permute-done((bf16[1,2,32,16,128]{4,3,2,1,0:T(8,128)(2,1)}, bf16[1,2,32,16,128]{4,3,2,1,0:T(8,128)(2,1)}, u32[]{:S(2)}, u32[]{:S(2)}) %collective-permute-start.9) | collective-permute-done | bytes 262176 | tf_op jit(solution)/shard_map/ppermute | solution.py:564
  67.1 2.5 collective-permute-start.23
  69.6 11.3 %collective-permute-done.10.refs_12_ = bf16[1,2,32,16,128]{4,3,2,1,0:T(8,128)(2,1)} collective-permute-done((bf16[1,2,32,16,128]{4,3,2,1,0:T(8,128)(2,1)}, bf16[1,2,32,16,128]{4,3,2,1,0:T(8,128)(2,1)}, u32[]{:S(2)}, u32[]{:S(2)}) %collective-permute-start.10) | collective-permute-done | bytes 262176 | tf_op jit(solution)/shard_map/ppermute | solution.py:564
  80.9 0.3 collective-permute-done.11.refs_13_
  81.2 10.3 %forward.10 = (bf16[1,2,32,32,128]{4,3,2,1,0:T(8,128)(2,1)}, bf16[1,2,32,32,128]{4,3,2,1,0:T(8,128)(2,1)}, bf16[1,2,32,32,128]{4,3,2,1,0:T(8,128)(2,1)}, bf16[1,...) custom-call(bf16[512,512]{1,0:T(8,128)(2,1)} %constant.11.table.fwd,, ...), custom_call_target="tpu_custom_call" | custom-call | flops 2147483648 | bytes 12582912 | tf_op jit(solution)/shard_map/forward/pallas_call | solution.py:134
  91.5 0.1 collective-permute-start.24
  91.5 3.2 collective-permute-start.25
  94.7 0.7 collective-permute-start.26
  95.4 1.7 collective-permute-start.28
  97.8 10.3 %forward.11 = (bf16[1,2,32,32,128]{4,3,2,1,0:T(8,128)(2,1)}, bf16[1,2,32,32,128]{4,3,2,1,0:T(8,128)(2,1)}, bf16[1,2,32,32,128]{4,3,2,1,0:T(8,128)(2,1)}, bf16[1,...) custom-call(bf16[512,512]{1,0:T(8,128)(2,1)} %constant.11.table.fwd,, ...), custom_call_target="tpu_custom_call" | custom-call | flops 2147483648 | bytes 12582912 | tf_op jit(solution)/shard_map/forward/pallas_call | solution.py:134
  108.1 8.3 %sort.1.sorted_samples = bf16[4,24,128,256]{3,2,1,0:T(8,128)(2,1)} custom-call(bf16[24,1024,128]{2,1,0:T(8,128)(2,1)} %bitcast.1), custom_call_target="tpu_custom_call" | custom-call | flops 3145728 | bytes 12582912 | tf_op jit(solution)/shard_map/sort/pallas_call | solution.py:168
  116.4 11.8 %collective-permute-start.29 = (bf16[1,2,32,32,128]{4,3,2,1,0:T(8,128)(2,1)}, bf16[1,2,32,32,128]{4,3,2,1,0:T(8,128)(2,1)}, u32[]{:S(2)}, u32[]{:S(2)}) collective-permute-start(bf16[1,2,32,32,128]{4,3,2,1,0:T(8,128)(2,1)} %get-tuple-element.153), channel_id=1, source_target_pairs={{0,2},{1,3},{2,4},{3,5},{4,6},{5,7},{6,0},{7,1},{8,10},{9,11},{10,... | collective-permute-start | bytes 1572872 | tf_op jit(solution)/shard_map/ppermute | solution.py:564
  128.3 1.7 collective-permute-start.30
  130.0 1.5 collective-permute-start.31
  131.5 3.1 collective-permute-start.32
  134.6 3.7 collective-permute-start.33
  138.3 20.9 %tile.4 = (bf16[2,1024,128]{2,1,0:T(8,128)(2,1)}, bf16[2,1024,128]{2,1,0:T(8,128)(2,1)}, bf16[2,1024,128]{2,1,0:T(8,128)(2,1)}, bf16[2,1024,128]{2,1,0:T(8,128)(...) custom-call(s32[1,24]{1,0:T(1,128)} %offsets.7, ...), custom_call_target="tpu_custom_call" | custom-call | flops 10737418240 | bytes 20971520 | tf_op jit(solution)/shard_map/tile/pallas_call | solution.py:315
  159.1 0.1 collective-permute-start.34
  159.2 1.7 collective-permute-start.35
  160.9 13.5 %collective-permute-done.31.refs_4_ = bf16[1,2,32,32,128]{4,3,2,1,0:T(8,128)(2,1)} collective-permute-done((bf16[1,2,32,32,128]{4,3,2,1,0:T(8,128)(2,1)}, bf16[1,2,32,32,128]{4,3,2,1,0:T(8,128)(2,1)}, u32[]{:S(2)}, u32[]{:S(2)}) %collective-permute-start.31) | collective-permute-done | bytes 524320 | tf_op jit(solution)/shard_map/ppermute | solution.py:564
  174.4 6.3 %collective-permute-start.36 = (bf16[1,2,32,32,128]{4,3,2,1,0:T(8,128)(2,1)}, bf16[1,2,32,32,128]{4,3,2,1,0:T(8,128)(2,1)}, u32[]{:S(2)}, u32[]{:S(2)}) collective-permute-start(bf16[1,2,32,32,128]{4,3,2,1,0:T(8,128)(2,1)} %get-tuple-element.170), channel_id=1, source_target_pairs={{0,2},{1,3},{2,4},{3,5},{4,6},{5,7},{6,0},{7,1},{8,10},{9,11},{10,... | collective-permute-start | bytes 1572872 | tf_op jit(solution)/shard_map/ppermute | solution.py:564
  180.7 2.3 collective-permute-start.38
  183.0 20.8 %tile.5 = (bf16[2,1024,128]{2,1,0:T(8,128)(2,1)}, bf16[2,1024,128]{2,1,0:T(8,128)(2,1)}, bf16[2,1024,128]{2,1,0:T(8,128)(2,1)}, bf16[2,1024,128]{2,1,0:T(8,128)(...) custom-call(s32[1,24]{1,0:T(1,128)} %offsets.7, ...), custom_call_target="tpu_custom_call" | custom-call | flops 10737418240 | bytes 20971520 | tf_op jit(solution)/shard_map/tile/pallas_call | solution.py:315
  203.8 2.9 collective-permute-start.39
  206.7 7.8 %collective-permute-start.40 = (bf16[1,2,32,32,128]{4,3,2,1,0:T(8,128)(2,1)}, bf16[1,2,32,32,128]{4,3,2,1,0:T(8,128)(2,1)}, u32[]{:S(2)}, u32[]{:S(2)}) collective-permute-start(bf16[1,2,32,32,128]{4,3,2,1,0:T(8,128)(2,1)} %get-tuple-element.174), channel_id=1, source_target_pairs={{0,6},{1,7},{2,0},{3,1},{4,2},{5,3},{6,4},{7,5},{8,14},{9,15},{10,... | collective-permute-start | bytes 1572872 | tf_op jit(solution)/shard_map/ppermute | solution.py:564
  214.5 1.7 collective-permute-start.14
  216.3 0.0 collective-permute-start.15
  216.3 20.7 %tile.6 = (bf16[2,1024,128]{2,1,0:T(8,128)(2,1)}, bf16[2,1024,128]{2,1,0:T(8,128)(2,1)}, bf16[2,1024,128]{2,1,0:T(8,128)(2,1)}, bf16[2,1024,128]{2,1,0:T(8,128)(...) custom-call(s32[1,24]{1,0:T(1,128)} %offsets.7, ...), custom_call_target="tpu_custom_call" | custom-call | flops 10737418240 | bytes 20971520 | tf_op jit(solution)/shard_map/tile/pallas_call | solution.py:315
  237.0 8.9 %collective-permute-start.16 = (bf16[2,1024,128]{2,1,0:T(8,128)(2,1)}, bf16[2,1024,128]{2,1,0:T(8,128)(2,1)}, u32[]{:S(2)}, u32[]{:S(2)}) collective-permute-start(bf16[2,1024,128]{2,1,0:T(8,128)(2,1)} %get-tuple-element.123), channel_id=1, source_target_pairs={{0,3},{1,4},{2,5},{3,6},{4,7},{5,0},{6,1},{7,2},{8,11},{9,12},{10,... | collective-permute-start | bytes 1572872 | tf_op jit(solution)/shard_map/ppermute | solution.py:564
  245.9 0.1 collective-permute-start.18
  246.0 2.5 collective-permute-start.19
  248.4 11.7 %collective-permute-done.15.refs_2_ = bf16[2,1024,128]{2,1,0:T(8,128)(2,1)} collective-permute-done((bf16[2,1024,128]{2,1,0:T(8,128)(2,1)}, bf16[2,1024,128]{2,1,0:T(8,128)(2,1)}, u32[]{:S(2)}, u32[]{:S(2)}) %collective-permute-start.15) | collective-permute-done | bytes 524320 | tf_op jit(solution)/shard_map/ppermute | solution.py:564
  260.1 20.8 %tile.7 = (bf16[2,1024,128]{2,1,0:T(8,128)(2,1)}, bf16[2,1024,128]{2,1,0:T(8,128)(2,1)}, bf16[2,1024,128]{2,1,0:T(8,128)(2,1)}, bf16[2,1024,128]{2,1,0:T(8,128)(...) custom-call(s32[1,24]{1,0:T(1,128)} %offsets.7, ...), custom_call_target="tpu_custom_call" | custom-call | flops 10737418240 | bytes 20971520 | tf_op jit(solution)/shard_map/tile/pallas_call | solution.py:315
  281.0 2.1 collective-permute-done.17.refs_4_
  283.1 0.1 collective-permute-done.18.refs_5_
  283.2 147.7 %finish.1 = (f32[2,32,64,128]{3,2,1,0:T(8,128)S(1)}, f32[2,32,64,128]{3,2,1,0:T(8,128)S(1)}, f32[2,32,64,128]{3,2,1,0:T(8,128)S(1)}) custom-call(bf16[512,512]{1,0:T(8,128)(2,1)} %constant.10.inv.table_ref, bf16[4,2,32,256,128]{4,3,2,1,0:T(8,128)(2,1)} %sens.13, f32[2,32,256,128]{3,2,1,0:T(8,128)} %image.13, f32[2,32,64,128]{3,2,1,0:T(8,128)} %auxiliary.1, ...), custom_call_target="tpu_custom_call" | custom-call | tf_op jit(solution)/shard_map/finish/pallas_call | solution.py:539
  430.9 2.8 store.1
  (33 shorter events, 0.1 us)
Async XLA Ops:
  5.7 15.8 %collective-permute-start.2 = (bf16[1,2,32,16,128]{4,3,2,1,0:T(8,128)(2,1)}, bf16[1,2,32,16,128]{4,3,2,1,0:T(8,128)(2,1)}, u32[]{:S(2)}, u32[]{:S(2)}) collective-permute-start(bf16[1,2,32,16,128]{4,3,2,1,0:T(8,128)(2,1)} %get-tuple-element.106), channel_id=1, source_target_pairs={{0,3},{1,4},{2,5},{3,6},{4,7},{5,0},{6,1},{7,2},{8,11},{9,12},{10,... | collective-permute-start | bytes 786440 | tf_op jit(solution)/shard_map/ppermute | solution.py:564
  7.5 14.0 %collective-permute-start.1 = (bf16[1,2,32,16,128]{4,3,2,1,0:T(8,128)(2,1)}, bf16[1,2,32,16,128]{4,3,2,1,0:T(8,128)(2,1)}, u32[]{:S(2)}, u32[]{:S(2)}) collective-permute-start(bf16[1,2,32,16,128]{4,3,2,1,0:T(8,128)(2,1)} %get-tuple-element.105), channel_id=1, source_target_pairs={{0,2},{1,3},{2,4},{3,5},{4,6},{5,7},{6,0},{7,1},{8,10},{9,11},{10,... | collective-permute-start | bytes 786440 | tf_op jit(solution)/shard_map/ppermute | solution.py:564
  8.7 21.9 %collective-permute-start.3 = (bf16[1,2,32,16,128]{4,3,2,1,0:T(8,128)(2,1)}, bf16[1,2,32,16,128]{4,3,2,1,0:T(8,128)(2,1)}, u32[]{:S(2)}, u32[]{:S(2)}) collective-permute-start(bf16[1,2,32,16,128]{4,3,2,1,0:T(8,128)(2,1)} %get-tuple-element.107), channel_id=1, source_target_pairs={{0,4},{1,5},{2,6},{3,7},{4,0},{5,1},{6,2},{7,3},{8,12},{9,13},{10,... | collective-permute-start | bytes 786440 | tf_op jit(solution)/shard_map/ppermute | solution.py:564
  8.9 21.7 %collective-permute-start.5 = (bf16[1,2,32,16,128]{4,3,2,1,0:T(8,128)(2,1)}, bf16[1,2,32,16,128]{4,3,2,1,0:T(8,128)(2,1)}, u32[]{:S(2)}, u32[]{:S(2)}) collective-permute-start(bf16[1,2,32,16,128]{4,3,2,1,0:T(8,128)(2,1)} %get-tuple-element.109), channel_id=1, source_target_pairs={{0,6},{1,7},{2,0},{3,1},{4,2},{5,3},{6,4},{7,5},{8,14},{9,15},{10,... | collective-permute-start | bytes 786440 | tf_op jit(solution)/shard_map/ppermute | solution.py:564
  15.1 17.9 %collective-permute-start = (bf16[1,2,32,16,128]{4,3,2,1,0:T(8,128)(2,1)}, bf16[1,2,32,16,128]{4,3,2,1,0:T(8,128)(2,1)}, u32[]{:S(2)}, u32[]{:S(2)}) collective-permute-start(bf16[1,2,32,16,128]{4,3,2,1,0:T(8,128)(2,1)} %get-tuple-element.104), channel_id=1, source_target_pairs={{0,1},{1,2},{2,3},{3,4},{4,5},{5,6},{6,7},{7,0},{8,9},{9,10},{10,1... | collective-permute-start | bytes 786440 | tf_op jit(solution)/shard_map/ppermute | solution.py:564
  21.5 11.5 %collective-permute-start.4 = (bf16[1,2,32,16,128]{4,3,2,1,0:T(8,128)(2,1)}, bf16[1,2,32,16,128]{4,3,2,1,0:T(8,128)(2,1)}, u32[]{:S(2)}, u32[]{:S(2)}) collective-permute-start(bf16[1,2,32,16,128]{4,3,2,1,0:T(8,128)(2,1)} %get-tuple-element.108), channel_id=1, source_target_pairs={{0,5},{1,6},{2,7},{3,0},{4,1},{5,2},{6,3},{7,4},{8,13},{9,14},{10,... | collective-permute-start | bytes 786440 | tf_op jit(solution)/shard_map/ppermute | solution.py:564
  21.5 13.5 %collective-permute-start.6 = (bf16[1,2,32,16,128]{4,3,2,1,0:T(8,128)(2,1)}, bf16[1,2,32,16,128]{4,3,2,1,0:T(8,128)(2,1)}, u32[]{:S(2)}, u32[]{:S(2)}) collective-permute-start(bf16[1,2,32,16,128]{4,3,2,1,0:T(8,128)(2,1)} %get-tuple-element.110), channel_id=1, source_target_pairs={{0,7},{1,0},{2,1},{3,2},{4,3},{5,4},{6,5},{7,6},{8,15},{9,8},{10,9... | collective-permute-start | bytes 786440 | tf_op jit(solution)/shard_map/ppermute | solution.py:564
  30.6 17.6 %collective-permute-start.7 = (bf16[1,2,32,16,128]{4,3,2,1,0:T(8,128)(2,1)}, bf16[1,2,32,16,128]{4,3,2,1,0:T(8,128)(2,1)}, u32[]{:S(2)}, u32[]{:S(2)}) collective-permute-start(bf16[1,2,32,16,128]{4,3,2,1,0:T(8,128)(2,1)} %get-tuple-element.112), channel_id=1, source_target_pairs={{0,1},{1,2},{2,3},{3,4},{4,5},{5,6},{6,7},{7,0},{8,9},{9,10},{10,1... | collective-permute-start | bytes 786440 | tf_op jit(solution)/shard_map/ppermute | solution.py:564
  30.6 17.6 %collective-permute-start.8 = (bf16[1,2,32,16,128]{4,3,2,1,0:T(8,128)(2,1)}, bf16[1,2,32,16,128]{4,3,2,1,0:T(8,128)(2,1)}, u32[]{:S(2)}, u32[]{:S(2)}) collective-permute-start(bf16[1,2,32,16,128]{4,3,2,1,0:T(8,128)(2,1)} %get-tuple-element.113), channel_id=1, source_target_pairs={{0,2},{1,3},{2,4},{3,5},{4,6},{5,7},{6,0},{7,1},{8,10},{9,11},{10,... | collective-permute-start | bytes 786440 | tf_op jit(solution)/shard_map/ppermute | solution.py:564
  32.9 34.1 %collective-permute-start.9 = (bf16[1,2,32,16,128]{4,3,2,1,0:T(8,128)(2,1)}, bf16[1,2,32,16,128]{4,3,2,1,0:T(8,128)(2,1)}, u32[]{:S(2)}, u32[]{:S(2)}) collective-permute-start(bf16[1,2,32,16,128]{4,3,2,1,0:T(8,128)(2,1)} %get-tuple-element.114), channel_id=1, source_target_pairs={{0,3},{1,4},{2,5},{3,6},{4,7},{5,0},{6,1},{7,2},{8,11},{9,12},{10,... | collective-permute-start | bytes 786440 | tf_op jit(solution)/shard_map/ppermute | solution.py:564
  32.9 47.9 %collective-permute-start.10 = (bf16[1,2,32,16,128]{4,3,2,1,0:T(8,128)(2,1)}, bf16[1,2,32,16,128]{4,3,2,1,0:T(8,128)(2,1)}, u32[]{:S(2)}, u32[]{:S(2)}) collective-permute-start(bf16[1,2,32,16,128]{4,3,2,1,0:T(8,128)(2,1)} %get-tuple-element.115), channel_id=1, source_target_pairs={{0,4},{1,5},{2,6},{3,7},{4,0},{5,1},{6,2},{7,3},{8,12},{9,13},{10,... | collective-permute-start | bytes 786440 | tf_op jit(solution)/shard_map/ppermute | solution.py:564
  35.0 46.2 %collective-permute-start.11 = (bf16[1,2,32,16,128]{4,3,2,1,0:T(8,128)(2,1)}, bf16[1,2,32,16,128]{4,3,2,1,0:T(8,128)(2,1)}, u32[]{:S(2)}, u32[]{:S(2)}) collective-permute-start(bf16[1,2,32,16,128]{4,3,2,1,0:T(8,128)(2,1)} %get-tuple-element.116), channel_id=1, source_target_pairs={{0,5},{1,6},{2,7},{3,0},{4,1},{5,2},{6,3},{7,4},{8,13},{9,14},{10,... | collective-permute-start | bytes 786440 | tf_op jit(solution)/shard_map/ppermute | solution.py:564
  48.1 46.6 %collective-permute-start.21 = (bf16[1,2,32,32,128]{4,3,2,1,0:T(8,128)(2,1)}, bf16[1,2,32,32,128]{4,3,2,1,0:T(8,128)(2,1)}, u32[]{:S(2)}, u32[]{:S(2)}) collective-permute-start(bf16[1,2,32,32,128]{4,3,2,1,0:T(8,128)(2,1)} %get-tuple-element.132), channel_id=1, source_target_pairs={{0,1},{1,2},{2,3},{3,4},{4,5},{5,6},{6,7},{7,0},{8,9},{9,10},{10,1... | collective-permute-start | bytes 1572872 | tf_op jit(solution)/shard_map/ppermute | solution.py:564
  48.2 47.2 %collective-permute-start.22 = (bf16[1,2,32,32,128]{4,3,2,1,0:T(8,128)(2,1)}, bf16[1,2,32,32,128]{4,3,2,1,0:T(8,128)(2,1)}, u32[]{:S(2)}, u32[]{:S(2)}) collective-permute-start(bf16[1,2,32,32,128]{4,3,2,1,0:T(8,128)(2,1)} %get-tuple-element.133), channel_id=1, source_target_pairs={{0,2},{1,3},{2,4},{3,5},{4,6},{5,7},{6,0},{7,1},{8,10},{9,11},{10,... | collective-permute-start | bytes 1572872 | tf_op jit(solution)/shard_map/ppermute | solution.py:564
  67.1 28.3 %collective-permute-start.23 = (bf16[1,2,32,32,128]{4,3,2,1,0:T(8,128)(2,1)}, bf16[1,2,32,32,128]{4,3,2,1,0:T(8,128)(2,1)}, u32[]{:S(2)}, u32[]{:S(2)}) collective-permute-start(bf16[1,2,32,32,128]{4,3,2,1,0:T(8,128)(2,1)} %get-tuple-element.134), channel_id=1, source_target_pairs={{0,3},{1,4},{2,5},{3,6},{4,7},{5,0},{6,1},{7,2},{8,11},{9,12},{10,... | collective-permute-start | bytes 1572872 | tf_op jit(solution)/shard_map/ppermute | solution.py:564
  80.9 10.6 %collective-permute-start.12 = (bf16[1,2,32,16,128]{4,3,2,1,0:T(8,128)(2,1)}, bf16[1,2,32,16,128]{4,3,2,1,0:T(8,128)(2,1)}, u32[]{:S(2)}, u32[]{:S(2)}) collective-permute-start(bf16[1,2,32,16,128]{4,3,2,1,0:T(8,128)(2,1)} %get-tuple-element.117), channel_id=1, source_target_pairs={{0,6},{1,7},{2,0},{3,1},{4,2},{5,3},{6,4},{7,5},{8,14},{9,15},{10,... | collective-permute-start | bytes 786440 | tf_op jit(solution)/shard_map/ppermute | solution.py:564
  81.2 10.4 %collective-permute-start.13 = (bf16[1,2,32,16,128]{4,3,2,1,0:T(8,128)(2,1)}, bf16[1,2,32,16,128]{4,3,2,1,0:T(8,128)(2,1)}, u32[]{:S(2)}, u32[]{:S(2)}) collective-permute-start(bf16[1,2,32,16,128]{4,3,2,1,0:T(8,128)(2,1)} %get-tuple-element.118), channel_id=1, source_target_pairs={{0,7},{1,0},{2,1},{3,2},{4,3},{5,4},{6,5},{7,6},{8,15},{9,8},{10,9... | collective-permute-start | bytes 786440 | tf_op jit(solution)/shard_map/ppermute | solution.py:564
  91.5 25.0 %collective-permute-start.24 = (bf16[1,2,32,32,128]{4,3,2,1,0:T(8,128)(2,1)}, bf16[1,2,32,32,128]{4,3,2,1,0:T(8,128)(2,1)}, u32[]{:S(2)}, u32[]{:S(2)}) collective-permute-start(bf16[1,2,32,32,128]{4,3,2,1,0:T(8,128)(2,1)} %get-tuple-element.135), channel_id=1, source_target_pairs={{0,4},{1,5},{2,6},{3,7},{4,0},{5,1},{6,2},{7,3},{8,12},{9,13},{10,... | collective-permute-start | bytes 1572872 | tf_op jit(solution)/shard_map/ppermute | solution.py:564
  91.5 36.8 %collective-permute-start.25 = (bf16[1,2,32,32,128]{4,3,2,1,0:T(8,128)(2,1)}, bf16[1,2,32,32,128]{4,3,2,1,0:T(8,128)(2,1)}, u32[]{:S(2)}, u32[]{:S(2)}) collective-permute-start(bf16[1,2,32,32,128]{4,3,2,1,0:T(8,128)(2,1)} %get-tuple-element.136), channel_id=1, source_target_pairs={{0,5},{1,6},{2,7},{3,0},{4,1},{5,2},{6,3},{7,4},{8,13},{9,14},{10,... | collective-permute-start | bytes 1572872 | tf_op jit(solution)/shard_map/ppermute | solution.py:564
  94.7 35.3 %collective-permute-start.26 = (bf16[1,2,32,32,128]{4,3,2,1,0:T(8,128)(2,1)}, bf16[1,2,32,32,128]{4,3,2,1,0:T(8,128)(2,1)}, u32[]{:S(2)}, u32[]{:S(2)}) collective-permute-start(bf16[1,2,32,32,128]{4,3,2,1,0:T(8,128)(2,1)} %get-tuple-element.137), channel_id=1, source_target_pairs={{0,6},{1,7},{2,0},{3,1},{4,2},{5,3},{6,4},{7,5},{8,14},{9,15},{10,... | collective-permute-start | bytes 1572872 | tf_op jit(solution)/shard_map/ppermute | solution.py:564
  95.4 36.1 %collective-permute-start.27 = (bf16[1,2,32,32,128]{4,3,2,1,0:T(8,128)(2,1)}, bf16[1,2,32,32,128]{4,3,2,1,0:T(8,128)(2,1)}, u32[]{:S(2)}, u32[]{:S(2)}) collective-permute-start(bf16[1,2,32,32,128]{4,3,2,1,0:T(8,128)(2,1)} %get-tuple-element.138), channel_id=1, source_target_pairs={{0,7},{1,0},{2,1},{3,2},{4,3},{5,4},{6,5},{7,6},{8,15},{9,8},{10,9... | collective-permute-start | bytes 1572872 | tf_op jit(solution)/shard_map/ppermute | solution.py:564
  95.4 39.2 %collective-permute-start.28 = (bf16[1,2,32,32,128]{4,3,2,1,0:T(8,128)(2,1)}, bf16[1,2,32,32,128]{4,3,2,1,0:T(8,128)(2,1)}, u32[]{:S(2)}, u32[]{:S(2)}) collective-permute-start(bf16[1,2,32,32,128]{4,3,2,1,0:T(8,128)(2,1)} %get-tuple-element.152), channel_id=1, source_target_pairs={{0,1},{1,2},{2,3},{3,4},{4,5},{5,6},{6,7},{7,0},{8,9},{9,10},{10,1... | collective-permute-start | bytes 1572872 | tf_op jit(solution)/shard_map/ppermute | solution.py:564
  116.4 42.7 %collective-permute-start.29 = (bf16[1,2,32,32,128]{4,3,2,1,0:T(8,128)(2,1)}, bf16[1,2,32,32,128]{4,3,2,1,0:T(8,128)(2,1)}, u32[]{:S(2)}, u32[]{:S(2)}) collective-permute-start(bf16[1,2,32,32,128]{4,3,2,1,0:T(8,128)(2,1)} %get-tuple-element.153), channel_id=1, source_target_pairs={{0,2},{1,3},{2,4},{3,5},{4,6},{5,7},{6,0},{7,1},{8,10},{9,11},{10,... | collective-permute-start | bytes 1572872 | tf_op jit(solution)/shard_map/ppermute | solution.py:564
  128.3 30.9 %collective-permute-start.30 = (bf16[1,2,32,32,128]{4,3,2,1,0:T(8,128)(2,1)}, bf16[1,2,32,32,128]{4,3,2,1,0:T(8,128)(2,1)}, u32[]{:S(2)}, u32[]{:S(2)}) collective-permute-start(bf16[1,2,32,32,128]{4,3,2,1,0:T(8,128)(2,1)} %get-tuple-element.154), channel_id=1, source_target_pairs={{0,3},{1,4},{2,5},{3,6},{4,7},{5,0},{6,1},{7,2},{8,11},{9,12},{10,... | collective-permute-start | bytes 1572872 | tf_op jit(solution)/shard_map/ppermute | solution.py:564
  130.0 44.4 %collective-permute-start.31 = (bf16[1,2,32,32,128]{4,3,2,1,0:T(8,128)(2,1)}, bf16[1,2,32,32,128]{4,3,2,1,0:T(8,128)(2,1)}, u32[]{:S(2)}, u32[]{:S(2)}) collective-permute-start(bf16[1,2,32,32,128]{4,3,2,1,0:T(8,128)(2,1)} %get-tuple-element.155), channel_id=1, source_target_pairs={{0,4},{1,5},{2,6},{3,7},{4,0},{5,1},{6,2},{7,3},{8,12},{9,13},{10,... | collective-permute-start | bytes 1572872 | tf_op jit(solution)/shard_map/ppermute | solution.py:564
  131.5 49.2 %collective-permute-start.32 = (bf16[1,2,32,32,128]{4,3,2,1,0:T(8,128)(2,1)}, bf16[1,2,32,32,128]{4,3,2,1,0:T(8,128)(2,1)}, u32[]{:S(2)}, u32[]{:S(2)}) collective-permute-start(bf16[1,2,32,32,128]{4,3,2,1,0:T(8,128)(2,1)} %get-tuple-element.156), channel_id=1, source_target_pairs={{0,5},{1,6},{2,7},{3,0},{4,1},{5,2},{6,3},{7,4},{8,13},{9,14},{10,... | collective-permute-start | bytes 1572872 | tf_op jit(solution)/shard_map/ppermute | solution.py:564
  134.6 46.1 %collective-permute-start.33 = (bf16[1,2,32,32,128]{4,3,2,1,0:T(8,128)(2,1)}, bf16[1,2,32,32,128]{4,3,2,1,0:T(8,128)(2,1)}, u32[]{:S(2)}, u32[]{:S(2)}) collective-permute-start(bf16[1,2,32,32,128]{4,3,2,1,0:T(8,128)(2,1)} %get-tuple-element.157), channel_id=1, source_target_pairs={{0,6},{1,7},{2,0},{3,1},{4,2},{5,3},{6,4},{7,5},{8,14},{9,15},{10,... | collective-permute-start | bytes 1572872 | tf_op jit(solution)/shard_map/ppermute | solution.py:564
  159.1 44.6 %collective-permute-start.34 = (bf16[1,2,32,32,128]{4,3,2,1,0:T(8,128)(2,1)}, bf16[1,2,32,32,128]{4,3,2,1,0:T(8,128)(2,1)}, u32[]{:S(2)}, u32[]{:S(2)}) collective-permute-start(bf16[1,2,32,32,128]{4,3,2,1,0:T(8,128)(2,1)} %get-tuple-element.158), channel_id=1, source_target_pairs={{0,7},{1,0},{2,1},{3,2},{4,3},{5,4},{6,5},{7,6},{8,15},{9,8},{10,9... | collective-permute-start | bytes 1572872 | tf_op jit(solution)/shard_map/ppermute | solution.py:564
  159.2 47.5 %collective-permute-start.35 = (bf16[1,2,32,32,128]{4,3,2,1,0:T(8,128)(2,1)}, bf16[1,2,32,32,128]{4,3,2,1,0:T(8,128)(2,1)}, u32[]{:S(2)}, u32[]{:S(2)}) collective-permute-start(bf16[1,2,32,32,128]{4,3,2,1,0:T(8,128)(2,1)} %get-tuple-element.169), channel_id=1, source_target_pairs={{0,1},{1,2},{2,3},{3,4},{4,5},{5,6},{6,7},{7,0},{8,9},{9,10},{10,1... | collective-permute-start | bytes 1572872 | tf_op jit(solution)/shard_map/ppermute | solution.py:564
  174.4 40.1 %collective-permute-start.36 = (bf16[1,2,32,32,128]{4,3,2,1,0:T(8,128)(2,1)}, bf16[1,2,32,32,128]{4,3,2,1,0:T(8,128)(2,1)}, u32[]{:S(2)}, u32[]{:S(2)}) collective-permute-start(bf16[1,2,32,32,128]{4,3,2,1,0:T(8,128)(2,1)} %get-tuple-element.170), channel_id=1, source_target_pairs={{0,2},{1,3},{2,4},{3,5},{4,6},{5,7},{6,0},{7,1},{8,10},{9,11},{10,... | collective-permute-start | bytes 1572872 | tf_op jit(solution)/shard_map/ppermute | solution.py:564
  180.7 33.8 %collective-permute-start.37 = (bf16[1,2,32,32,128]{4,3,2,1,0:T(8,128)(2,1)}, bf16[1,2,32,32,128]{4,3,2,1,0:T(8,128)(2,1)}, u32[]{:S(2)}, u32[]{:S(2)}) collective-permute-start(bf16[1,2,32,32,128]{4,3,2,1,0:T(8,128)(2,1)} %get-tuple-element.171), channel_id=1, source_target_pairs={{0,3},{1,4},{2,5},{3,6},{4,7},{5,0},{6,1},{7,2},{8,11},{9,12},{10,... | collective-permute-start | bytes 1572872 | tf_op jit(solution)/shard_map/ppermute | solution.py:564
  180.7 35.6 %collective-permute-start.38 = (bf16[1,2,32,32,128]{4,3,2,1,0:T(8,128)(2,1)}, bf16[1,2,32,32,128]{4,3,2,1,0:T(8,128)(2,1)}, u32[]{:S(2)}, u32[]{:S(2)}) collective-permute-start(bf16[1,2,32,32,128]{4,3,2,1,0:T(8,128)(2,1)} %get-tuple-element.172), channel_id=1, source_target_pairs={{0,4},{1,5},{2,6},{3,7},{4,0},{5,1},{6,2},{7,3},{8,12},{9,13},{10,... | collective-permute-start | bytes 1572872 | tf_op jit(solution)/shard_map/ppermute | solution.py:564
  203.8 33.2 %collective-permute-start.39 = (bf16[1,2,32,32,128]{4,3,2,1,0:T(8,128)(2,1)}, bf16[1,2,32,32,128]{4,3,2,1,0:T(8,128)(2,1)}, u32[]{:S(2)}, u32[]{:S(2)}) collective-permute-start(bf16[1,2,32,32,128]{4,3,2,1,0:T(8,128)(2,1)} %get-tuple-element.173), channel_id=1, source_target_pairs={{0,5},{1,6},{2,7},{3,0},{4,1},{5,2},{6,3},{7,4},{8,13},{9,14},{10,... | collective-permute-start | bytes 1572872 | tf_op jit(solution)/shard_map/ppermute | solution.py:564
  206.7 39.2 %collective-permute-start.40 = (bf16[1,2,32,32,128]{4,3,2,1,0:T(8,128)(2,1)}, bf16[1,2,32,32,128]{4,3,2,1,0:T(8,128)(2,1)}, u32[]{:S(2)}, u32[]{:S(2)}) collective-permute-start(bf16[1,2,32,32,128]{4,3,2,1,0:T(8,128)(2,1)} %get-tuple-element.174), channel_id=1, source_target_pairs={{0,6},{1,7},{2,0},{3,1},{4,2},{5,3},{6,4},{7,5},{8,14},{9,15},{10,... | collective-permute-start | bytes 1572872 | tf_op jit(solution)/shard_map/ppermute | solution.py:564
  214.5 31.4 %collective-permute-start.41 = (bf16[1,2,32,32,128]{4,3,2,1,0:T(8,128)(2,1)}, bf16[1,2,32,32,128]{4,3,2,1,0:T(8,128)(2,1)}, u32[]{:S(2)}, u32[]{:S(2)}) collective-permute-start(bf16[1,2,32,32,128]{4,3,2,1,0:T(8,128)(2,1)} %get-tuple-element.175), channel_id=1, source_target_pairs={{0,7},{1,0},{2,1},{3,2},{4,3},{5,4},{6,5},{7,6},{8,15},{9,8},{10,9... | collective-permute-start | bytes 1572872 | tf_op jit(solution)/shard_map/ppermute | solution.py:564
  214.5 31.4 %collective-permute-start.14 = (bf16[2,1024,128]{2,1,0:T(8,128)(2,1)}, bf16[2,1024,128]{2,1,0:T(8,128)(2,1)}, u32[]{:S(2)}, u32[]{:S(2)}) collective-permute-start(bf16[2,1024,128]{2,1,0:T(8,128)(2,1)} %get-tuple-element.121), channel_id=1, source_target_pairs={{0,1},{1,2},{2,3},{3,4},{4,5},{5,6},{6,7},{7,0},{8,9},{9,10},{10,1... | collective-permute-start | bytes 1572872 | tf_op jit(solution)/shard_map/ppermute | solution.py:564
  216.3 43.9 %collective-permute-start.15 = (bf16[2,1024,128]{2,1,0:T(8,128)(2,1)}, bf16[2,1024,128]{2,1,0:T(8,128)(2,1)}, u32[]{:S(2)}, u32[]{:S(2)}) collective-permute-start(bf16[2,1024,128]{2,1,0:T(8,128)(2,1)} %get-tuple-element.122), channel_id=1, source_target_pairs={{0,2},{1,3},{2,4},{3,5},{4,6},{5,7},{6,0},{7,1},{8,10},{9,11},{10,... | collective-permute-start | bytes 1572872 | tf_op jit(solution)/shard_map/ppermute | solution.py:564
  237.0 44.0 %collective-permute-start.16 = (bf16[2,1024,128]{2,1,0:T(8,128)(2,1)}, bf16[2,1024,128]{2,1,0:T(8,128)(2,1)}, u32[]{:S(2)}, u32[]{:S(2)}) collective-permute-start(bf16[2,1024,128]{2,1,0:T(8,128)(2,1)} %get-tuple-element.123), channel_id=1, source_target_pairs={{0,3},{1,4},{2,5},{3,6},{4,7},{5,0},{6,1},{7,2},{8,11},{9,12},{10,... | collective-permute-start | bytes 1572872 | tf_op jit(solution)/shard_map/ppermute | solution.py:564
  245.9 37.2 %collective-permute-start.17 = (bf16[2,1024,128]{2,1,0:T(8,128)(2,1)}, bf16[2,1024,128]{2,1,0:T(8,128)(2,1)}, u32[]{:S(2)}, u32[]{:S(2)}) collective-permute-start(bf16[2,1024,128]{2,1,0:T(8,128)(2,1)} %get-tuple-element.124), channel_id=1, source_target_pairs={{0,4},{1,5},{2,6},{3,7},{4,0},{5,1},{6,2},{7,3},{8,12},{9,13},{10,... | collective-permute-start | bytes 1572872 | tf_op jit(solution)/shard_map/ppermute | solution.py:564
  245.9 37.3 %collective-permute-start.18 = (bf16[2,1024,128]{2,1,0:T(8,128)(2,1)}, bf16[2,1024,128]{2,1,0:T(8,128)(2,1)}, u32[]{:S(2)}, u32[]{:S(2)}) collective-permute-start(bf16[2,1024,128]{2,1,0:T(8,128)(2,1)} %get-tuple-element.125), channel_id=1, source_target_pairs={{0,5},{1,6},{2,7},{3,0},{4,1},{5,2},{6,3},{7,4},{8,13},{9,14},{10,... | collective-permute-start | bytes 1572872 | tf_op jit(solution)/shard_map/ppermute | solution.py:564
  246.0 37.2 %collective-permute-start.19 = (bf16[2,1024,128]{2,1,0:T(8,128)(2,1)}, bf16[2,1024,128]{2,1,0:T(8,128)(2,1)}, u32[]{:S(2)}, u32[]{:S(2)}) collective-permute-start(bf16[2,1024,128]{2,1,0:T(8,128)(2,1)} %get-tuple-element.126), channel_id=1, source_target_pairs={{0,6},{1,7},{2,0},{3,1},{4,2},{5,3},{6,4},{7,5},{8,14},{9,15},{10,... | collective-permute-start | bytes 1572872 | tf_op jit(solution)/shard_map/ppermute | solution.py:564
  260.1 23.0 %collective-permute-start.20 = (bf16[2,1024,128]{2,1,0:T(8,128)(2,1)}, bf16[2,1024,128]{2,1,0:T(8,128)(2,1)}, u32[]{:S(2)}, u32[]{:S(2)}) collective-permute-start(bf16[2,1024,128]{2,1,0:T(8,128)(2,1)} %get-tuple-element.127), channel_id=1, source_target_pairs={{0,7},{1,0},{2,1},{3,2},{4,3},{5,4},{6,5},{7,6},{8,15},{9,8},{10,9... | collective-permute-start | bytes 1572872 | tf_op jit(solution)/shard_map/ppermute | solution.py:564

commit v10 on v8

--- a/solution.py
+++ b/solution.py
@@ -13,7 +13,7 @@
 penalty = 1.0
 threshold = 0.3
 VMEM_LIMIT = 67000000
-SPLIT = 4
+SPLIT = 1
 F32 = jnp.float32
 BF16 = jnp.bfloat16
 
@@ -109,7 +109,7 @@
             flat[where, :] = half[:, h * depth : (h + 1) * depth]
         return carry
 
-    lax.fori_loop(0, rows // 2, pair, 0, unroll=2)
+    lax.fori_loop(0, rows // 2, pair, 0, unroll=4)
 
     @pl.when(step == pl.num_programs(1) - 1)
     def last():
@@ -154,7 +154,7 @@
     psize = out.shape[2]
     depth = samples.shape[2]
     for g in range(samples.shape[0]):
-        flat[...] = samples[g].astype(F32)
+        flat[0 : samples.shape[1], :] = samples[g].astype(F32)
         for c in range(parts):
             for p in range(2):
                 rows = flat[pl.ds(2 * c + p, psize, stride=2 * parts), :]
@@ -171,7 +171,7 @@
         in_specs=[pl.BlockSpec((group, lines, depth), lambda i: (i, 0, 0))],
         out_specs=pl.BlockSpec((coils, group, psize, parts * depth), lambda i: (0, i, 0, 0)),
         out_shape=jax.ShapeDtypeStruct((coils, slots, psize, parts * depth), BF16),
-        scratch_shapes=[pltpu.VMEM((lines, depth), F32)],
+        scratch_shapes=[pltpu.VMEM((lines + 2 * coils * parts, depth), F32)],
         compiler_params=params(),
         cost_estimate=cost(samples.size, 4 * samples.size),
         name="sort",

time: 438 us -> 436 us (level)
  transfers between devices with their start and end apart: 42 -> 42, of which waited for: 9 -> 9; matrix products, arithmetic and copies ran while one was open for 0% -> 0% of each run, Pallas kernels for 31% -> 30%
where the time goes in v10:
time: 436 us; the launch traced here: 433 us
  Pallas kernels  287 us (66%)
  starting transfers between devices  78.1 us (18%)
  waiting for transfers between devices  66.5 us (15%)
    pallas_call x1, Pallas kernels, finish_call(): pl.pallas_call(functools.partial(finish_kernel, n, shares, kl, xl, chunks...  148 us
    pallas_call x4, Pallas kernels, tile_call(): pl.pallas_call(functools.partial(tile_kernel, n, kl, xl, cells // kl, par...  83.2 us
    ppermute x42, starting transfers between devices, swap(): lax.ppermute(parts[turn], 'slab', [(i, ahead(i, off, n)) for i in range(n)])  78.1 us
    ppermute x42, waiting for transfers between devices, swap(): lax.ppermute(parts[turn], 'slab', [(i, ahead(i, off, n)) for i in range(n)])  66.5 us
    pallas_call x6, Pallas kernels, forward_call(): pl.pallas_call(functools.partial(forward_kernel, n, kl, xp, offs), grid=(...  44.1 us
  transfers between devices with their start and end apart: 42, of which 9 were waited for; matrix products, arithmetic and copies ran while one was open for 0% of the time, Pallas kernels for 30%

profile of v10, /device:TPU:9, one launch (start us, length us, event | category | flops | bytes accessed | tf_op | source)
XLA Modules:
  0.0 432.8 jit_solution(17812980721076904403)
XLA Ops:
  0.6 4.8 %forward.6 = (bf16[1,2,32,16,128]{4,3,2,1,0:T(8,128)(2,1)}, bf16[1,2,32,16,128]{4,3,2,1,0:T(8,128)(2,1)}, bf16[1,2,32,16,128]{4,3,2,1,0:T(8,128)(2,1)}, bf16[1,2,32,16,128]{4,3,2,1,0:T(8,128)(2,1)}) custom-call(bf16[512,512]{1,0:T(8,128)(2,1)} %constant.11.table.fwd, f32[2,32,256,128]{3,2,1,0:T(8,128)} %image.13, bf16[4,2,32,256,128]{4,3,2,1,0:T(8,128)(2,1)} %sens.13), custom_call_target="tpu_custom_call" | custom-call | flops 1073741824 | bytes 6291456 | tf_op jit(solution)/shard_map/forward/pallas_call | solution.py:134
  5.4 1.8 collective-permute-start.2
  7.2 1.2 collective-permute-start.1
  8.4 0.2 collective-permute-start.3
  8.6 1.2 collective-permute-start.5
  9.8 4.7 %forward.7 = (bf16[1,2,32,16,128]{4,3,2,1,0:T(8,128)(2,1)}, bf16[1,2,32,16,128]{4,3,2,1,0:T(8,128)(2,1)}, bf16[1,2,32,16,128]{4,3,2,1,0:T(8,128)(2,1)}, bf16[1,2,32,16,128]{4,3,2,1,0:T(8,128)(2,1)}) custom-call(bf16[512,512]{1,0:T(8,128)(2,1)} %constant.11.table.fwd, f32[2,32,256,128]{3,2,1,0:T(8,128)} %image.13, bf16[4,2,32,256,128]{4,3,2,1,0:T(8,128)(2,1)} %sens.13), custom_call_target="tpu_custom_call" | custom-call | flops 1073741824 | bytes 6291456 | tf_op jit(solution)/shard_map/forward/pallas_call | solution.py:134
  14.5 0.9 collective-permute-start
  15.5 5.7 %collective-permute-done.2.refs_3_ = bf16[1,2,32,16,128]{4,3,2,1,0:T(8,128)(2,1)} collective-permute-done((bf16[1,2,32,16,128]{4,3,2,1,0:T(8,128)(2,1)}, bf16[1,2,32,16,128]{4,3,2,1,0:T(8,128)(2,1)}, u32[]{:S(2)}, u32[]{:S(2)}) %collective-permute-start.2) | collective-permute-done | bytes 262176 | tf_op jit(solution)/shard_map/ppermute | solution.py:586
  21.2 0.0 collective-permute-start.4
  21.2 0.0 collective-permute-done.1.refs_2_
  21.2 1.1 collective-permute-start.6
  22.3 5.7 %forward.8 = (bf16[1,2,32,16,128]{4,3,2,1,0:T(8,128)(2,1)}, bf16[1,2,32,16,128]{4,3,2,1,0:T(8,128)(2,1)}, bf16[1,2,32,16,128]{4,3,2,1,0:T(8,128)(2,1)}, bf16[1,2...) custom-call(bf16[512,512]{1,0:T(8,128)(2,1)} %constant.11.table.fwd,, ...), custom_call_target="tpu_custom_call" | custom-call | flops 1073741824 | bytes 6291456 | tf_op jit(solution)/shard_map/forward/pallas_call | solution.py:134
  28.1 2.2 collective-permute-done.3.refs_4_
  30.3 0.0 collective-permute-start.7
  30.3 0.0 collective-permute-done.5.refs_6_
  30.3 1.8 collective-permute-start.8
  32.1 0.0 collective-permute-done.refs_1_
  32.1 0.0 collective-permute-start.9
  32.2 0.0 collective-permute-done.4.refs_5_
  32.2 2.0 collective-permute-start.10
  34.2 0.0 collective-permute-done.6.refs_7_
  34.2 2.9 collective-permute-start.11
  37.0 9.6 %forward.9 = (bf16[1,2,32,32,128]{4,3,2,1,0:T(8,128)(2,1)}, bf16[1,2,32,32,128]{4,3,2,1,0:T(8,128)(2,1)}, bf16[1,2,32,32,128]{4,3,2,1,0:T(8,128)(2,1)}, bf16[1,2...) custom-call(bf16[512,512]{1,0:T(8,128)(2,1)} %constant.11.table.fwd,, ...), custom_call_target="tpu_custom_call" | custom-call | flops 2147483648 | bytes 12582912 | tf_op jit(solution)/shard_map/forward/pallas_call | solution.py:134
  46.6 0.0 collective-permute-done.7.refs_9_
  46.6 0.1 collective-permute-start.21
  46.7 0.0 collective-permute-done.8.refs_10_
  46.7 0.1 collective-permute-start.22
  46.8 19.5 %collective-permute-done.9.refs_11_ = bf16[1,2,32,16,128]{4,3,2,1,0:T(8,128)(2,1)} collective-permute-done((bf16[1,2,32,16,128]{4,3,2,1,0:T(8,128)(2,1)}, bf16[1,2,32,16,128]{4,3,2,1,0:T(8,128)(2,1)}, u32[]{:S(2)}, u32[]{:S(2)}) %collective-permute-start.9) | collective-permute-done | bytes 262176 | tf_op jit(solution)/shard_map/ppermute | solution.py:586
  66.3 2.5 collective-permute-start.23
  68.8 11.3 %collective-permute-done.10.refs_12_ = bf16[1,2,32,16,128]{4,3,2,1,0:T(8,128)(2,1)} collective-permute-done((bf16[1,2,32,16,128]{4,3,2,1,0:T(8,128)(2,1)}, bf16[1,2,32,16,128]{4,3,2,1,0:T(8,128)(2,1)}, u32[]{:S(2)}, u32[]{:S(2)}) %collective-permute-start.10) | collective-permute-done | bytes 262176 | tf_op jit(solution)/shard_map/ppermute | solution.py:586
  80.0 0.4 collective-permute-done.11.refs_13_
  80.4 9.6 %forward.10 = (bf16[1,2,32,32,128]{4,3,2,1,0:T(8,128)(2,1)}, bf16[1,2,32,32,128]{4,3,2,1,0:T(8,128)(2,1)}, bf16[1,2,32,32,128]{4,3,2,1,0:T(8,128)(2,1)}, bf16[1,...) custom-call(bf16[512,512]{1,0:T(8,128)(2,1)} %constant.11.table.fwd,, ...), custom_call_target="tpu_custom_call" | custom-call | flops 2147483648 | bytes 12582912 | tf_op jit(solution)/shard_map/forward/pallas_call | solution.py:134
  90.0 0.1 collective-permute-start.24
  90.1 3.2 collective-permute-start.25
  93.2 0.6 collective-permute-start.26
  93.8 1.7 collective-permute-start.28
  96.2 9.6 %forward.11 = (bf16[1,2,32,32,128]{4,3,2,1,0:T(8,128)(2,1)}, bf16[1,2,32,32,128]{4,3,2,1,0:T(8,128)(2,1)}, bf16[1,2,32,32,128]{4,3,2,1,0:T(8,128)(2,1)}, bf16[1,...) custom-call(bf16[512,512]{1,0:T(8,128)(2,1)} %constant.11.table.fwd,, ...), custom_call_target="tpu_custom_call" | custom-call | flops 2147483648 | bytes 12582912 | tf_op jit(solution)/shard_map/forward/pallas_call | solution.py:134
  105.9 8.3 %sort.1.sorted_samples = bf16[4,24,128,256]{3,2,1,0:T(8,128)(2,1)} custom-call(bf16[24,1024,128]{2,1,0:T(8,128)(2,1)} %bitcast.1), custom_call_target="tpu_custom_call" | custom-call | flops 3145728 | bytes 12582912 | tf_op jit(solution)/shard_map/sort/pallas_call | solution.py:168
  114.2 12.5 %collective-permute-start.29 = (bf16[1,2,32,32,128]{4,3,2,1,0:T(8,128)(2,1)}, bf16[1,2,32,32,128]{4,3,2,1,0:T(8,128)(2,1)}, u32[]{:S(2)}, u32[]{:S(2)}) collective-permute-start(bf16[1,2,32,32,128]{4,3,2,1,0:T(8,128)(2,1)} %get-tuple-element.153), channel_id=1, source_target_pairs={{0,2},{1,3},{2,4},{3,5},{4,6},{5,7},{6,0},{7,1},{8,10},{9,11},{10,... | collective-permute-start | bytes 1572872 | tf_op jit(solution)/shard_map/ppermute | solution.py:586
  126.7 1.8 collective-permute-start.30
  128.4 1.5 collective-permute-start.31
  129.9 3.1 collective-permute-start.32
  133.0 3.7 collective-permute-start.33
  136.7 20.9 %tile.4 = (bf16[2,1024,128]{2,1,0:T(8,128)(2,1)}, bf16[2,1024,128]{2,1,0:T(8,128)(2,1)}, bf16[2,1024,128]{2,1,0:T(8,128)(2,1)}, bf16[2,1024,128]{2,1,0:T(8,128)(...) custom-call(s32[1,24]{1,0:T(1,128)} %offsets.7, ...), custom_call_target="tpu_custom_call" | custom-call | flops 10737418240 | bytes 20971520 | tf_op jit(solution)/shard_map/tile/pallas_call | solution.py:315
  157.6 0.1 collective-permute-start.34
  157.7 1.7 collective-permute-start.35
  159.4 13.4 %collective-permute-done.31.refs_4_ = bf16[1,2,32,32,128]{4,3,2,1,0:T(8,128)(2,1)} collective-permute-done((bf16[1,2,32,32,128]{4,3,2,1,0:T(8,128)(2,1)}, bf16[1,2,32,32,128]{4,3,2,1,0:T(8,128)(2,1)}, u32[]{:S(2)}, u32[]{:S(2)}) %collective-permute-start.31) | collective-permute-done | bytes 524320 | tf_op jit(solution)/shard_map/ppermute | solution.py:586
  172.8 6.3 %collective-permute-start.36 = (bf16[1,2,32,32,128]{4,3,2,1,0:T(8,128)(2,1)}, bf16[1,2,32,32,128]{4,3,2,1,0:T(8,128)(2,1)}, u32[]{:S(2)}, u32[]{:S(2)}) collective-permute-start(bf16[1,2,32,32,128]{4,3,2,1,0:T(8,128)(2,1)} %get-tuple-element.170), channel_id=1, source_target_pairs={{0,2},{1,3},{2,4},{3,5},{4,6},{5,7},{6,0},{7,1},{8,10},{9,11},{10,... | collective-permute-start | bytes 1572872 | tf_op jit(solution)/shard_map/ppermute | solution.py:586
  179.1 0.0 collective-permute-start.37
  179.1 2.3 collective-permute-start.38
  181.4 20.8 %tile.5 = (bf16[2,1024,128]{2,1,0:T(8,128)(2,1)}, bf16[2,1024,128]{2,1,0:T(8,128)(2,1)}, bf16[2,1024,128]{2,1,0:T(8,128)(2,1)}, bf16[2,1024,128]{2,1,0:T(8,128)(...) custom-call(s32[1,24]{1,0:T(1,128)} %offsets.7, ...), custom_call_target="tpu_custom_call" | custom-call | flops 10737418240 | bytes 20971520 | tf_op jit(solution)/shard_map/tile/pallas_call | solution.py:315
  202.2 2.9 collective-permute-start.39
  205.1 7.8 %collective-permute-start.40 = (bf16[1,2,32,32,128]{4,3,2,1,0:T(8,128)(2,1)}, bf16[1,2,32,32,128]{4,3,2,1,0:T(8,128)(2,1)}, u32[]{:S(2)}, u32[]{:S(2)}) collective-permute-start(bf16[1,2,32,32,128]{4,3,2,1,0:T(8,128)(2,1)} %get-tuple-element.174), channel_id=1, source_target_pairs={{0,6},{1,7},{2,0},{3,1},{4,2},{5,3},{6,4},{7,5},{8,14},{9,15},{10,... | collective-permute-start | bytes 1572872 | tf_op jit(solution)/shard_map/ppermute | solution.py:586
  213.0 1.7 collective-permute-start.14
  214.7 20.7 %tile.6 = (bf16[2,1024,128]{2,1,0:T(8,128)(2,1)}, bf16[2,1024,128]{2,1,0:T(8,128)(2,1)}, bf16[2,1024,128]{2,1,0:T(8,128)(2,1)}, bf16[2,1024,128]{2,1,0:T(8,128)(...) custom-call(s32[1,24]{1,0:T(1,128)} %offsets.7, ...), custom_call_target="tpu_custom_call" | custom-call | flops 10737418240 | bytes 20971520 | tf_op jit(solution)/shard_map/tile/pallas_call | solution.py:315
  235.4 8.9 %collective-permute-start.16 = (bf16[2,1024,128]{2,1,0:T(8,128)(2,1)}, bf16[2,1024,128]{2,1,0:T(8,128)(2,1)}, u32[]{:S(2)}, u32[]{:S(2)}) collective-permute-start(bf16[2,1024,128]{2,1,0:T(8,128)(2,1)} %get-tuple-element.123), channel_id=1, source_target_pairs={{0,3},{1,4},{2,5},{3,6},{4,7},{5,0},{6,1},{7,2},{8,11},{9,12},{10,... | collective-permute-start | bytes 1572872 | tf_op jit(solution)/shard_map/ppermute | solution.py:586
  244.3 0.1 collective-permute-start.18
  244.4 2.5 collective-permute-start.19
  246.9 11.7 %collective-permute-done.15.refs_2_ = bf16[2,1024,128]{2,1,0:T(8,128)(2,1)} collective-permute-done((bf16[2,1024,128]{2,1,0:T(8,128)(2,1)}, bf16[2,1024,128]{2,1,0:T(8,128)(2,1)}, u32[]{:S(2)}, u32[]{:S(2)}) %collective-permute-start.15) | collective-permute-done | bytes 524320 | tf_op jit(solution)/shard_map/ppermute | solution.py:586
  258.6 20.8 %tile.7 = (bf16[2,1024,128]{2,1,0:T(8,128)(2,1)}, bf16[2,1024,128]{2,1,0:T(8,128)(2,1)}, bf16[2,1024,128]{2,1,0:T(8,128)(2,1)}, bf16[2,1024,128]{2,1,0:T(8,128)(...) custom-call(s32[1,24]{1,0:T(1,128)} %offsets.7, ...), custom_call_target="tpu_custom_call" | custom-call | flops 10737418240 | bytes 20971520 | tf_op jit(solution)/shard_map/tile/pallas_call | solution.py:315
  279.4 2.1 collective-permute-done.17.refs_4_
  281.5 0.1 collective-permute-done.18.refs_5_
  281.6 148.3 %finish.1 = (f32[2,32,64,128]{3,2,1,0:T(8,128)S(1)}, f32[2,32,64,128]{3,2,1,0:T(8,128)S(1)}, f32[2,32,64,128]{3,2,1,0:T(8,128)S(1)}) custom-call(bf16[512,512]{1,0:T(8,128)(2,1)} %constant.10.inv.table_ref, bf16[4,2,32,256,128]{4,3,2,1,0:T(8,128)(2,1)} %sens.13, f32[2,32,256,128]{3,2,1,0:T(8,128)} %image.13, f32[2,32,64,128]{3,2,1,0:T(8,128)} %auxiliary.1, ...), custom_call_target="tpu_custom_call" | custom-call | tf_op jit(solution)/shard_map/finish/pallas_call | solution.py:561
  429.9 2.7 store.1
  (33 shorter events, 0.1 us)
Async XLA Ops:
  5.4 15.8 %collective-permute-start.2 = (bf16[1,2,32,16,128]{4,3,2,1,0:T(8,128)(2,1)}, bf16[1,2,32,16,128]{4,3,2,1,0:T(8,128)(2,1)}, u32[]{:S(2)}, u32[]{:S(2)}) collective-permute-start(bf16[1,2,32,16,128]{4,3,2,1,0:T(8,128)(2,1)} %get-tuple-element.106), channel_id=1, source_target_pairs={{0,3},{1,4},{2,5},{3,6},{4,7},{5,0},{6,1},{7,2},{8,11},{9,12},{10,... | collective-permute-start | bytes 786440 | tf_op jit(solution)/shard_map/ppermute | solution.py:586
  7.2 14.0 %collective-permute-start.1 = (bf16[1,2,32,16,128]{4,3,2,1,0:T(8,128)(2,1)}, bf16[1,2,32,16,128]{4,3,2,1,0:T(8,128)(2,1)}, u32[]{:S(2)}, u32[]{:S(2)}) collective-permute-start(bf16[1,2,32,16,128]{4,3,2,1,0:T(8,128)(2,1)} %get-tuple-element.105), channel_id=1, source_target_pairs={{0,2},{1,3},{2,4},{3,5},{4,6},{5,7},{6,0},{7,1},{8,10},{9,11},{10,... | collective-permute-start | bytes 786440 | tf_op jit(solution)/shard_map/ppermute | solution.py:586
  8.4 21.9 %collective-permute-start.3 = (bf16[1,2,32,16,128]{4,3,2,1,0:T(8,128)(2,1)}, bf16[1,2,32,16,128]{4,3,2,1,0:T(8,128)(2,1)}, u32[]{:S(2)}, u32[]{:S(2)}) collective-permute-start(bf16[1,2,32,16,128]{4,3,2,1,0:T(8,128)(2,1)} %get-tuple-element.107), channel_id=1, source_target_pairs={{0,4},{1,5},{2,6},{3,7},{4,0},{5,1},{6,2},{7,3},{8,12},{9,13},{10,... | collective-permute-start | bytes 786440 | tf_op jit(solution)/shard_map/ppermute | solution.py:586
  8.6 21.7 %collective-permute-start.5 = (bf16[1,2,32,16,128]{4,3,2,1,0:T(8,128)(2,1)}, bf16[1,2,32,16,128]{4,3,2,1,0:T(8,128)(2,1)}, u32[]{:S(2)}, u32[]{:S(2)}) collective-permute-start(bf16[1,2,32,16,128]{4,3,2,1,0:T(8,128)(2,1)} %get-tuple-element.109), channel_id=1, source_target_pairs={{0,6},{1,7},{2,0},{3,1},{4,2},{5,3},{6,4},{7,5},{8,14},{9,15},{10,... | collective-permute-start | bytes 786440 | tf_op jit(solution)/shard_map/ppermute | solution.py:586
  14.5 17.6 %collective-permute-start = (bf16[1,2,32,16,128]{4,3,2,1,0:T(8,128)(2,1)}, bf16[1,2,32,16,128]{4,3,2,1,0:T(8,128)(2,1)}, u32[]{:S(2)}, u32[]{:S(2)}) collective-permute-start(bf16[1,2,32,16,128]{4,3,2,1,0:T(8,128)(2,1)} %get-tuple-element.104), channel_id=1, source_target_pairs={{0,1},{1,2},{2,3},{3,4},{4,5},{5,6},{6,7},{7,0},{8,9},{9,10},{10,1... | collective-permute-start | bytes 786440 | tf_op jit(solution)/shard_map/ppermute | solution.py:586
  21.2 11.0 %collective-permute-start.4 = (bf16[1,2,32,16,128]{4,3,2,1,0:T(8,128)(2,1)}, bf16[1,2,32,16,128]{4,3,2,1,0:T(8,128)(2,1)}, u32[]{:S(2)}, u32[]{:S(2)}) collective-permute-start(bf16[1,2,32,16,128]{4,3,2,1,0:T(8,128)(2,1)} %get-tuple-element.108), channel_id=1, source_target_pairs={{0,5},{1,6},{2,7},{3,0},{4,1},{5,2},{6,3},{7,4},{8,13},{9,14},{10,... | collective-permute-start | bytes 786440 | tf_op jit(solution)/shard_map/ppermute | solution.py:586
  21.2 13.0 %collective-permute-start.6 = (bf16[1,2,32,16,128]{4,3,2,1,0:T(8,128)(2,1)}, bf16[1,2,32,16,128]{4,3,2,1,0:T(8,128)(2,1)}, u32[]{:S(2)}, u32[]{:S(2)}) collective-permute-start(bf16[1,2,32,16,128]{4,3,2,1,0:T(8,128)(2,1)} %get-tuple-element.110), channel_id=1, source_target_pairs={{0,7},{1,0},{2,1},{3,2},{4,3},{5,4},{6,5},{7,6},{8,15},{9,8},{10,9... | collective-permute-start | bytes 786440 | tf_op jit(solution)/shard_map/ppermute | solution.py:586
  30.3 16.3 %collective-permute-start.7 = (bf16[1,2,32,16,128]{4,3,2,1,0:T(8,128)(2,1)}, bf16[1,2,32,16,128]{4,3,2,1,0:T(8,128)(2,1)}, u32[]{:S(2)}, u32[]{:S(2)}) collective-permute-start(bf16[1,2,32,16,128]{4,3,2,1,0:T(8,128)(2,1)} %get-tuple-element.112), channel_id=1, source_target_pairs={{0,1},{1,2},{2,3},{3,4},{4,5},{5,6},{6,7},{7,0},{8,9},{9,10},{10,1... | collective-permute-start | bytes 786440 | tf_op jit(solution)/shard_map/ppermute | solution.py:586
  30.3 16.4 %collective-permute-start.8 = (bf16[1,2,32,16,128]{4,3,2,1,0:T(8,128)(2,1)}, bf16[1,2,32,16,128]{4,3,2,1,0:T(8,128)(2,1)}, u32[]{:S(2)}, u32[]{:S(2)}) collective-permute-start(bf16[1,2,32,16,128]{4,3,2,1,0:T(8,128)(2,1)} %get-tuple-element.113), channel_id=1, source_target_pairs={{0,2},{1,3},{2,4},{3,5},{4,6},{5,7},{6,0},{7,1},{8,10},{9,11},{10,... | collective-permute-start | bytes 786440 | tf_op jit(solution)/shard_map/ppermute | solution.py:586
  32.1 34.1 %collective-permute-start.9 = (bf16[1,2,32,16,128]{4,3,2,1,0:T(8,128)(2,1)}, bf16[1,2,32,16,128]{4,3,2,1,0:T(8,128)(2,1)}, u32[]{:S(2)}, u32[]{:S(2)}) collective-permute-start(bf16[1,2,32,16,128]{4,3,2,1,0:T(8,128)(2,1)} %get-tuple-element.114), channel_id=1, source_target_pairs={{0,3},{1,4},{2,5},{3,6},{4,7},{5,0},{6,1},{7,2},{8,11},{9,12},{10,... | collective-permute-start | bytes 786440 | tf_op jit(solution)/shard_map/ppermute | solution.py:586
  32.2 47.9 %collective-permute-start.10 = (bf16[1,2,32,16,128]{4,3,2,1,0:T(8,128)(2,1)}, bf16[1,2,32,16,128]{4,3,2,1,0:T(8,128)(2,1)}, u32[]{:S(2)}, u32[]{:S(2)}) collective-permute-start(bf16[1,2,32,16,128]{4,3,2,1,0:T(8,128)(2,1)} %get-tuple-element.115), channel_id=1, source_target_pairs={{0,4},{1,5},{2,6},{3,7},{4,0},{5,1},{6,2},{7,3},{8,12},{9,13},{10,... | collective-permute-start | bytes 786440 | tf_op jit(solution)/shard_map/ppermute | solution.py:586
  34.2 46.2 %collective-permute-start.11 = (bf16[1,2,32,16,128]{4,3,2,1,0:T(8,128)(2,1)}, bf16[1,2,32,16,128]{4,3,2,1,0:T(8,128)(2,1)}, u32[]{:S(2)}, u32[]{:S(2)}) collective-permute-start(bf16[1,2,32,16,128]{4,3,2,1,0:T(8,128)(2,1)} %get-tuple-element.116), channel_id=1, source_target_pairs={{0,5},{1,6},{2,7},{3,0},{4,1},{5,2},{6,3},{7,4},{8,13},{9,14},{10,... | collective-permute-start | bytes 786440 | tf_op jit(solution)/shard_map/ppermute | solution.py:586
  46.6 46.6 %collective-permute-start.21 = (bf16[1,2,32,32,128]{4,3,2,1,0:T(8,128)(2,1)}, bf16[1,2,32,32,128]{4,3,2,1,0:T(8,128)(2,1)}, u32[]{:S(2)}, u32[]{:S(2)}) collective-permute-start(bf16[1,2,32,32,128]{4,3,2,1,0:T(8,128)(2,1)} %get-tuple-element.132), channel_id=1, source_target_pairs={{0,1},{1,2},{2,3},{3,4},{4,5},{5,6},{6,7},{7,0},{8,9},{9,10},{10,1... | collective-permute-start | bytes 1572872 | tf_op jit(solution)/shard_map/ppermute | solution.py:586
  46.7 47.2 %collective-permute-start.22 = (bf16[1,2,32,32,128]{4,3,2,1,0:T(8,128)(2,1)}, bf16[1,2,32,32,128]{4,3,2,1,0:T(8,128)(2,1)}, u32[]{:S(2)}, u32[]{:S(2)}) collective-permute-start(bf16[1,2,32,32,128]{4,3,2,1,0:T(8,128)(2,1)} %get-tuple-element.133), channel_id=1, source_target_pairs={{0,2},{1,3},{2,4},{3,5},{4,6},{5,7},{6,0},{7,1},{8,10},{9,11},{10,... | collective-permute-start | bytes 1572872 | tf_op jit(solution)/shard_map/ppermute | solution.py:586
  66.3 27.6 %collective-permute-start.23 = (bf16[1,2,32,32,128]{4,3,2,1,0:T(8,128)(2,1)}, bf16[1,2,32,32,128]{4,3,2,1,0:T(8,128)(2,1)}, u32[]{:S(2)}, u32[]{:S(2)}) collective-permute-start(bf16[1,2,32,32,128]{4,3,2,1,0:T(8,128)(2,1)} %get-tuple-element.134), channel_id=1, source_target_pairs={{0,3},{1,4},{2,5},{3,6},{4,7},{5,0},{6,1},{7,2},{8,11},{9,12},{10,... | collective-permute-start | bytes 1572872 | tf_op jit(solution)/shard_map/ppermute | solution.py:586
  80.0 10.0 %collective-permute-start.12 = (bf16[1,2,32,16,128]{4,3,2,1,0:T(8,128)(2,1)}, bf16[1,2,32,16,128]{4,3,2,1,0:T(8,128)(2,1)}, u32[]{:S(2)}, u32[]{:S(2)}) collective-permute-start(bf16[1,2,32,16,128]{4,3,2,1,0:T(8,128)(2,1)} %get-tuple-element.117), channel_id=1, source_target_pairs={{0,6},{1,7},{2,0},{3,1},{4,2},{5,3},{6,4},{7,5},{8,14},{9,15},{10,... | collective-permute-start | bytes 786440 | tf_op jit(solution)/shard_map/ppermute | solution.py:586
  80.4 9.7 %collective-permute-start.13 = (bf16[1,2,32,16,128]{4,3,2,1,0:T(8,128)(2,1)}, bf16[1,2,32,16,128]{4,3,2,1,0:T(8,128)(2,1)}, u32[]{:S(2)}, u32[]{:S(2)}) collective-permute-start(bf16[1,2,32,16,128]{4,3,2,1,0:T(8,128)(2,1)} %get-tuple-element.118), channel_id=1, source_target_pairs={{0,7},{1,0},{2,1},{3,2},{4,3},{5,4},{6,5},{7,6},{8,15},{9,8},{10,9... | collective-permute-start | bytes 786440 | tf_op jit(solution)/shard_map/ppermute | solution.py:586
  90.0 24.2 %collective-permute-start.24 = (bf16[1,2,32,32,128]{4,3,2,1,0:T(8,128)(2,1)}, bf16[1,2,32,32,128]{4,3,2,1,0:T(8,128)(2,1)}, u32[]{:S(2)}, u32[]{:S(2)}) collective-permute-start(bf16[1,2,32,32,128]{4,3,2,1,0:T(8,128)(2,1)} %get-tuple-element.135), channel_id=1, source_target_pairs={{0,4},{1,5},{2,6},{3,7},{4,0},{5,1},{6,2},{7,3},{8,12},{9,13},{10,... | collective-permute-start | bytes 1572872 | tf_op jit(solution)/shard_map/ppermute | solution.py:586
  90.1 36.6 %collective-permute-start.25 = (bf16[1,2,32,32,128]{4,3,2,1,0:T(8,128)(2,1)}, bf16[1,2,32,32,128]{4,3,2,1,0:T(8,128)(2,1)}, u32[]{:S(2)}, u32[]{:S(2)}) collective-permute-start(bf16[1,2,32,32,128]{4,3,2,1,0:T(8,128)(2,1)} %get-tuple-element.136), channel_id=1, source_target_pairs={{0,5},{1,6},{2,7},{3,0},{4,1},{5,2},{6,3},{7,4},{8,13},{9,14},{10,... | collective-permute-start | bytes 1572872 | tf_op jit(solution)/shard_map/ppermute | solution.py:586
  93.2 35.2 %collective-permute-start.26 = (bf16[1,2,32,32,128]{4,3,2,1,0:T(8,128)(2,1)}, bf16[1,2,32,32,128]{4,3,2,1,0:T(8,128)(2,1)}, u32[]{:S(2)}, u32[]{:S(2)}) collective-permute-start(bf16[1,2,32,32,128]{4,3,2,1,0:T(8,128)(2,1)} %get-tuple-element.137), channel_id=1, source_target_pairs={{0,6},{1,7},{2,0},{3,1},{4,2},{5,3},{6,4},{7,5},{8,14},{9,15},{10,... | collective-permute-start | bytes 1572872 | tf_op jit(solution)/shard_map/ppermute | solution.py:586
  93.8 36.1 %collective-permute-start.27 = (bf16[1,2,32,32,128]{4,3,2,1,0:T(8,128)(2,1)}, bf16[1,2,32,32,128]{4,3,2,1,0:T(8,128)(2,1)}, u32[]{:S(2)}, u32[]{:S(2)}) collective-permute-start(bf16[1,2,32,32,128]{4,3,2,1,0:T(8,128)(2,1)} %get-tuple-element.138), channel_id=1, source_target_pairs={{0,7},{1,0},{2,1},{3,2},{4,3},{5,4},{6,5},{7,6},{8,15},{9,8},{10,9... | collective-permute-start | bytes 1572872 | tf_op jit(solution)/shard_map/ppermute | solution.py:586
  93.8 39.2 %collective-permute-start.28 = (bf16[1,2,32,32,128]{4,3,2,1,0:T(8,128)(2,1)}, bf16[1,2,32,32,128]{4,3,2,1,0:T(8,128)(2,1)}, u32[]{:S(2)}, u32[]{:S(2)}) collective-permute-start(bf16[1,2,32,32,128]{4,3,2,1,0:T(8,128)(2,1)} %get-tuple-element.152), channel_id=1, source_target_pairs={{0,1},{1,2},{2,3},{3,4},{4,5},{5,6},{6,7},{7,0},{8,9},{9,10},{10,1... | collective-permute-start | bytes 1572872 | tf_op jit(solution)/shard_map/ppermute | solution.py:586
  114.2 43.4 %collective-permute-start.29 = (bf16[1,2,32,32,128]{4,3,2,1,0:T(8,128)(2,1)}, bf16[1,2,32,32,128]{4,3,2,1,0:T(8,128)(2,1)}, u32[]{:S(2)}, u32[]{:S(2)}) collective-permute-start(bf16[1,2,32,32,128]{4,3,2,1,0:T(8,128)(2,1)} %get-tuple-element.153), channel_id=1, source_target_pairs={{0,2},{1,3},{2,4},{3,5},{4,6},{5,7},{6,0},{7,1},{8,10},{9,11},{10,... | collective-permute-start | bytes 1572872 | tf_op jit(solution)/shard_map/ppermute | solution.py:586
  126.7 31.0 %collective-permute-start.30 = (bf16[1,2,32,32,128]{4,3,2,1,0:T(8,128)(2,1)}, bf16[1,2,32,32,128]{4,3,2,1,0:T(8,128)(2,1)}, u32[]{:S(2)}, u32[]{:S(2)}) collective-permute-start(bf16[1,2,32,32,128]{4,3,2,1,0:T(8,128)(2,1)} %get-tuple-element.154), channel_id=1, source_target_pairs={{0,3},{1,4},{2,5},{3,6},{4,7},{5,0},{6,1},{7,2},{8,11},{9,12},{10,... | collective-permute-start | bytes 1572872 | tf_op jit(solution)/shard_map/ppermute | solution.py:586
  128.4 44.3 %collective-permute-start.31 = (bf16[1,2,32,32,128]{4,3,2,1,0:T(8,128)(2,1)}, bf16[1,2,32,32,128]{4,3,2,1,0:T(8,128)(2,1)}, u32[]{:S(2)}, u32[]{:S(2)}) collective-permute-start(bf16[1,2,32,32,128]{4,3,2,1,0:T(8,128)(2,1)} %get-tuple-element.155), channel_id=1, source_target_pairs={{0,4},{1,5},{2,6},{3,7},{4,0},{5,1},{6,2},{7,3},{8,12},{9,13},{10,... | collective-permute-start | bytes 1572872 | tf_op jit(solution)/shard_map/ppermute | solution.py:586
  129.9 49.2 %collective-permute-start.32 = (bf16[1,2,32,32,128]{4,3,2,1,0:T(8,128)(2,1)}, bf16[1,2,32,32,128]{4,3,2,1,0:T(8,128)(2,1)}, u32[]{:S(2)}, u32[]{:S(2)}) collective-permute-start(bf16[1,2,32,32,128]{4,3,2,1,0:T(8,128)(2,1)} %get-tuple-element.156), channel_id=1, source_target_pairs={{0,5},{1,6},{2,7},{3,0},{4,1},{5,2},{6,3},{7,4},{8,13},{9,14},{10,... | collective-permute-start | bytes 1572872 | tf_op jit(solution)/shard_map/ppermute | solution.py:586
  133.0 46.1 %collective-permute-start.33 = (bf16[1,2,32,32,128]{4,3,2,1,0:T(8,128)(2,1)}, bf16[1,2,32,32,128]{4,3,2,1,0:T(8,128)(2,1)}, u32[]{:S(2)}, u32[]{:S(2)}) collective-permute-start(bf16[1,2,32,32,128]{4,3,2,1,0:T(8,128)(2,1)} %get-tuple-element.157), channel_id=1, source_target_pairs={{0,6},{1,7},{2,0},{3,1},{4,2},{5,3},{6,4},{7,5},{8,14},{9,15},{10,... | collective-permute-start | bytes 1572872 | tf_op jit(solution)/shard_map/ppermute | solution.py:586
  157.6 44.6 %collective-permute-start.34 = (bf16[1,2,32,32,128]{4,3,2,1,0:T(8,128)(2,1)}, bf16[1,2,32,32,128]{4,3,2,1,0:T(8,128)(2,1)}, u32[]{:S(2)}, u32[]{:S(2)}) collective-permute-start(bf16[1,2,32,32,128]{4,3,2,1,0:T(8,128)(2,1)} %get-tuple-element.158), channel_id=1, source_target_pairs={{0,7},{1,0},{2,1},{3,2},{4,3},{5,4},{6,5},{7,6},{8,15},{9,8},{10,9... | collective-permute-start | bytes 1572872 | tf_op jit(solution)/shard_map/ppermute | solution.py:586
  157.7 47.5 %collective-permute-start.35 = (bf16[1,2,32,32,128]{4,3,2,1,0:T(8,128)(2,1)}, bf16[1,2,32,32,128]{4,3,2,1,0:T(8,128)(2,1)}, u32[]{:S(2)}, u32[]{:S(2)}) collective-permute-start(bf16[1,2,32,32,128]{4,3,2,1,0:T(8,128)(2,1)} %get-tuple-element.169), channel_id=1, source_target_pairs={{0,1},{1,2},{2,3},{3,4},{4,5},{5,6},{6,7},{7,0},{8,9},{9,10},{10,1... | collective-permute-start | bytes 1572872 | tf_op jit(solution)/shard_map/ppermute | solution.py:586
  172.8 40.2 %collective-permute-start.36 = (bf16[1,2,32,32,128]{4,3,2,1,0:T(8,128)(2,1)}, bf16[1,2,32,32,128]{4,3,2,1,0:T(8,128)(2,1)}, u32[]{:S(2)}, u32[]{:S(2)}) collective-permute-start(bf16[1,2,32,32,128]{4,3,2,1,0:T(8,128)(2,1)} %get-tuple-element.170), channel_id=1, source_target_pairs={{0,2},{1,3},{2,4},{3,5},{4,6},{5,7},{6,0},{7,1},{8,10},{9,11},{10,... | collective-permute-start | bytes 1572872 | tf_op jit(solution)/shard_map/ppermute | solution.py:586
  179.1 33.8 %collective-permute-start.37 = (bf16[1,2,32,32,128]{4,3,2,1,0:T(8,128)(2,1)}, bf16[1,2,32,32,128]{4,3,2,1,0:T(8,128)(2,1)}, u32[]{:S(2)}, u32[]{:S(2)}) collective-permute-start(bf16[1,2,32,32,128]{4,3,2,1,0:T(8,128)(2,1)} %get-tuple-element.171), channel_id=1, source_target_pairs={{0,3},{1,4},{2,5},{3,6},{4,7},{5,0},{6,1},{7,2},{8,11},{9,12},{10,... | collective-permute-start | bytes 1572872 | tf_op jit(solution)/shard_map/ppermute | solution.py:586
  179.1 35.6 %collective-permute-start.38 = (bf16[1,2,32,32,128]{4,3,2,1,0:T(8,128)(2,1)}, bf16[1,2,32,32,128]{4,3,2,1,0:T(8,128)(2,1)}, u32[]{:S(2)}, u32[]{:S(2)}) collective-permute-start(bf16[1,2,32,32,128]{4,3,2,1,0:T(8,128)(2,1)} %get-tuple-element.172), channel_id=1, source_target_pairs={{0,4},{1,5},{2,6},{3,7},{4,0},{5,1},{6,2},{7,3},{8,12},{9,13},{10,... | collective-permute-start | bytes 1572872 | tf_op jit(solution)/shard_map/ppermute | solution.py:586
  202.2 33.2 %collective-permute-start.39 = (bf16[1,2,32,32,128]{4,3,2,1,0:T(8,128)(2,1)}, bf16[1,2,32,32,128]{4,3,2,1,0:T(8,128)(2,1)}, u32[]{:S(2)}, u32[]{:S(2)}) collective-permute-start(bf16[1,2,32,32,128]{4,3,2,1,0:T(8,128)(2,1)} %get-tuple-element.173), channel_id=1, source_target_pairs={{0,5},{1,6},{2,7},{3,0},{4,1},{5,2},{6,3},{7,4},{8,13},{9,14},{10,... | collective-permute-start | bytes 1572872 | tf_op jit(solution)/shard_map/ppermute | solution.py:586
  205.1 39.2 %collective-permute-start.40 = (bf16[1,2,32,32,128]{4,3,2,1,0:T(8,128)(2,1)}, bf16[1,2,32,32,128]{4,3,2,1,0:T(8,128)(2,1)}, u32[]{:S(2)}, u32[]{:S(2)}) collective-permute-start(bf16[1,2,32,32,128]{4,3,2,1,0:T(8,128)(2,1)} %get-tuple-element.174), channel_id=1, source_target_pairs={{0,6},{1,7},{2,0},{3,1},{4,2},{5,3},{6,4},{7,5},{8,14},{9,15},{10,... | collective-permute-start | bytes 1572872 | tf_op jit(solution)/shard_map/ppermute | solution.py:586
  212.9 31.4 %collective-permute-start.41 = (bf16[1,2,32,32,128]{4,3,2,1,0:T(8,128)(2,1)}, bf16[1,2,32,32,128]{4,3,2,1,0:T(8,128)(2,1)}, u32[]{:S(2)}, u32[]{:S(2)}) collective-permute-start(bf16[1,2,32,32,128]{4,3,2,1,0:T(8,128)(2,1)} %get-tuple-element.175), channel_id=1, source_target_pairs={{0,7},{1,0},{2,1},{3,2},{4,3},{5,4},{6,5},{7,6},{8,15},{9,8},{10,9... | collective-permute-start | bytes 1572872 | tf_op jit(solution)/shard_map/ppermute | solution.py:586
  213.0 31.4 %collective-permute-start.14 = (bf16[2,1024,128]{2,1,0:T(8,128)(2,1)}, bf16[2,1024,128]{2,1,0:T(8,128)(2,1)}, u32[]{:S(2)}, u32[]{:S(2)}) collective-permute-start(bf16[2,1024,128]{2,1,0:T(8,128)(2,1)} %get-tuple-element.121), channel_id=1, source_target_pairs={{0,1},{1,2},{2,3},{3,4},{4,5},{5,6},{6,7},{7,0},{8,9},{9,10},{10,1... | collective-permute-start | bytes 1572872 | tf_op jit(solution)/shard_map/ppermute | solution.py:586
  214.7 43.9 %collective-permute-start.15 = (bf16[2,1024,128]{2,1,0:T(8,128)(2,1)}, bf16[2,1024,128]{2,1,0:T(8,128)(2,1)}, u32[]{:S(2)}, u32[]{:S(2)}) collective-permute-start(bf16[2,1024,128]{2,1,0:T(8,128)(2,1)} %get-tuple-element.122), channel_id=1, source_target_pairs={{0,2},{1,3},{2,4},{3,5},{4,6},{5,7},{6,0},{7,1},{8,10},{9,11},{10,... | collective-permute-start | bytes 1572872 | tf_op jit(solution)/shard_map/ppermute | solution.py:586
  235.4 44.0 %collective-permute-start.16 = (bf16[2,1024,128]{2,1,0:T(8,128)(2,1)}, bf16[2,1024,128]{2,1,0:T(8,128)(2,1)}, u32[]{:S(2)}, u32[]{:S(2)}) collective-permute-start(bf16[2,1024,128]{2,1,0:T(8,128)(2,1)} %get-tuple-element.123), channel_id=1, source_target_pairs={{0,3},{1,4},{2,5},{3,6},{4,7},{5,0},{6,1},{7,2},{8,11},{9,12},{10,... | collective-permute-start | bytes 1572872 | tf_op jit(solution)/shard_map/ppermute | solution.py:586
  244.3 37.2 %collective-permute-start.17 = (bf16[2,1024,128]{2,1,0:T(8,128)(2,1)}, bf16[2,1024,128]{2,1,0:T(8,128)(2,1)}, u32[]{:S(2)}, u32[]{:S(2)}) collective-permute-start(bf16[2,1024,128]{2,1,0:T(8,128)(2,1)} %get-tuple-element.124), channel_id=1, source_target_pairs={{0,4},{1,5},{2,6},{3,7},{4,0},{5,1},{6,2},{7,3},{8,12},{9,13},{10,... | collective-permute-start | bytes 1572872 | tf_op jit(solution)/shard_map/ppermute | solution.py:586
  244.3 37.3 %collective-permute-start.18 = (bf16[2,1024,128]{2,1,0:T(8,128)(2,1)}, bf16[2,1024,128]{2,1,0:T(8,128)(2,1)}, u32[]{:S(2)}, u32[]{:S(2)}) collective-permute-start(bf16[2,1024,128]{2,1,0:T(8,128)(2,1)} %get-tuple-element.125), channel_id=1, source_target_pairs={{0,5},{1,6},{2,7},{3,0},{4,1},{5,2},{6,3},{7,4},{8,13},{9,14},{10,... | collective-permute-start | bytes 1572872 | tf_op jit(solution)/shard_map/ppermute | solution.py:586
  244.4 37.2 %collective-permute-start.19 = (bf16[2,1024,128]{2,1,0:T(8,128)(2,1)}, bf16[2,1024,128]{2,1,0:T(8,128)(2,1)}, u32[]{:S(2)}, u32[]{:S(2)}) collective-permute-start(bf16[2,1024,128]{2,1,0:T(8,128)(2,1)} %get-tuple-element.126), channel_id=1, source_target_pairs={{0,6},{1,7},{2,0},{3,1},{4,2},{5,3},{6,4},{7,5},{8,14},{9,15},{10,... | collective-permute-start | bytes 1572872 | tf_op jit(solution)/shard_map/ppermute | solution.py:586
  258.6 23.0 %collective-permute-start.20 = (bf16[2,1024,128]{2,1,0:T(8,128)(2,1)}, bf16[2,1024,128]{2,1,0:T(8,128)(2,1)}, u32[]{:S(2)}, u32[]{:S(2)}) collective-permute-start(bf16[2,1024,128]{2,1,0:T(8,128)(2,1)} %get-tuple-element.127), channel_id=1, source_target_pairs={{0,7},{1,0},{2,1},{3,2},{4,3},{5,4},{6,5},{7,6},{8,15},{9,8},{10,9... | collective-permute-start | bytes 1572872 | tf_op jit(solution)/shard_map/ppermute | solution.py:586
